TPU v7x, 32 devices: a whole 2x2x4 slice. The times are simulated.
32 devices in a mesh: pairs: 16 (over z, y, core), mod: 2 (over x).
Axes of the slice: x: 2, y: 2, z: 4, core: 2. Of those that a mesh axis runs over, the one named last changes fastest.
Arguments:
- tokens: bfloat16 [64, 280, 768], P('pairs', 'mod'), may hold values from -6 to 6
- patch_counts: int32 [64], P('pairs'), may hold values from 100 to 240, as said below
- token_mask: int32 [64, 280], P('pairs', 'mod'), may hold values from 0 to 1, as said below
- ln1_gain: float32 [768], replicated, may hold values from 0.5 to 1.5
- ln1_bias: float32 [768], replicated, may hold values from -1 to 1
- qkv_weight: bfloat16 [768, 2304], replicated, may hold values from -0.3125 to 0.3125
- qv_bias: float32 [1536], replicated, may hold values from -1 to 1
- out_weight: bfloat16 [768, 768], replicated, may hold values from -0.625 to 0.625
- out_bias: float32 [768], replicated, may hold values from -1 to 1
- ln2_gain: float32 [768], replicated, may hold values from 0.5 to 1.5
- ln2_bias: float32 [768], replicated, may hold values from -1 to 1
- up_weight: bfloat16 [768, 3072], replicated, may hold values from -0.21875 to 0.21875
- up_bias: float32 [3072], replicated, may hold values from -1 to 1
- down_weight: bfloat16 [3072, 768], replicated, may hold values from -0.15625 to 0.15625
- down_bias: float32 [768], replicated, may hold values from -1 to 1
- cotangent: bfloat16 [64, 280, 768], P('pairs', 'mod'), may hold values from -6 to 6
Outputs:
- layer_out: bfloat16 [64, 280, 768], P('pairs', 'mod')
- input_grad: bfloat16 [64, 280, 768], P('pairs', 'mod')
- ln1_gain_grad: float32 [768], P(('pairs', 'mod'))
- ln1_bias_grad: float32 [768], P(('pairs', 'mod'))
- qkv_weight_grad: float32 [768, 2304], P(('pairs', 'mod'))
- qv_bias_grad: float32 [1536], P(('pairs', 'mod'))
- out_weight_grad: float32 [768, 768], P(('pairs', 'mod'))
- out_bias_grad: float32 [768], P(('pairs', 'mod'))
- ln2_gain_grad: float32 [768], P(('pairs', 'mod'))
- ln2_bias_grad: float32 [768], P(('pairs', 'mod'))
- up_weight_grad: float32 [768, 3072], P(('pairs', 'mod'))
- up_bias_grad: float32 [3072], P(('pairs', 'mod'))
- down_weight_grad: float32 [3072, 768], P(('pairs', 'mod'))
- down_bias_grad: float32 [768], P(('pairs', 'mod'))
Inputs may be any that keep to these rules, and one draw needn't show every extreme that they name: `patch_counts`: each pair's number of patches; some pair has 240 and some 100. `token_mask`: row 0 of every pair is 1; the text rows of a pair are 1 up to a drawn text length and 0 after it.
All inputs are finite; a program needn't handle non-finite values.
Results may differ from a plain program's by a relative error of at most 0.015.
Values may be sent and summed in bfloat16 or wider, within the bound.
No kernel may reach another device: no remote copies, remote signals or barrier semaphores. Data moves between devices by JAX's collectives and lax.ppermute only.
A program may use at most 192 MiB of HBM per device.

v0:
```python
from functools import partial

import jax
import jax.numpy as jnp
from jax import lax
from jax.sharding import PartitionSpec as P

HEAD_DIM = 64
TXT = 40


EPS = 1e-06
MASKED = -1e30


def from_partner(block, axis, bit):
    count = lax.axis_size(axis)
    route = []
    for low in range(count):
        high = low | 1 << bit
        if high != low and high < count:
            route += [(low, high), (high, low)]
    return lax.ppermute(block, axis, route)


def norm_rows(rows_in, gain, shift):
    center = rows_in - jnp.mean(rows_in, axis=-1, keepdims=True)
    spread = jnp.mean(center * center, axis=-1, keepdims=True)
    return center * lax.rsqrt(spread + EPS) * gain + shift


def rows_times_t(left, right):
    return lax.dot_general(
        left, right, (((1,), (1,)), ((), ())), preferred_element_type=jnp.float32
    )


def t_times_rows(left, right):
    return lax.dot_general(
        left, right, (((0,), (0,)), ((), ())), preferred_element_type=jnp.float32
    )


def layer_pass(tokens, cotangent, live, own_ok, params):
    (
        ln1_gain,
        ln1_bias,
        qkv_weight,
        qv_bias,
        out_weight,
        out_bias,
        ln2_gain,
        ln2_bias,
        up_weight,
        up_bias,
        down_weight,
        down_bias,
    ) = params
    pairs_here, half, width = tokens.shape
    head_size = HEAD_DIM
    heads = width // head_size
    flat = pairs_here * half
    scale = head_size ** (-0.5)
    live_flat = live.reshape(flat, 1)
    inputs = tokens.reshape(flat, width).astype(jnp.float32)
    first_norm = norm_rows(inputs, ln1_gain, ln1_bias).astype(jnp.bfloat16)
    projected = jnp.dot(first_norm, qkv_weight, preferred_element_type=jnp.float32)
    queries = (projected[:, :width] + qv_bias[:width]).astype(jnp.bfloat16)
    own_keys = projected[:, width : 2 * width].astype(jnp.bfloat16)
    own_values = (projected[:, 2 * width :] + qv_bias[width:]).astype(jnp.bfloat16)
    shape4 = (pairs_here, half, heads, head_size)
    query_heads = queries.reshape(shape4)
    ok_wire = own_ok.astype(jnp.bfloat16)
    far_keys, far_values, far_ok = from_partner((own_keys, own_values, ok_wire), "mod", 0)
    key_heads = jnp.concatenate([own_keys.reshape(shape4), far_keys.reshape(shape4)], axis=1)
    value_heads = jnp.concatenate([own_values.reshape(shape4), far_values.reshape(shape4)], axis=1)
    key_ok = jnp.concatenate([own_ok, far_ok > 0], axis=1)
    scores = (
        jnp.einsum("pqhd,pkhd->phqk", query_heads, key_heads, preferred_element_type=jnp.float32)
        * scale
    )
    scores = jnp.where(key_ok[:, None, None, :], scores, MASKED)
    probs = jax.nn.softmax(scores, axis=-1)
    probs_low = probs.astype(jnp.bfloat16)
    mixed = jnp.einsum(
        "phqk,pkhd->pqhd", probs_low, value_heads, preferred_element_type=jnp.float32
    )
    mixed = mixed.reshape(flat, width).astype(jnp.bfloat16)
    attended = inputs + jnp.dot(mixed, out_weight, preferred_element_type=jnp.float32) + out_bias
    second_norm = norm_rows(attended, ln2_gain, ln2_bias).astype(jnp.bfloat16)
    pre_act = jnp.dot(second_norm, up_weight, preferred_element_type=jnp.float32) + up_bias
    hidden = jax.nn.gelu(pre_act, approximate=False).astype(jnp.bfloat16)
    final = attended + jnp.dot(hidden, down_weight, preferred_element_type=jnp.float32) + down_bias
    layer_out = jnp.where(live_flat, final, 0.0).astype(jnp.bfloat16).reshape(tokens.shape)
    grad_y = jnp.where(live_flat, cotangent.reshape(flat, width), jnp.zeros((), jnp.bfloat16))
    down_weight_grad = t_times_rows(hidden, grad_y)
    down_bias_grad = jnp.sum(grad_y.astype(jnp.float32), axis=0)
    grad_hidden = rows_times_t(grad_y, down_weight)
    _, gelu_pull = jax.vjp(partial(jax.nn.gelu, approximate=False), pre_act)
    grad_pre = gelu_pull(grad_hidden)[0].astype(jnp.bfloat16)
    up_weight_grad = t_times_rows(second_norm, grad_pre)
    up_bias_grad = jnp.sum(grad_pre.astype(jnp.float32), axis=0)
    grad_second = rows_times_t(grad_pre, up_weight)
    _, second_pull = jax.vjp(norm_rows, attended, ln2_gain, ln2_bias)
    grad_through, ln2_gain_grad, ln2_bias_grad = second_pull(grad_second)
    grad_attended = grad_y.astype(jnp.float32) + grad_through
    grad_branch = grad_attended.astype(jnp.bfloat16)
    out_weight_grad = t_times_rows(mixed, grad_branch)
    out_bias_grad = jnp.sum(grad_branch.astype(jnp.float32), axis=0)
    grad_mixed = rows_times_t(grad_branch, out_weight).astype(jnp.bfloat16).reshape(shape4)
    grad_probs = jnp.einsum(
        "pqhd,pkhd->phqk", grad_mixed, value_heads, preferred_element_type=jnp.float32
    )
    grad_value_heads = jnp.einsum(
        "phqk,pqhd->pkhd", probs_low, grad_mixed, preferred_element_type=jnp.float32
    )
    grad_scores = probs * (grad_probs - jnp.sum(grad_probs * probs, axis=-1, keepdims=True))
    grad_scores = grad_scores.astype(jnp.bfloat16)
    grad_queries = (
        jnp.einsum("phqk,pkhd->pqhd", grad_scores, key_heads, preferred_element_type=jnp.float32)
        * scale
    )
    grad_queries = grad_queries.astype(jnp.bfloat16).reshape(flat, width)
    grad_key_heads = (
        jnp.einsum("phqk,pqhd->pkhd", grad_scores, query_heads, preferred_element_type=jnp.float32)
        * scale
    )
    back_keys, back_values = (
        from_partner(grad_key_heads[:, half:].astype(jnp.bfloat16), "mod", 0).astype(jnp.float32),
        from_partner(grad_value_heads[:, half:].astype(jnp.bfloat16), "mod", 0).astype(jnp.float32),
    )
    grad_keys = (grad_key_heads[:, :half] + back_keys).astype(jnp.bfloat16).reshape(flat, width)
    grad_values = (
        (grad_value_heads[:, :half] + back_values).astype(jnp.bfloat16).reshape(flat, width)
    )
    grad_proj = jnp.concatenate([grad_queries, grad_keys, grad_values], axis=1)
    qkv_weight_grad = t_times_rows(first_norm, grad_proj)
    qv_bias_grad = jnp.concatenate(
        [
            jnp.sum(grad_queries.astype(jnp.float32), axis=0),
            jnp.sum(grad_values.astype(jnp.float32), axis=0),
        ]
    )
    grad_first = rows_times_t(grad_proj, qkv_weight)
    _, first_pull = jax.vjp(norm_rows, inputs, ln1_gain, ln1_bias)
    grad_inputs, ln1_gain_grad, ln1_bias_grad = first_pull(grad_first)
    input_grad = (grad_attended + grad_inputs).astype(jnp.bfloat16).reshape(tokens.shape)
    local_grads = (
        ln1_gain_grad,
        ln1_bias_grad,
        qkv_weight_grad,
        qv_bias_grad,
        out_weight_grad,
        out_bias_grad,
        ln2_gain_grad,
        ln2_bias_grad,
        up_weight_grad,
        up_bias_grad,
        down_weight_grad,
        down_bias_grad,
    )
    return (layer_out, input_grad, local_grads)


def on_device(
    tokens,
    patch_counts,
    token_mask,
    ln1_gain,
    ln1_bias,
    qkv_weight,
    qv_bias,
    out_weight,
    out_bias,
    ln2_gain,
    ln2_bias,
    up_weight,
    up_bias,
    down_weight,
    down_bias,
    cotangent,
):
    params = (
        ln1_gain,
        ln1_bias,
        qkv_weight,
        qv_bias,
        out_weight,
        out_bias,
        ln2_gain,
        ln2_bias,
        up_weight,
        up_bias,
        down_weight,
        down_bias,
    )
    pairs_here, half, width = tokens.shape
    side = lax.axis_index("mod")
    row_ids = side * half + jnp.arange(half, dtype=jnp.int32)
    live = row_ids[None, :] < (TXT + patch_counts)[:, None]
    own_ok = jnp.logical_and(live, token_mask == 1)
    layer_out, input_grad, local_grads = layer_pass(tokens, cotangent, live, own_ok, params)
    summed = (
        lax.psum_scatter(local_grads[0], ("pairs", "mod"), scatter_dimension=0, tiled=True),
        lax.psum_scatter(local_grads[1], ("pairs", "mod"), scatter_dimension=0, tiled=True),
        lax.psum_scatter(local_grads[2], ("pairs", "mod"), scatter_dimension=0, tiled=True),
        lax.psum_scatter(local_grads[3], ("pairs", "mod"), scatter_dimension=0, tiled=True),
        lax.psum_scatter(local_grads[4], ("pairs", "mod"), scatter_dimension=0, tiled=True),
        lax.psum_scatter(local_grads[5], ("pairs", "mod"), scatter_dimension=0, tiled=True),
        lax.psum_scatter(local_grads[6], ("pairs", "mod"), scatter_dimension=0, tiled=True),
        lax.psum_scatter(local_grads[7], ("pairs", "mod"), scatter_dimension=0, tiled=True),
        lax.psum_scatter(local_grads[8], ("pairs", "mod"), scatter_dimension=0, tiled=True),
        lax.psum_scatter(local_grads[9], ("pairs", "mod"), scatter_dimension=0, tiled=True),
        lax.psum_scatter(local_grads[10], ("pairs", "mod"), scatter_dimension=0, tiled=True),
        lax.psum_scatter(local_grads[11], ("pairs", "mod"), scatter_dimension=0, tiled=True),
    )
    return (
        layer_out,
        input_grad,
        summed[0],
        summed[1],
        summed[2],
        summed[3],
        summed[4],
        summed[5],
        summed[6],
        summed[7],
        summed[8],
        summed[9],
        summed[10],
        summed[11],
    )


def solution(mesh):
    placed = (
        P("pairs", "mod", None),
        P("pairs"),
        P("pairs", "mod"),
        P(),
        P(),
        P(),
        P(),
        P(),
        P(),
        P(),
        P(),
        P(),
        P(),
        P(),
        P(),
        P("pairs", "mod", None),
    )
    return jax.shard_map(
        on_device,
        mesh=mesh,
        in_specs=placed,
        out_specs=(
            P("pairs", "mod", None),
            P("pairs", "mod", None),
            P(("pairs", "mod")),
            P(("pairs", "mod")),
            P(("pairs", "mod"), None),
            P(("pairs", "mod")),
            P(("pairs", "mod"), None),
            P(("pairs", "mod")),
            P(("pairs", "mod")),
            P(("pairs", "mod")),
            P(("pairs", "mod"), None),
            P(("pairs", "mod")),
            P(("pairs", "mod"), None),
            P(("pairs", "mod")),
        ),
        check_vma=False,
    )
```

profile of v0, /device:TPU:0, one launch (start us, length us, event | category | flops | bytes accessed | tf_op | source)
XLA Modules:
  0.0 716.9 jit_solution(3449104162630767792)
XLA Ops:
  17.3 2.8 reshape.200
  20.2 3.8 fusion.42
  25.0 2.9 collective-permute-start.2
  31.6 3.9 reshape.203
  35.5 3.9 reshape.201
  39.5 3.9 reshape.205
  43.4 4.5 copy.105
  47.8 4.4 copy.103
  52.3 4.5 copy.98
  61.8 4.0 collective-permute-done.1
  66.0 3.9 reshape.204
  69.9 4.5 copy.104
  74.3 3.9 reshape.202
  78.2 4.6 copy.99
  82.8 7.9 %fusion.29 = f32[4,12,140,280]{3,2,1,0:T(8,128)} fusion(bf16[4,140,12,64]{1,3,2,0:T(8,128)(2,1)} %copy.105, bf16[4,140,12,64]{1,3,2,0:T(8,128)(2,1)} %copy.104, bf16[4,140,12,64]{1,3,2,0:T(8,128)(2,1)} %copy.103), kind=kOutput, calls=%fused_computation.70 | convolution fusion | flops 244285440 | bytes 10106880 | tf_op jit(solution)/shard_map/pqhd,pkhd->phqk/dot_general | solution.py:79
  90.7 14.2 %fusion.52 = (f32[4,12,140]{2,1,0:T(8,128)S(1)}, f32[4,12,140,280]{3,2,1,0:T(8,128)}) fusion(f32[4,12,140,280]{3,2,1,0:T(8,128)} %fusion.29, pred[4,280]{1,0:T(4,128)(4,1)S(1)} %pad_add_fusion), kind=kOutput, calls=%fused_computation.110 | output fusion | flops 11289879 | bytes 15080800 | tf_op jit(solution)/shard_map/sub | solution.py:83
  104.9 5.6 fusion.26
  112.9 3.9 convert_element_type.110
  116.9 3.3 fusion.53
  120.6 22.3 %multiply_convert_fusion.1 = (bf16[560,3072]{1,0:T(8,128)(2,1)}, f32[560,3072]{1,0:T(8,128)}, f32[560,3072]{1,0:T(8,128)}) fusion(f32[3072]{0:T(1024)} %param.28, bf16[768,3072]{1,0:T(8,128)(2,1)} %param.27, f32[560,768]{1,0:T(8,128)S(1)} %get-tuple-element.104, f32[768]{0:T(1024)S(1)} %copy-done.23, f32[768]{0:T(1024)S(1)} %copy-done.22, ...), kind=kOutput, calls=%fused_computation.10 | convolution fusion | flops 2758103040 | bytes 23665024 | tf_op jit(solution)/shard_map/dot_general | solution.py:91
  143.0 8.8 %convert_reduce_fusion = (f32[3072]{0:T(1024)}, bf16[560,3072]{1,0:T(8,128)(2,1)S(1)}) fusion(f32[560,3072]{1,0:T(8,128)} %get-tuple-element.93, bf16[3072,768]{1,0:T(8,128)(2,1)S(1)} %bitcast.43, bf16[560,768]{1,0:T(8,128)(2,1)S(1)} %copy-done.7, pred[560]{0:T(1024)(128)(4,1)S(1)} %copy-done.37, f32[560,3072]{1,0:T(8,128)} %get-tuple-element.105, ...), kind=kOutput, calls=%fused_computation.8 | convolution fusion | flops 2672083968 | bytes 22807088 | tf_op jit(solution)/shard_map/dot_general | solution.py:33
  151.7 3.7 multiply_reduce_fusion.1
  161.1 3.9 reshape.206
  165.0 4.6 copy.109
  169.6 7.9 %fusion.17 = f32[4,280,12,64]{1,3,2,0:T(8,128)} fusion(bf16[4,140,12,64]{1,3,2,0:T(8,128)(2,1)} %copy.109, f32[4,12,140,280]{3,2,1,0:T(8,128)} %get-tuple-element.102, f32[4,12,140]{2,1,0:T(8,128)} %copy-done.24), kind=kOutput, calls=%fused_computation.46 | convolution fusion | flops 244608000 | bytes 11854080 | tf_op jit(solution)/shard_map/phqk,pqhd->pkhd/dot_general | solution.py:114
  177.6 12.3 %multiply_reduce_fusion = (f32[4,12,140]{2,1,0:T(8,128)}, f32[4,12,140,280]{3,2,1,0:T(8,128)}) fusion(f32[4,12,140,280]{3,2,1,0:T(8,128)} %get-tuple-element.102, f32[4,12,140]{2,1,0:T(8,128)S(1)} %copy-done.25, bf16[4,140,12,64]{1,3,2,0:T(8,128)(2,1)S(1)} %copy-done.17, bf16[4,140,12,64]{1,3,2,0:T(8,128)(2,1)S(1)} %copy-done.16, ...), kind=kOutput, calls=%fused_computation.2 | convolution fusion | flops 249923520 | bytes 17687040 | tf_op jit(solution)/shard_map/pqhd,pkhd->phqk/dot_general | solution.py:111
  189.9 2.5 fusion.54
  192.4 3.6 slice.61
  197.9 8.3 %multiply_convert_fusion = bf16[4,12,140,280]{3,2,1,0:T(8,128)(2,1)S(1)} fusion(f32[4,12,140,280]{3,2,1,0:T(8,128)} %get-tuple-element.108, f32[4,12,140]{2,1,0:T(8,128)} %get-tuple-element.107, f32[4,12,140,280]{3,2,1,0:T(8,128)} %get-tuple-element.102, f32[4,12,140]{2,1,0:T(8,128)} %copy-done.24), kind=kLoop, calls=%fused_computation.1 | loop fusion | flops 7526400 | bytes 18869760 | tf_op jit(solution)/shard_map/convert_element_type | solution.py:118
  211.9 3.2 convert_reduce_fusion.2
  217.5 3.9 reshape.196
  223.7 10.0 %collective-permute-done.4 = bf16[4,140,12,64]{1,3,2,0:T(8,128)(2,1)} collective-permute-done((bf16[4,140,12,64]{1,3,2,0:T(8,128)(2,1)}, bf16[4,140,12,64]{1,3,2,0:T(8,128)(2,1)}, u32[]{:S(2)}, u32[]{:S(2)}) %collective-permute-start.4) | collective-permute-done | bytes 860192 | tf_op jit(solution)/shard_map/ppermute | solution.py:23
  233.7 3.5 convert_reduce_fusion.1
  239.6 3.9 reshape.198
  243.5 26.4 %collective-permute-done.3 = bf16[4,140,12,64]{1,3,2,0:T(8,128)(2,1)} collective-permute-done((bf16[4,140,12,64]{1,3,2,0:T(8,128)(2,1)}, bf16[4,140,12,64]{1,3,2,0:T(8,128)(2,1)}, u32[]{:S(2)}, u32[]{:S(2)}) %collective-permute-start.3) | collective-permute-done | bytes 860192 | tf_op jit(solution)/shard_map/ppermute | solution.py:23
  269.9 3.0 fusion.12
  275.3 4.1 reshape.197
  284.1 7.4 %fusion.41 = f32[768,2304]{1,0:T(8,128)} fusion(bf16[560,2304]{0,1:T(8,128)(2,1)} %constant_dynamic-update-slice_fusion, f32[560,768]{1,0:T(8,128)S(1)} %copy-done.9, f32[768]{0:T(1024)S(1)} %copy-done.47, f32[768]{0:T(1024)S(1)} %copy-done.43, f32[560]{0:T(1024)S(1)} %copy-done.32, f32[560]{0:T(1024)S(1)} %copy-done.34), kind=kOutput, calls=%fused_computation.102 | convolution fusion | flops 1983959040 | bytes 11389312 | tf_op jit(solution)/shard_map/dot_general | solution.py:39
  291.5 10.3 %fusion.43 = f32[768,3072]{1,0:T(8,128)} fusion(bf16[560,3072]{1,0:T(8,128)(2,1)} %copy-done.12, f32[560,768]{1,0:T(8,128)} %copy-done.5, f32[768]{0:T(1024)S(1)} %copy-done.23, f32[768]{0:T(1024)S(1)} %copy-done.22, f32[560]{0:T(1024)S(1)} %fusion.32, f32[560]{0:T(1024)S(1)} %broadcast_multiply_fusion.1), kind=kOutput, calls=%fused_computation.104 | convolution fusion | flops 2644561920 | bytes 14608768 | tf_op jit(solution)/shard_map/dot_general | solution.py:39
  302.5 9.8 %fusion.39 = f32[3072,768]{1,0:T(8,128)} fusion(bf16[560,3072]{1,0:T(8,128)(2,1)} %get-tuple-element.92, bf16[560,768]{1,0:T(8,128)(2,1)} %reshape.194, pred[560]{0:T(1024)(128)(4,1)S(1)} %copy-done.38), kind=kOutput, calls=%fused_computation.100 | convolution fusion | flops 2642841600 | bytes 13738544 | tf_op jit(solution)/shard_map/dot_general | solution.py:39
  316.6 7.9 %select_convert_fusion = bf16[560,768]{1,0:T(8,128)(2,1)} fusion(f32[560,768]{1,0:T(8,128)} %copy-done.5, bf16[560,3072]{1,0:T(8,128)(2,1)} %get-tuple-element.92, bf16[3072,768]{1,0:T(8,128)(2,1)} %param.29, f32[768]{0:T(1024)} %param.30, pred[560]{0:T(1024)(128)(4,1)S(1)} %copy-done.38), kind=kOutput, calls=%fused_computation.60 | convolution fusion | flops 2644131840 | bytes 10743344 | tf_op jit(solution)/shard_map/dot_general | solution.py:93
  326.8 2.6 copy.116
  330.8 7.1 multiply_reduce_fusion.2
  337.9 42.7 %all-reduce.8 = (f32[768]{0:T(1024)}, f32[768]{0:T(1024)}, f32[1536]{0:T(1024)}, f32[768]{0:T(1024)}, f32[768]{0:T(1024)}, /*index=5*/f32[768]{0:T(1024)}, f32[3072]{0:T(1024)}, f32[768]{0:T(1024)}) all-reduce(f32[768]{0:T(1024)} %get-tuple-element.72, ...), channel_id=2, replica_groups=mesh['pairs'=16,'mod'=2] {'pairs','mod'}, use_global_device_ids=true, to_apply=%region_12.13.clone | all-reduce | flops 9216 | bytes 73728
  389.0 2.6 fusion.47
  400.3 26.5 %reduce-scatter.5.cloned.1.call-done = f32[24,2304]{1,0:T(8,128)} async-done(((f32[768,2304]{1,0:T(8,128)}), f32[24,2304]{1,0:T(8,128)}) %reduce-scatter.5.cloned.1.call-update) | async-done | bytes 221200 | tf_op jit(solution)/shard_map/reduce_scatter | solution.py:206
  426.9 141.4 %reduce-scatter.9.cloned.1.call-done = f32[24,3072]{1,0:T(8,128)} async-done(((f32[768,3072]{1,0:T(8,128)}), f32[24,3072]{1,0:T(8,128)}) %reduce-scatter.9.cloned.1.call-update) | async-done | bytes 294928 | tf_op jit(solution)/shard_map/reduce_scatter | solution.py:212
  568.3 142.0 %reduce-scatter.11.cloned.1.call-done = f32[96,768]{1,0:T(8,128)} async-done(((f32[3072,768]{1,0:T(8,128)}), f32[96,768]{1,0:T(8,128)}) %reduce-scatter.11.cloned.1.call-update) | async-done | bytes 294928 | tf_op jit(solution)/shard_map/reduce_scatter | solution.py:214
  (180 shorter events, 75.7 us)
Async XLA Ops:
  7.2 13.0 %copy-start = (bf16[768,2304]{1,0:T(8,128)(2,1)S(1)}, bf16[768,2304]{1,0:T(8,128)(2,1)}, u32[]{:S(2)}) copy-start(bf16[768,2304]{1,0:T(8,128)(2,1)} %param.21) | copy-start | bytes 10616836
  7.2 393.1 %reduce-scatter.7.cloned.1.call-start = ((), (), s32[]{:S(2)}) async-start(), calls=%async_computation.5 | async-start | bytes 2433024 | tf_op jit(solution)/shard_map/reduce_scatter | solution.py:208
  7.2 4.9 copy-start.6
  17.2 6.8 copy-start.26
  17.2 6.8 copy-start.31
  20.2 3.8 copy-start.33
  20.2 7.8 %copy-start.41 = (f32[1536]{0:T(1024)S(1)}, f32[1536]{0:T(1024)}, u32[]{:S(2)}) copy-start(f32[1536]{0:T(1024)} %param.22) | copy-start | bytes 18436
  24.0 5.5 copy-start.48
  25.0 4.5 copy-start.42
  25.0 40.9 %collective-permute-start.2 = (bf16[560,768]{1,0:T(8,128)(2,1)}, bf16[560,768]{1,0:T(8,128)(2,1)}, u32[]{:S(2)}, u32[]{:S(2)}) collective-permute-start(bf16[560,768]{1,0:T(8,128)(2,1)} %slice.63), channel_id=1, source_target_pairs={{0,1},{1,0},{2,3},{3,2},{4,5},{5,4},{6,7},{7,6},{8,9},{9,8},{10,11... | collective-permute-start | bytes 2580488 | tf_op jit(solution)/shard_map/ppermute | solution.py:23
  29.5 44.8 %collective-permute-start = (bf16[560,768]{1,0:T(8,128)(2,1)}, bf16[560,768]{1,0:T(8,128)(2,1)}, u32[]{:S(2)}, u32[]{:S(2)}) collective-permute-start(bf16[560,768]{1,0:T(8,128)(2,1)} %get-tuple-element.98), channel_id=1, source_target_pairs={{0,1},{1,0},{2,3},{3,2},{4,5},{5,4},{6,7},{7,6},{8,9},{9,8},{10,11... | collective-permute-start | bytes 2580488 | tf_op jit(solution)/shard_map/ppermute | solution.py:23
  29.6 27.1 %copy-start.35 = (pred[4,140]{1,0:T(4,128)(4,1)}, pred[4,140]{1,0:T(4,128)(4,1)S(1)}, u32[]{:S(2)}) copy-start(pred[4,140]{1,0:T(4,128)(4,1)S(1)} %get-tuple-element.96) | copy-start | bytes 1684
  29.6 36.3 %collective-permute-start.1 = (bf16[4,140]{1,0:T(4,128)(2,1)S(1)}, bf16[4,140]{1,0:T(4,128)(2,1)S(1)}, u32[]{:S(2)}, u32[]{:S(2)}) collective-permute-start(bf16[4,140]{1,0:T(4,128)(2,1)S(1)} %get-tuple-element.94), channel_id=1, source_target_pairs={{0,1},{1,0},{2,3},{3,2},{4,5},{5,4},{6,7},{7,6},{8,9},{9,8},{10,11... | collective-permute-start | bytes 3368 | tf_op jit(solution)/shard_map/ppermute | solution.py:23
  90.7 14.2 %copy-start.13 = (bf16[4,140,12,64]{1,3,2,0:T(8,128)(2,1)S(1)}, bf16[4,140,12,64]{1,3,2,0:T(8,128)(2,1)}, u32[]{:S(2)}) copy-start(bf16[4,140,12,64]{1,3,2,0:T(8,128)(2,1)} %copy.98) | copy-start | bytes 2580484
  90.7 14.2 %copy-start.15 = (bf16[4,140,12,64]{1,3,2,0:T(8,128)(2,1)S(1)}, bf16[4,140,12,64]{1,3,2,0:T(8,128)(2,1)}, u32[]{:S(2)}) copy-start(bf16[4,140,12,64]{1,3,2,0:T(8,128)(2,1)} %copy.99) | copy-start | bytes 2580484
  104.9 5.6 copy-start.24
  110.5 6.3 copy-start.46
  116.8 26.1 %slice-start.2 = ((s8[4718592]{0:T(1024)(128)(4,1)}), s8[4194304]{0:T(1024)(128)(4,1)S(1)}, s32[]{:S(2)}) async-start(s8[4718592]{0:T(1024)(128)(4,1)} %bitcast.42), calls=%async_computation.10 | async-start | bytes 8388608
  116.8 34.9 %slice-start = ((s8[4718592]{0:T(1024)(128)(4,1)}), s8[4194304]{0:T(1024)(128)(4,1)S(1)}, s32[]{:S(2)}) async-start(s8[4718592]{0:T(1024)(128)(4,1)} %bitcast.40), calls=%async_computation.8 | async-start | bytes 8388608
  120.1 35.3 %copy-start.5 = (f32[560,768]{1,0:T(8,128)}, f32[560,768]{1,0:T(8,128)S(1)}, u32[]{:S(2)}) copy-start(f32[560,768]{1,0:T(8,128)S(1)} %get-tuple-element.104) | copy-start | bytes 5160964
  120.5 22.4 %copy-start.7 = (bf16[560,768]{1,0:T(8,128)(2,1)S(1)}, bf16[560,768]{1,0:T(8,128)(2,1)}, u32[]{:S(2)}) copy-start(bf16[560,768]{1,0:T(8,128)(2,1)} %reshape.194) | copy-start | bytes 2580484
  120.5 22.4 %copy-start.37 = (pred[560]{0:T(1024)(128)(4,1)S(1)}, pred[560]{0:T(1024)(128)(4,1)}, u32[]{:S(2)}) copy-start(pred[560]{0:T(1024)(128)(4,1)} %lt.24) | copy-start | bytes 1684
  120.6 22.4 %slice-start.3 = ((s8[4718592]{0:T(1024)(128)(4,1)}), s8[524288]{0:T(1024)(128)(4,1)S(1)}, s32[]{:S(2)}) async-start(s8[4718592]{0:T(1024)(128)(4,1)} %bitcast.42), calls=%async_computation.11 | async-start | bytes 1048576
  120.6 22.4 %copy-start.45 = (f32[3072]{0:T(1024)S(1)}, f32[3072]{0:T(1024)}, u32[]{:S(2)}) copy-start(f32[3072]{0:T(1024)} %param.28) | copy-start | bytes 36868
  120.6 31.1 %slice-start.1 = ((s8[4718592]{0:T(1024)(128)(4,1)}), s8[524288]{0:T(1024)(128)(4,1)S(1)}, s32[]{:S(2)}) async-start(s8[4718592]{0:T(1024)(128)(4,1)} %bitcast.40), calls=%async_computation.9 | async-start | bytes 1048576
  169.6 7.9 %copy-start.14 = (bf16[4,140,12,64]{1,3,2,0:T(8,128)(2,1)S(1)}, bf16[4,140,12,64]{1,3,2,0:T(8,128)(2,1)}, u32[]{:S(2)}) copy-start(bf16[4,140,12,64]{1,3,2,0:T(8,128)(2,1)} %copy.98) | copy-start | bytes 2580484
  169.6 7.9 %copy-start.16 = (bf16[4,140,12,64]{1,3,2,0:T(8,128)(2,1)S(1)}, bf16[4,140,12,64]{1,3,2,0:T(8,128)(2,1)}, u32[]{:S(2)}) copy-start(bf16[4,140,12,64]{1,3,2,0:T(8,128)(2,1)} %copy.99) | copy-start | bytes 2580484
  169.6 7.9 %copy-start.17 = (bf16[4,140,12,64]{1,3,2,0:T(8,128)(2,1)S(1)}, bf16[4,140,12,64]{1,3,2,0:T(8,128)(2,1)}, u32[]{:S(2)}) copy-start(bf16[4,140,12,64]{1,3,2,0:T(8,128)(2,1)} %copy.109) | copy-start | bytes 2580484
  169.6 7.9 %copy-start.25 = (f32[4,12,140]{2,1,0:T(8,128)S(1)}, f32[4,12,140]{2,1,0:T(8,128)}, u32[]{:S(2)}) copy-start(f32[4,12,140]{2,1,0:T(8,128)} %copy-done.24) | copy-start | bytes 80644
  177.6 12.3 %copy-start.18 = (bf16[560,768]{0,1:T(8,128)(2,1)S(1)}, bf16[560,768]{0,1:T(8,128)(2,1)}, u32[]{:S(2)}) copy-start(bf16[560,768]{0,1:T(8,128)(2,1)} %convert_element_type.110) | copy-start | bytes 2580484
  177.6 12.3 %copy-start.20 = (bf16[560,768]{1,0:T(8,128)(2,1)S(1)}, bf16[560,768]{1,0:T(8,128)(2,1)}, u32[]{:S(2)}) copy-start(bf16[560,768]{1,0:T(8,128)(2,1)} %copy-done.19) | copy-start | bytes 2580484
  196.1 37.6 %collective-permute-start.4 = (bf16[4,140,12,64]{1,3,2,0:T(8,128)(2,1)}, bf16[4,140,12,64]{1,3,2,0:T(8,128)(2,1)}, u32[]{:S(2)}, u32[]{:S(2)}) collective-permute-start(bf16[4,140,12,64]{1,3,2,0:T(8,128)(2,1)} %slice.61), channel_id=1, source_target_pairs={{0,1},{1,0},{2,3},{3,2},{4,5},{5,4},{6,7},{7,6},{8,9},{9,8},{10,11... | collective-permute-start | bytes 2580488 | tf_op jit(solution)/shard_map/ppermute | solution.py:23
  197.8 229.1 %reduce-scatter.5.cloned.1.call-start = ((), (), s32[]{:S(2)}) async-start(), calls=%async_computation.4 | async-start | bytes 7299072 | tf_op jit(solution)/shard_map/reduce_scatter | solution.py:206
  197.9 8.3 %copy-start.1 = (bf16[4,140,12,64]{1,3,2,0:T(8,128)(2,1)S(1)}, bf16[4,140,12,64]{1,3,2,0:T(8,128)(2,1)}, u32[]{:S(2)}) copy-start(bf16[4,140,12,64]{1,3,2,0:T(8,128)(2,1)} %copy.105) | copy-start | bytes 2580484
  211.2 58.7 %collective-permute-start.3 = (bf16[4,140,12,64]{1,3,2,0:T(8,128)(2,1)}, bf16[4,140,12,64]{1,3,2,0:T(8,128)(2,1)}, u32[]{:S(2)}, u32[]{:S(2)}) collective-permute-start(bf16[4,140,12,64]{1,3,2,0:T(8,128)(2,1)} %slice.62), channel_id=1, source_target_pairs={{0,1},{1,0},{2,3},{3,2},{4,5},{5,4},{6,7},{7,6},{8,9},{9,8},{10,11... | collective-permute-start | bytes 2580488 | tf_op jit(solution)/shard_map/ppermute | solution.py:23
  279.4 4.7 copy-start.9
  279.4 4.7 copy-start.32
  279.4 4.7 copy-start.34
  279.4 4.7 copy-start.43
  279.4 4.7 copy-start.47
  291.5 276.8 %reduce-scatter.9.cloned.1.call-start = ((), (), s32[]{:S(2)}) async-start(), calls=%async_computation.6 | async-start | bytes 9732096 | tf_op jit(solution)/shard_map/reduce_scatter | solution.py:212
  301.8 408.4 %reduce-scatter.11.cloned.1.call-start = ((), (), s32[]{:S(2)}) async-start(), calls=%async_computation.7 | async-start | bytes 9732096 | tf_op jit(solution)/shard_map/reduce_scatter | solution.py:214
  324.6 4.8 copy-start.30
  330.8 57.5 %copy-start.27 = (f32[560]{0:T(1024)S(1)}, f32[560]{0:T(1024)}, u32[]{:S(2)}) copy-start(f32[560]{0:T(1024)} %copy-done.26) | copy-start | bytes 6724
  337.9 53.8 %copy-start.29 = (f32[560]{0:T(1024)S(1)}, f32[560]{0:T(1024)}, u32[]{:S(2)}) copy-start(f32[560]{0:T(1024)} %copy-done.28) | copy-start | bytes 6724
  380.6 11.1 %copy-start.4 = (f32[560,768]{1,0:T(8,128)S(1)}, f32[560,768]{1,0:T(8,128)}, u32[]{:S(2)}) copy-start(f32[560,768]{1,0:T(8,128)} %copy-done.3) | copy-start | bytes 5160964
  380.6 11.1 %copy-start.8 = (bf16[560,768]{1,0:T(8,128)(2,1)S(1)}, bf16[560,768]{1,0:T(8,128)(2,1)}, u32[]{:S(2)}) copy-start(bf16[560,768]{1,0:T(8,128)(2,1)} %reshape.194) | copy-start | bytes 2580484
  380.6 11.1 %copy-start.39 = (pred[560]{0:T(1024)(128)(4,1)S(1)}, pred[560]{0:T(1024)(128)(4,1)}, u32[]{:S(2)}) copy-start(pred[560]{0:T(1024)(128)(4,1)} %lt.24) | copy-start | bytes 1684
  (14 other events, 31.5 us)
Sparse Core Ops, SparseCore 0:
  197.9 103.5 reduce-scatter.6
  308.7 118.0 reduce-scatter.4
  433.4 134.8 reduce-scatter.8
  575.6 134.5 reduce-scatter.10
where the time goes:
time: 727 us; the launch traced here: 717 us
  waiting for transfers between devices  350 us (48%)
  local copies, waits for them, and re-layouts  130 us (18%)
  matrix products  127 us (17%)
  other arithmetic  45.3 us (6%)
  blocking collectives  42.7 us (6%)
  between operations  14.5 us (2%)
  starting transfers between devices  7.51 us (1%)
    reduce_scatter x1, waiting for transfers between devices, on_device(): lax.psum_scatter(local_grads[10], ('pairs', 'mod'), scatter_dimension=0,...  142 us
    reduce_scatter x1, waiting for transfers between devices, on_device(): lax.psum_scatter(local_grads[8], ('pairs', 'mod'), scatter_dimension=0, t...  141 us
    unnamed x1, blocking collectives  42.7 us
    ppermute x5, waiting for transfers between devices, from_partner(): return lax.ppermute(block, axis, route)  40.5 us
    unnamed x121, local copies, waits for them, and re-layouts  30.4 us
    dot_general x4, matrix products, t_times_rows(): lax.dot_general(left, right, (((0,), (0,)), ((), ())), preferred_element_...  29.9 us
    reduce_scatter x1, waiting for transfers between devices, on_device(): lax.psum_scatter(local_grads[2], ('pairs', 'mod'), scatter_dimension=0, t...  26.5 us
    dot_general x1, matrix products, layer_pass(): jnp.dot(second_norm, up_weight, preferred_element_type=jnp.float32)  22.3 us
  transfers between devices with their start and end apart: 9, of which 6 were waited for; matrix products, arithmetic and copies ran while one was open for 22% of the time, Pallas kernels for 0%

commit v1 on v0

v1 whole, which is shorter than its diff:
```python
from functools import partial

import jax
import jax.numpy as jnp
import numpy as np
from jax import lax
from jax.experimental import pallas as pl
from jax.experimental.pallas import tpu as pltpu
from jax.sharding import PartitionSpec as P

HEAD_DIM = 64
TXT = 40
EPS = 1e-06
MASKED = -1e30
AXES = ("pairs", "mod")
BF16 = jnp.bfloat16
F32 = jnp.float32
LANES = 128
MIB = 1 << 20

CORE_BIT = 2
ORDERS = ((4, 8, 1, 16), (8, 4, 1, 16))


def dot_nn(a, b):
    return jnp.dot(a, b, preferred_element_type=F32)


def dot_nt(a, b):
    return lax.dot_general(a, b, (((1,), (1,)), ((), ())), preferred_element_type=F32)


def dot_tn(a, b):
    return lax.dot_general(a, b, (((0,), (0,)), ((), ())), preferred_element_type=F32)


def norm_parts(v):
    center = v - jnp.mean(v, axis=-1, keepdims=True)
    rstd = lax.rsqrt(jnp.mean(center * center, axis=-1, keepdims=True) + EPS)
    return center * rstd, rstd


def norm_back(grad, unit, rstd, gain):
    d = grad * gain
    return rstd * (
        d
        - jnp.mean(d, axis=-1, keepdims=True)
        - unit * jnp.mean(d * unit, axis=-1, keepdims=True)
    )


def gelu_and_slope(v):
    u = jnp.abs(v) * 0.7071067811865476
    t = 1.0 / (1.0 + 0.3275911 * u)
    bell = jnp.exp(-u * u)
    poly = t * (
        0.127414796
        + t * (-0.142248368 + t * (0.7107068705 + t * (-0.7265760135 + t * 0.5307027145)))
    )
    tail = poly * bell
    phi = jnp.where(v >= 0, 1.0 - tail, tail)
    return v * phi, phi + v * bell * 0.3989422804014327


def norm_qkv_kernel(x_ref, g_ref, b_ref, w_ref, qvb_ref, fn_ref, qkv_ref):
    j = pl.program_id(0)
    rows, width = fn_ref.shape[0] * fn_ref.shape[1], fn_ref.shape[2]

    @pl.when(j == 0)
    def _():
        x = x_ref[...].reshape(rows, width).astype(F32)
        unit, _ = norm_parts(x)
        fn_ref[...] = (unit * g_ref[...] + b_ref[...]).astype(BF16).reshape(fn_ref.shape)

    fn = fn_ref[...].reshape(rows, width)
    bias = jnp.where(j == 1, 0.0, 1.0) * qvb_ref[0]
    out = dot_nn(fn, w_ref[...]) + bias
    qkv_ref[...] = out.astype(BF16).reshape(qkv_ref.shape)


def norm_qkv(x, gain, shift, weight, qv_bias):
    pairs, half, width = x.shape
    whole = lambda j: (0, 0, 0)
    return pl.pallas_call(
        norm_qkv_kernel,
        grid=(3,),
        in_specs=[
            pl.BlockSpec((pairs, half, width), whole),
            pl.BlockSpec((1, width), lambda j: (0, 0)),
            pl.BlockSpec((1, width), lambda j: (0, 0)),
            pl.BlockSpec((width, width), lambda j: (0, j)),
            pl.BlockSpec((1, 1, width), lambda j: (j // 2, 0, 0)),
        ],
        out_specs=[
            pl.BlockSpec((pairs, half, width), whole),
            pl.BlockSpec((pairs, half, width), lambda j: (0, 0, j)),
        ],
        out_shape=[
            jax.ShapeDtypeStruct((pairs, half, width), BF16),
            jax.ShapeDtypeStruct((pairs, half, 3 * width), BF16),
        ],
        compiler_params=pltpu.CompilerParams(vmem_limit_bytes=24 * MIB),
        cost_estimate=pl.CostEstimate(
            flops=2 * pairs * half * width * 3 * width,
            bytes_accessed=2 * (3 * width * width + 5 * pairs * half * width),
            transcendentals=0,
        ),
        name="norm_qkv",
    )(x, gain, shift, weight, qv_bias)


def attend_kernel(
    qo, qr, xo, xr, okrow, ow, ob, g2, b2, mixed_ref, att_ref, sn_ref, p_ref, mix_s
):
    half, width = xo.shape[1], xo.shape[2]
    rows = 2 * half
    key_ok = (okrow[0] + xr[0, half - 4 : half - 3, :]).astype(F32)[:, :rows] > 0.5
    bias = jnp.where(key_ok, 0.0, MASKED)
    first = lax.broadcasted_iota(jnp.int32, (1, LANES), 1) < HEAD_DIM
    zero = jnp.zeros((), BF16)

    def both(col):
        cols = pl.ds(pl.multiple_of(col, LANES), LANES)
        return jnp.concatenate([qo[0, :, cols], qr[0, :, cols]], axis=0)

    def two_heads(hp, carry):
        q = both(hp * LANES) * jnp.asarray(HEAD_DIM**-0.5, BF16)
        k = both(width + hp * LANES)
        v = both(2 * width + hp * LANES)
        outs = []
        for h in range(2):
            kh = jnp.where(first if h == 0 else jnp.logical_not(first), k, zero)
            s = dot_nt(q, kh) + bias
            e = jnp.exp(s - jnp.max(s, axis=-1, keepdims=True))
            p = (e * (1.0 / jnp.sum(e, axis=-1, keepdims=True))).astype(BF16)
            p_ref[0, 2 * hp + h] = p
            outs.append(dot_nn(p, v))
        cols = pl.ds(pl.multiple_of(hp * LANES, LANES), LANES)
        mix_s[:, cols] = jnp.where(first, outs[0], outs[1]).astype(BF16)
        return carry

    lax.fori_loop(0, width // LANES, two_heads, 0)
    mixed = mix_s[...]
    mixed_ref[...] = mixed.reshape(mixed_ref.shape)
    x = jnp.concatenate([xo[0], xr[0]], axis=0).astype(F32)
    att = x + dot_nn(mixed, ow[...]) + ob[...]
    att_ref[...] = att.reshape(att_ref.shape)
    unit, _ = norm_parts(att)
    sn_ref[...] = (unit * g2[...] + b2[...]).astype(BF16).reshape(sn_ref.shape)


def attend(qkv_own, qkv_far, x_own, x_far, okrow, out_weight, out_bias, gain, shift):
    pairs, half, width = x_own.shape
    heads = width // HEAD_DIM
    rows = 2 * half
    pair3 = lambda p: (p, 0, 0)
    const = lambda p: (0, 0)
    both = lambda p: (0, p, 0, 0)
    return pl.pallas_call(
        attend_kernel,
        grid=(pairs,),
        in_specs=[
            pl.BlockSpec((1, half, 3 * width), pair3),
            pl.BlockSpec((1, half, 3 * width), pair3),
            pl.BlockSpec((1, half, width), pair3),
            pl.BlockSpec((1, half, width), pair3),
            pl.BlockSpec((1, 1, width), pair3),
            pl.BlockSpec((width, width), const),
            pl.BlockSpec((1, width), const),
            pl.BlockSpec((1, width), const),
            pl.BlockSpec((1, width), const),
        ],
        out_specs=[
            pl.BlockSpec((2, 1, half, width), both),
            pl.BlockSpec((2, 1, half, width), both),
            pl.BlockSpec((2, 1, half, width), both),
            pl.BlockSpec((1, heads, rows, rows), lambda p: (p, 0, 0, 0)),
        ],
        out_shape=[
            jax.ShapeDtypeStruct((2, pairs, half, width), BF16),
            jax.ShapeDtypeStruct((2, pairs, half, width), F32),
            jax.ShapeDtypeStruct((2, pairs, half, width), BF16),
            jax.ShapeDtypeStruct((pairs, heads, rows, rows), BF16),
        ],
        scratch_shapes=[pltpu.VMEM((rows, width), BF16)],
        compiler_params=pltpu.CompilerParams(vmem_limit_bytes=40 * MIB),
        cost_estimate=pl.CostEstimate(
            flops=pairs * heads * 8 * rows * rows * LANES,
            bytes_accessed=2 * pairs * rows * width * 8 + 2 * pairs * heads * rows * rows,
            transcendentals=pairs * heads * rows * rows,
        ),
        name="attend",
    )(qkv_own, qkv_far, x_own, x_far, okrow, out_weight, out_bias, gain, shift)


def live_rows(info, p, far, half):
    side = info[2] if far == 0 else 1 - info[2]
    row = lax.broadcasted_iota(jnp.int32, (half, 1), 0)
    real = half - 4
    limit = jnp.minimum(TXT + info[p] - side * real, real)
    return row < limit


def mlp_up_kernel(
    info, inv, sn, att, co, cr, up, upb, down, downb,
    slope_ref, own_ref, far_ref, gy_ref, dbg_ref, keep_ref, send_ref, acc, wdn,
    *, shard,
):
    j = pl.program_id(0)
    last = pl.num_programs(0) - 1
    pairs, half, width = co.shape
    tile = up.shape[1]

    @pl.when(j == 0)
    def _():
        for far, c in enumerate((co, cr)):
            for p in range(pairs):
                at = (far * pairs + p) * half
                gy_ref[at : at + half, :] = jnp.where(
                    live_rows(info, p, far, half), c[p].astype(F32), 0.0
                ).astype(BF16)
        dbg_ref[...] = jnp.sum(gy_ref[...].astype(F32), axis=0, keepdims=True)

    h, slope = gelu_and_slope(dot_nn(sn[...], up[...]) + upb[...])
    slope_ref[...] = slope.astype(BF16)
    h = h.astype(BF16)
    part = dot_nn(h, down[...])

    @pl.when(j == 0)
    def _():
        acc[...] = part

    @pl.when(j > 0)
    def _():
        acc[...] += part

    wdn[pl.ds(pl.multiple_of(j * tile, tile), tile), :] = dot_tn(h, gy_ref[...]).astype(wdn.dtype)

    @pl.when(j == last)
    def _():
        final = att[...] + acc[...] + downb[...]
        for far, o in enumerate((own_ref, far_ref)):
            for p in range(pairs):
                at = (far * pairs + p) * half
                o[p] = jnp.where(
                    live_rows(info, p, far, half), final[at : at + half, :], 0.0
                ).astype(BF16)
        if shard:
            n = keep_ref.shape[0]

            def fill(p, carry):
                at = lambda q: pl.ds(pl.multiple_of(inv[q] * shard, shard), shard)
                keep_ref[p] = wdn[at(p), :]
                send_ref[p] = wdn[at(n + p), :]
                return carry

            lax.fori_loop(0, n, fill, 0)
        else:
            keep_ref[...] = wdn[...]
            send_ref[...] = jnp.zeros_like(send_ref)


def mlp_up(info, inv, sn, att, cot_own, cot_far, up, up_bias, down, down_bias, shards, packed):
    pairs, half, width = cot_own.shape
    rows = 2 * pairs * half
    ff = up.shape[1]
    tile = width
    shard = ff // shards
    if packed:
        wire = [jax.ShapeDtypeStruct((shards // 2, shard, width), BF16)] * 2
    else:
        wire = [jax.ShapeDtypeStruct((ff, width), F32), jax.ShapeDtypeStruct((8, LANES), F32)]
    z = lambda j, *_: (0, 0)
    z3 = lambda j, *_: (0, 0, 0)
    return pl.pallas_call(
        partial(mlp_up_kernel, shard=shard if packed else 0),
        grid_spec=pltpu.PrefetchScalarGridSpec(
            num_scalar_prefetch=2,
            grid=(ff // tile,),
            in_specs=[
                pl.BlockSpec((rows, width), z),
                pl.BlockSpec((rows, width), z),
                pl.BlockSpec((pairs, half, width), z3),
                pl.BlockSpec((pairs, half, width), z3),
                pl.BlockSpec((width, tile), lambda j, *_: (0, j)),
                pl.BlockSpec((1, tile), lambda j, *_: (0, j)),
                pl.BlockSpec((tile, width), lambda j, *_: (j, 0)),
                pl.BlockSpec((1, width), z),
            ],
            out_specs=[
                pl.BlockSpec((rows, tile), lambda j, *_: (0, j)),
                pl.BlockSpec((pairs, half, width), z3),
                pl.BlockSpec((pairs, half, width), z3),
                pl.BlockSpec((rows, width), z),
                pl.BlockSpec((1, width), z),
            ]
            + [pl.BlockSpec(w.shape, z3 if packed else z) for w in wire],
            scratch_shapes=[
                pltpu.VMEM((rows, width), F32),
                pltpu.VMEM((ff, width), BF16 if packed else F32),
            ],
        ),
        out_shape=[
            jax.ShapeDtypeStruct((rows, ff), BF16),
            jax.ShapeDtypeStruct((pairs, half, width), BF16),
            jax.ShapeDtypeStruct((pairs, half, width), BF16),
            jax.ShapeDtypeStruct((rows, width), BF16),
            jax.ShapeDtypeStruct((1, width), F32),
        ]
        + wire,
        compiler_params=pltpu.CompilerParams(vmem_limit_bytes=(48 if packed else 60) * MIB),
        cost_estimate=pl.CostEstimate(
            flops=6 * rows * width * ff, bytes_accessed=24 * MIB, transcendentals=rows * ff
        ),
        name="mlp_up",
    )(info, inv, sn, att, cot_own, cot_far, up, up_bias, down, down_bias)


def pack_tile(acc, inv, keep_ref, send_ref, t, rows):
    n = keep_ref.shape[0]
    groups, cut = rows // 8, acc.shape[1] // 2

    def fill(ref, base):
        def one(p, carry):
            top = inv[base + p] * rows
            for g in range(groups):
                blk = acc[pl.ds(pl.multiple_of(top + 8 * g, 8), 8), :]
                val = jnp.concatenate([blk[:, :cut], blk[:, cut:]], axis=0).astype(BF16)
                ref[p, :, pl.ds(pl.multiple_of((t * groups + g) * cut, LANES), cut)] = val
            return carry

        lax.fori_loop(0, n, one, 0, unroll=2)

    fill(keep_ref, 0)
    fill(send_ref, n)


def mlp_back_kernel(
    inv, gs_in, gy, slope, sn, up, down, gs_ref, upb_ref, keep_ref, send_ref, tile_acc, *, shard, first
):
    j = pl.program_id(0)
    gh = dot_nt(gy[...], down[...])
    gp = gh * slope[...].astype(F32)
    gp = gp.astype(BF16)
    upb_ref[...] = jnp.sum(gp.astype(F32), axis=0, keepdims=True)
    part = dot_nt(gp, up[...])

    @pl.when(j == 0)
    def _():
        gs_ref[...] = part if first else gs_in[...] + part

    @pl.when(j > 0)
    def _():
        gs_ref[...] += part

    if shard:
        tile_acc[...] = dot_tn(sn[...], gp)
        pack_tile(tile_acc, inv, keep_ref, send_ref, j, shard)
    else:
        keep_ref[...] = dot_tn(sn[...], gp)
        send_ref[...] = jnp.zeros_like(send_ref)


def mlp_back(inv, gs, gy, slope, sn, up, down, start, tiles, shards, packed):
    rows, width = gy.shape
    tile = width
    shard = width // shards
    first = gs is None
    if first:
        gs, gs_spec = jnp.zeros((8, LANES), F32), pl.BlockSpec((8, LANES), lambda j, *_: (0, 0))
    else:
        gs_spec = pl.BlockSpec((rows, width), lambda j, *_: (0, 0))
    z = lambda j, *_: (0, 0)
    z3 = lambda j, *_: (0, 0, 0)
    cols = lambda j, *_: (0, j + start)
    own = lambda j, *_: (0, j)
    if packed:
        wire = [jax.ShapeDtypeStruct((shards // 2, 16, shard * tiles * tile // 16), BF16)] * 2
        wire_specs = [pl.BlockSpec(w.shape, z3) for w in wire]
    else:
        wire = [
            jax.ShapeDtypeStruct((width, tiles * tile), F32),
            jax.ShapeDtypeStruct((8, LANES), F32),
        ]
        wire_specs = [pl.BlockSpec((width, tile), own), pl.BlockSpec((8, LANES), z)]
    return pl.pallas_call(
        partial(mlp_back_kernel, shard=shard if packed else 0, first=first),
        grid_spec=pltpu.PrefetchScalarGridSpec(
            num_scalar_prefetch=1,
            grid=(tiles,),
            in_specs=[
                gs_spec,
                pl.BlockSpec((rows, width), z),
                pl.BlockSpec((rows, tile), cols),
                pl.BlockSpec((rows, width), z),
                pl.BlockSpec((width, tile), cols),
                pl.BlockSpec((tile, width), lambda j, *_: (j + start, 0)),
            ],
            out_specs=[pl.BlockSpec((rows, width), z), pl.BlockSpec((1, tile), own)] + wire_specs,
            scratch_shapes=[pltpu.VMEM((width, tile), F32)],
        ),
        out_shape=[
            jax.ShapeDtypeStruct((rows, width), F32),
            jax.ShapeDtypeStruct((1, tiles * tile), F32),
        ]
        + wire,
        compiler_params=pltpu.CompilerParams(vmem_limit_bytes=48 * MIB),
        cost_estimate=pl.CostEstimate(
            flops=6 * rows * width * tile * tiles, bytes_accessed=10 * MIB, transcendentals=0
        ),
        name="mlp_back",
    )(inv, gs, gy, slope, sn, up, down)


def attend_back_kernel(
    gs, gy, att, xo, xr, qo, qr, p_ref, qkvw, ow, g1, g2,
    own_ref, far_ref, vec_ref, dqkv, gbs, gms,
):
    half, width = xo.shape[1], xo.shape[2]
    rows = 2 * half
    first = lax.broadcasted_iota(jnp.int32, (1, LANES), 1) < HEAD_DIM
    zero = jnp.zeros((), BF16)
    scale = HEAD_DIM**-0.5

    def set_vec(i, value):
        vec_ref[i : i + 1, :] = jnp.sum(value, axis=0, keepdims=True)

    grad_second = gs[...].reshape(rows, width)
    unit, rstd = norm_parts(att[...].reshape(rows, width))
    set_vec(5, grad_second * unit)
    set_vec(6, grad_second)
    grad_att = gy[...].reshape(rows, width).astype(F32) + norm_back(
        grad_second, unit, rstd, g2[...]
    )
    branch = grad_att.astype(BF16)
    set_vec(4, branch.astype(F32))
    vec_ref[7:8, :] = jnp.zeros((1, width), F32)
    gbs[...] = branch
    gms[...] = dot_nt(branch, ow[...]).astype(BF16)

    def both(col):
        cols = pl.ds(pl.multiple_of(col, LANES), LANES)
        return jnp.concatenate([qo[0, :, cols], qr[0, :, cols]], axis=0)

    def two_heads(hp, carry):
        q = both(hp * LANES) * jnp.asarray(scale, BF16)
        k = both(width + hp * LANES) * jnp.asarray(scale, BF16)
        v = both(2 * width + hp * LANES)
        gm = gms[:, pl.ds(pl.multiple_of(hp * LANES, LANES), LANES)]
        dq, dk, dv = [], [], []
        for h in range(2):
            vh = jnp.where(first if h == 0 else jnp.logical_not(first), v, zero)
            prob = p_ref[0, 2 * hp + h]
            dp = dot_nt(gm, vh)
            pf = prob.astype(F32)
            delta = jnp.sum(dp * pf, axis=-1, keepdims=True)
            ds = (pf * (dp - delta)).astype(BF16)
            dv.append(dot_tn(prob, gm))
            dq.append(dot_nn(ds, k))
            dk.append(dot_tn(ds, q))
        for i, pair_of in enumerate((dq, dk, dv)):
            cols = pl.ds(pl.multiple_of(i * width + hp * LANES, LANES), LANES)
            dqkv[:, cols] = jnp.where(first, pair_of[0], pair_of[1]).astype(BF16)
        return carry

    lax.fori_loop(0, width // LANES, two_heads, 0)
    mine = dqkv[...]
    grad_first = dot_nt(mine, qkvw[...])
    x = jnp.concatenate([xo[0], xr[0]], axis=0).astype(F32)
    unit1, rstd1 = norm_parts(x)
    set_vec(0, grad_first * unit1)
    set_vec(1, grad_first)
    set_vec(2, mine[:, :width].astype(F32))
    set_vec(3, mine[:, 2 * width :].astype(F32))
    result = (grad_att + norm_back(grad_first, unit1, rstd1, g1[...])).astype(BF16)
    own_ref[...] = result[:half]
    far_ref[...] = result[half:]


def attend_back(
    pair, gs, gy, att, x_own, x_far, qkv_own, qkv_far, probs, qkv_weight, out_weight, gain1, gain2,
):
    pairs, half, width = x_own.shape
    rows = 2 * half
    heads = width // HEAD_DIM
    pair3 = lambda i: (pair, 0, 0)
    both = lambda i: (0, pair, 0, 0)
    const = lambda i: (0, 0)
    return pl.pallas_call(
        attend_back_kernel,
        grid=(1,),
        in_specs=[
            pl.BlockSpec((2, 1, half, width), both),
            pl.BlockSpec((2, 1, half, width), both),
            pl.BlockSpec((2, 1, half, width), both),
            pl.BlockSpec((1, half, width), pair3),
            pl.BlockSpec((1, half, width), pair3),
            pl.BlockSpec((1, half, 3 * width), pair3),
            pl.BlockSpec((1, half, 3 * width), pair3),
            pl.BlockSpec((1, heads, rows, rows), lambda i: (pair, 0, 0, 0)),
            pl.BlockSpec((width, 3 * width), const),
            pl.BlockSpec((width, width), const),
            pl.BlockSpec((1, width), const),
            pl.BlockSpec((1, width), const),
        ],
        out_specs=[
            pl.BlockSpec((half, width), const),
            pl.BlockSpec((half, width), const),
            pl.BlockSpec((8, width), const),
            pl.BlockSpec((rows, 3 * width), const),
            pl.BlockSpec((rows, width), const),
        ],
        scratch_shapes=[pltpu.VMEM((rows, width), BF16)],
        out_shape=[
            jax.ShapeDtypeStruct((half, width), BF16),
            jax.ShapeDtypeStruct((half, width), BF16),
            jax.ShapeDtypeStruct((8, width), F32),
            jax.ShapeDtypeStruct((rows, 3 * width), BF16),
            jax.ShapeDtypeStruct((rows, width), BF16),
        ],
        compiler_params=pltpu.CompilerParams(vmem_limit_bytes=36 * MIB),
        cost_estimate=pl.CostEstimate(
            flops=heads * 16 * rows * rows * LANES + 8 * rows * width * width,
            bytes_accessed=12 * MIB,
            transcendentals=0,
        ),
        name="attend_back",
    )(gs, gy, att, x_own, x_far, qkv_own, qkv_far, probs, qkv_weight, out_weight, gain1, gain2)


def weight_grads_kernel(
    inv, dq0, dq1, gb0, gb1, mixed, fno, fnr, v0, v1, upa, upb, dbg,
    vec_ref, keep_ref, send_ref, dqkv, gbs, fns, mxs, tile_acc, *, shard,
):
    pairs, half, width = fno.shape
    rows = 2 * half
    for i, (d, g) in enumerate(((dq0, gb0), (dq1, gb1))):
        at = i * rows
        dqkv[at : at + rows, :] = d[...]
        gbs[at : at + rows, :] = g[...]
        fns[at : at + half, :] = fno[i]
        fns[at + half : at + rows, :] = fnr[i]
        mxs[at : at + rows, :] = mixed[:, i].reshape(rows, width)
    vec_ref[0:8, :] = v0[...] + v1[...]
    vec_ref[7:8, :] = dbg[...]
    for i in range(4):
        src = (upa, upb)[i // 2]
        vec_ref[8 + i : 9 + i, :] = src[:, i % 2 * width : (i % 2 + 1) * width]
    vec_ref[12:16, :] = jnp.zeros((4, width), F32)

    for t in range(4):
        if t < 3:
            val = dot_tn(fns[...], dqkv[:, t * width : (t + 1) * width])
        else:
            val = dot_tn(mxs[...], gbs[...])
        if shard:
            tile_acc[...] = val
            pack_tile(tile_acc, inv, keep_ref, send_ref, t, shard)
        elif t < 3:
            keep_ref[:, t * width : (t + 1) * width] = val
        else:
            send_ref[...] = val
    if shard:
        n = keep_ref.shape[0]
        at = keep_ref.shape[2] - LANES
        v = vec_ref[...]
        small = jnp.concatenate([v[0:2], v[4:8], v[0:2]], axis=0)
        rowid = lax.broadcasted_iota(jnp.int32, (8, LANES), 0)
        per_q, per_u = width // (2 * shard), width // (4 * shard)

        def piece(block, start):
            return pltpu.roll(block, lax.rem(width - start, width), 1)[:, :LANES]

        def block(i):
            a = piece(small, i * shard)
            b = piece(v[2:4], lax.rem(i, per_q) * 2 * shard)
            brow = jnp.where(i < per_q, b[0:1], b[1:2])
            c = piece(v[8:12], lax.rem(i, per_u) * 4 * shard)
            ci = lax.div(i, per_u)
            crow = jnp.where(
                ci == 0, c[0:1], jnp.where(ci == 1, c[1:2], jnp.where(ci == 2, c[2:3], c[3:4]))
            )
            top = jnp.where(rowid < 6, a, jnp.where(rowid == 6, brow, crow))
            return jnp.concatenate([top, jnp.zeros_like(top)], axis=0).astype(BF16)

        def fill(p, carry):
            keep_ref[p, :, at : at + LANES] = block(inv[p])
            send_ref[p, :, at : at + LANES] = block(inv[n + p])
            return carry

        lax.fori_loop(0, n, fill, 0)


def weight_grads(
    inv, dqkv0, dqkv1, gb0, gb1, mixed, fn_own, fn_far, vec0, vec1, upa, upb, dbg, shards, packed
):
    pairs, half, width = fn_own.shape
    rows = 2 * half
    shard = width // shards
    if packed:
        wire = [jax.ShapeDtypeStruct((shards // 2, 16, shard * 4 * width // 16 + LANES), BF16)] * 2
    else:
        wire = [
            jax.ShapeDtypeStruct((width, 3 * width), F32),
            jax.ShapeDtypeStruct((width, width), F32),
        ]
    full = lambda a: pl.BlockSpec(a.shape, lambda i, *_: (0,) * len(a.shape))
    args = (dqkv0, dqkv1, gb0, gb1, mixed, fn_own, fn_far, vec0, vec1, upa, upb, dbg)
    outs = [jax.ShapeDtypeStruct((16, width), F32)] + wire
    return pl.pallas_call(
        partial(weight_grads_kernel, shard=shard if packed else 0),
        grid_spec=pltpu.PrefetchScalarGridSpec(
            num_scalar_prefetch=1,
            grid=(1,),
            in_specs=[full(a) for a in args],
            out_specs=[full(o) for o in outs],
            scratch_shapes=[
                pltpu.VMEM((pairs * rows, 3 * width), BF16),
                pltpu.VMEM((pairs * rows, width), BF16),
                pltpu.VMEM((pairs * rows, width), BF16),
                pltpu.VMEM((pairs * rows, width), BF16),
                pltpu.VMEM((width, width), F32),
            ],
        ),
        out_shape=outs,
        compiler_params=pltpu.CompilerParams(vmem_limit_bytes=48 * MIB),
        cost_estimate=pl.CostEstimate(
            flops=8 * pairs * rows * width * width, bytes_accessed=14 * MIB, transcendentals=0
        ),
        name="weight_grads",
    )(inv, *args)


def core_of(i):
    return 1 if i & CORE_BIT else 0


def shard_order(me, shards):
    half = shards // 2
    bits = half.bit_length() - 1
    tables = []
    for order in ORDERS:
        row = []
        for p in range(half):
            rel = 0
            for i, bit in enumerate(order):
                if p >> (bits - 1 - i) & 1:
                    rel |= bit
            row.append(rel)
        tables.append(row)
    tables = jnp.asarray(np.array(tables, np.int32))
    core = jnp.where(me & CORE_BIT, 1, 0)
    keep = jnp.where(core == 0, tables[0], tables[1])
    send = jnp.where(core == 0, tables[1], tables[0]) | CORE_BIT
    return me ^ jnp.concatenate([keep, send])


def add_up(terms):
    total = terms[0].astype(F32)
    for t in terms[1:]:
        total = total + t.astype(F32)
    return total


class Reduction:
    def __init__(self, keep, send, shards):
        self.shards, self.stage, self.n = shards, 0, keep.shape[0]
        self.terms = [keep]
        self.incoming = lax.ppermute(send, AXES, [(i, i ^ CORE_BIT) for i in range(shards)])

    def step(self, *after):
        recv = lax.optimization_barrier((self.incoming,) + after)[0]
        self.terms.append(recv)
        self.n //= 2
        out = add_up([t[self.n :] for t in self.terms]).astype(BF16)
        self.terms = [t[: self.n] for t in self.terms]
        route = [(i, i ^ ORDERS[core_of(i)][self.stage]) for i in range(self.shards)]
        self.incoming = lax.ppermute(out, AXES, route)
        self.stage += 1
        return out

    def result(self):
        return add_up(self.terms + [self.incoming])[0]


def unpack_rows(block, tiles, rows):
    groups = rows // 8
    cut = block.shape[1] // (tiles * groups)
    block = block.reshape(2, 8, tiles, groups, cut)
    return block.transpose(3, 1, 2, 0, 4).reshape(rows, tiles * 2 * cut)


def tie(*values):
    return lax.optimization_barrier(values)


def swap_sides(block):
    return lax.ppermute(block, "mod", [(0, 1), (1, 0)])


def on_device(
    tokens, patch_counts, token_mask, ln1_gain, ln1_bias, qkv_weight, qv_bias, out_weight,
    out_bias, ln2_gain, ln2_bias, up_weight, up_bias, down_weight, down_bias, cotangent,
):
    shards = lax.axis_size("pairs") * lax.axis_size("mod")
    pairs_here, real, width = tokens.shape
    pairs = pairs_here // 2
    half = real + 4
    packed = shards == 32 and width % (8 * shards) == 0
    side = lax.axis_index("mod")
    me = lax.axis_index("pairs") * 2 + side
    mine, theirs = side * pairs, (1 - side) * pairs

    def pick(arr, at):
        return lax.dynamic_slice_in_dim(arr, at, pairs, 0)

    row_ids = side * real + jnp.arange(real, dtype=jnp.int32)
    live = row_ids[None, :] < (TXT + patch_counts)[:, None]
    ok = jnp.logical_and(live, token_mask == 1).astype(BF16)
    ok_send = jnp.pad(pick(ok, theirs), ((0, 0), (half, width - half - real)))
    ok_own = jnp.pad(pick(ok, mine), ((0, 0), (0, width - real)))[:, None, :]
    pad3 = ((0, 0), (0, 4), (0, 0))
    tok_send = jnp.concatenate(
        [pick(tokens, theirs), ok_send[:, None, :], jnp.zeros((pairs, 3, width), BF16)], axis=1
    )
    x_far = swap_sides(tok_send)
    x_own = jnp.pad(pick(tokens, mine), pad3)
    cot_own = jnp.pad(pick(cotangent, mine), pad3)
    cot_send = jnp.pad(pick(cotangent, theirs), pad3)

    counts = pick(patch_counts, mine)
    info = jnp.concatenate([counts, side[None].astype(jnp.int32)])
    if packed:
        inv = shard_order(me, shards).astype(jnp.int32)
    else:
        inv = jnp.zeros((8,), jnp.int32)

    row = lambda v: v.reshape(1, -1)
    g1, b1, g2, b2 = row(ln1_gain), row(ln1_bias), row(ln2_gain), row(ln2_bias)
    qvb = qv_bias.reshape(2, 1, width)
    fn_own, qkv_own = norm_qkv(x_own, g1, b1, qkv_weight, qvb)
    x_far, cot_send = tie(x_far, cot_send)
    cot_far = swap_sides(cot_send)
    fn_far, qkv_far = norm_qkv(x_far, g1, b1, qkv_weight, qvb)
    mixed, att, sn, probs = attend(
        qkv_own, qkv_far, x_own, x_far, ok_own, out_weight, row(out_bias), g2, b2
    )
    flat = lambda a: a.reshape(-1, width)
    slope, lo_own, lo_far, gy, dbg, keep1, send1 = mlp_up(
        info, inv, flat(sn), flat(att), cot_own, cot_far, up_weight, row(up_bias),
        down_weight, row(down_bias), shards, packed,
    )
    lo_back = swap_sides(lo_far)
    tiles = up_weight.shape[1] // width // 2
    back = lambda gs, gy, start: mlp_back(
        inv, gs, gy, slope, flat(sn), up_weight, down_weight, start, tiles, shards, packed
    )
    if packed:
        r1 = Reduction(keep1, send1, shards)
    gs, upa, keep2, send2 = back(None, gy, 0)
    if packed:
        sent = r1.step(upa)
        r2 = Reduction(keep2, send2, shards)
        gs, sent = tie(gs, sent)
    gs, upb, keep3, send3 = back(gs, gy, tiles)
    shape4 = (2, pairs, half, width)
    gy4, gs4 = gy.reshape(shape4), gs.reshape(shape4)
    pair_back = lambda pair, gs4: attend_back(
        pair, gs4, gy4, att, x_own, x_far, qkv_own, qkv_far, probs, qkv_weight, out_weight, g1, g2
    )
    if packed:
        sent = r1.step(upb), r2.step(upb)
        r3 = Reduction(keep3, send3, shards)
        gs4, _ = tie(gs4, sent)
    own0, far0, vec0, dqkv0, gb0 = pair_back(0, gs4)
    if packed:
        sent = r1.step(vec0), r2.step(vec0), r3.step(vec0)
        gs4, _ = tie(gs4, sent)
    own1, far1, vec1, dqkv1, gb1 = pair_back(1, gs4)
    if packed:
        sent = r1.step(vec1), r2.step(vec1), r3.step(vec1)
        dqkv1, _ = tie(dqkv1, sent)
    vec, keep4, send4 = weight_grads(
        inv, dqkv0, dqkv1, gb0, gb1, mixed, fn_own, fn_far, vec0, vec1, upa, upb, dbg, shards, packed
    )
    ig_back = swap_sides(jnp.stack([far0, far1]))
    ig_own = jnp.stack([own0, own1])

    def settle(own, back):
        own, back = own[:, :real], back[:, :real]
        return jnp.where(
            side == 0, jnp.concatenate([own, back]), jnp.concatenate([back, own])
        )

    layer_out = settle(lo_own, lo_back)

    if packed:
        r4 = Reduction(keep4, send4, shards)
        r2.step(vec), r3.step(vec), r4.step()
        rows = width // shards
        down_g = r1.result()
        r3.step(), r4.step()
        up_g = jnp.concatenate(
            [unpack_rows(r.result(), tiles, rows) for r in (r2, r3)], axis=1
        )
        r4.step(), r4.step()
        rest = r4.result()
        mats = unpack_rows(rest[:, :-LANES], 4, rows)
        qkv_g, out_g = mats[:, : 3 * width], mats[:, 3 * width :]
        vecs = rest[:, -LANES:]
        one = lambda i: vecs[i, :rows]
        ln1g, ln1b, outb, ln2g, ln2b, downb = (one(i) for i in range(6))
        qvg, upg = vecs[6, : 2 * rows], vecs[7, : 4 * rows]
    else:
        total = lambda v: lax.psum_scatter(v, AXES, scatter_dimension=0, tiled=True)
        up_all = jnp.concatenate([keep2, keep3], axis=1)
        down_g, up_g, qkv_g, out_g = total(keep1), total(up_all), total(keep4), total(send4)
        ln1g, ln1b, outb, ln2g, ln2b, downb = (total(vec[i]) for i in (0, 1, 4, 5, 6, 7))
        qvg, upg = total(vec[2:4].reshape(-1)), total(vec[8:12].reshape(-1))
    input_grad = settle(ig_own, ig_back)
    return (
        layer_out, input_grad, ln1g, ln1b, qkv_g, qvg, out_g, outb, ln2g, ln2b, up_g, upg,
        down_g, downb,
    )


def solution(mesh):
    rows3 = P("pairs", "mod", None)
    vec, mat = P(AXES), P(AXES, None)
    return jax.shard_map(
        on_device,
        mesh=mesh,
        in_specs=(rows3, P("pairs"), P("pairs", "mod")) + (P(),) * 12 + (rows3,),
        out_specs=(rows3, rows3, vec, vec, mat, vec, mat, vec, vec, vec, mat, vec, mat, vec),
        check_vma=False,
    )
```

time: 727 us -> 229 us (0.31); the launches traced: 717 us -> 228 us
  waiting for transfers between devices: 350 us -> 52.6 us
  matrix products: 127 us -> 0 us
  local copies, waits for them, and re-layouts: 130 us -> 24.1 us
  Pallas kernels: 0 us -> 96.9 us
  blocking collectives: 42.7 us -> 0 us
  other arithmetic: 45.3 us -> 26.5 us
  starting transfers between devices: 7.51 us -> 26.2 us
  between operations: 14.5 us -> 1.53 us
    reduce_scatter x4 -> x0, waiting for transfers between devices: 310 us -> none  [the longest x1 142 us: on_device(): lax.psum_scatter(local_grads[10], ('pairs', 'mod'), scatter_dimension=0,...]
    dot_general x18 -> x0, matrix products: 127 us -> none  [the longest x4 29.9 us: t_times_rows(): lax.dot_general(left, right, (((0,), (0,)), ((), ())), preferred_element_...]
    pallas_call x0 -> x9, Pallas kernels: none -> 96.9 us  [the longest x1 22 us: mlp_up(): pl.pallas_call(partial(mlp_up_kernel, shard=shard if packed else 0), grid...]
    reshape x18 -> x7, local copies, waits for them, and re-layouts: 69.1 us -> 0.73 us  [the longest x1 0.71 us: on_device(): qvb = qv_bias.reshape(2, 1, width)]
    unnamed x1 -> x0, blocking collectives: 42.7 us -> none
    ppermute x5 -> x24, starting transfers between devices: 6.94 us -> 26.2 us  [the longest x16 18.8 us: step(): self.incoming = lax.ppermute(out, AXES, route)]
    convert_element_type x7 -> x0, local copies, waits for them, and re-layouts: 18.8 us -> none  [the longest x2 6.28 us: layer_pass(): mixed = mixed.reshape(flat, width).astype(jnp.bfloat16)]
    unnamed x121 -> x126, local copies, waits for them, and re-layouts: 30.4 us -> 14.3 us
  transfers between devices with their start and end apart: 9 -> 24, of which waited for: 6 -> 10; matrix products, arithmetic and copies ran while one was open for 22% -> 13% of each run, Pallas kernels for 0% -> 28%
where the time goes in v1:
time: 229 us; the launch traced here: 228 us
  Pallas kernels  96.9 us (42%)
  waiting for transfers between devices  52.6 us (23%)
  other arithmetic  26.5 us (12%)
  starting transfers between devices  26.2 us (11%)
  local copies, waits for them, and re-layouts  24.1 us (11%)
    ppermute x16, waiting for transfers between devices, step(): self.incoming = lax.ppermute(out, AXES, route)  34.6 us
    pallas_call x1, Pallas kernels, mlp_up(): pl.pallas_call(partial(mlp_up_kernel, shard=shard if packed else 0), grid...  22 us
    pallas_call x2, Pallas kernels, attend_back(): pl.pallas_call(attend_back_kernel, grid=(1,), in_specs=[pl.BlockSpec((2,...  21.4 us
    pallas_call x2, Pallas kernels, mlp_back(): pl.pallas_call(partial(mlp_back_kernel, shard=shard if packed else 0, fir...  21.2 us
    ppermute x16, starting transfers between devices, step(): self.incoming = lax.ppermute(out, AXES, route)  18.8 us
    ppermute x4, waiting for transfers between devices, swap_sides(): return lax.ppermute(block, 'mod', [(0, 1), (1, 0)])  17.9 us
    convert_element_type x16, other arithmetic, step(): out = add_up([t[self.n:] for t in self.terms]).astype(BF16)  17.6 us
    pallas_call x1, Pallas kernels, attend(): pl.pallas_call(attend_kernel, grid=(pairs,), in_specs=[pl.BlockSpec((1, h...  15.1 us
  transfers between devices with their start and end apart: 24, of which 10 were waited for; matrix products, arithmetic and copies ran while one was open for 13% of the time, Pallas kernels for 28%

profile of v1, /device:TPU:0, one launch (start us, length us, event | category | flops | bytes accessed | tf_op | source)
XLA Modules:
  0.0 227.8 jit_solution(5642852099390186635)
XLA Ops:
  2.7 4.7 %constant_dynamic-slice_fusion = (bf16[2,140,768]{2,0,1:T(2,128)(2,1)}, bf16[2,140,768]{2,0,1:T(2,128)(2,1)}, bf16[2,140,768]{2,0,1:T(2,128)(2,1)}, bf16[2,140,768]{2,0,1:T(2,128)(2,1)S(1)}) fusion(bf16[4,140,768]{2,0,1:T(4,128)(2,1)} %param.32, s32[]{:T(128)S(6)} %select_n.44, s32[]{:T(128)S(6)} %select_n.50, bf16[4,140,768]{2,0,1:T(4,128)(2,1)} %param.17), kind=kLoop, calls=%fused_computation.29 | loop fusion | bytes 3440648 | tf_op jit(solution)/shard_map/dynamic_slice | solution.py:715
  8.5 2.9 %collective-permute-start = (bf16[2,144,768]{2,1,0:T(8,128)(2,1)}, bf16[2,144,768]{2,1,0:T(8,128)(2,1)}, u32[]{:S(2)}, u32[]{:S(2)}) collective-permute-start(bf16[2,144,768]{2,1,0:T(8,128)(2,1)} %maximum_maximum_fusion), channel_id=1, source_target_pairs={{0,1},{1,0},{2,3},{3,2},{4,5},{5,4},{6,7},{7,6},{8,9},{9,8},{10,11... | collective-permute-start | bytes 1327112 | tf_op jit(solution)/shard_map/ppermute | solution.py:698
  12.7 1.1 copy.64
  13.9 1.1 copy.62
  15.2 6.7 %collective-permute-done.x_ref.xr = bf16[2,144,768]{2,1,0:T(8,128)(2,1)} collective-permute-done((bf16[2,144,768]{2,1,0:T(8,128)(2,1)}, bf16[2,144,768]{2,1,0:T(8,128)(2,1)}, u32[]{:S(2)}, u32[]{:S(2)}) %collective-permute-start) | collective-permute-done | bytes 442400 | tf_op jit(solution)/shard_map/ppermute | solution.py:698
  21.9 1.7 collective-permute-start.1
  23.6 2.3 norm_qkv.2
  26.2 3.3 %norm_qkv.3 = (bf16[2,144,768]{2,1,0:T(8,128)(2,1)S(1)}, bf16[2,144,2304]{2,1,0:T(8,128)(2,1)S(1)}) custom-call(bf16[2,144,768]{2,1,0:T(8,128)(2,1)} %collective-permute-done.x_ref.xr, f32[1,768]{1,0:T(1,128)S(1)} %reshape.89.g_ref.g1, f32[1,768]{1,0:T(1,128)S(1)} %reshape.90.b_ref, bf16[768,2304]{1,0:T(8,128)(2,1)S(1)} %copy-done, ...), custom_call_target="tpu_custom_call" | custom-call | flops 1019215872 | bytes 5750784 | tf_op jit(solution)/shard_map/norm_qkv/pallas_call | solution.py:84
  30.3 15.1 %attend.1 = (bf16[2,2,144,768]{3,2,1,0:T(8,128)(2,1)S(1)}, f32[2,2,144,768]{3,2,1,0:T(8,128)S(1)}, bf16[2,2,144,768]{3,2,1,0:T(8,128)(2,1)S(1)}, bf16[2,12,288,288]{3,2,1,0:T(8,128)(2,1)S(1)}) custom-call(bf16[2,144,2304]{2,1,0:T(8,128)(2,1)S(1)} %get-tuple-element.67.qo, bf16[2,144,2304]{2,1,0:T(8,128)(2,1)S(1)} %get-tuple-element.69.qr, ...), custom_call_target="tpu_custom_call" | custom-call | flops 2038431744 | bytes 11059200 | tf_op jit(solution)/shard_map/attend/pallas_call | solution.py:159
  45.5 2.3 %copy-done.1 = bf16[2,12,288,288]{3,2,1,0:T(8,128)(2,1)} copy-done((bf16[2,12,288,288]{3,2,1,0:T(8,128)(2,1)}, bf16[2,12,288,288]{3,2,1,0:T(8,128)(2,1)S(1)}, u32[]{:S(2)}) %copy-start.1) | copy-done | bytes 3981336
  48.7 22.0 %mlp_up.1 = (bf16[576,3072]{1,0:T(8,128)(2,1)}, bf16[2,144,768]{2,1,0:T(8,128)(2,1)S(1)}, bf16[2,144,768]{2,1,0:T(8,128)(2,1)S(1)}, bf16[576,768]{1,0:T(8,128)(2...) custom-call(s32[3]{0:T(128)S(1)} %pad_add_fusion.info, ...), custom_call_target="tpu_custom_call" | custom-call | flops 8153726976 | bytes 25165824 | tf_op jit(solution)/shard_map/mlp_up/pallas_call | solution.py:275
  72.3 10.6 %mlp_back.2 = (f32[576,768]{1,0:T(8,128)S(1)}, f32[1,1536]{1,0:T(1,128)S(1)}, bf16[16,16,2304]{2,1,0:T(8,128)(2,1)S(1)}, bf16[16,16,2304]{2,1,0:T(8,128)(2,1)}) custom-call(s32[32]{0:T(128)S(1)} %add_xor_fusion.inv, f32[8,128]{1,0:T(8,128)S(1)} %broadcast_in_dim.21.gs_in, bf16[576,768]{1,0:T(8,128)(2,1)S(1)} %get-tuple-element.75.gy, ...), custom_call_target="tpu_custom_call" | custom-call | flops 4076863488 | bytes 10485760 | tf_op jit(solution)/shard_map/mlp_back/pallas_call | solution.py:386
  83.4 3.1 %add_convert_fusion.1 = bf16[8,96,768]{2,1,0:T(8,128)(2,1)} fusion(bf16[16,96,768]{2,1,0:T(8,128)(2,1)} %collective-permute-done.3, bf16[16,96,768]{2,1,0:T(8,128)(2,1)S(1)} %copy-done.35), kind=kLoop, calls=%fused_computation.1 | loop fusion | flops 2359296 | bytes 3538944 | tf_op jit(solution)/shard_map/convert_element_type | solution.py:675
  86.5 1.5 collective-permute-start.4
  88.1 10.7 %mlp_back.3 = (f32[576,768]{1,0:T(8,128)S(1)}, f32[1,1536]{1,0:T(1,128)S(1)}, bf16[16,16,2304]{2,1,0:T(8,128)(2,1)S(1)}, bf16[16,16,2304]{2,1,0:T(8,128)(2,1)S(1)}) custom-call(s32[32]{0:T(128)S(1)} %add_xor_fusion.inv, f32[576,768]{1,0:T(8,128)} %copy-done.6, bf16[576,768]{1,0:T(8,128)(2,1)S(1)} %get-tuple-element.75.gy, ...), custom_call_target="tpu_custom_call" | custom-call | flops 4076863488 | bytes 10485760 | tf_op jit(solution)/shard_map/mlp_back/pallas_call | solution.py:386
  99.9 1.3 add_convert_fusion.4
  101.3 1.6 collective-permute-start.7
  102.9 1.9 add_convert_fusion.5
  104.8 1.7 collective-permute-start.6
  106.5 10.7 %attend_back.2 = (bf16[144,768]{1,0:T(8,128)(2,1)S(1)}, bf16[144,768]{1,0:T(8,128)(2,1)S(1)}, f32[8,768]{1,0:T(8,128)S(1)}, bf16[288,2304]{1,0:T(8,128)(2,1)S(1)}, bf16[288,768]{1,0:T(8,128)(2,1)S(1)}) custom-call(f32[2,2,144,768]{3,2,1,0:T(8,128)S(1)} %bitcast.56, bf16[2,2,144,768]{3,2,1,0:T(8,128)(2,1)S(1)} %bitcast.53, ...), custom_call_target="tpu_custom_call" | custom-call | flops 3397386240 | bytes 12582912 | tf_op jit(solution)/shard_map/attend_back/pallas_call | solution.py:489
  117.4 1.6 collective-permute-start.12
  119.0 1.2 add_convert_fusion.8
  120.7 1.5 add_convert_fusion.9
  122.8 10.7 %attend_back.3 = (bf16[144,768]{1,0:T(8,128)(2,1)S(1)}, bf16[144,768]{1,0:T(8,128)(2,1)S(1)}, f32[8,768]{1,0:T(8,128)S(1)}, bf16[288,2304]{1,0:T(8,128)(2,1)S(1)}, bf16[288,768]{1,0:T(8,128)(2,1)S(1)}) custom-call(f32[2,2,144,768]{3,2,1,0:T(8,128)S(1)} %bitcast.57, bf16[2,2,144,768]{3,2,1,0:T(8,128)(2,1)S(1)} %bitcast.54, ...), custom_call_target="tpu_custom_call" | custom-call | flops 3397386240 | bytes 12582912 | tf_op jit(solution)/shard_map/attend_back/pallas_call | solution.py:489
  134.5 2.5 %add_convert_fusion.12 = bf16[2,16,2304]{2,1,0:T(8,128)(2,1)} fusion(bf16[4,16,2304]{2,1,0:T(8,128)(2,1)S(1)} %collective-permute-done.11, bf16[8,16,2304]{2,1,0:T(8,128)(2,1)S(1)} %collective-permute-done.7, bf16[16,16,2304]{2,1,0:T(8,128)(2,1)} %collective-permute-done.5, bf16[16,16,2304]{2,1,0:T(8,128)(2,1)} %copy-done.9), kind=kLoop, calls=%fused_computation.20 | loop fusion | flops 589824 | bytes 737280 | tf_op jit(solution)/shard_map/convert_element_type | solution.py:675
  137.1 1.3 add_convert_fusion.13
  138.4 1.3 copy-done.24
  139.7 1.2 copy-done.33
  140.9 11.6 %weight_grads.1 = (f32[16,768]{1,0:T(8,128)}, bf16[16,16,4736]{2,1,0:T(8,128)(2,1)}, bf16[16,16,4736]{2,1,0:T(8,128)(2,1)}) custom-call(s32[32]{0:T(128)S(1)} %add_xor_fusion.inv, bf16[288,2304]{1,0:T(8,128)(2,1)S(1)} %copy-done.22, bf16[288,2304]{1,0:T(8,128)(2,1)S(1)} %copy-done.24, bf16[288,768]{1,0:T(8,128)(2,1)S(1)} %get-tuple-element.109.gb0, ...), custom_call_target="tpu_custom_call" | custom-call | flops 2717908992 | bytes 14680064 | tf_op jit(solution)/shard_map/weight_grads/pallas_call | solution.py:610
  152.5 1.5 collective-permute-start.2
  154.0 11.2 %collective-permute-done.2 = bf16[2,144,768]{2,1,0:T(8,128)(2,1)} collective-permute-done((bf16[2,144,768]{2,1,0:T(8,128)(2,1)S(1)}, bf16[2,144,768]{2,1,0:T(8,128)(2,1)}, u32[]{:S(2)}, u32[]{:S(2)}) %collective-permute-start.2) | collective-permute-done | bytes 442400 | tf_op jit(solution)/shard_map/ppermute | solution.py:698
  165.2 1.4 maximum_select_fusion
  166.6 1.3 copy.60
  168.0 1.5 collective-permute-start.18
  169.5 1.6 collective-permute-start.20
  171.7 2.7 %collective-permute-start.23 = (bf16[1,96,768]{2,1,0:T(8,128)(2,1)S(1)}, bf16[1,96,768]{2,1,0:T(8,128)(2,1)S(1)}, u32[]{:S(2)}, u32[]{:S(2)}) collective-permute-start(bf16[1,96,768]{2,1,0:T(8,128)(2,1)S(1)} %add_convert_fusion.13), channel_id=1, source_target_pairs={{0,16},{1,17},{2,18},{3,19},{4,20},{5,21},{6,22},{7,23},{8,24},{9,... | collective-permute-start | bytes 442376 | tf_op jit(solution)/shard_map/ppermute | solution.py:678
  175.7 2.6 %collective-permute-start.19 = (bf16[1,16,2304]{2,1,0:T(8,128)(2,1)S(1)}, bf16[1,16,2304]{2,1,0:T(8,128)(2,1)S(1)}, u32[]{:S(2)}, u32[]{:S(2)}) collective-permute-start(bf16[1,16,2304]{2,1,0:T(8,128)(2,1)S(1)} %add_convert_fusion.15), channel_id=1, source_target_pairs={{0,16},{1,17},{2,18},{3,19},{4,20},{5,21},{6,22},{7,23},{8,24},{9,... | collective-permute-start | bytes 221192 | tf_op jit(solution)/shard_map/ppermute | solution.py:678
  178.3 3.1 %collective-permute-done.20 = bf16[4,16,2304]{2,1,0:T(8,128)(2,1)S(1)} collective-permute-done((bf16[4,16,2304]{2,1,0:T(8,128)(2,1)S(1)}, bf16[4,16,2304]{2,1,0:T(8,128)(2,1)S(1)}, u32[]{:S(2)}, u32[]{:S(2)}) %collective-permute-start.20) | collective-permute-done | bytes 294944 | tf_op jit(solution)/shard_map/ppermute | solution.py:678
  181.7 1.1 collective-permute-start.14
  182.8 1.1 add_convert_fusion.11
  185.0 4.1 %collective-permute-done.21 = bf16[2,16,2304]{2,1,0:T(8,128)(2,1)S(1)} collective-permute-done((bf16[2,16,2304]{2,1,0:T(8,128)(2,1)S(1)}, bf16[2,16,2304]{2,1,0:T(8,128)(2,1)S(1)}, u32[]{:S(2)}, u32[]{:S(2)}) %collective-permute-start.21) | collective-permute-done | bytes 147488 | tf_op jit(solution)/shard_map/ppermute | solution.py:678
  189.0 10.6 %collective-permute-done.14 = bf16[8,16,4736]{2,1,0:T(8,128)(2,1)S(1)} collective-permute-done((bf16[8,16,4736]{2,1,0:T(8,128)(2,1)S(1)}, bf16[8,16,4736]{2,1,0:T(8,128)(2,1)S(1)}, u32[]{:S(2)}, u32[]{:S(2)}) %collective-permute-start.14) | collective-permute-done | bytes 1212448 | tf_op jit(solution)/shard_map/ppermute | solution.py:678
  201.1 1.3 copy.61
  202.4 1.6 collective-permute-start.22
  204.1 2.0 add_bitcast_fusion.1
  206.0 4.8 %collective-permute-done.15 = bf16[4,16,4736]{2,1,0:T(8,128)(2,1)S(1)} collective-permute-done((bf16[4,16,4736]{2,1,0:T(8,128)(2,1)S(1)}, bf16[4,16,4736]{2,1,0:T(8,128)(2,1)S(1)}, u32[]{:S(2)}, u32[]{:S(2)}) %collective-permute-start.15) | collective-permute-done | bytes 606240 | tf_op jit(solution)/shard_map/ppermute | solution.py:678
  212.1 5.8 %collective-permute-done.16 = bf16[2,16,4736]{2,1,0:T(8,128)(2,1)S(1)} collective-permute-done((bf16[2,16,4736]{2,1,0:T(8,128)(2,1)S(1)}, bf16[2,16,4736]{2,1,0:T(8,128)(2,1)S(1)}, u32[]{:S(2)}, u32[]{:S(2)}) %collective-permute-start.16) | collective-permute-done | bytes 303136 | tf_op jit(solution)/shard_map/ppermute | solution.py:678
  218.8 5.9 %collective-permute-done.17 = bf16[1,16,4736]{2,1,0:T(8,128)(2,1)S(1)} collective-permute-done((bf16[1,16,4736]{2,1,0:T(8,128)(2,1)S(1)}, bf16[1,16,4736]{2,1,0:T(8,128)(2,1)S(1)}, u32[]{:S(2)}, u32[]{:S(2)}) %collective-permute-start.17) | collective-permute-done | bytes 151584 | tf_op jit(solution)/shard_map/ppermute | solution.py:678
  (196 shorter events, 22.3 us)
Async XLA Ops:
  7.6 16.1 %copy-start = (bf16[768,2304]{1,0:T(8,128)(2,1)S(1)}, bf16[768,2304]{1,0:T(8,128)(2,1)}, u32[]{:S(2)}) copy-start(bf16[768,2304]{1,0:T(8,128)(2,1)} %qkvw.3) | copy-start | bytes 10616836
  8.5 13.4 %collective-permute-start = (bf16[2,144,768]{2,1,0:T(8,128)(2,1)}, bf16[2,144,768]{2,1,0:T(8,128)(2,1)}, u32[]{:S(2)}, u32[]{:S(2)}) collective-permute-start(bf16[2,144,768]{2,1,0:T(8,128)(2,1)} %maximum_maximum_fusion), channel_id=1, source_target_pairs={{0,1},{1,0},{2,3},{3,2},{4,5},{5,4},{6,7},{7,6},{8,9},{9,8},{10,11... | collective-permute-start | bytes 1327112 | tf_op jit(solution)/shard_map/ppermute | solution.py:698
  15.1 10.8 %copy-start.51 = (f32[768]{0:T(1024)S(1)}, f32[768]{0:T(1024)}, u32[]{:S(2)}) copy-start(f32[768]{0:T(1024)} %param.26) | copy-start | bytes 9220
  15.1 10.8 %copy-start.52 = (f32[768]{0:T(1024)S(1)}, f32[768]{0:T(1024)}, u32[]{:S(2)}) copy-start(f32[768]{0:T(1024)} %param.25) | copy-start | bytes 9220
  15.1 10.9 %copy-start.53 = (f32[768]{0:T(1024)S(1)}, f32[768]{0:T(1024)}, u32[]{:S(2)}) copy-start(f32[768]{0:T(1024)} %param.27) | copy-start | bytes 9220
  15.2 10.9 %copy-start.54 = (f32[768]{0:T(1024)S(1)}, f32[768]{0:T(1024)}, u32[]{:S(2)}) copy-start(f32[768]{0:T(1024)} %param.31) | copy-start | bytes 9220
  15.2 10.9 %copy-start.36 = (bf16[2,140,768]{2,0,1:T(2,128)(2,1)S(1)}, bf16[2,140,768]{2,0,1:T(2,128)(2,1)}, u32[]{:S(2)}) copy-start(bf16[2,140,768]{2,0,1:T(2,128)(2,1)} %get-tuple-element.162) | copy-start | bytes 1290244
  21.9 26.8 %collective-permute-start.1 = (bf16[2,144,768]{2,1,0:T(8,128)(2,1)S(1)}, bf16[2,144,768]{2,1,0:T(8,128)(2,1)S(1)}, u32[]{:S(2)}, u32[]{:S(2)}) collective-permute-start(bf16[2,144,768]{2,1,0:T(8,128)(2,1)S(1)} %pad.20), channel_id=1, source_target_pairs={{0,1},{1,0},{2,3},{3,2},{4,5},{5,4},{6,7},{7,6},{8,9},{9,8},{10,11... | collective-permute-start | bytes 1327112 | tf_op jit(solution)/shard_map/ppermute | solution.py:698
  30.3 15.1 %copy-start.2 = (bf16[2,144,2304]{2,1,0:T(8,128)(2,1)}, bf16[2,144,2304]{2,1,0:T(8,128)(2,1)S(1)}, u32[]{:S(2)}) copy-start(bf16[2,144,2304]{2,1,0:T(8,128)(2,1)S(1)} %get-tuple-element.69.qr) | copy-start | bytes 3981316
  30.3 18.4 %copy-start.31 = (f32[3072]{0:T(1024)S(1)}, f32[3072]{0:T(1024)}, u32[]{:S(2)}) copy-start(f32[3072]{0:T(1024)} %param.29) | copy-start | bytes 36868
  72.3 11.1 %collective-permute-start.3 = (bf16[16,96,768]{2,1,0:T(8,128)(2,1)}, bf16[16,96,768]{2,1,0:T(8,128)(2,1)}, u32[]{:S(2)}, u32[]{:S(2)}) collective-permute-start(bf16[16,96,768]{2,1,0:T(8,128)(2,1)} %get-tuple-element.79), channel_id=1, source_target_pairs={{0,2},{1,3},{2,0},{3,1},{4,6},{5,7},{6,4},{7,5},{8,10},{9,11},{10,... | collective-permute-start | bytes 7077896 | tf_op jit(solution)/shard_map/ppermute | solution.py:669
  72.3 11.1 %copy-start.35 = (bf16[16,96,768]{2,1,0:T(8,128)(2,1)S(1)}, bf16[16,96,768]{2,1,0:T(8,128)(2,1)}, u32[]{:S(2)}) copy-start(bf16[16,96,768]{2,1,0:T(8,128)(2,1)} %get-tuple-element.78) | copy-start | bytes 7077892
  82.9 17.0 %collective-permute-start.5 = (bf16[16,16,2304]{2,1,0:T(8,128)(2,1)}, bf16[16,16,2304]{2,1,0:T(8,128)(2,1)}, u32[]{:S(2)}, u32[]{:S(2)}) collective-permute-start(bf16[16,16,2304]{2,1,0:T(8,128)(2,1)} %get-tuple-element.87), channel_id=1, source_target_pairs={{0,2},{1,3},{2,0},{3,1},{4,6},{5,7},{6,4},{7,5},{8,10},{9,11},{10,... | collective-permute-start | bytes 3538952 | tf_op jit(solution)/shard_map/ppermute | solution.py:669
  86.5 16.4 %collective-permute-start.4 = (bf16[8,96,768]{2,1,0:T(8,128)(2,1)}, bf16[8,96,768]{2,1,0:T(8,128)(2,1)S(1)}, u32[]{:S(2)}, u32[]{:S(2)}) collective-permute-start(bf16[8,96,768]{2,1,0:T(8,128)(2,1)} %add_convert_fusion.1), channel_id=1, source_target_pairs={{0,4},{1,5},{2,10},{3,11},{4,0},{5,1},{6,14},{7,15},{8,12},{9,13},... | collective-permute-start | bytes 3538952 | tf_op jit(solution)/shard_map/ppermute | solution.py:678
  88.1 11.9 %copy-start.10 = (bf16[16,16,2304]{2,1,0:T(8,128)(2,1)S(1)}, bf16[16,16,2304]{2,1,0:T(8,128)(2,1)}, u32[]{:S(2)}) copy-start(bf16[16,16,2304]{2,1,0:T(8,128)(2,1)} %copy-done.9) | copy-start | bytes 3538948
  99.8 17.5 %collective-permute-start.8 = (bf16[16,16,2304]{2,1,0:T(8,128)(2,1)S(1)}, bf16[16,16,2304]{2,1,0:T(8,128)(2,1)S(1)}, u32[]{:S(2)}, u32[]{:S(2)}) collective-permute-start(bf16[16,16,2304]{2,1,0:T(8,128)(2,1)S(1)} %get-tuple-element.96), channel_id=1, source_target_pairs={{0,2},{1,3},{2,0},{3,1},{4,6},{5,7},{6,4},{7,5},{8,10},{9,11},{10,... | collective-permute-start | bytes 3538952 | tf_op jit(solution)/shard_map/ppermute | solution.py:669
  99.9 6.6 %copy-start.5 = (bf16[768,768]{1,0:T(8,128)(2,1)S(1)}, bf16[768,768]{1,0:T(8,128)(2,1)}, u32[]{:S(2)}) copy-start(bf16[768,768]{1,0:T(8,128)(2,1)} %ow.5) | copy-start | bytes 3538948
  101.2 5.3 %copy-start.3 = (bf16[2,144,2304]{2,1,0:T(8,128)(2,1)S(1)}, bf16[2,144,2304]{2,1,0:T(8,128)(2,1)}, u32[]{:S(2)}) copy-start(bf16[2,144,2304]{2,1,0:T(8,128)(2,1)} %copy-done.2) | copy-start | bytes 3981316
  101.3 16.0 %collective-permute-start.7 = (bf16[8,16,2304]{2,1,0:T(8,128)(2,1)S(1)}, bf16[8,16,2304]{2,1,0:T(8,128)(2,1)S(1)}, u32[]{:S(2)}, u32[]{:S(2)}) collective-permute-start(bf16[8,16,2304]{2,1,0:T(8,128)(2,1)S(1)} %add_convert_fusion.4), channel_id=1, source_target_pairs={{0,4},{1,5},{2,10},{3,11},{4,0},{5,1},{6,14},{7,15},{8,12},{9,13},... | collective-permute-start | bytes 1769480 | tf_op jit(solution)/shard_map/ppermute | solution.py:678
  104.8 15.9 %collective-permute-start.6 = (bf16[4,96,768]{2,1,0:T(8,128)(2,1)S(1)}, bf16[4,96,768]{2,1,0:T(8,128)(2,1)S(1)}, u32[]{:S(2)}, u32[]{:S(2)}) collective-permute-start(bf16[4,96,768]{2,1,0:T(8,128)(2,1)S(1)} %add_convert_fusion.5), channel_id=1, source_target_pairs={{0,8},{1,9},{2,6},{3,7},{4,12},{5,13},{6,2},{7,3},{8,0},{9,1},{10,... | collective-permute-start | bytes 1769480 | tf_op jit(solution)/shard_map/ppermute | solution.py:678
  106.5 10.8 %copy-start.8 = (bf16[16,16,2304]{2,1,0:T(8,128)(2,1)S(1)}, bf16[16,16,2304]{2,1,0:T(8,128)(2,1)}, u32[]{:S(2)}) copy-start(bf16[16,16,2304]{2,1,0:T(8,128)(2,1)} %copy-done.7) | copy-start | bytes 3538948
  117.2 16.5 %copy-start.37 = (bf16[16,16,2304]{2,1,0:T(8,128)(2,1)}, bf16[16,16,2304]{2,1,0:T(8,128)(2,1)S(1)}, u32[]{:S(2)}) copy-start(bf16[16,16,2304]{2,1,0:T(8,128)(2,1)S(1)} %collective-permute-done.8) | copy-start | bytes 3538948
  117.3 17.3 %copy-start.42 = (bf16[8,16,2304]{2,1,0:T(8,128)(2,1)}, bf16[8,16,2304]{2,1,0:T(8,128)(2,1)S(1)}, u32[]{:S(2)}) copy-start(bf16[8,16,2304]{2,1,0:T(8,128)(2,1)S(1)} %collective-permute-done.7) | copy-start | bytes 1769476
  117.4 16.3 %collective-permute-start.12 = (bf16[8,16,2304]{2,1,0:T(8,128)(2,1)S(1)}, bf16[8,16,2304]{2,1,0:T(8,128)(2,1)S(1)}, u32[]{:S(2)}, u32[]{:S(2)}) collective-permute-start(bf16[8,16,2304]{2,1,0:T(8,128)(2,1)S(1)} %add_convert_fusion.3), channel_id=1, source_target_pairs={{0,4},{1,5},{2,10},{3,11},{4,0},{5,1},{6,14},{7,15},{8,12},{9,13},... | collective-permute-start | bytes 1769480 | tf_op jit(solution)/shard_map/ppermute | solution.py:678
  120.2 13.4 %collective-permute-start.11 = (bf16[4,16,2304]{2,1,0:T(8,128)(2,1)S(1)}, bf16[4,16,2304]{2,1,0:T(8,128)(2,1)S(1)}, u32[]{:S(2)}, u32[]{:S(2)}) collective-permute-start(bf16[4,16,2304]{2,1,0:T(8,128)(2,1)S(1)} %add_convert_fusion.8), channel_id=1, source_target_pairs={{0,8},{1,9},{2,6},{3,7},{4,12},{5,13},{6,2},{7,3},{8,0},{9,1},{10,... | collective-permute-start | bytes 884744 | tf_op jit(solution)/shard_map/ppermute | solution.py:678
  120.7 16.3 %copy-start.39 = (bf16[4,96,768]{2,1,0:T(8,128)(2,1)}, bf16[4,96,768]{2,1,0:T(8,128)(2,1)S(1)}, u32[]{:S(2)}) copy-start(bf16[4,96,768]{2,1,0:T(8,128)(2,1)S(1)} %collective-permute-done.6) | copy-start | bytes 1769476
  122.2 14.8 %collective-permute-start.10 = (bf16[2,96,768]{2,1,0:T(8,128)(2,1)S(1)}, bf16[2,96,768]{2,1,0:T(8,128)(2,1)S(1)}, u32[]{:S(2)}, u32[]{:S(2)}) collective-permute-start(bf16[2,96,768]{2,1,0:T(8,128)(2,1)S(1)} %add_convert_fusion.9), channel_id=1, source_target_pairs={{0,1},{1,0},{2,3},{3,2},{4,5},{5,4},{6,7},{7,6},{8,9},{9,8},{10,11... | collective-permute-start | bytes 884744 | tf_op jit(solution)/shard_map/ppermute | solution.py:678
  133.6 4.7 %copy-start.22 = (bf16[288,2304]{1,0:T(8,128)(2,1)S(1)}, bf16[288,2304]{1,0:T(8,128)(2,1)}, u32[]{:S(2)}) copy-start(bf16[288,2304]{1,0:T(8,128)(2,1)} %copy-done.21) | copy-start | bytes 3981316
  133.7 4.7 %copy-start.26 = (bf16[2,144,768]{2,1,0:T(8,128)(2,1)S(1)}, bf16[2,144,768]{2,1,0:T(8,128)(2,1)}, u32[]{:S(2)}) copy-start(bf16[2,144,768]{2,1,0:T(8,128)(2,1)} %copy-done.25) | copy-start | bytes 1327108
  140.9 11.6 %copy-start.28 = (bf16[2,144,768]{2,1,0:T(8,128)(2,1)S(1)}, bf16[2,144,768]{2,1,0:T(8,128)(2,1)}, u32[]{:S(2)}) copy-start(bf16[2,144,768]{2,1,0:T(8,128)(2,1)} %copy-done.27) | copy-start | bytes 1327108
  140.9 24.3 %copy-start.12 = (bf16[2,144,768]{2,1,0:T(8,128)(2,1)S(1)}, bf16[2,144,768]{2,1,0:T(8,128)(2,1)}, u32[]{:S(2)}) copy-start(bf16[2,144,768]{2,1,0:T(8,128)(2,1)} %copy-done.11) | copy-start | bytes 1327108
  152.5 28.9 %collective-permute-start.13 = (bf16[16,16,4736]{2,1,0:T(8,128)(2,1)}, bf16[16,16,4736]{2,1,0:T(8,128)(2,1)S(1)}, u32[]{:S(2)}, u32[]{:S(2)}) collective-permute-start(bf16[16,16,4736]{2,1,0:T(8,128)(2,1)} %get-tuple-element.116), channel_id=1, source_target_pairs={{0,2},{1,3},{2,0},{3,1},{4,6},{5,7},{6,4},{7,5},{8,10},{9,11},{10,... | collective-permute-start | bytes 7274504 | tf_op jit(solution)/shard_map/ppermute | solution.py:669
  152.5 12.7 %collective-permute-start.2 = (bf16[2,144,768]{2,1,0:T(8,128)(2,1)S(1)}, bf16[2,144,768]{2,1,0:T(8,128)(2,1)}, u32[]{:S(2)}, u32[]{:S(2)}) collective-permute-start(bf16[2,144,768]{2,1,0:T(8,128)(2,1)S(1)} %copy-done.28), channel_id=1, source_target_pairs={{0,1},{1,0},{2,3},{3,2},{4,5},{5,4},{6,7},{7,6},{8,9},{9,8},{10,11... | collective-permute-start | bytes 1327112 | tf_op jit(solution)/shard_map/ppermute | solution.py:698
  165.2 9.5 %copy-start.46 = (bf16[4,16,2304]{2,1,0:T(8,128)(2,1)S(1)}, bf16[4,16,2304]{2,1,0:T(8,128)(2,1)}, u32[]{:S(2)}) copy-start(bf16[4,16,2304]{2,1,0:T(8,128)(2,1)} %copy-done.45) | copy-start | bytes 884740
  166.6 5.1 %copy-start.14 = (bf16[144,768]{1,0:T(8,128)(2,1)S(1)}, bf16[144,768]{1,0:T(8,128)(2,1)}, u32[]{:S(2)}) copy-start(bf16[144,768]{1,0:T(8,128)(2,1)} %copy-done.13) | copy-start | bytes 663556
  166.6 5.1 %copy-start.18 = (bf16[144,768]{1,0:T(8,128)(2,1)S(1)}, bf16[144,768]{1,0:T(8,128)(2,1)}, u32[]{:S(2)}) copy-start(bf16[144,768]{1,0:T(8,128)(2,1)} %copy-done.17) | copy-start | bytes 663556
  166.6 14.8 %copy-start.34 = (bf16[16,16,4736]{2,1,0:T(8,128)(2,1)S(1)}, bf16[16,16,4736]{2,1,0:T(8,128)(2,1)}, u32[]{:S(2)}) copy-start(bf16[16,16,4736]{2,1,0:T(8,128)(2,1)} %get-tuple-element.115) | copy-start | bytes 7274500
  168.0 6.7 %collective-permute-start.18 = (bf16[2,16,2304]{2,1,0:T(8,128)(2,1)S(1)}, bf16[2,16,2304]{2,1,0:T(8,128)(2,1)S(1)}, u32[]{:S(2)}, u32[]{:S(2)}) collective-permute-start(bf16[2,16,2304]{2,1,0:T(8,128)(2,1)S(1)} %copy-done.48), channel_id=1, source_target_pairs={{0,1},{1,0},{2,3},{3,2},{4,5},{5,4},{6,7},{7,6},{8,9},{9,8},{10,11... | collective-permute-start | bytes 442376 | tf_op jit(solution)/shard_map/ppermute | solution.py:678
  169.5 11.9 %collective-permute-start.20 = (bf16[4,16,2304]{2,1,0:T(8,128)(2,1)S(1)}, bf16[4,16,2304]{2,1,0:T(8,128)(2,1)S(1)}, u32[]{:S(2)}, u32[]{:S(2)}) collective-permute-start(bf16[4,16,2304]{2,1,0:T(8,128)(2,1)S(1)} %copy-done.47), channel_id=1, source_target_pairs={{0,8},{1,9},{2,6},{3,7},{4,12},{5,13},{6,2},{7,3},{8,0},{9,1},{10,... | collective-permute-start | bytes 884744 | tf_op jit(solution)/shard_map/ppermute | solution.py:678
  171.1 29.8 %collective-permute-start.9 = (bf16[2,144,768]{2,1,0:T(8,128)(2,1)S(1)}, bf16[2,144,768]{2,1,0:T(8,128)(2,1)S(1)}, u32[]{:S(2)}, u32[]{:S(2)}) collective-permute-start(bf16[2,144,768]{2,1,0:T(8,128)(2,1)S(1)} %pad_maximum_fusion.1), channel_id=1, source_target_pairs={{0,1},{1,0},{2,3},{3,2},{4,5},{5,4},{6,7},{7,6},{8,9},{9,8},{10,11... | collective-permute-start | bytes 1327112 | tf_op jit(solution)/shard_map/ppermute | solution.py:698
  171.7 32.3 %collective-permute-start.23 = (bf16[1,96,768]{2,1,0:T(8,128)(2,1)S(1)}, bf16[1,96,768]{2,1,0:T(8,128)(2,1)S(1)}, u32[]{:S(2)}, u32[]{:S(2)}) collective-permute-start(bf16[1,96,768]{2,1,0:T(8,128)(2,1)S(1)} %add_convert_fusion.13), channel_id=1, source_target_pairs={{0,16},{1,17},{2,18},{3,19},{4,20},{5,21},{6,22},{7,23},{8,24},{9,... | collective-permute-start | bytes 442376 | tf_op jit(solution)/shard_map/ppermute | solution.py:678
  175.7 8.2 %collective-permute-start.19 = (bf16[1,16,2304]{2,1,0:T(8,128)(2,1)S(1)}, bf16[1,16,2304]{2,1,0:T(8,128)(2,1)S(1)}, u32[]{:S(2)}, u32[]{:S(2)}) collective-permute-start(bf16[1,16,2304]{2,1,0:T(8,128)(2,1)S(1)} %add_convert_fusion.15), channel_id=1, source_target_pairs={{0,16},{1,17},{2,18},{3,19},{4,20},{5,21},{6,22},{7,23},{8,24},{9,... | collective-permute-start | bytes 221192 | tf_op jit(solution)/shard_map/ppermute | solution.py:678
  181.7 17.9 %collective-permute-start.14 = (bf16[8,16,4736]{2,1,0:T(8,128)(2,1)S(1)}, bf16[8,16,4736]{2,1,0:T(8,128)(2,1)S(1)}, u32[]{:S(2)}, u32[]{:S(2)}) collective-permute-start(bf16[8,16,4736]{2,1,0:T(8,128)(2,1)S(1)} %add_convert_fusion), channel_id=1, source_target_pairs={{0,4},{1,5},{2,10},{3,11},{4,0},{5,1},{6,14},{7,15},{8,12},{9,13},... | collective-permute-start | bytes 3637256 | tf_op jit(solution)/shard_map/ppermute | solution.py:678
  183.8 5.2 %collective-permute-start.21 = (bf16[2,16,2304]{2,1,0:T(8,128)(2,1)S(1)}, bf16[2,16,2304]{2,1,0:T(8,128)(2,1)S(1)}, u32[]{:S(2)}, u32[]{:S(2)}) collective-permute-start(bf16[2,16,2304]{2,1,0:T(8,128)(2,1)S(1)} %add_convert_fusion.11), channel_id=1, source_target_pairs={{0,1},{1,0},{2,3},{3,2},{4,5},{5,4},{6,7},{7,6},{8,9},{9,8},{10,11... | collective-permute-start | bytes 442376 | tf_op jit(solution)/shard_map/ppermute | solution.py:678
  199.9 10.9 %collective-permute-start.15 = (bf16[4,16,4736]{2,1,0:T(8,128)(2,1)S(1)}, bf16[4,16,4736]{2,1,0:T(8,128)(2,1)S(1)}, u32[]{:S(2)}, u32[]{:S(2)}) collective-permute-start(bf16[4,16,4736]{2,1,0:T(8,128)(2,1)S(1)} %add_convert_fusion.2), channel_id=1, source_target_pairs={{0,8},{1,9},{2,6},{3,7},{4,12},{5,13},{6,2},{7,3},{8,0},{9,1},{10,... | collective-permute-start | bytes 1818632 | tf_op jit(solution)/shard_map/ppermute | solution.py:678
  202.4 8.6 %collective-permute-start.22 = (bf16[1,16,2304]{2,1,0:T(8,128)(2,1)S(1)}, bf16[1,16,2304]{2,1,0:T(8,128)(2,1)S(1)}, u32[]{:S(2)}, u32[]{:S(2)}) collective-permute-start(bf16[1,16,2304]{2,1,0:T(8,128)(2,1)S(1)} %add_convert_fusion.14), channel_id=1, source_target_pairs={{0,16},{1,17},{2,18},{3,19},{4,20},{5,21},{6,22},{7,23},{8,24},{9,... | collective-permute-start | bytes 221192 | tf_op jit(solution)/shard_map/ppermute | solution.py:678
  211.0 6.9 %collective-permute-start.16 = (bf16[2,16,4736]{2,1,0:T(8,128)(2,1)S(1)}, bf16[2,16,4736]{2,1,0:T(8,128)(2,1)S(1)}, u32[]{:S(2)}, u32[]{:S(2)}) collective-permute-start(bf16[2,16,4736]{2,1,0:T(8,128)(2,1)S(1)} %add_convert_fusion.6), channel_id=1, source_target_pairs={{0,1},{1,0},{2,3},{3,2},{4,5},{5,4},{6,7},{7,6},{8,9},{9,8},{10,11... | collective-permute-start | bytes 909320 | tf_op jit(solution)/shard_map/ppermute | solution.py:678
  218.0 6.8 %collective-permute-start.17 = (bf16[1,16,4736]{2,1,0:T(8,128)(2,1)S(1)}, bf16[1,16,4736]{2,1,0:T(8,128)(2,1)S(1)}, u32[]{:S(2)}, u32[]{:S(2)}) collective-permute-start(bf16[1,16,4736]{2,1,0:T(8,128)(2,1)S(1)} %add_convert_fusion.10), channel_id=1, source_target_pairs={{0,16},{1,17},{2,18},{3,19},{4,20},{5,21},{6,22},{7,23},{8,24},{9,... | collective-permute-start | bytes 454664 | tf_op jit(solution)/shard_map/ppermute | solution.py:678
  (36 other events, 104.8 us)

commit v2 on v1

v2 whole, which is shorter than its diff:
```python
from functools import partial

import jax
import jax.numpy as jnp
import numpy as np
from jax import lax
from jax.experimental import pallas as pl
from jax.experimental.pallas import tpu as pltpu
from jax.sharding import PartitionSpec as P

HEAD_DIM = 64
TXT = 40
EPS = 1e-06
MASKED = -1e30
AXES = ("pairs", "mod")
BF16 = jnp.bfloat16
F32 = jnp.float32
LANES = 128
PAD = 4
MIB = 1 << 20

CORE_BIT = 2
ORDERS = ((4, 8, 1, 16), (8, 4, 1, 16))
EARLY = 4


def dot_nn(a, b):
    return jnp.dot(a, b, preferred_element_type=F32)


def dot_nt(a, b):
    return lax.dot_general(a, b, (((1,), (1,)), ((), ())), preferred_element_type=F32)


def dot_tn(a, b):
    return lax.dot_general(a, b, (((0,), (0,)), ((), ())), preferred_element_type=F32)


def norm_parts(v):
    center = v - jnp.mean(v, axis=-1, keepdims=True)
    rstd = lax.rsqrt(jnp.mean(center * center, axis=-1, keepdims=True) + EPS)
    return center * rstd, rstd


def norm_back(grad, unit, rstd, gain):
    d = grad * gain
    return rstd * (
        d
        - jnp.mean(d, axis=-1, keepdims=True)
        - unit * jnp.mean(d * unit, axis=-1, keepdims=True)
    )


def gelu_and_slope(v):
    phi = 0.5 + 0.5 * lax.erf(v * 0.7071067811865476)
    bell = jnp.exp2(v * v * -0.7213475204444817)
    return v * phi, phi + v * bell * 0.3989422804014327


def lane_block(i, size=LANES):
    return pl.ds(pl.multiple_of(i * size, LANES), size)


def spec_of(a):
    return pl.BlockSpec(a.shape, lambda *_: (0,) * len(a.shape))


def struct(shape, dtype):
    return jax.ShapeDtypeStruct(shape, dtype)


def kept(shape, dtype):
    return pltpu.HBM(shape, dtype)


def params_of(mib):
    return pltpu.CompilerParams(vmem_limit_bytes=mib * MIB)


def column_sums(value):
    return jnp.sum(value, axis=0, keepdims=True)


def wire_rows(left, inv, tall, out, shard):
    tall[...] = jnp.transpose(left.astype(F32))
    count = tall.shape[0] // shard

    def two(i, carry):
        rows = [
            tall[pl.ds(pl.multiple_of(inv[2 * i + k] * shard + 8 * g, 8), 8), :]
            for k in range(2)
            for g in range(shard // 8)
        ]
        at = pl.multiple_of(2 * shard * i, 2 * shard)
        out[pl.ds(at, 2 * shard), :] = jnp.concatenate(rows, axis=0).astype(BF16)
        return carry

    lax.fori_loop(0, count // 2, two, 0)


def own_rows(info, p, far, half):
    side = info[2] if far == 0 else 1 - info[2]
    real = half - PAD
    row = lax.broadcasted_iota(jnp.int32, (half, 1), 0)
    return row < jnp.minimum(TXT + info[p] - side * real, real)


def norm_qkv_kernel(x_ref, g_ref, b_ref, w_ref, qvb_ref, fn_ref, qkv_ref):
    j = pl.program_id(0)
    rows, width = fn_ref.shape[0] * fn_ref.shape[1], fn_ref.shape[2]

    @pl.when(j == 0)
    def _():
        unit, _ = norm_parts(x_ref[...].reshape(rows, width).astype(F32))
        fn_ref[...] = (unit * g_ref[...] + b_ref[...]).astype(BF16).reshape(fn_ref.shape)

    fn = fn_ref[...].reshape(rows, width)
    out = dot_nn(fn, w_ref[...]) + jnp.where(j == 1, 0.0, 1.0) * qvb_ref[0]
    qkv_ref[...] = out.astype(BF16).reshape(qkv_ref.shape)


def norm_qkv(x, gain, shift, weight, qv_bias):
    pairs, half, width = x.shape
    return pl.pallas_call(
        norm_qkv_kernel,
        grid=(3,),
        in_specs=[
            spec_of(x),
            spec_of(gain),
            spec_of(shift),
            pl.BlockSpec((width, width), lambda j: (0, j)),
            pl.BlockSpec((1, 1, width), lambda j: (j // 2, 0, 0)),
        ],
        out_specs=[spec_of(x), pl.BlockSpec((pairs, half, width), lambda j: (0, 0, j))],
        out_shape=[kept((pairs, half, width), BF16), kept((pairs, half, 3 * width), BF16)],
        compiler_params=params_of(24),
        cost_estimate=pl.CostEstimate(
            flops=6 * pairs * half * width * width,
            bytes_accessed=2 * (3 * width * width + 5 * pairs * half * width),
            transcendentals=0,
        ),
        name="norm_qkv",
    )(x, gain, shift, weight, qv_bias)


def stacked(block):
    first = lax.broadcasted_iota(jnp.int32, (1, LANES), 1) < HEAD_DIM
    zero = jnp.zeros((), block.dtype)
    return jnp.concatenate([jnp.where(first, block, zero), jnp.where(first, zero, block)], axis=0)


def attend_kernel(
    qo, qr, xo, xr, okrow, ow, ob, g2, b2, mixed_ref, att_ref, sn_ref, p_ref, mix_s
):
    half, width = xo.shape[1], xo.shape[2]
    rows = 2 * half
    ok8 = jnp.concatenate([okrow[0].astype(F32), jnp.zeros((7, rows), F32)], axis=0).astype(BF16)
    ok_col = dot_tn(ok8, jnp.ones((8, LANES), BF16))
    bias = jnp.where(ok_col > 0.5, 0.0, MASKED)[:, :1]

    def both(col):
        cols = lane_block(col)
        return jnp.concatenate([qo[0, :, cols], qr[0, :, cols]], axis=0)

    tiles = width // LANES

    def two_heads(hp, carry):
        q = both(hp) * jnp.asarray(HEAD_DIM**-0.5, BF16)
        s = dot_nt(stacked(both(tiles + hp)), q)
        probs = []
        for h in range(2):
            sh = s[h * rows : (h + 1) * rows, :] + bias
            e = jnp.exp(sh - jnp.max(sh, axis=0, keepdims=True))
            probs.append((e * (1.0 / column_sums(e))).astype(BF16))
        prob = jnp.concatenate(probs, axis=0)
        p_ref[0, hp] = prob
        mix_s[:, lane_block(hp)] = dot_tn(prob, stacked(both(2 * tiles + hp))).astype(BF16)
        return carry

    lax.fori_loop(0, tiles, two_heads, 0)
    mixed = mix_s[...]
    mixed_ref[...] = mixed.reshape(mixed_ref.shape)
    x = jnp.concatenate([xo[0], xr[0]], axis=0).astype(F32)
    att = x + dot_nn(mixed, ow[...]) + ob[...]
    att_ref[...] = att.reshape(att_ref.shape)
    unit, _ = norm_parts(att)
    sn_ref[...] = (unit * g2[...] + b2[...]).astype(BF16).reshape(sn_ref.shape)


def attend(qkv_own, qkv_far, x_own, x_far, okrow, out_weight, out_bias, gain, shift):
    pairs, half, width = x_own.shape
    tiles = width // LANES
    rows = 2 * half
    pair3 = lambda p: (p, 0, 0)
    rows4 = pl.BlockSpec((2, 1, half, width), lambda p: (0, p, 0, 0))
    return pl.pallas_call(
        attend_kernel,
        grid=(pairs,),
        in_specs=[
            pl.BlockSpec((1, half, 3 * width), pair3),
            pl.BlockSpec((1, half, 3 * width), pair3),
            pl.BlockSpec((1, half, width), pair3),
            pl.BlockSpec((1, half, width), pair3),
            pl.BlockSpec((1, 1, rows), pair3),
        ]
        + [spec_of(a) for a in (out_weight, out_bias, gain, shift)],
        out_specs=[
            rows4,
            rows4,
            rows4,
            pl.BlockSpec((1, tiles, 2 * rows, rows), lambda p: (p, 0, 0, 0)),
        ],
        out_shape=[
            kept((2, pairs, half, width), BF16),
            kept((2, pairs, half, width), F32),
            struct((2, pairs, half, width), BF16),
            kept((pairs, tiles, 2 * rows, rows), BF16),
        ],
        scratch_shapes=[pltpu.VMEM((rows, width), BF16)],
        compiler_params=params_of(32),
        cost_estimate=pl.CostEstimate(
            flops=pairs * 16 * tiles * rows * rows * LANES,
            bytes_accessed=2 * pairs * rows * width * 8 + 4 * pairs * tiles * rows * rows,
            transcendentals=2 * pairs * tiles * rows * rows,
        ),
        name="attend",
    )(qkv_own, qkv_far, x_own, x_far, okrow, out_weight, out_bias, gain, shift)


def mlp_up_kernel(
    info, place, sn, att, co, cr, up, upb, down, downb,
    slope_ref, own_ref, far_ref, gy_ref, dbg_ref, keep, send, acc, wbuf, sems, *, shard,
):
    j = pl.program_id(0)
    last = pl.num_programs(0) - 1
    pairs, half, width = co.shape
    tile = up.shape[1]

    @pl.when(j == 0)
    def _():
        for far, c in enumerate((co, cr)):
            for p in range(pairs):
                at = (far * pairs + p) * half
                gy_ref[at : at + half, :] = jnp.where(
                    own_rows(info, p, far, half), c[p].astype(F32), 0.0
                ).astype(BF16)
        dbg_ref[...] = column_sums(gy_ref[...].astype(F32))

    h, slope = gelu_and_slope(dot_nn(sn[...], up[...]) + upb[...])
    slope_ref[...] = slope.astype(BF16)
    h = h.astype(BF16)
    part = dot_nn(h, down[...])

    @pl.when(j == 0)
    def _():
        acc[...] = part

    @pl.when(j > 0)
    def _():
        acc[...] += part

    grad = dot_tn(h, gy_ref[...])
    if not shard:
        keep[...] = grad
        send[...] = jnp.zeros_like(send)
    else:
        count = tile // shard
        slot = lax.rem(j, 2)

        def copy_of(step, i, act):
            pos = place[step * count + i]
            src = wbuf.at[lax.rem(step, 2), pl.ds(i * shard, shard), :]
            n = keep.shape[0] // shard
            for ref, ours in ((keep, pos < n), (send, pos >= n)):

                @pl.when(ours)
                def _():
                    at = pl.multiple_of(lax.rem(pos, n) * shard, shard)
                    act(pltpu.make_async_copy(src, ref.at[pl.ds(at, shard), :], sems.at[lax.rem(step, 2), i]))

        @pl.when(j > 1)
        def _():
            for i in range(count):
                copy_of(j - 2, i, lambda c: c.wait())

        wbuf[slot] = grad.astype(BF16)
        for i in range(count):
            copy_of(j, i, lambda c: c.start())

    @pl.when(j == last)
    def _():
        final = att[...] + acc[...] + downb[...]
        for far, o in enumerate((own_ref, far_ref)):
            for p in range(pairs):
                at = (far * pairs + p) * half
                o[p] = jnp.where(
                    own_rows(info, p, far, half), final[at : at + half, :], 0.0
                ).astype(BF16)
        if shard:
            for step in (last - 1, last):
                for i in range(count):
                    copy_of(step, i, lambda c: c.wait())


def mlp_up(info, place, sn, att, cot_own, cot_far, up, up_bias, down, down_bias, shards, packed):
    pairs, half, width = cot_own.shape
    rows = 2 * pairs * half
    ff = up.shape[1]
    tile = width
    shard = ff // shards
    tiled = lambda j, *_: (j, 0)
    if packed:
        wire = [kept((ff // 2, width), BF16)] * 2
        wire_specs = [pl.BlockSpec(memory_space=pl.ANY)] * 2
        count = tile // shard
    else:
        wire = [struct((ff, width), F32), struct((8, LANES), F32)]
        wire_specs = [pl.BlockSpec((tile, width), tiled), spec_of(wire[1])]
        count = 1
    rows3 = kept((pairs, half, width), BF16)
    return pl.pallas_call(
        partial(mlp_up_kernel, shard=shard if packed else 0),
        grid_spec=pltpu.PrefetchScalarGridSpec(
            num_scalar_prefetch=2,
            grid=(ff // tile,),
            in_specs=[
                spec_of(sn),
                spec_of(att),
                spec_of(cot_own),
                spec_of(cot_far),
                pl.BlockSpec((width, tile), lambda j, *_: (0, j)),
                pl.BlockSpec((1, tile), lambda j, *_: (0, j)),
                pl.BlockSpec((tile, width), tiled),
                spec_of(down_bias),
            ],
            out_specs=[
                pl.BlockSpec((rows, tile), lambda j, *_: (0, j)),
                spec_of(rows3),
                spec_of(rows3),
                spec_of(sn),
                spec_of(down_bias),
            ]
            + wire_specs,
            scratch_shapes=[
                pltpu.VMEM((rows, width), F32),
                pltpu.VMEM((2, tile, width), BF16),
                pltpu.SemaphoreType.DMA((2, count)),
            ],
        ),
        out_shape=[struct((rows, ff), BF16), rows3, rows3, struct((rows, width), BF16), kept((1, width), F32)]
        + wire,
        compiler_params=params_of(40),
        cost_estimate=pl.CostEstimate(
            flops=6 * rows * width * ff, bytes_accessed=22 * MIB, transcendentals=2 * rows * ff
        ),
        name="mlp_up",
    )(info, place, sn, att, cot_own, cot_far, up, up_bias, down, down_bias)


def mlp_back_kernel(
    inv, gy, slope, sn, up, down, gs_ref, upb_ref, keep, send, tall, snt, wbuf, sems, *, shard
):
    j = pl.program_id(0)
    last = pl.num_programs(0) - 1
    gp = (dot_nt(gy[...], down[...]) * slope[...].astype(F32)).astype(BF16)
    upb_ref[...] = column_sums(gp.astype(F32))
    part = dot_nt(gp, up[...])

    @pl.when(j == 0)
    def _():
        gs_ref[...] = part

    @pl.when(j > 0)
    def _():
        gs_ref[...] += part

    if not shard:
        keep[...] = dot_tn(sn[...], gp)
        send[...] = jnp.zeros_like(send)
        return

    @pl.when(j == 0)
    def _():
        wire_rows(sn[...], inv, tall, snt, shard)

    n, tile = keep.shape[0], up.shape[1]

    def copies(step):
        slot = lax.rem(step, 2)
        cols = lane_block(step, tile)
        for i, ref in enumerate((keep, send)):
            yield pltpu.make_async_copy(
                wbuf.at[slot, pl.ds(i * n, n), :], ref.at[:, cols], sems.at[slot, i]
            )

    @pl.when(j > 1)
    def _():
        for c in copies(j - 2):
            c.wait()

    wbuf[lax.rem(j, 2)] = dot_nn(snt[...], gp).astype(BF16)
    for c in copies(j):
        c.start()

    @pl.when(j == last)
    def _():
        for step in (last - 1, last):
            for c in copies(step):
                c.wait()


def mlp_back(inv, gy, slope, sn, up, down, shards, packed):
    rows, width = gy.shape
    ff = up.shape[1]
    tile = width
    cols = lambda j, *_: (0, j)
    if packed:
        wire = [kept((width // 2, ff), BF16)] * 2
        wire_specs = [pl.BlockSpec(memory_space=pl.ANY)] * 2
    else:
        wire = [struct((width, ff), F32), struct((8, LANES), F32)]
        wire_specs = [pl.BlockSpec((width, tile), cols), spec_of(wire[1])]
    return pl.pallas_call(
        partial(mlp_back_kernel, shard=width // shards if packed else 0),
        grid_spec=pltpu.PrefetchScalarGridSpec(
            num_scalar_prefetch=1,
            grid=(ff // tile,),
            in_specs=[
                spec_of(gy),
                pl.BlockSpec((rows, tile), cols),
                spec_of(sn),
                pl.BlockSpec((width, tile), cols),
                pl.BlockSpec((tile, width), lambda j, *_: (j, 0)),
            ],
            out_specs=[spec_of(gy), pl.BlockSpec((1, tile), cols)] + wire_specs,
            scratch_shapes=[
                pltpu.VMEM((width, rows), F32),
                pltpu.VMEM((width, rows), BF16),
                pltpu.VMEM((2, width, tile), BF16),
                pltpu.SemaphoreType.DMA((2, 2)),
            ],
        ),
        out_shape=[struct((rows, width), F32), kept((1, ff), F32)] + wire,
        compiler_params=params_of(40),
        cost_estimate=pl.CostEstimate(
            flops=6 * rows * width * ff, bytes_accessed=20 * MIB, transcendentals=0
        ),
        name="mlp_back",
    )(inv, gy, slope, sn, up, down)


def heads_back(qo, qr, gm_ref, p_ref, dqkv, base, rows, hp0, count):
    first = lax.broadcasted_iota(jnp.int32, (1, LANES), 1) < HEAD_DIM
    tiles = gm_ref.shape[-1] // LANES
    scale = jnp.asarray(HEAD_DIM**-0.5, BF16)

    def both(col):
        cols = lane_block(col)
        return jnp.concatenate([qo[0, :, cols], qr[0, :, cols]], axis=0)

    def two_heads(i, carry):
        hp = hp0 + i
        gm = gm_ref[:, lane_block(hp)]
        dp = dot_nt(stacked(both(2 * tiles + hp)), gm)
        prob = p_ref[0, i]
        ds = []
        for h in range(2):
            dph = dp[h * rows : (h + 1) * rows, :]
            pf = prob[h * rows : (h + 1) * rows, :].astype(F32)
            ds.append((pf * (dph - column_sums(dph * pf))).astype(BF16))
        ds = jnp.concatenate(ds, axis=0)
        dv = dot_nn(prob, gm)
        dk = dot_nn(ds, both(hp) * scale)
        dq = dot_tn(ds, stacked(both(tiles + hp) * scale))
        pick = lambda d: jnp.where(first, d[:rows, :], d[rows:, :])
        for part, d in enumerate((dq, pick(dk), pick(dv))):
            dqkv[pl.ds(base, rows), lane_block(part * count + i)] = d.astype(BF16)
        return carry

    lax.fori_loop(0, count, two_heads, 0)


def wire_out(left_t, right, keep, send, at):
    n = keep.shape[0]
    grad = dot_nn(left_t, right).astype(BF16)
    keep[:, at : at + grad.shape[1]] = grad[:n]
    send[:, at : at + grad.shape[1]] = grad[n:]


def attend_back_kernel(
    inv, gs, gy, att, mixed, fno, fnr, qo, qr, p_ref, ow, g2,
    ga_ref, gm_ref, dqkv, fnt, vec_ref, keep, send, gbs, fns, mxs, tall, *, shard,
):
    pair = pl.program_id(0)
    half, width = fno.shape[1], fno.shape[2]
    rows = 2 * half

    @pl.when(pair == 0)
    def _():
        vec_ref[...] = jnp.zeros_like(vec_ref)

    grad_second = gs[...].reshape(rows, width)
    unit, rstd = norm_parts(att[...].reshape(rows, width))
    grad_att = gy[...].reshape(rows, width).astype(F32) + norm_back(
        grad_second, unit, rstd, g2[...]
    )
    ga_ref[0] = grad_att
    branch = grad_att.astype(BF16)
    for i, v in enumerate((branch.astype(F32), grad_second * unit, grad_second)):
        vec_ref[i : i + 1, :] += column_sums(v)
    base = pl.multiple_of(pair * rows, rows)
    gbs[pl.ds(base, rows), :] = branch
    gm_ref[0] = dot_nt(branch, ow[...]).astype(BF16)
    fns[pl.ds(base, half), :] = fno[0]
    fns[pl.ds(base + half, half), :] = fnr[0]
    mxs[pl.ds(base, rows), :] = mixed[...].reshape(rows, width)
    heads_back(qo, qr, gm_ref.at[0], p_ref, dqkv, base, rows, 0, EARLY)

    @pl.when(pair == pl.num_programs(0) - 1)
    def _():
        early = dqkv.shape[1]
        if not shard:
            keep[:, :early] = dot_tn(fns[...], dqkv[...])
            keep[:, early:] = dot_tn(mxs[...], gbs[...])
            fnt[...] = jnp.transpose(fns[...].astype(F32)).astype(BF16)
            send[...] = jnp.zeros_like(send)
            return
        wire_rows(mxs[...], inv, tall, fnt, shard)
        wire_out(fnt[...], gbs[...], keep, send, early)
        wire_rows(fns[...], inv, tall, fnt, shard)
        for at in range(0, early, width):
            wire_out(fnt[...], dqkv[:, at : at + width], keep, send, at)


def attend_back(
    inv, gs, gy, att, mixed, fn_own, fn_far, qkv_own, qkv_far, probs, out_weight, gain, shards, packed
):
    pairs, half, width = fn_own.shape
    rows = 2 * half
    early = 3 * EARLY * LANES
    pair3 = lambda p, *_: (p, 0, 0)
    rows4 = pl.BlockSpec((2, 1, half, width), lambda p, *_: (0, p, 0, 0))
    if packed:
        wire = [kept((width // 2, early + width), BF16)] * 2
    else:
        wire = [struct((width, early + width), F32), struct((8, LANES), F32)]
    outs = [
        struct((pairs * rows, early), BF16),
        struct((width, pairs * rows), BF16),
        kept((8, width), F32),
    ] + wire
    return pl.pallas_call(
        partial(attend_back_kernel, shard=width // shards if packed else 0),
        grid_spec=pltpu.PrefetchScalarGridSpec(
            num_scalar_prefetch=1,
            grid=(pairs,),
            in_specs=[
                rows4,
                rows4,
                rows4,
                rows4,
                pl.BlockSpec((1, half, width), pair3),
                pl.BlockSpec((1, half, width), pair3),
                pl.BlockSpec((1, half, 3 * width), pair3),
                pl.BlockSpec((1, half, 3 * width), pair3),
                pl.BlockSpec((1, EARLY, 2 * rows, rows), lambda p, *_: (p, 0, 0, 0)),
                spec_of(out_weight),
                spec_of(gain),
            ],
            out_specs=[
                pl.BlockSpec((1, rows, width), pair3),
                pl.BlockSpec((1, rows, width), pair3),
            ]
            + [spec_of(o) for o in outs],
            scratch_shapes=[
                pltpu.VMEM((pairs * rows, width), BF16),
                pltpu.VMEM((pairs * rows, width), BF16),
                pltpu.VMEM((pairs * rows, width), BF16),
                pltpu.VMEM((width, pairs * rows), F32),
            ],
        ),
        out_shape=[struct((pairs, rows, width), F32), struct((pairs, rows, width), BF16)] + outs,
        compiler_params=params_of(44),
        cost_estimate=pl.CostEstimate(
            flops=pairs * 32 * EARLY * rows * rows * LANES + 8 * pairs * rows * width * width,
            bytes_accessed=20 * MIB,
            transcendentals=0,
        ),
        name="attend_back",
    )(inv, gs, gy, att, mixed, fn_own, fn_far, qkv_own, qkv_far, probs, out_weight, gain)


def last_back_kernel(
    inv, qo, qr, p_ref, gm_ref, fnt, dqa, ga, xo, xr, w, g1, v2, upbg, dbg,
    own_ref, far_ref, vec_ref, keep, send, dqb, *, shard,
):
    pair = pl.program_id(0)
    half, width = xo.shape[1], xo.shape[2]
    rows = 2 * half
    tiles = width // LANES
    base = pl.multiple_of(pair * rows, rows)
    ca, cb = dqa.shape[1] // 3, dqb.shape[1] // 3

    @pl.when(pair == 0)
    def _():
        vec_ref[...] = jnp.zeros_like(vec_ref)
        vec_ref[4:7, :] = v2[0:3, :]
        vec_ref[7:8, :] = dbg[...]
        for i in range(4):
            vec_ref[8 + i : 9 + i, :] = upbg[:, i * width : (i + 1) * width]

    def add_vec(i, at, value):
        vec_ref[i : i + 1, at : at + value.shape[1]] += column_sums(value.astype(F32))

    heads_back(qo, qr, gm_ref.at[0], p_ref, dqb, base, rows, EARLY, tiles - EARLY)

    grad = None
    late = dqb[pl.ds(base, rows), :]
    for d, cols, at in ((dqa[...], ca, 0), (late, cb, ca)):
        for part in range(3):
            left = part * width + at
            term = dot_nt(d[:, part * cols : (part + 1) * cols], w[:, left : left + cols])
            grad = term if grad is None else grad + term
        add_vec(2, at, d[:, :cols])
        add_vec(3, at, d[:, 2 * cols :])
    unit, rstd = norm_parts(jnp.concatenate([xo[0], xr[0]], axis=0).astype(F32))
    add_vec(0, 0, grad * unit)
    add_vec(1, 0, grad)
    result = (ga[0] + norm_back(grad, unit, rstd, g1[...])).astype(BF16)
    own_ref[0] = result[:half]
    far_ref[0] = result[half:]

    @pl.when(pair == pl.num_programs(0) - 1)
    def _():
        if not shard:
            keep[...] = dot_nn(fnt[...], dqb[...])
            send[...] = jnp.zeros_like(send)
            return
        wire_out(fnt[...], dqb[...], keep, send, 0)
        v = vec_ref[...]
        small = jnp.concatenate([v[0:2], v[4:8], v[0:2]], axis=0)
        rowid = lax.broadcasted_iota(jnp.int32, (8, LANES), 0)
        per_q, per_u = width // (2 * shard), width // (4 * shard)
        none = jnp.zeros((shard - 8, LANES), F32)

        def piece(block, start):
            return pltpu.roll(block, lax.rem(width - start, width), 1)[:, :LANES]

        def block(i):
            a = piece(small, i * shard)
            b = piece(v[2:4], lax.rem(i, per_q) * 2 * shard)
            brow = jnp.where(i < per_q, b[0:1], b[1:2])
            c = piece(v[8:12], lax.rem(i, per_u) * 4 * shard)
            ci = lax.div(i, per_u)
            crow = jnp.where(
                ci == 0, c[0:1], jnp.where(ci == 1, c[1:2], jnp.where(ci == 2, c[2:3], c[3:4]))
            )
            return jnp.where(rowid < 6, a, jnp.where(rowid == 6, brow, crow))

        n = keep.shape[0] // shard
        right = keep.shape[1] - LANES

        def fill(p, carry):
            at = pl.ds(pl.multiple_of(2 * shard * p, 2 * shard), 2 * shard)
            for ref, first in ((keep, 0), (send, n)):
                two = [block(inv[first + 2 * p]), none, block(inv[first + 2 * p + 1]), none]
                ref[at, right:] = jnp.concatenate(two, axis=0).astype(BF16)
            return carry

        lax.fori_loop(0, n // 2, fill, 0)


def last_back(
    inv, qkv_own, qkv_far, probs, gm, fnt, dqa, ga, x_own, x_far, weight, gain, v2, upbg, dbg,
    shards, packed,
):
    pairs, rows, width = gm.shape
    half = rows // 2
    late = width // LANES - EARLY
    cols = 3 * late * LANES
    pair3 = lambda p, *_: (p, 0, 0)
    pair2 = lambda p, *_: (p, 0)
    if packed:
        wire = [kept((width // 2, cols + LANES), BF16)] * 2
    else:
        wire = [struct((width, cols), F32), struct((8, LANES), F32)]
    vec = kept((16, width), F32)
    return pl.pallas_call(
        partial(last_back_kernel, shard=width // shards if packed else 0),
        grid_spec=pltpu.PrefetchScalarGridSpec(
            num_scalar_prefetch=1,
            grid=(pairs,),
            in_specs=[
                pl.BlockSpec((1, half, 3 * width), pair3),
                pl.BlockSpec((1, half, 3 * width), pair3),
                pl.BlockSpec((1, late, 2 * rows, rows), lambda p, *_: (p, EARLY // late, 0, 0)),
                pl.BlockSpec((1, rows, width), pair3),
                spec_of(fnt),
                pl.BlockSpec((rows, dqa.shape[1]), pair2),
                pl.BlockSpec((1, rows, width), pair3),
                pl.BlockSpec((1, half, width), pair3),
                pl.BlockSpec((1, half, width), pair3),
            ]
            + [spec_of(a) for a in (weight, gain, v2, upbg, dbg)],
            out_specs=[
                pl.BlockSpec((1, half, width), pair3),
                pl.BlockSpec((1, half, width), pair3),
                spec_of(vec),
            ]
            + [spec_of(o) for o in wire],
            scratch_shapes=[pltpu.VMEM((pairs * rows, cols), BF16)],
        ),
        out_shape=[kept((pairs, half, width), BF16)] * 2 + [vec] + wire,
        compiler_params=params_of(36),
        cost_estimate=pl.CostEstimate(
            flops=pairs * 32 * late * rows * rows * LANES + 8 * pairs * rows * width * width,
            bytes_accessed=16 * MIB,
            transcendentals=0,
        ),
        name="last_back",
    )(inv, qkv_own, qkv_far, probs, gm, fnt, dqa, ga, x_own, x_far, weight, gain, v2, upbg, dbg)


def core_of(i):
    return 1 if i & CORE_BIT else 0


def shard_order(me, shards):
    half = shards // 2
    bits = half.bit_length() - 1
    tables = []
    for order in ORDERS:
        row = []
        for p in range(half):
            rel = 0
            for i, bit in enumerate(order):
                if p >> (bits - 1 - i) & 1:
                    rel |= bit
            row.append(rel)
        tables.append(row)
    both = []
    for core in range(2):
        row = tables[core] + [r | CORE_BIT for r in tables[1 - core]]
        both.append(row)
    both = np.array(both, np.int32)
    back = np.argsort(both, axis=1).astype(np.int32)
    core = jnp.where(me & CORE_BIT, 1, 0)
    rel = jnp.where(core == 0, jnp.asarray(both[0]), jnp.asarray(both[1]))
    ids = jnp.arange(shards, dtype=jnp.int32) ^ me
    hot = (ids[:, None] == jnp.arange(shards, dtype=jnp.int32)[None, :]).astype(jnp.int32)
    table = jnp.where(core == 0, jnp.asarray(back[0]), jnp.asarray(back[1]))
    return me ^ rel, jnp.sum(hot * table[None, :], axis=1)


def add_up(terms):
    total = terms[0].astype(F32)
    for t in terms[1:]:
        total = total + t.astype(F32)
    return total


def tie(*values):
    return lax.optimization_barrier(values)


class Reduction:
    def __init__(self, keep, send, shards):
        self.shards, self.stage, self.n = shards, 0, keep.shape[0]
        self.terms = [keep]
        self.incoming = lax.ppermute(send, AXES, [(i, i ^ CORE_BIT) for i in range(shards)])

    def hold(self, *others):
        self.incoming = after(self.incoming, *others)

    def step(self):
        self.terms.append(self.incoming)
        self.n //= 2
        out = add_up([t[self.n :] for t in self.terms]).astype(BF16)
        self.terms = [t[: self.n] for t in self.terms]
        route = [(i, i ^ ORDERS[core_of(i)][self.stage]) for i in range(self.shards)]
        self.incoming = lax.ppermute(out, AXES, route)
        self.stage += 1
        return out

    def result(self):
        return add_up(self.terms + [self.incoming])


def after(value, *others):
    return tie(value, *others)[0]


def swap_sides(block):
    return lax.ppermute(block, "mod", [(0, 1), (1, 0)])


def on_device(
    tokens, patch_counts, token_mask, ln1_gain, ln1_bias, qkv_weight, qv_bias, out_weight,
    out_bias, ln2_gain, ln2_bias, up_weight, up_bias, down_weight, down_bias, cotangent,
):
    shards = lax.axis_size("pairs") * lax.axis_size("mod")
    pairs_here, real, width = tokens.shape
    pairs = pairs_here // 2
    half = real + PAD
    rows = width // shards
    packed = shards == 32 and width % (8 * shards) == 0
    side = lax.axis_index("mod").astype(jnp.int32)
    me = lax.axis_index("pairs").astype(jnp.int32) * 2 + side
    ours = lambda a: jnp.where(side == 0, a[:pairs], a[pairs:])
    theirs = lambda a: jnp.where(side == 0, a[pairs:], a[:pairs])
    padded = lambda a: jnp.pad(a, ((0, 0), (0, PAD), (0, 0)))
    x_sent = theirs(tokens)
    x_raw = swap_sides(x_sent)
    row_ids = side * real + jnp.arange(real, dtype=jnp.int32)
    ok = jnp.logical_and(row_ids[None, :] < (TXT + patch_counts)[:, None], token_mask == 1)
    ok = ok.astype(BF16)
    ok_far = swap_sides(after(theirs(ok), x_sent))
    gap = jnp.zeros((pairs, PAD), BF16)
    ok_row = jnp.concatenate([ours(ok), gap, ok_far, gap], axis=1)[:, None, :]
    tokens, cotangent = tie(tokens, cotangent, x_sent)[:2]
    x_own = padded(ours(tokens))
    cot_own = padded(ours(cotangent))
    cot_sent = theirs(cotangent)

    counts = ours(patch_counts)
    info = jnp.concatenate([counts, side[None]])
    if packed:
        inv, place = shard_order(me, shards)
    else:
        inv = place = jnp.zeros((8,), jnp.int32)

    row = lambda v: v.reshape(1, -1)
    g1, b1, g2, b2 = row(ln1_gain), row(ln1_bias), row(ln2_gain), row(ln2_bias)
    qvb = qv_bias.reshape(2, 1, width)
    fn_own, qkv_own = norm_qkv(x_own, g1, b1, qkv_weight, qvb)
    x_raw, cot_sent, _ = tie(x_raw, cot_sent, fn_own)
    x_far = padded(x_raw)
    cot_far = padded(swap_sides(cot_sent))
    fn_far, qkv_far = norm_qkv(x_far, g1, b1, qkv_weight, qvb)
    mixed, att, sn, probs = attend(
        qkv_own, qkv_far, x_own, x_far, ok_row, out_weight, row(out_bias), g2, b2
    )
    flat = lambda a: a.reshape(-1, width)
    slope, lo_own, lo_far, gy, dbg, keep1, send1 = mlp_up(
        info, place, flat(sn), flat(att), cot_own, cot_far, up_weight, row(up_bias),
        down_weight, row(down_bias), shards, packed,
    )
    shape4 = (2, pairs, half, width)
    if packed:
        r1 = Reduction(keep1, send1, shards)
        inv = after(inv, r1.step())
    gs, upbg, keep2, send2 = mlp_back(inv, gy, slope, flat(sn), up_weight, down_weight, shards, packed)
    if packed:
        r1.hold(upbg)
        r2 = Reduction(keep2, after(send2, r1.step()), shards)
        inv = after(inv, r2.step())
    ga, gm, dqa, fnt, v2, keep3, send3 = attend_back(
        inv, gs.reshape(shape4), gy.reshape(shape4), att, mixed, fn_own, fn_far, qkv_own, qkv_far,
        probs, out_weight, g2, shards, packed,
    )
    if packed:
        r1.hold(v2)
        sent = r1.step()
        r2.hold(sent)
        sent = r2.step()
        r3 = Reduction(keep3, after(send3, sent), shards)
        inv = after(inv, r3.step())
    lo_back = swap_sides(after(lo_far, v2))
    ig_own, ig_far, vec, keep4, send4 = last_back(
        inv, qkv_own, qkv_far, probs, gm, fnt, dqa, ga, x_own, x_far, qkv_weight, g1, v2, upbg,
        dbg, shards, packed,
    )
    ig_back = swap_sides(ig_far)

    def settle(own, back):
        own, back = own[:, :real], back[:, :real]
        return jnp.where(
            side == 0, jnp.concatenate([own, back]), jnp.concatenate([back, own])
        )

    early = 3 * EARLY * LANES
    if packed:
        r1.hold(ig_own)
        r2.hold(r1.step())
        r3.hold(r2.step())
        r4 = Reduction(keep4, after(send4, r3.step()), shards)
        sent = r4.step()
        for r in (r2, r3, r4, r3, r4, r4):
            r.hold(sent)
            sent = r.step()
        layer_out = settle(lo_own, lo_back)
        down_g, up_g, mid, last = (r.result() for r in (r1, r2, r3, r4))
        vecs = last[:8, -LANES:]
        last = last[:, :-LANES]
        ln1g, ln1b, outb, ln2g, ln2b, downb = (vecs[i, :rows] for i in range(6))
        qvg, upg = vecs[6, : 2 * rows], vecs[7, : 4 * rows]
    else:
        layer_out = settle(lo_own, lo_back)
        total = lambda v: lax.psum_scatter(v, AXES, scatter_dimension=0, tiled=True)
        down_g, up_g, mid, last = total(keep1), total(keep2), total(keep3), total(keep4)
        ln1g, ln1b, outb, ln2g, ln2b, downb = (total(vec[i]) for i in (0, 1, 4, 5, 6, 7))
        qvg, upg = total(vec[2:4].reshape(-1)), total(vec[8:12].reshape(-1))
    out_g = mid[:, early:]
    ca, cb = early // 3, last.shape[1] // 3
    parts = []
    for i in range(3):
        parts += [mid[:, i * ca : (i + 1) * ca], last[:, i * cb : (i + 1) * cb]]
    qkv_g = jnp.concatenate(parts, axis=1)
    input_grad = settle(ig_own, ig_back)
    return (
        layer_out, input_grad, ln1g, ln1b, qkv_g, qvg, out_g, outb, ln2g, ln2b, up_g, upg,
        down_g, downb,
    )


def solution(mesh):
    rows3 = P("pairs", "mod", None)
    vec, mat = P(AXES), P(AXES, None)
    return jax.shard_map(
        on_device,
        mesh=mesh,
        in_specs=(rows3, P("pairs"), P("pairs", "mod")) + (P(),) * 12 + (rows3,),
        out_specs=(rows3, rows3, vec, vec, mat, vec, mat, vec, vec, vec, mat, vec, mat, vec),
        check_vma=False,
    )
```

time: 229 us -> 189 us (0.83)
  Pallas kernels: 96.9 us -> 82.8 us
  waiting for transfers between devices: 52.6 us -> 40.8 us
  local copies, waits for them, and re-layouts: 24.1 us -> 12.8 us
  other arithmetic: 26.5 us -> 21.9 us
  starting transfers between devices: 26.2 us -> 29 us
    ppermute x4 -> x5, waiting for transfers between devices: 17.9 us -> 5.47 us  [swap_sides(): return lax.ppermute(block, 'mod', [(0, 1), (1, 0)])]
    ppermute x4, waiting for transfers between devices: 0.01 us -> 10.4 us  [__init__(): lax.ppermute(send, AXES, [(i, i ^ CORE_BIT) for i in range(shards)])]
    ppermute x16, waiting for transfers between devices: 34.6 us -> 25 us  [step(): self.incoming = lax.ppermute(out, AXES, route)]
    pallas_call x7 -> x5, Pallas kernels: 59.8 us -> 52 us  [the longest x1 17.9 us: attend_back(): pl.pallas_call(partial(attend_back_kernel, shard=width // shards if packe...]
    unnamed x126 -> x103, local copies, waits for them, and re-layouts: 14.3 us -> 7.99 us
    dynamic_slice x3 -> x0, local copies, waits for them, and re-layouts: 5.85 us -> none  [pick(): return lax.dynamic_slice_in_dim(arr, at, pairs, 0)]
    pallas_call x1, Pallas kernels: 22 us -> 18.6 us  [mlp_up(): pl.pallas_call(partial(mlp_up_kernel, shard=shard if packed else 0), grid...]
    pallas_call x1, Pallas kernels: 15.1 us -> 12.3 us  [attend(): pl.pallas_call(attend_kernel, grid=(pairs,), in_specs=[pl.BlockSpec((1, h...]
  transfers between devices with their start and end apart: 24 -> 25, of which waited for: 10 -> 15; matrix products, arithmetic and copies ran while one was open for 13% -> 8% of each run, Pallas kernels for 28% -> 34%
where the time goes in v2:
time: 189 us
  Pallas kernels  82.8 us (44%)
  waiting for transfers between devices  40.8 us (22%)
  starting transfers between devices  29 us (15%)
  other arithmetic  21.9 us (12%)
  local copies, waits for them, and re-layouts  12.8 us (7%)
    ppermute x16, waiting for transfers between devices, step(): self.incoming = lax.ppermute(out, AXES, route)  25 us
    ppermute x16, starting transfers between devices, step(): self.incoming = lax.ppermute(out, AXES, route)  21 us
    pallas_call x1, Pallas kernels, mlp_up(): pl.pallas_call(partial(mlp_up_kernel, shard=shard if packed else 0), grid...  18.6 us
    pallas_call x1, Pallas kernels, attend_back(): pl.pallas_call(partial(attend_back_kernel, shard=width // shards if packe...  17.9 us
    pallas_call x1, Pallas kernels, mlp_back(): pl.pallas_call(partial(mlp_back_kernel, shard=width // shards if packed e...  17.3 us
    convert_element_type x16, other arithmetic, step(): out = add_up([t[self.n:] for t in self.terms]).astype(BF16)  17 us
    pallas_call x1, Pallas kernels, attend(): pl.pallas_call(attend_kernel, grid=(pairs,), in_specs=[pl.BlockSpec((1, h...  12.3 us
    pallas_call x1, Pallas kernels, last_back(): pl.pallas_call(partial(last_back_kernel, shard=width // shards if packed...  10.5 us
  transfers between devices with their start and end apart: 25, of which 15 were waited for; matrix products, arithmetic and copies ran while one was open for 8% of the time, Pallas kernels for 34%

profile of v2, /device:TPU:0, one launch (start us, length us, event | category | flops | bytes accessed | tf_op | source)
XLA Modules:
  0.0 188.7 jit_solution(8461396853214326558)
XLA Ops:
  0.7 2.2 %fusion.1 = (bf16[2,140,768]{2,0,1:T(2,128)(2,1)S(1)}, bf16[2,140,768]{2,0,1:T(2,128)(2,1)S(1)}) fusion(bf16[4,140,768]{2,0,1:T(4,128)(2,1)} %param.20), kind=kLoop, calls=%fused_computation.54 | loop fusion | bytes 1720320 | tf_op jit(solution)/shard_map/slice | solution.py:810
  3.1 3.0 %collective-permute-start = (bf16[2,140,768]{2,1,0:T(8,128)(2,1)S(1)}, bf16[2,140,768]{2,1,0:T(8,128)(2,1)S(1)}, u32[]{:S(2)}, u32[]{:S(2)}) collective-permute-start(bf16[2,140,768]{2,1,0:T(8,128)(2,1)S(1)} %copy_select_fusion), channel_id=1, source_target_pairs={{0,1},{1,0},{2,3},{3,2},{4,5},{5,4},{6,7},{7,6},{8,9},{9,8},{10,11... | collective-permute-start | bytes 1290248 | tf_op jit(solution)/shard_map/ppermute | solution.py:794
  7.3 1.2 copy-done
  8.5 3.1 %norm_qkv.2 = (bf16[2,144,768]{2,1,0:T(8,128)(2,1)}, bf16[2,144,2304]{2,1,0:T(8,128)(2,1)}) custom-call(bf16[2,144,768]{2,1,0:T(8,128)(2,1)S(1)} %pad.13.x_ref.xo, f32[1,768]{1,0:T(1,128)S(1)} %reshape.75.g_ref.g1, f32[1,768]{1,0:T(1,128)S(1)} %reshape.76.b_ref, bf16[768,2304]{1,0:T(8,128)(2,1)S(1)} %copy-done, f32[2,1,768]{2,1,0:T(1,128)S(1)} %reshape.77.qvb_ref), custom_call_target="tpu_custom_call" | custom-call | flops 1019215872 | bytes 5750784 | tf_op jit(solution)/shard_map/norm_qkv/pallas_call | solution.py:124
  11.8 4.5 %collective-permute-done = bf16[2,140,768]{2,1,0:T(8,128)(2,1)S(1)} collective-permute-done((bf16[2,140,768]{2,1,0:T(8,128)(2,1)S(1)}, bf16[2,140,768]{2,1,0:T(8,128)(2,1)S(1)}, u32[]{:S(2)}, u32[]{:S(2)}) %collective-permute-start) | collective-permute-done | bytes 430112 | tf_op jit(solution)/shard_map/ppermute | solution.py:794
  16.3 1.7 collective-permute-start.2
  18.4 3.2 %norm_qkv.3 = (bf16[2,144,768]{2,1,0:T(8,128)(2,1)}, bf16[2,144,2304]{2,1,0:T(8,128)(2,1)}) custom-call(bf16[2,144,768]{2,1,0:T(8,128)(2,1)S(1)} %pad.14.x_ref.xr, f32[1,768]{1,0:T(1,128)S(1)} %reshape.75.g_ref.g1, f32[1,768]{1,0:T(1,128)S(1)} %reshape.76.b_ref, bf16[768,2304]{1,0:T(8,128)(2,1)S(1)} %copy-done, f32[2,1,768]{2,1,0:T(1,128)S(1)} %reshape.77.qvb_ref), custom_call_target="tpu_custom_call" | custom-call | flops 1019215872 | bytes 5750784 | tf_op jit(solution)/shard_map/norm_qkv/pallas_call | solution.py:124
  21.6 1.3 copy-done.6
  22.9 12.3 %attend.1 = (bf16[2,2,144,768]{3,2,1,0:T(8,128)(2,1)}, f32[2,2,144,768]{3,2,1,0:T(8,128)}, bf16[2,2,144,768]{3,2,1,0:T(8,128)(2,1)S(1)}, bf16[2,6,576,288]{3,2,1,0:T(8,128)(2,1)}) custom-call(bf16[2,144,2304]{2,1,0:T(8,128)(2,1)S(1)} %copy-done.4, bf16[2,144,2304]{2,1,0:T(8,128)(2,1)S(1)} %copy-done.6, bf16[2,144,768]{2,1,0:T(8,128)(2,1)S(1)} %pad.13.x_ref.xo, ...), custom_call_target="tpu_custom_call" | custom-call | flops 2038431744 | bytes 11059200 | tf_op jit(solution)/shard_map/attend/pallas_call | solution.py:196
  35.3 1.5 copy-done.16
  36.7 18.6 %mlp_up.1 = (bf16[576,3072]{1,0:T(8,128)(2,1)S(1)}, bf16[2,144,768]{2,1,0:T(8,128)(2,1)}, bf16[2,144,768]{2,1,0:T(8,128)(2,1)}, bf16[576,768]{1,0:T(8,128)(2,1)S...) custom-call(s32[3]{0:T(128)S(1)} %pad_add_fusion.info, ...), custom_call_target="tpu_custom_call" | custom-call | flops 8153726976 | bytes 23068672 | tf_op jit(solution)/shard_map/mlp_up/pallas_call | solution.py:321
  55.4 4.7 %collective-permute-done.3 = bf16[1536,768]{1,0:T(8,128)(2,1)S(1)} collective-permute-done((bf16[1536,768]{1,0:T(8,128)(2,1)}, bf16[1536,768]{1,0:T(8,128)(2,1)S(1)}, u32[]{:S(2)}, u32[]{:S(2)}) %collective-permute-start.3) | collective-permute-done | bytes 2359328 | tf_op jit(solution)/shard_map/ppermute | solution.py:770
  60.1 2.5 %add_convert_fusion.1 = bf16[768,768]{1,0:T(8,128)(2,1)S(1)} fusion(bf16[1536,768]{1,0:T(8,128)(2,1)S(1)} %collective-permute-done.3, bf16[1536,768]{1,0:T(8,128)(2,1)} %get-tuple-element.80), kind=kLoop, calls=%fused_computation.1 | loop fusion | flops 2359296 | bytes 3538944 | tf_op jit(solution)/shard_map/convert_element_type | solution.py:778
  62.6 1.6 collective-permute-start.4
  64.2 17.3 %mlp_back.1 = (f32[576,768]{1,0:T(8,128)S(1)}, f32[1,3072]{1,0:T(1,128)}, bf16[384,3072]{1,0:T(8,128)(2,1)}, bf16[384,3072]{1,0:T(8,128)(2,1)}) custom-call(s32[32]{0:T(128)S(1)} %fusion.inv, bf16[576,768]{1,0:T(8,128)(2,1)S(1)} %get-tuple-element.83.gy, bf16[576,3072]{1,0:T(8,128)(2,1)S(1)} %get-tuple-element.84.slope, bf16[576,768]{1,0:T(8,128)(2,1)S(1)} %bitcast.37, ...), custom_call_target="tpu_custom_call" | custom-call | flops 8153726976 | bytes 20971520 | tf_op jit(solution)/shard_map/mlp_back/pallas_call | solution.py:423
  81.6 2.7 %add_convert_fusion.4 = bf16[384,768]{1,0:T(8,128)(2,1)} fusion(bf16[1536,768]{1,0:T(8,128)(2,1)S(1)} %collective-permute-done.3, bf16[768,768]{1,0:T(8,128)(2,1)S(1)} %collective-permute-done.4, bf16[1536,768]{1,0:T(8,128)(2,1)} %get-tuple-element.80), kind=kLoop, calls=%fused_computation.4 | loop fusion | flops 1769472 | bytes 2359296 | tf_op jit(solution)/shard_map/convert_element_type | solution.py:778
  84.3 4.7 %collective-permute-done.5 = bf16[384,3072]{1,0:T(8,128)(2,1)S(1)} collective-permute-done((bf16[384,3072]{1,0:T(8,128)(2,1)}, bf16[384,3072]{1,0:T(8,128)(2,1)S(1)}, u32[]{:S(2)}, u32[]{:S(2)}) %collective-permute-start.5) | collective-permute-done | bytes 2359328 | tf_op jit(solution)/shard_map/ppermute | solution.py:770
  89.0 3.6 %add_convert_fusion = bf16[192,3072]{1,0:T(8,128)(2,1)} fusion(bf16[384,3072]{1,0:T(8,128)(2,1)S(1)} %collective-permute-done.5, bf16[384,3072]{1,0:T(8,128)(2,1)} %get-tuple-element.85), kind=kLoop, calls=%fused_computation | loop fusion | flops 2359296 | bytes 3538944 | tf_op jit(solution)/shard_map/convert_element_type | solution.py:778
  92.6 1.0 collective-permute-start.7
  93.7 1.0 collective-permute-start.8
  94.8 17.9 %attend_back.1 = (f32[2,288,768]{2,1,0:T(8,128)S(1)}, bf16[2,288,768]{2,1,0:T(8,128)(2,1)S(1)}, bf16[576,1536]{1,0:T(8,128)(2,1)}, bf16[768,576]{1,0:T(8,128)(2,...) custom-call(s32[32]{0:T(128)S(1)} %fusion.inv, f32[2,2,144,768]{3,2,1,0:T(8,128)} %bitcast.34, ...), custom_call_target="tpu_custom_call" | custom-call | flops 5435817984 | bytes 20971520 | tf_op jit(solution)/shard_map/attend_back/pallas_call | solution.py:552
  112.6 2.0 %add_convert_fusion.8 = bf16[192,768]{1,0:T(8,128)(2,1)S(1)} fusion(bf16[1536,768]{1,0:T(8,128)(2,1)} %copy-done.21, bf16[384,768]{1,0:T(8,128)(2,1)S(1)} %collective-permute-done.8, bf16[768,768]{1,0:T(8,128)(2,1)} %copy-done.23, bf16[1536,768]{1,0:T(8,128)(2,1)} %get-tuple-element.80), kind=kLoop, calls=%fused_computation.10 | loop fusion | flops 1179648 | bytes 1474560 | tf_op jit(solution)/shard_map/convert_element_type | solution.py:778
  115.5 1.8 add_convert_fusion.3
  118.0 1.5 collective-permute-start.6
  121.5 1.0 collective-permute-start.11
  122.5 10.5 %last_back.1 = (bf16[2,144,768]{2,1,0:T(8,128)(2,1)}, bf16[2,144,768]{2,1,0:T(8,128)(2,1)}, f32[16,768]{1,0:T(8,128)}, bf16[384,896]{1,0:T(8,128)(2,1)}, bf16[384,896]{1,0:T(8,128)(2,1)}) custom-call(s32[32]{0:T(128)S(1)} %fusion.inv, bf16[2,144,2304]{2,1,0:T(8,128)(2,1)S(1)} %copy-done.5, bf16[2,144,2304]{2,1,0:T(8,128)(2,1)S(1)} %copy-done.7, ...), custom_call_target="tpu_custom_call" | custom-call | flops 4076863488 | bytes 16777216 | tf_op jit(solution)/shard_map/last_back/pallas_call | solution.py:688
  133.0 1.2 add_convert_fusion.12
  134.4 1.4 add_convert_fusion.7
  135.8 2.0 %collective-permute-done.11 = bf16[192,2304]{1,0:T(8,128)(2,1)S(1)} collective-permute-done((bf16[192,2304]{1,0:T(8,128)(2,1)S(1)}, bf16[192,2304]{1,0:T(8,128)(2,1)S(1)}, u32[]{:S(2)}, u32[]{:S(2)}) %collective-permute-start.11) | collective-permute-done | bytes 884768 | tf_op jit(solution)/shard_map/ppermute | solution.py:781
  139.4 2.6 %collective-permute-start.24 = (bf16[96,768]{1,0:T(8,128)(2,1)S(1)}, bf16[96,768]{1,0:T(8,128)(2,1)S(1)}, u32[]{:S(2)}, u32[]{:S(2)}) collective-permute-start(bf16[96,768]{1,0:T(8,128)(2,1)S(1)} %add_convert_fusion.12), channel_id=1, source_target_pairs={{0,16},{1,17},{2,18},{3,19},{4,20},{5,21},{6,22},{7,23},{8,24},{9,... | collective-permute-start | bytes 442376 | tf_op jit(solution)/shard_map/ppermute | solution.py:781
  142.2 1.3 copy.58
  143.5 1.5 collective-permute-start.17
  145.0 4.0 %collective-permute-done.24 = bf16[96,768]{1,0:T(8,128)(2,1)S(1)} collective-permute-done((bf16[96,768]{1,0:T(8,128)(2,1)S(1)}, bf16[96,768]{1,0:T(8,128)(2,1)S(1)}, u32[]{:S(2)}, u32[]{:S(2)}) %collective-permute-start.24) | collective-permute-done | bytes 147488 | tf_op jit(solution)/shard_map/ppermute | solution.py:781
  149.1 1.9 convert_add_fusion
  152.1 1.3 copy.59
  154.4 1.2 collective-permute-start.15
  155.7 1.7 collective-permute-done.17
  157.4 1.1 add_convert_fusion.11
  158.5 2.6 %collective-permute-start.23 = (bf16[24,3072]{1,0:T(8,128)(2,1)S(1)}, bf16[24,3072]{1,0:T(8,128)(2,1)S(1)}, u32[]{:S(2)}, u32[]{:S(2)}) collective-permute-start(bf16[24,3072]{1,0:T(8,128)(2,1)S(1)} %add_convert_fusion.11), channel_id=1, source_target_pairs={{0,16},{1,17},{2,18},{3,19},{4,20},{5,21},{6,22},{7,23},{8,24},{9,... | collective-permute-start | bytes 442376 | tf_op jit(solution)/shard_map/ppermute | solution.py:781
  161.2 5.7 %collective-permute-done.16 = bf16[96,2304]{1,0:T(8,128)(2,1)S(1)} collective-permute-done((bf16[96,2304]{1,0:T(8,128)(2,1)S(1)}, bf16[96,2304]{1,0:T(8,128)(2,1)S(1)}, u32[]{:S(2)}, u32[]{:S(2)}) %collective-permute-start.16) | collective-permute-done | bytes 442400 | tf_op jit(solution)/shard_map/ppermute | solution.py:781
  167.0 1.6 collective-permute-start.19
  168.6 1.9 convert_add_fusion.1
  171.4 1.8 collective-permute-done.19
  173.2 1.4 collective-permute-start.22
  174.6 1.4 collective-permute-done.18
  176.6 4.1 %collective-permute-done.22 = bf16[24,2304]{1,0:T(8,128)(2,1)S(1)} collective-permute-done((bf16[24,2304]{1,0:T(8,128)(2,1)S(1)}, bf16[24,2304]{1,0:T(8,128)(2,1)S(1)}, u32[]{:S(2)}, u32[]{:S(2)}) %collective-permute-start.22) | collective-permute-done | bytes 110624 | tf_op jit(solution)/shard_map/ppermute | solution.py:781
  180.9 1.6 collective-permute-start.21
  183.2 3.2 %collective-permute-done.21 = bf16[24,896]{1,0:T(8,128)(2,1)S(1)} collective-permute-done((bf16[24,896]{1,0:T(8,128)(2,1)S(1)}, bf16[24,896]{1,0:T(8,128)(2,1)S(1)}, u32[]{:S(2)}, u32[]{:S(2)}) %collective-permute-start.21) | collective-permute-done | bytes 43040 | tf_op jit(solution)/shard_map/ppermute | solution.py:781
  (170 shorter events, 14.3 us)
Async XLA Ops:
  0.6 5.7 %copy-start.19 = (bf16[4,140,768]{2,0,1:T(4,128)(2,1)S(1)}, bf16[4,140,768]{2,0,1:T(4,128)(2,1)}, u32[]{:S(2)}) copy-start(bf16[4,140,768]{2,0,1:T(4,128)(2,1)} %param.20) | copy-start | bytes 2580484
  3.1 13.2 %collective-permute-start = (bf16[2,140,768]{2,1,0:T(8,128)(2,1)S(1)}, bf16[2,140,768]{2,1,0:T(8,128)(2,1)S(1)}, u32[]{:S(2)}, u32[]{:S(2)}) collective-permute-start(bf16[2,140,768]{2,1,0:T(8,128)(2,1)S(1)} %copy_select_fusion), channel_id=1, source_target_pairs={{0,1},{1,0},{2,3},{3,2},{4,5},{5,4},{6,7},{7,6},{8,9},{9,8},{10,11... | collective-permute-start | bytes 1290248 | tf_op jit(solution)/shard_map/ppermute | solution.py:794
  6.2 12.0 %collective-permute-start.1 = (bf16[2,140]{1,0:T(2,128)(2,1)S(1)}, bf16[2,140]{1,0:T(2,128)(2,1)S(1)}, u32[]{:S(2)}, u32[]{:S(2)}) collective-permute-start(bf16[2,140]{1,0:T(2,128)(2,1)S(1)} %get-tuple-element.74), channel_id=1, source_target_pairs={{0,1},{1,0},{2,3},{3,2},{4,5},{5,4},{6,7},{7,6},{8,9},{9,8},{10,11... | collective-permute-start | bytes 1688 | tf_op jit(solution)/shard_map/ppermute | solution.py:794
  11.6 6.5 %copy-start.32 = (f32[768]{0:T(1024)S(1)}, f32[768]{0:T(1024)}, u32[]{:S(2)}) copy-start(f32[768]{0:T(1024)} %param.29) | copy-start | bytes 9220
  11.6 6.5 %copy-start.33 = (f32[768]{0:T(1024)S(1)}, f32[768]{0:T(1024)}, u32[]{:S(2)}) copy-start(f32[768]{0:T(1024)} %param.28) | copy-start | bytes 9220
  11.6 6.5 %copy-start.34 = (f32[768]{0:T(1024)S(1)}, f32[768]{0:T(1024)}, u32[]{:S(2)}) copy-start(f32[768]{0:T(1024)} %param.30) | copy-start | bytes 9220
  11.6 6.5 %copy-start.35 = (f32[768]{0:T(1024)S(1)}, f32[768]{0:T(1024)}, u32[]{:S(2)}) copy-start(f32[768]{0:T(1024)} %param.34) | copy-start | bytes 9220
  16.3 18.9 %collective-permute-start.2 = (bf16[2,140,768]{2,1,0:T(8,128)(2,1)S(1)}, bf16[2,140,768]{2,1,0:T(8,128)(2,1)S(1)}, u32[]{:S(2)}, u32[]{:S(2)}) collective-permute-start(bf16[2,140,768]{2,1,0:T(8,128)(2,1)S(1)} %get-tuple-element.77), channel_id=1, source_target_pairs={{0,1},{1,0},{2,3},{3,2},{4,5},{5,4},{6,7},{7,6},{8,9},{9,8},{10,11... | collective-permute-start | bytes 1290248 | tf_op jit(solution)/shard_map/ppermute | solution.py:794
  18.4 16.8 %slice-start.2 = ((s8[4718592]{0:T(1024)(128)(4,1)}), s8[524288]{0:T(1024)(128)(4,1)S(1)}, s32[]{:S(2)}) async-start(s8[4718592]{0:T(1024)(128)(4,1)} %bitcast.30), calls=%async_computation.2 | async-start | bytes 1048576
  22.9 12.4 %slice-start.3 = ((s8[4718592]{0:T(1024)(128)(4,1)}), s8[4194304]{0:T(1024)(128)(4,1)S(1)}, s32[]{:S(2)}) async-start(s8[4718592]{0:T(1024)(128)(4,1)} %bitcast.30), calls=%async_computation.3 | async-start | bytes 8388608
  22.9 12.4 %copy-start.15 = (f32[3072]{0:T(1024)S(1)}, f32[3072]{0:T(1024)}, u32[]{:S(2)}) copy-start(f32[3072]{0:T(1024)} %param.32) | copy-start | bytes 36868
  55.3 4.8 %collective-permute-start.3 = (bf16[1536,768]{1,0:T(8,128)(2,1)}, bf16[1536,768]{1,0:T(8,128)(2,1)S(1)}, u32[]{:S(2)}, u32[]{:S(2)}) collective-permute-start(bf16[1536,768]{1,0:T(8,128)(2,1)} %get-tuple-element.81), channel_id=1, source_target_pairs={{0,2},{1,3},{2,0},{3,1},{4,6},{5,7},{6,4},{7,5},{8,10},{9,11},{10,... | collective-permute-start | bytes 7077896 | tf_op jit(solution)/shard_map/ppermute | solution.py:770
  60.1 21.4 %copy-start.21 = (bf16[1536,768]{1,0:T(8,128)(2,1)}, bf16[1536,768]{1,0:T(8,128)(2,1)S(1)}, u32[]{:S(2)}) copy-start(bf16[1536,768]{1,0:T(8,128)(2,1)S(1)} %collective-permute-done.3) | copy-start | bytes 7077892
  62.6 18.9 %collective-permute-start.4 = (bf16[768,768]{1,0:T(8,128)(2,1)S(1)}, bf16[768,768]{1,0:T(8,128)(2,1)S(1)}, u32[]{:S(2)}, u32[]{:S(2)}) collective-permute-start(bf16[768,768]{1,0:T(8,128)(2,1)S(1)} %add_convert_fusion.1), channel_id=1, source_target_pairs={{0,4},{1,5},{2,10},{3,11},{4,0},{5,1},{6,14},{7,15},{8,12},{9,13},... | collective-permute-start | bytes 3538952 | tf_op jit(solution)/shard_map/ppermute | solution.py:781
  81.5 11.1 %copy-start.17 = (f32[576,768]{1,0:T(8,128)}, f32[576,768]{1,0:T(8,128)S(1)}, u32[]{:S(2)}) copy-start(f32[576,768]{1,0:T(8,128)S(1)} %get-tuple-element.91) | copy-start | bytes 5308420
  81.5 7.5 %copy-start.23 = (bf16[768,768]{1,0:T(8,128)(2,1)}, bf16[768,768]{1,0:T(8,128)(2,1)S(1)}, u32[]{:S(2)}) copy-start(bf16[768,768]{1,0:T(8,128)(2,1)S(1)} %collective-permute-done.4) | copy-start | bytes 3538948
  81.5 13.2 %copy-start.12 = (bf16[768,768]{1,0:T(8,128)(2,1)S(1)}, bf16[768,768]{1,0:T(8,128)(2,1)}, u32[]{:S(2)}) copy-start(bf16[768,768]{1,0:T(8,128)(2,1)} %ow.3) | copy-start | bytes 3538948
  81.5 13.2 %copy-start.18 = (bf16[2,2,144,768]{3,2,1,0:T(8,128)(2,1)S(1)}, bf16[2,2,144,768]{3,2,1,0:T(8,128)(2,1)}, u32[]{:S(2)}) copy-start(bf16[2,2,144,768]{3,2,1,0:T(8,128)(2,1)} %get-tuple-element.92.mixed) | copy-start | bytes 2654212
  84.3 4.7 %collective-permute-start.5 = (bf16[384,3072]{1,0:T(8,128)(2,1)}, bf16[384,3072]{1,0:T(8,128)(2,1)S(1)}, u32[]{:S(2)}, u32[]{:S(2)}) collective-permute-start(bf16[384,3072]{1,0:T(8,128)(2,1)} %get-tuple-element.89), channel_id=1, source_target_pairs={{0,2},{1,3},{2,0},{3,1},{4,6},{5,7},{6,4},{7,5},{8,10},{9,11},{10,... | collective-permute-start | bytes 7077896 | tf_op jit(solution)/shard_map/ppermute | solution.py:770
  89.0 5.7 %copy-start.5 = (bf16[2,144,2304]{2,1,0:T(8,128)(2,1)S(1)}, bf16[2,144,2304]{2,1,0:T(8,128)(2,1)}, u32[]{:S(2)}) copy-start(bf16[2,144,2304]{2,1,0:T(8,128)(2,1)} %get-tuple-element.69.qo) | copy-start | bytes 3981316
  89.0 5.7 %copy-start.7 = (bf16[2,144,2304]{2,1,0:T(8,128)(2,1)S(1)}, bf16[2,144,2304]{2,1,0:T(8,128)(2,1)}, u32[]{:S(2)}) copy-start(bf16[2,144,2304]{2,1,0:T(8,128)(2,1)} %get-tuple-element.73.qr) | copy-start | bytes 3981316
  89.0 5.7 %copy-start.13 = (bf16[2,144,768]{2,1,0:T(8,128)(2,1)S(1)}, bf16[2,144,768]{2,1,0:T(8,128)(2,1)}, u32[]{:S(2)}) copy-start(bf16[2,144,768]{2,1,0:T(8,128)(2,1)} %get-tuple-element.71.fno) | copy-start | bytes 1327108
  89.0 5.7 %copy-start.14 = (bf16[2,144,768]{2,1,0:T(8,128)(2,1)S(1)}, bf16[2,144,768]{2,1,0:T(8,128)(2,1)}, u32[]{:S(2)}) copy-start(bf16[2,144,768]{2,1,0:T(8,128)(2,1)} %get-tuple-element.93.fnr) | copy-start | bytes 1327108
  92.6 22.8 %collective-permute-start.7 = (bf16[192,3072]{1,0:T(8,128)(2,1)}, bf16[192,3072]{1,0:T(8,128)(2,1)}, u32[]{:S(2)}, u32[]{:S(2)}) collective-permute-start(bf16[192,3072]{1,0:T(8,128)(2,1)} %add_convert_fusion), channel_id=1, source_target_pairs={{0,4},{1,5},{2,10},{3,11},{4,0},{5,1},{6,14},{7,15},{8,12},{9,13},... | collective-permute-start | bytes 3538952 | tf_op jit(solution)/shard_map/ppermute | solution.py:781
  93.7 19.0 %collective-permute-start.8 = (bf16[384,768]{1,0:T(8,128)(2,1)}, bf16[384,768]{1,0:T(8,128)(2,1)S(1)}, u32[]{:S(2)}, u32[]{:S(2)}) collective-permute-start(bf16[384,768]{1,0:T(8,128)(2,1)} %add_convert_fusion.4), channel_id=1, source_target_pairs={{0,8},{1,9},{2,6},{3,7},{4,12},{5,13},{6,2},{7,3},{8,0},{9,1},{10,... | collective-permute-start | bytes 1769480 | tf_op jit(solution)/shard_map/ppermute | solution.py:781
  94.7 27.8 %slice-start = ((s8[5308416]{0:T(1024)(128)(4,1)}), s8[4194304]{0:T(1024)(128)(4,1)S(1)}, s32[]{:S(2)}) async-start(s8[5308416]{0:T(1024)(128)(4,1)} %bitcast.28), calls=%async_computation | async-start | bytes 8388608
  94.7 27.8 %slice-start.1 = ((s8[5308416]{0:T(1024)(128)(4,1)}), s8[1114112]{0:T(1024)(128)(4,1)S(1)}, s32[]{:S(2)}) async-start(s8[5308416]{0:T(1024)(128)(4,1)} %bitcast.28), calls=%async_computation.1 | async-start | bytes 2228224
  112.6 8.6 %copy-start.22 = (bf16[384,2304]{1,0:T(8,128)(2,1)S(1)}, bf16[384,2304]{1,0:T(8,128)(2,1)}, u32[]{:S(2)}) copy-start(bf16[384,2304]{1,0:T(8,128)(2,1)} %get-tuple-element.97) | copy-start | bytes 5308420
  115.5 7.0 %copy-start.3 = (bf16[576,1536]{1,0:T(8,128)(2,1)S(1)}, bf16[576,1536]{1,0:T(8,128)(2,1)}, u32[]{:S(2)}) copy-start(bf16[576,1536]{1,0:T(8,128)(2,1)} %get-tuple-element.105.dqa) | copy-start | bytes 5308420
  117.3 4.0 %collective-permute-start.9 = (bf16[384,2304]{1,0:T(8,128)(2,1)}, bf16[384,2304]{1,0:T(8,128)(2,1)S(1)}, u32[]{:S(2)}, u32[]{:S(2)}) collective-permute-start(bf16[384,2304]{1,0:T(8,128)(2,1)} %get-tuple-element.101), channel_id=1, source_target_pairs={{0,2},{1,3},{2,0},{3,1},{4,6},{5,7},{6,4},{7,5},{8,10},{9,11},{10,... | collective-permute-start | bytes 5308424 | tf_op jit(solution)/shard_map/ppermute | solution.py:770
  117.4 15.7 %collective-permute-start.13 = (bf16[192,768]{1,0:T(8,128)(2,1)S(1)}, bf16[192,768]{1,0:T(8,128)(2,1)S(1)}, u32[]{:S(2)}, u32[]{:S(2)}) collective-permute-start(bf16[192,768]{1,0:T(8,128)(2,1)S(1)} %add_convert_fusion.8), channel_id=1, source_target_pairs={{0,1},{1,0},{2,3},{3,2},{4,5},{5,4},{6,7},{7,6},{8,9},{9,8},{10,11... | collective-permute-start | bytes 884744 | tf_op jit(solution)/shard_map/ppermute | solution.py:781
  118.0 24.0 %collective-permute-start.6 = (bf16[2,144,768]{2,1,0:T(8,128)(2,1)}, bf16[2,144,768]{2,1,0:T(8,128)(2,1)S(1)}, u32[]{:S(2)}, u32[]{:S(2)}) collective-permute-start(bf16[2,144,768]{2,1,0:T(8,128)(2,1)} %get-tuple-element.96), channel_id=1, source_target_pairs={{0,1},{1,0},{2,3},{3,2},{4,5},{5,4},{6,7},{7,6},{8,9},{9,8},{10,11... | collective-permute-start | bytes 1327112 | tf_op jit(solution)/shard_map/ppermute | solution.py:794
  119.5 14.9 %collective-permute-start.12 = (bf16[96,3072]{1,0:T(8,128)(2,1)S(1)}, bf16[96,3072]{1,0:T(8,128)(2,1)S(1)}, u32[]{:S(2)}, u32[]{:S(2)}) collective-permute-start(bf16[96,3072]{1,0:T(8,128)(2,1)S(1)} %add_convert_fusion.3), channel_id=1, source_target_pairs={{0,8},{1,9},{2,6},{3,7},{4,12},{5,13},{6,2},{7,3},{8,0},{9,1},{10,... | collective-permute-start | bytes 1769480 | tf_op jit(solution)/shard_map/ppermute | solution.py:781
  121.5 16.3 %collective-permute-start.11 = (bf16[192,2304]{1,0:T(8,128)(2,1)S(1)}, bf16[192,2304]{1,0:T(8,128)(2,1)S(1)}, u32[]{:S(2)}, u32[]{:S(2)}) collective-permute-start(bf16[192,2304]{1,0:T(8,128)(2,1)S(1)} %add_convert_fusion.2), channel_id=1, source_target_pairs={{0,4},{1,5},{2,10},{3,11},{4,0},{5,1},{6,14},{7,15},{8,12},{9,13},... | collective-permute-start | bytes 2654216 | tf_op jit(solution)/shard_map/ppermute | solution.py:781
  134.2 7.8 %copy-start.26 = (bf16[2,144,768]{2,1,0:T(8,128)(2,1)S(1)}, bf16[2,144,768]{2,1,0:T(8,128)(2,1)}, u32[]{:S(2)}) copy-start(bf16[2,144,768]{2,1,0:T(8,128)(2,1)} %get-tuple-element.78) | copy-start | bytes 1327108
  137.9 16.4 %collective-permute-start.14 = (bf16[384,896]{1,0:T(8,128)(2,1)S(1)}, bf16[384,896]{1,0:T(8,128)(2,1)S(1)}, u32[]{:S(2)}, u32[]{:S(2)}) collective-permute-start(bf16[384,896]{1,0:T(8,128)(2,1)S(1)} %copy-done.42), channel_id=1, source_target_pairs={{0,2},{1,3},{2,0},{3,1},{4,6},{5,7},{6,4},{7,5},{8,10},{9,11},{10,... | collective-permute-start | bytes 2064392 | tf_op jit(solution)/shard_map/ppermute | solution.py:770
  138.9 13.0 %collective-permute-start.10 = (bf16[2,144,768]{2,1,0:T(8,128)(2,1)S(1)}, bf16[2,144,768]{2,1,0:T(8,128)(2,1)S(1)}, u32[]{:S(2)}, u32[]{:S(2)}) collective-permute-start(bf16[2,144,768]{2,1,0:T(8,128)(2,1)S(1)} %copy-done.43), channel_id=1, source_target_pairs={{0,1},{1,0},{2,3},{3,2},{4,5},{5,4},{6,7},{7,6},{8,9},{9,8},{10,11... | collective-permute-start | bytes 1327112 | tf_op jit(solution)/shard_map/ppermute | solution.py:794
  139.4 9.6 %collective-permute-start.24 = (bf16[96,768]{1,0:T(8,128)(2,1)S(1)}, bf16[96,768]{1,0:T(8,128)(2,1)S(1)}, u32[]{:S(2)}, u32[]{:S(2)}) collective-permute-start(bf16[96,768]{1,0:T(8,128)(2,1)S(1)} %add_convert_fusion.12), channel_id=1, source_target_pairs={{0,16},{1,17},{2,18},{3,19},{4,20},{5,21},{6,22},{7,23},{8,24},{9,... | collective-permute-start | bytes 442376 | tf_op jit(solution)/shard_map/ppermute | solution.py:781
  142.2 9.8 %copy-start.27 = (bf16[2,144,768]{2,1,0:T(8,128)(2,1)S(1)}, bf16[2,144,768]{2,1,0:T(8,128)(2,1)}, u32[]{:S(2)}) copy-start(bf16[2,144,768]{2,1,0:T(8,128)(2,1)} %get-tuple-element.108) | copy-start | bytes 1327108
  143.5 13.9 %collective-permute-start.17 = (bf16[48,3072]{1,0:T(8,128)(2,1)S(1)}, bf16[48,3072]{1,0:T(8,128)(2,1)S(1)}, u32[]{:S(2)}, u32[]{:S(2)}) collective-permute-start(bf16[48,3072]{1,0:T(8,128)(2,1)S(1)} %add_convert_fusion.7), channel_id=1, source_target_pairs={{0,1},{1,0},{2,3},{3,2},{4,5},{5,4},{6,7},{7,6},{8,9},{9,8},{10,11... | collective-permute-start | bytes 884744 | tf_op jit(solution)/shard_map/ppermute | solution.py:781
  153.4 13.5 %collective-permute-start.16 = (bf16[96,2304]{1,0:T(8,128)(2,1)S(1)}, bf16[96,2304]{1,0:T(8,128)(2,1)S(1)}, u32[]{:S(2)}, u32[]{:S(2)}) collective-permute-start(bf16[96,2304]{1,0:T(8,128)(2,1)S(1)} %add_convert_fusion.5), channel_id=1, source_target_pairs={{0,8},{1,9},{2,6},{3,7},{4,12},{5,13},{6,2},{7,3},{8,0},{9,1},{10,... | collective-permute-start | bytes 1327112 | tf_op jit(solution)/shard_map/ppermute | solution.py:781
  154.4 16.0 %collective-permute-start.15 = (bf16[192,896]{1,0:T(8,128)(2,1)S(1)}, bf16[192,896]{1,0:T(8,128)(2,1)S(1)}, u32[]{:S(2)}, u32[]{:S(2)}) collective-permute-start(bf16[192,896]{1,0:T(8,128)(2,1)S(1)} %add_convert_fusion.6), channel_id=1, source_target_pairs={{0,4},{1,5},{2,10},{3,11},{4,0},{5,1},{6,14},{7,15},{8,12},{9,13},... | collective-permute-start | bytes 1032200 | tf_op jit(solution)/shard_map/ppermute | solution.py:781
  158.5 10.1 %collective-permute-start.23 = (bf16[24,3072]{1,0:T(8,128)(2,1)S(1)}, bf16[24,3072]{1,0:T(8,128)(2,1)S(1)}, u32[]{:S(2)}, u32[]{:S(2)}) collective-permute-start(bf16[24,3072]{1,0:T(8,128)(2,1)S(1)} %add_convert_fusion.11), channel_id=1, source_target_pairs={{0,16},{1,17},{2,18},{3,19},{4,20},{5,21},{6,22},{7,23},{8,24},{9,... | collective-permute-start | bytes 442376 | tf_op jit(solution)/shard_map/ppermute | solution.py:781
  167.0 6.1 %collective-permute-start.19 = (bf16[48,2304]{1,0:T(8,128)(2,1)S(1)}, bf16[48,2304]{1,0:T(8,128)(2,1)S(1)}, u32[]{:S(2)}, u32[]{:S(2)}) collective-permute-start(bf16[48,2304]{1,0:T(8,128)(2,1)S(1)} %add_convert_fusion.9), channel_id=1, source_target_pairs={{0,1},{1,0},{2,3},{3,2},{4,5},{5,4},{6,7},{7,6},{8,9},{9,8},{10,11... | collective-permute-start | bytes 663560 | tf_op jit(solution)/shard_map/ppermute | solution.py:781
  170.5 5.5 %collective-permute-start.18 = (bf16[96,896]{1,0:T(8,128)(2,1)S(1)}, bf16[96,896]{1,0:T(8,128)(2,1)S(1)}, u32[]{:S(2)}, u32[]{:S(2)}) collective-permute-start(bf16[96,896]{1,0:T(8,128)(2,1)S(1)} %add_convert_fusion.10), channel_id=1, source_target_pairs={{0,8},{1,9},{2,6},{3,7},{4,12},{5,13},{6,2},{7,3},{8,0},{9,1},{10,... | collective-permute-start | bytes 516104 | tf_op jit(solution)/shard_map/ppermute | solution.py:781
  173.2 7.6 %collective-permute-start.22 = (bf16[24,2304]{1,0:T(8,128)(2,1)S(1)}, bf16[24,2304]{1,0:T(8,128)(2,1)S(1)}, u32[]{:S(2)}, u32[]{:S(2)}) collective-permute-start(bf16[24,2304]{1,0:T(8,128)(2,1)S(1)} %add_convert_fusion.13), channel_id=1, source_target_pairs={{0,16},{1,17},{2,18},{3,19},{4,20},{5,21},{6,22},{7,23},{8,24},{9,... | collective-permute-start | bytes 331784 | tf_op jit(solution)/shard_map/ppermute | solution.py:781
  176.0 4.8 %collective-permute-start.20 = (bf16[48,896]{1,0:T(8,128)(2,1)S(1)}, bf16[48,896]{1,0:T(8,128)(2,1)S(1)}, u32[]{:S(2)}, u32[]{:S(2)}) collective-permute-start(bf16[48,896]{1,0:T(8,128)(2,1)S(1)} %add_convert_fusion.14), channel_id=1, source_target_pairs={{0,1},{1,0},{2,3},{3,2},{4,5},{5,4},{6,7},{7,6},{8,9},{9,8},{10,11... | collective-permute-start | bytes 258056 | tf_op jit(solution)/shard_map/ppermute | solution.py:781
  180.9 5.4 %collective-permute-start.21 = (bf16[24,896]{1,0:T(8,128)(2,1)S(1)}, bf16[24,896]{1,0:T(8,128)(2,1)S(1)}, u32[]{:S(2)}, u32[]{:S(2)}) collective-permute-start(bf16[24,896]{1,0:T(8,128)(2,1)S(1)} %add_convert_fusion.15), channel_id=1, source_target_pairs={{0,16},{1,17},{2,18},{3,19},{4,20},{5,21},{6,22},{7,23},{8,24},{9,... | collective-permute-start | bytes 129032 | tf_op jit(solution)/shard_map/ppermute | solution.py:781
  (25 other events, 93.7 us)

commit v3 on v2

--- a/solution.py
+++ b/solution.py
@@ -18,9 +18,12 @@
 LANES = 128
 PAD = 4
 MIB = 1 << 20
+MLP_MIB = 34
 
 CORE_BIT = 2
 ORDERS = ((4, 8, 1, 16), (8, 4, 1, 16))
+SIDE_STAGES = (2, 0, 1, 3)
+SIDE = 512
 EARLY = 4
 
 
@@ -63,6 +66,10 @@
 
 def spec_of(a):
     return pl.BlockSpec(a.shape, lambda *_: (0,) * len(a.shape))
+
+
+def resident():
+    return pl.BlockSpec(memory_space=pltpu.VMEM)
 
 
 def struct(shape, dtype):
@@ -227,17 +234,24 @@
     )(qkv_own, qkv_far, x_own, x_far, okrow, out_weight, out_bias, gain, shift)
 
 
-def mlp_up_kernel(
-    info, place, sn, att, co, cr, up, upb, down, downb,
-    slope_ref, own_ref, far_ref, gy_ref, dbg_ref, keep, send, acc, wbuf, sems, *, shard,
+def mlp_kernel(
+    info, inv, place, sn, att_hbm, co, cr, up, upb, down, downb,
+    own_ref, far_ref, gy_ref, dbg_ref, gs_ref, upbg_ref, keep, send,
+    acc, att, down_buf, up_buf, tall, snt, att_sem, down_sems, up_sems, *, shards,
 ):
     j = pl.program_id(0)
     last = pl.num_programs(0) - 1
     pairs, half, width = co.shape
-    tile = up.shape[1]
+    tile = upb.shape[1]
+    up_j = up[:, lane_block(j, tile)]
+    down_j = down[pl.ds(pl.multiple_of(j * tile, tile), tile), :]
+    att_copy = pltpu.make_async_copy(att_hbm, att, att_sem)
+    slot = lax.rem(j, 2)
+    tall_shard, wide_shard = down.shape[0] // shards if shards else 0, width // shards if shards else 0
 
     @pl.when(j == 0)
     def _():
+        att_copy.start()
         for far, c in enumerate((co, cr)):
             for p in range(pairs):
                 at = (far * pairs + p) * half
@@ -245,50 +259,59 @@
                     own_rows(info, p, far, half), c[p].astype(F32), 0.0
                 ).astype(BF16)
         dbg_ref[...] = column_sums(gy_ref[...].astype(F32))
-
-    h, slope = gelu_and_slope(dot_nn(sn[...], up[...]) + upb[...])
-    slope_ref[...] = slope.astype(BF16)
-    h = h.astype(BF16)
-    part = dot_nn(h, down[...])
-
-    @pl.when(j == 0)
-    def _():
-        acc[...] = part
-
-    @pl.when(j > 0)
-    def _():
-        acc[...] += part
-
-    grad = dot_tn(h, gy_ref[...])
-    if not shard:
-        keep[...] = grad
-        send[...] = jnp.zeros_like(send)
-    else:
-        count = tile // shard
-        slot = lax.rem(j, 2)
-
-        def copy_of(step, i, act):
+        acc[...] = jnp.zeros_like(acc)
+        gs_ref[...] = jnp.zeros_like(gs_ref)
+        if shards:
+            wire_rows(sn[...], inv, tall, snt, wide_shard)
+
+    def down_copies(step, act):
+        count = tile // tall_shard
+        for i in range(count):
             pos = place[step * count + i]
-            src = wbuf.at[lax.rem(step, 2), pl.ds(i * shard, shard), :]
-            n = keep.shape[0] // shard
+            src = down_buf.at[lax.rem(step, 2), pl.ds(i * tall_shard, tall_shard), :]
+            sem = down_sems.at[lax.rem(step, 2), i]
+            n = 2 * keep.shape[0]
             for ref, ours in ((keep, pos < n), (send, pos >= n)):
 
                 @pl.when(ours)
                 def _():
-                    at = pl.multiple_of(lax.rem(pos, n) * shard, shard)
-                    act(pltpu.make_async_copy(src, ref.at[pl.ds(at, shard), :], sems.at[lax.rem(step, 2), i]))
+                    q = lax.rem(pos, n)
+                    at = pl.multiple_of(lax.rem(q, 2) * tall_shard, tall_shard)
+                    act(pltpu.make_async_copy(src, ref.at[lax.div(q, 2), pl.ds(at, tall_shard), :], sem))
+
+    def up_copies(step, act):
+        n = keep.shape[0]
+        rows = 2 * wide_shard
+        at = pl.multiple_of(2 * tall_shard + step * rows, rows)
+        for i, ref in enumerate((keep, send)):
+            src = up_buf.at[lax.rem(step, 2), pl.ds(i * n, n), :, :]
+            act(pltpu.make_async_copy(src, ref.at[:, pl.ds(at, rows), :], up_sems.at[lax.rem(step, 2), i]))
+
+    if shards:
 
         @pl.when(j > 1)
         def _():
-            for i in range(count):
-                copy_of(j - 2, i, lambda c: c.wait())
-
-        wbuf[slot] = grad.astype(BF16)
-        for i in range(count):
-            copy_of(j, i, lambda c: c.start())
+            down_copies(j - 2, lambda c: c.wait())
+            up_copies(j - 2, lambda c: c.wait())
+
+    h, slope = gelu_and_slope(dot_nn(sn[...], up_j) + upb[...])
+    h = h.astype(BF16)
+    acc[...] += dot_nn(h, down_j)
+    gp = (dot_nt(gy_ref[...], down_j) * slope).astype(BF16)
+    upbg_ref[...] = column_sums(gp.astype(F32))
+    gs_ref[...] += dot_nt(gp, up_j)
+    if not shards:
+        keep[...] = dot_tn(h, gy_ref[...])
+        send[...] = dot_tn(sn[...], gp)
+    else:
+        down_buf[slot] = dot_tn(h, gy_ref[...]).astype(BF16)
+        down_copies(j, lambda c: c.start())
+        up_buf[slot] = dot_nn(snt[...], gp).astype(BF16).reshape(up_buf.shape[1:])
+        up_copies(j, lambda c: c.start())
 
     @pl.when(j == last)
     def _():
+        att_copy.wait()
         final = att[...] + acc[...] + downb[...]
         for far, o in enumerate((own_ref, far_ref)):
             for p in range(pairs):
@@ -296,157 +319,78 @@
                 o[p] = jnp.where(
                     own_rows(info, p, far, half), final[at : at + half, :], 0.0
                 ).astype(BF16)
-        if shard:
+        if shards:
             for step in (last - 1, last):
-                for i in range(count):
-                    copy_of(step, i, lambda c: c.wait())
-
-
-def mlp_up(info, place, sn, att, cot_own, cot_far, up, up_bias, down, down_bias, shards, packed):
+                down_copies(step, lambda c: c.wait())
+                up_copies(step, lambda c: c.wait())
+
+
+def mlp(info, inv, place, sn, att, cot_own, cot_far, up, up_bias, down, down_bias, shards):
     pairs, half, width = cot_own.shape
     rows = 2 * pairs * half
     ff = up.shape[1]
     tile = width
-    shard = ff // shards
-    tiled = lambda j, *_: (j, 0)
-    if packed:
-        wire = [kept((ff // 2, width), BF16)] * 2
+    cols = lambda j, *_: (0, j)
+    if shards:
+        wire = [kept((shards // 4, 4 * ff // shards, width), BF16)] * 2
         wire_specs = [pl.BlockSpec(memory_space=pl.ANY)] * 2
-        count = tile // shard
+        blocks, count = (shards // 2, 2 * width // shards), tile * shards // ff
     else:
-        wire = [struct((ff, width), F32), struct((8, LANES), F32)]
-        wire_specs = [pl.BlockSpec((tile, width), tiled), spec_of(wire[1])]
-        count = 1
+        wire = [struct((ff, width), F32), struct((width, ff), F32)]
+        wire_specs = [pl.BlockSpec((tile, width), lambda j, *_: (j, 0)), pl.BlockSpec((width, tile), cols)]
+        blocks, count = (width // 16, 16), 1
     rows3 = kept((pairs, half, width), BF16)
     return pl.pallas_call(
-        partial(mlp_up_kernel, shard=shard if packed else 0),
+        partial(mlp_kernel, shards=shards),
         grid_spec=pltpu.PrefetchScalarGridSpec(
-            num_scalar_prefetch=2,
+            num_scalar_prefetch=3,
             grid=(ff // tile,),
             in_specs=[
                 spec_of(sn),
-                spec_of(att),
+                pl.BlockSpec(memory_space=pl.ANY),
                 spec_of(cot_own),
                 spec_of(cot_far),
-                pl.BlockSpec((width, tile), lambda j, *_: (0, j)),
-                pl.BlockSpec((1, tile), lambda j, *_: (0, j)),
-                pl.BlockSpec((tile, width), tiled),
+                resident(),
+                pl.BlockSpec((1, tile), cols),
+                resident(),
                 spec_of(down_bias),
             ],
             out_specs=[
-                pl.BlockSpec((rows, tile), lambda j, *_: (0, j)),
                 spec_of(rows3),
                 spec_of(rows3),
                 spec_of(sn),
                 spec_of(down_bias),
+                spec_of(sn),
+                pl.BlockSpec((1, tile), cols),
             ]
             + wire_specs,
             scratch_shapes=[
                 pltpu.VMEM((rows, width), F32),
+                pltpu.VMEM((rows, width), F32),
                 pltpu.VMEM((2, tile, width), BF16),
-                pltpu.SemaphoreType.DMA((2, count)),
-            ],
-        ),
-        out_shape=[struct((rows, ff), BF16), rows3, rows3, struct((rows, width), BF16), kept((1, width), F32)]
-        + wire,
-        compiler_params=params_of(40),
-        cost_estimate=pl.CostEstimate(
-            flops=6 * rows * width * ff, bytes_accessed=22 * MIB, transcendentals=2 * rows * ff
-        ),
-        name="mlp_up",
-    )(info, place, sn, att, cot_own, cot_far, up, up_bias, down, down_bias)
-
-
-def mlp_back_kernel(
-    inv, gy, slope, sn, up, down, gs_ref, upb_ref, keep, send, tall, snt, wbuf, sems, *, shard
-):
-    j = pl.program_id(0)
-    last = pl.num_programs(0) - 1
-    gp = (dot_nt(gy[...], down[...]) * slope[...].astype(F32)).astype(BF16)
-    upb_ref[...] = column_sums(gp.astype(F32))
-    part = dot_nt(gp, up[...])
-
-    @pl.when(j == 0)
-    def _():
-        gs_ref[...] = part
-
-    @pl.when(j > 0)
-    def _():
-        gs_ref[...] += part
-
-    if not shard:
-        keep[...] = dot_tn(sn[...], gp)
-        send[...] = jnp.zeros_like(send)
-        return
-
-    @pl.when(j == 0)
-    def _():
-        wire_rows(sn[...], inv, tall, snt, shard)
-
-    n, tile = keep.shape[0], up.shape[1]
-
-    def copies(step):
-        slot = lax.rem(step, 2)
-        cols = lane_block(step, tile)
-        for i, ref in enumerate((keep, send)):
-            yield pltpu.make_async_copy(
-                wbuf.at[slot, pl.ds(i * n, n), :], ref.at[:, cols], sems.at[slot, i]
-            )
-
-    @pl.when(j > 1)
-    def _():
-        for c in copies(j - 2):
-            c.wait()
-
-    wbuf[lax.rem(j, 2)] = dot_nn(snt[...], gp).astype(BF16)
-    for c in copies(j):
-        c.start()
-
-    @pl.when(j == last)
-    def _():
-        for step in (last - 1, last):
-            for c in copies(step):
-                c.wait()
-
-
-def mlp_back(inv, gy, slope, sn, up, down, shards, packed):
-    rows, width = gy.shape
-    ff = up.shape[1]
-    tile = width
-    cols = lambda j, *_: (0, j)
-    if packed:
-        wire = [kept((width // 2, ff), BF16)] * 2
-        wire_specs = [pl.BlockSpec(memory_space=pl.ANY)] * 2
-    else:
-        wire = [struct((width, ff), F32), struct((8, LANES), F32)]
-        wire_specs = [pl.BlockSpec((width, tile), cols), spec_of(wire[1])]
-    return pl.pallas_call(
-        partial(mlp_back_kernel, shard=width // shards if packed else 0),
-        grid_spec=pltpu.PrefetchScalarGridSpec(
-            num_scalar_prefetch=1,
-            grid=(ff // tile,),
-            in_specs=[
-                spec_of(gy),
-                pl.BlockSpec((rows, tile), cols),
-                spec_of(sn),
-                pl.BlockSpec((width, tile), cols),
-                pl.BlockSpec((tile, width), lambda j, *_: (j, 0)),
-            ],
-            out_specs=[spec_of(gy), pl.BlockSpec((1, tile), cols)] + wire_specs,
-            scratch_shapes=[
+                pltpu.VMEM((2,) + blocks + (tile,), BF16),
                 pltpu.VMEM((width, rows), F32),
                 pltpu.VMEM((width, rows), BF16),
-                pltpu.VMEM((2, width, tile), BF16),
+                pltpu.SemaphoreType.DMA,
+                pltpu.SemaphoreType.DMA((2, count)),
                 pltpu.SemaphoreType.DMA((2, 2)),
             ],
         ),
-        out_shape=[struct((rows, width), F32), kept((1, ff), F32)] + wire,
-        compiler_params=params_of(40),
+        out_shape=[
+            rows3,
+            rows3,
+            struct((rows, width), BF16),
+            kept((1, width), F32),
+            struct((rows, width), F32),
+            kept((1, ff), F32),
+        ]
+        + wire,
+        compiler_params=params_of(MLP_MIB if shards else 56),
         cost_estimate=pl.CostEstimate(
-            flops=6 * rows * width * ff, bytes_accessed=20 * MIB, transcendentals=0
+            flops=12 * rows * width * ff, bytes_accessed=24 * MIB, transcendentals=2 * rows * ff
         ),
-        name="mlp_back",
-    )(inv, gy, slope, sn, up, down)
+        name="mlp",
+    )(info, inv, place, sn, att, cot_own, cot_far, up, up_bias, down, down_bias)
 
 
 def heads_back(qo, qr, gm_ref, p_ref, dqkv, base, rows, hp0, count):
@@ -487,15 +431,10 @@
     send[:, at : at + grad.shape[1]] = grad[n:]
 
 
-def attend_back_kernel(
-    inv, gs, gy, att, mixed, fno, fnr, qo, qr, p_ref, ow, g2,
-    ga_ref, gm_ref, dqkv, fnt, vec_ref, keep, send, gbs, fns, mxs, tall, *, shard,
-):
-    pair = pl.program_id(0)
-    half, width = fno.shape[1], fno.shape[2]
-    rows = 2 * half
-
-    @pl.when(pair == 0)
+def second_back_kernel(gs, gy, att, ow, g2, ga_ref, br_ref, gm_ref, vec_ref):
+    rows, width = gm_ref.shape[1], gm_ref.shape[2]
+
+    @pl.when(pl.program_id(0) == 0)
     def _():
         vec_ref[...] = jnp.zeros_like(vec_ref)
 
@@ -506,11 +445,47 @@
     )
     ga_ref[0] = grad_att
     branch = grad_att.astype(BF16)
+    br_ref[0] = branch
+    gm_ref[0] = dot_nt(branch, ow[...]).astype(BF16)
     for i, v in enumerate((branch.astype(F32), grad_second * unit, grad_second)):
         vec_ref[i : i + 1, :] += column_sums(v)
+
+
+def second_back(gs, gy, att, out_weight, gain):
+    _, pairs, half, width = gs.shape
+    rows = 2 * half
+    rows4 = pl.BlockSpec((2, 1, half, width), lambda p: (0, p, 0, 0))
+    rows3 = pl.BlockSpec((1, rows, width), lambda p: (p, 0, 0))
+    vec = kept((8, width), F32)
+    return pl.pallas_call(
+        second_back_kernel,
+        grid=(pairs,),
+        in_specs=[rows4, rows4, rows4, spec_of(out_weight), spec_of(gain)],
+        out_specs=[rows3, rows3, rows3, spec_of(vec)],
+        out_shape=[
+            kept((pairs, rows, width), F32),
+            struct((pairs, rows, width), BF16),
+            struct((pairs, rows, width), BF16),
+            vec,
+        ],
+        compiler_params=params_of(24),
+        cost_estimate=pl.CostEstimate(
+            flops=2 * pairs * rows * width * width, bytes_accessed=10 * MIB, transcendentals=0
+        ),
+        name="second_back",
+    )(gs, gy, att, out_weight, gain)
+
+
+def attend_back_kernel(
+    inv, br, mixed, fno, fnr, qo, qr, p_ref, gm_ref, dqkv, fnt, tok_ref, keep, send, gbs, fns, mxs, tall,
+    *, shard,
+):
+    pair = pl.program_id(0)
+    half, width = fno.shape[1], fno.shape[2]
+    rows = 2 * half
     base = pl.multiple_of(pair * rows, rows)
-    gbs[pl.ds(base, rows), :] = branch
-    gm_ref[0] = dot_nt(branch, ow[...]).astype(BF16)
+    tok_ref[...] = jnp.zeros_like(tok_ref)
+    gbs[pl.ds(base, rows), :] = br[0]
     fns[pl.ds(base, half), :] = fno[0]
     fns[pl.ds(base + half, half), :] = fnr[0]
     mxs[pl.ds(base, rows), :] = mixed[...].reshape(rows, width)
@@ -533,7 +508,7 @@
 
 
 def attend_back(
-    inv, gs, gy, att, mixed, fn_own, fn_far, qkv_own, qkv_far, probs, out_weight, gain, shards, packed
+    inv, branch, mixed, fn_own, fn_far, qkv_own, qkv_far, probs, gm, shards, packed
 ):
     pairs, half, width = fn_own.shape
     rows = 2 * half
@@ -547,7 +522,7 @@
     outs = [
         struct((pairs * rows, early), BF16),
         struct((width, pairs * rows), BF16),
-        kept((8, width), F32),
+        kept((8, LANES), F32),
     ] + wire
     return pl.pallas_call(
         partial(attend_back_kernel, shard=width // shards if packed else 0),
@@ -555,23 +530,16 @@
             num_scalar_prefetch=1,
             grid=(pairs,),
             in_specs=[
-                rows4,
-                rows4,
-                rows4,
+                pl.BlockSpec((1, rows, width), pair3),
                 rows4,
                 pl.BlockSpec((1, half, width), pair3),
                 pl.BlockSpec((1, half, width), pair3),
                 pl.BlockSpec((1, half, 3 * width), pair3),
                 pl.BlockSpec((1, half, 3 * width), pair3),
                 pl.BlockSpec((1, EARLY, 2 * rows, rows), lambda p, *_: (p, 0, 0, 0)),
-                spec_of(out_weight),
-                spec_of(gain),
+                pl.BlockSpec((1, rows, width), pair3),
             ],
-            out_specs=[
-                pl.BlockSpec((1, rows, width), pair3),
-                pl.BlockSpec((1, rows, width), pair3),
-            ]
-            + [spec_of(o) for o in outs],
+            out_specs=[spec_of(o) for o in outs],
             scratch_shapes=[
                 pltpu.VMEM((pairs * rows, width), BF16),
                 pltpu.VMEM((pairs * rows, width), BF16),
@@ -579,15 +547,15 @@
                 pltpu.VMEM((width, pairs * rows), F32),
             ],
         ),
-        out_shape=[struct((pairs, rows, width), F32), struct((pairs, rows, width), BF16)] + outs,
-        compiler_params=params_of(44),
+        out_shape=outs,
+        compiler_params=params_of(40 if packed else 50),
         cost_estimate=pl.CostEstimate(
-            flops=pairs * 32 * EARLY * rows * rows * LANES + 8 * pairs * rows * width * width,
-            bytes_accessed=20 * MIB,
+            flops=pairs * 32 * EARLY * rows * rows * LANES + 6 * pairs * rows * width * width,
+            bytes_accessed=16 * MIB,
             transcendentals=0,
         ),
         name="attend_back",
-    )(inv, gs, gy, att, mixed, fn_own, fn_far, qkv_own, qkv_far, probs, out_weight, gain)
+    )(inv, branch, mixed, fn_own, fn_far, qkv_own, qkv_far, probs, gm)
 
 
 def last_back_kernel(
@@ -763,27 +731,111 @@
     return lax.optimization_barrier(values)
 
 
+def exchange(block, stage, shards):
+    bits = [CORE_BIT if stage is None else ORDERS[core_of(i)][stage] for i in range(shards)]
+    return lax.ppermute(block, AXES, [(i, i ^ bit) for i, bit in enumerate(bits)])
+
+
+def halves(block, axis):
+    if axis < 3:
+        return tuple(lax.slice_in_dim(block, i, i + 1, axis=axis) for i in range(2))
+    return block[0, 0, 0, 0], block[0, 0, 0, 1]
+
+
 class Reduction:
-    def __init__(self, keep, send, shards):
-        self.shards, self.stage, self.n = shards, 0, keep.shape[0]
-        self.terms = [keep]
-        self.incoming = lax.ppermute(send, AXES, [(i, i ^ CORE_BIT) for i in range(shards)])
+    def __init__(self, terms, shards, stages=(0, 1, 2, 3)):
+        self.terms, self.shards, self.stages, self.done = terms, shards, stages, 0
+        self.incoming, self.came = None, []
 
     def hold(self, *others):
         self.incoming = after(self.incoming, *others)
 
+    def fold(self):
+        if self.incoming is not None:
+            self.terms.append(self.incoming)
+            self.came.append(self.incoming)
+            self.incoming = None
+
+    def parts(self):
+        self.fold()
+        stage = self.stages[self.done]
+        self.done += 1
+        pieces = [halves(t, stage) for t in self.terms]
+        self.terms = [p[0] for p in pieces]
+        return add_up([p[1] for p in pieces]).astype(BF16)
+
     def step(self):
-        self.terms.append(self.incoming)
-        self.n //= 2
-        out = add_up([t[self.n :] for t in self.terms]).astype(BF16)
-        self.terms = [t[: self.n] for t in self.terms]
-        route = [(i, i ^ ORDERS[core_of(i)][self.stage]) for i in range(self.shards)]
-        self.incoming = lax.ppermute(out, AXES, route)
-        self.stage += 1
+        stage = self.stages[self.done]
+        out = self.parts()
+        self.incoming = exchange(out, stage, self.shards)
         return out
 
     def result(self):
-        return add_up(self.terms + [self.incoming])
+        self.fold()
+        return add_up(self.terms)
+
+
+def part_pairs_kernel(keep, got, p1, p2, p3, q1, q2, q3, mine, sent, *, tall, short):
+    take = lambda ref: ref[...].reshape(ref.shape[-2:]).astype(F32)
+    wide = take(keep) + take(got)
+    left = wide[:, :SIDE] + take(p1) + take(p2) + take(p3)
+    right = wide[:, SIDE:] + take(q1) + take(q2) + take(q3)
+    for cols, block in ((slice(0, SIDE), left), (slice(SIDE, wide.shape[1]), right)):
+        mine[:tall, cols] = block[:tall]
+        theirs = [block[tall : 2 * tall]]
+        for at in range(2 * tall, block.shape[0], 2 * short):
+            to = tall + (at - 2 * tall) // 2
+            mine[to : to + short, cols] = block[at : at + short]
+            theirs.append(block[at + short : at + 2 * short])
+        sent[:, cols] = jnp.concatenate(theirs, axis=0).astype(BF16)
+
+
+def part_pairs(keep, got, left, right, tall, short):
+    rows, width = keep.shape[-2], keep.shape[-1]
+    first = lambda a: pl.BlockSpec(
+        (1,) * (len(a.shape) - 2) + a.shape[-2:], lambda i: (0,) * len(a.shape)
+    )
+    args = (keep, got, *left, *right)
+    outs = [struct((rows // 2, width), F32), struct((rows // 2, width), BF16)]
+    return pl.pallas_call(
+        partial(part_pairs_kernel, tall=tall, short=short),
+        grid=(1,),
+        in_specs=[first(a) for a in args],
+        out_specs=[spec_of(o) for o in outs],
+        out_shape=outs,
+        cost_estimate=pl.CostEstimate(flops=0, bytes_accessed=4 * MIB, transcendentals=0),
+        name="part_pairs",
+    )(*args)
+
+
+def finish_pair_kernel(mine, got, down_ref, up_ref):
+    total = mine[...] + got[...].astype(F32)
+    tall, short, width = down_ref.shape[0], up_ref.shape[0], total.shape[1]
+    down_ref[...] = total[:tall]
+    for i in range(up_ref.shape[1] // width):
+        at = tall + i * short
+        up_ref[:, i * width : (i + 1) * width] = total[at : at + short]
+
+
+def finish_pair(mine, got, tall, short):
+    width = mine.shape[1]
+    outs = [
+        struct((tall, width), F32),
+        struct((short, (mine.shape[0] - tall) // short * width), F32),
+    ]
+    return pl.pallas_call(
+        finish_pair_kernel,
+        grid=(1,),
+        in_specs=[spec_of(mine), spec_of(got)],
+        out_specs=[spec_of(o) for o in outs],
+        out_shape=outs,
+        cost_estimate=pl.CostEstimate(flops=0, bytes_accessed=2 * MIB, transcendentals=0),
+        name="finish_pair",
+    )(mine, got)
+
+
+def by_bits(block, shards):
+    return block.reshape(2, 2, 2, 2, block.shape[0] // (shards // 2), block.shape[1])
 
 
 def after(value, *others):
@@ -841,36 +893,40 @@
         qkv_own, qkv_far, x_own, x_far, ok_row, out_weight, row(out_bias), g2, b2
     )
     flat = lambda a: a.reshape(-1, width)
-    slope, lo_own, lo_far, gy, dbg, keep1, send1 = mlp_up(
-        info, place, flat(sn), flat(att), cot_own, cot_far, up_weight, row(up_bias),
-        down_weight, row(down_bias), shards, packed,
+    tall = down_weight.shape[0] // shards
+    tiles = up_weight.shape[1] // width
+    lo_own, lo_far, gy, dbg, gs, upbg, keep1, send1 = mlp(
+        info, inv, place, flat(sn), flat(att), cot_own, cot_far, up_weight, row(up_bias),
+        down_weight, row(down_bias), shards if packed else 0,
     )
     shape4 = (2, pairs, half, width)
+
+    gy4, gs4 = gy.reshape(shape4), gs.reshape(shape4)
     if packed:
-        r1 = Reduction(keep1, send1, shards)
-        inv = after(inv, r1.step())
-    gs, upbg, keep2, send2 = mlp_back(inv, gy, slope, flat(sn), up_weight, down_weight, shards, packed)
+        got1 = exchange(send1, None, shards)
+    ga, branch, gm, v2 = second_back(gs4, gy4, att, out_weight, g2)
     if packed:
-        r1.hold(upbg)
-        r2 = Reduction(keep2, after(send2, r1.step()), shards)
-        inv = after(inv, r2.step())
-    ga, gm, dqa, fnt, v2, keep3, send3 = attend_back(
-        inv, gs.reshape(shape4), gy.reshape(shape4), att, mixed, fn_own, fn_far, qkv_own, qkv_far,
-        probs, out_weight, g2, shards, packed,
+        got1 = after(got1, v2)
+        eight = lambda t: t.reshape((2, 2, 2) + t.shape[1:])
+        r1 = Reduction([eight(keep1)[..., :SIDE], eight(got1)[..., :SIDE]], shards)
+        r2 = Reduction(
+            [eight(keep1)[..., SIDE:], eight(got1)[..., SIDE:]], shards, SIDE_STAGES
+        )
+        inv = after(inv, r1.step(), r2.step())
+    dqa, fnt, token, keep3, send3 = attend_back(
+        inv, branch, mixed, fn_own, fn_far, qkv_own, qkv_far, probs, gm, shards, packed
     )
     if packed:
-        r1.hold(v2)
-        sent = r1.step()
-        r2.hold(sent)
-        sent = r2.step()
-        r3 = Reduction(keep3, after(send3, sent), shards)
-        inv = after(inv, r3.step())
-    lo_back = swap_sides(after(lo_far, v2))
+        r1.incoming, r2.incoming, _ = tie(r1.incoming, r2.incoming, token)
+        inv = after(inv, r1.step(), r2.step())
+        got3 = exchange(send3, None, shards)
+    lo_back = swap_sides(after(lo_far, token))
     ig_own, ig_far, vec, keep4, send4 = last_back(
         inv, qkv_own, qkv_far, probs, gm, fnt, dqa, ga, x_own, x_far, qkv_weight, g1, v2, upbg,
         dbg, shards, packed,
     )
-    ig_back = swap_sides(ig_far)
+    if not packed:
+        ig_back = swap_sides(ig_far)
 
     def settle(own, back):
         own, back = own[:, :real], back[:, :real]
@@ -880,24 +936,40 @@
 
     early = 3 * EARLY * LANES
     if packed:
-        r1.hold(ig_own)
-        r2.hold(r1.step())
-        r3.hold(r2.step())
-        r4 = Reduction(keep4, after(send4, r3.step()), shards)
+        whole1 = got1
+        r1.incoming, r2.incoming, lo_back, got3, _ = tie(
+            r1.incoming, r2.incoming, lo_back, got3, ig_own
+        )
+        sent = r1.step(), r2.step()
+        r3 = Reduction([by_bits(keep3, shards), by_bits(after(got3, *sent), shards)], shards)
+        got4 = after(exchange(send4, None, shards), r3.step())
+        r4 = Reduction([by_bits(keep4, shards), by_bits(got4, shards)], shards)
+        layer_out = settle(lo_own, lo_back)
         sent = r4.step()
-        for r in (r2, r3, r4, r3, r4, r4):
+        r1.hold(sent, layer_out)
+        r2.hold(sent, layer_out)
+        r1.fold()
+        r2.fold()
+        mine1, sent = part_pairs(keep1, whole1, r1.came, r2.came, tall, rows)
+        got1 = exchange(sent, 3, shards)
+        ig_back = swap_sides(after(ig_far, sent))
+        for r in (r3, r4, r3, r4, r3):
             r.hold(sent)
             sent = r.step()
-        layer_out = settle(lo_own, lo_back)
-        down_g, up_g, mid, last = (r.result() for r in (r1, r2, r3, r4))
+        input_grad = settle(ig_own, after(ig_back, sent))
+        r4.hold(sent, input_grad)
+        got1 = after(got1, r4.step())
+        down_g, up_g = finish_pair(mine1, got1, tall, rows)
+        mid, last = r3.result(), r4.result()
         vecs = last[:8, -LANES:]
         last = last[:, :-LANES]
         ln1g, ln1b, outb, ln2g, ln2b, downb = (vecs[i, :rows] for i in range(6))
         qvg, upg = vecs[6, : 2 * rows], vecs[7, : 4 * rows]
     else:
         layer_out = settle(lo_own, lo_back)
+        input_grad = settle(ig_own, ig_back)
         total = lambda v: lax.psum_scatter(v, AXES, scatter_dimension=0, tiled=True)
-        down_g, up_g, mid, last = total(keep1), total(keep2), total(keep3), total(keep4)
+        down_g, up_g, mid, last = total(keep1), total(send1), total(keep3), total(keep4)
         ln1g, ln1b, outb, ln2g, ln2b, downb = (total(vec[i]) for i in (0, 1, 4, 5, 6, 7))
         qvg, upg = total(vec[2:4].reshape(-1)), total(vec[8:12].reshape(-1))
     out_g = mid[:, early:]
@@ -906,7 +978,6 @@
     for i in range(3):
         parts += [mid[:, i * ca : (i + 1) * ca], last[:, i * cb : (i + 1) * cb]]
     qkv_g = jnp.concatenate(parts, axis=1)
-    input_grad = settle(ig_own, ig_back)
     return (
         layer_out, input_grad, ln1g, ln1b, qkv_g, qvg, out_g, outb, ln2g, ln2b, up_g, upg,
         down_g, downb,

time: 189 us -> 170 us (0.90)
  waiting for transfers between devices: 40.8 us -> 30.5 us
  Pallas kernels: 82.8 us -> 75.7 us
  other arithmetic: 21.9 us -> 18.6 us
  local copies, waits for them, and re-layouts: 12.8 us -> 15.5 us
  starting transfers between devices: 29 us -> 27.1 us
    ppermute x20 -> x18, waiting for transfers between devices: 35.3 us -> 26 us  [exchange(): lax.ppermute(block, AXES, [(i, i ^ bit) for i, bit in enumerate(bits)])]
    pallas_call x1, Pallas kernels: 17.9 us -> 12.5 us  [attend_back(): pl.pallas_call(partial(attend_back_kernel, shard=width // shards if packe...]
    unnamed x103 -> x121, local copies, waits for them, and re-layouts: 7.99 us -> 10.6 us
    add x4 -> x2, other arithmetic: 3.88 us -> 1.9 us  [add_up(): total = total + t.astype(F32)]
    pallas_call x2 -> x4, Pallas kernels: 35.9 us -> 34 us  [the longest x1 25.9 us: mlp(): pl.pallas_call(partial(mlp_kernel, shards=shards), grid_spec=pltpu.Prefet...]
    convert_element_type x16 -> x14, other arithmetic: 17 us -> 15.7 us  [parts(): return add_up([p[1] for p in pieces]).astype(BF16)]
    ppermute x20 -> x18, starting transfers between devices: 22.2 us -> 21.2 us  [exchange(): lax.ppermute(block, AXES, [(i, i ^ bit) for i, bit in enumerate(bits)])]
  transfers between devices with their start and end apart: 25 -> 23, of which waited for: 15 -> 9; matrix products, arithmetic and copies ran while one was open for 8% -> 13% of each run, Pallas kernels for 34% -> 29%
where the time goes in v3:
time: 170 us; the launch traced here: 169 us
  Pallas kernels  75.7 us (45%)
  waiting for transfers between devices  30.5 us (18%)
  starting transfers between devices  27.1 us (16%)
  other arithmetic  18.6 us (11%)
  local copies, waits for them, and re-layouts  15.5 us (9%)
    ppermute x18, waiting for transfers between devices, exchange(): lax.ppermute(block, AXES, [(i, i ^ bit) for i, bit in enumerate(bits)])  26 us
    pallas_call x1, Pallas kernels, mlp(): pl.pallas_call(partial(mlp_kernel, shards=shards), grid_spec=pltpu.Prefet...  25.9 us
    ppermute x18, starting transfers between devices, exchange(): lax.ppermute(block, AXES, [(i, i ^ bit) for i, bit in enumerate(bits)])  21.2 us
    convert_element_type x14, other arithmetic, parts(): return add_up([p[1] for p in pieces]).astype(BF16)  15.7 us
    pallas_call x1, Pallas kernels, attend_back(): pl.pallas_call(partial(attend_back_kernel, shard=width // shards if packe...  12.5 us
    pallas_call x1, Pallas kernels, attend(): pl.pallas_call(attend_kernel, grid=(pairs,), in_specs=[pl.BlockSpec((1, h...  12.3 us
    unnamed x121, local copies, waits for them, and re-layouts  10.6 us
    pallas_call x1, Pallas kernels, last_back(): pl.pallas_call(partial(last_back_kernel, shard=width // shards if packed...  10.5 us
  transfers between devices with their start and end apart: 23, of which 9 were waited for; matrix products, arithmetic and copies ran while one was open for 13% of the time, Pallas kernels for 29%

profile of v3, /device:TPU:0, one launch (start us, length us, event | category | flops | bytes accessed | tf_op | source)
XLA Modules:
  0.0 168.9 jit_solution(12228954294325511559)
XLA Ops:
  0.7 2.2 %fusion.3 = (bf16[2,140,768]{2,0,1:T(2,128)(2,1)S(1)}, bf16[2,140,768]{2,0,1:T(2,128)(2,1)S(1)}) fusion(bf16[4,140,768]{2,0,1:T(4,128)(2,1)} %param.20), kind=kLoop, calls=%fused_computation.52 | loop fusion | bytes 1720320 | tf_op jit(solution)/shard_map/slice | solution.py:862
  3.1 3.0 %collective-permute-start = (bf16[2,140,768]{2,1,0:T(8,128)(2,1)S(1)}, bf16[2,140,768]{2,1,0:T(8,128)(2,1)S(1)}, u32[]{:S(2)}, u32[]{:S(2)}) collective-permute-start(bf16[2,140,768]{2,1,0:T(8,128)(2,1)S(1)} %copy_select_fusion), channel_id=1, source_target_pairs={{0,1},{1,0},{2,3},{3,2},{4,5},{5,4},{6,7},{7,6},{8,9},{9,8},{10,11... | collective-permute-start | bytes 1290248 | tf_op jit(solution)/shard_map/ppermute | solution.py:846
  7.3 1.2 copy-done
  8.5 3.1 %norm_qkv.2 = (bf16[2,144,768]{2,1,0:T(8,128)(2,1)}, bf16[2,144,2304]{2,1,0:T(8,128)(2,1)}) custom-call(bf16[2,144,768]{2,1,0:T(8,128)(2,1)S(1)} %pad.13.x_ref.xo, f32[1,768]{1,0:T(1,128)S(1)} %reshape.202.g_ref.g1, f32[1,768]{1,0:T(1,128)S(1)} %reshape.203.b_ref, bf16[768,2304]{1,0:T(8,128)(2,1)S(1)} %copy-done, f32[2,1,768]{2,1,0:T(1,128)S(1)} %reshape.204.qvb_ref), custom_call_target="tpu_custom_call" | custom-call | flops 1019215872 | bytes 5750784 | tf_op jit(solution)/shard_map/norm_qkv/pallas_call | solution.py:131
  11.8 4.5 %collective-permute-done = bf16[2,140,768]{2,1,0:T(8,128)(2,1)S(1)} collective-permute-done((bf16[2,140,768]{2,1,0:T(8,128)(2,1)S(1)}, bf16[2,140,768]{2,1,0:T(8,128)(2,1)S(1)}, u32[]{:S(2)}, u32[]{:S(2)}) %collective-permute-start) | collective-permute-done | bytes 430112 | tf_op jit(solution)/shard_map/ppermute | solution.py:846
  16.3 1.7 %collective-permute-start.2 = (bf16[2,140,768]{2,1,0:T(8,128)(2,1)S(1)}, bf16[2,140,768]{2,1,0:T(8,128)(2,1)S(1)}, u32[]{:S(2)}, u32[]{:S(2)}) collective-permute-start(bf16[2,140,768]{2,1,0:T(8,128)(2,1)S(1)} %get-tuple-element.84), channel_id=1, source_target_pairs={{0,1},{1,0},{2,3},{3,2},{4,5},{5,4},{6,7},{7,6},{8,9},{9,8},{10,11... | collective-permute-start | bytes 1290248 | tf_op jit(solution)/shard_map/ppermute | solution.py:846
  18.4 3.2 %norm_qkv.3 = (bf16[2,144,768]{2,1,0:T(8,128)(2,1)}, bf16[2,144,2304]{2,1,0:T(8,128)(2,1)}) custom-call(bf16[2,144,768]{2,1,0:T(8,128)(2,1)S(1)} %pad.14.x_ref.xr, f32[1,768]{1,0:T(1,128)S(1)} %reshape.202.g_ref.g1, f32[1,768]{1,0:T(1,128)S(1)} %reshape.203.b_ref, bf16[768,2304]{1,0:T(8,128)(2,1)S(1)} %copy-done, f32[2,1,768]{2,1,0:T(1,128)S(1)} %reshape.204.qvb_ref), custom_call_target="tpu_custom_call" | custom-call | flops 1019215872 | bytes 5750784 | tf_op jit(solution)/shard_map/norm_qkv/pallas_call | solution.py:131
  21.6 1.3 copy-done.5
  22.9 12.3 %attend.1 = (bf16[2,2,144,768]{3,2,1,0:T(8,128)(2,1)}, f32[2,2,144,768]{3,2,1,0:T(8,128)}, bf16[2,2,144,768]{3,2,1,0:T(8,128)(2,1)S(1)}, bf16[2,6,576,288]{3,2,1,0:T(8,128)(2,1)}) custom-call(bf16[2,144,2304]{2,1,0:T(8,128)(2,1)S(1)} %copy-done.3, bf16[2,144,2304]{2,1,0:T(8,128)(2,1)S(1)} %copy-done.5, bf16[2,144,768]{2,1,0:T(8,128)(2,1)S(1)} %pad.13.x_ref.xo, ...), custom_call_target="tpu_custom_call" | custom-call | flops 2038431744 | bytes 11059200 | tf_op jit(solution)/shard_map/attend/pallas_call | solution.py:203
  35.3 1.6 copy-done.2
  36.9 25.9 %mlp.1 = (bf16[2,144,768]{2,1,0:T(8,128)(2,1)}, bf16[2,144,768]{2,1,0:T(8,128)(2,1)}, bf16[576,768]{1,0:T(8,128)(2,1)S(1)}, f32[1,768]{1,0:T(1,128)}, f32[576,76...) custom-call(s32[3]{0:T(128)S(1)} %pad_add_fusion.info, ...), custom_call_target="tpu_custom_call" | custom-call | flops 16307453952 | bytes 25165824 | tf_op jit(solution)/shard_map/mlp/pallas_call | solution.py:343
  63.0 3.1 %second_back.1 = (f32[2,288,768]{2,1,0:T(8,128)}, bf16[2,288,768]{2,1,0:T(8,128)(2,1)S(1)}, bf16[2,288,768]{2,1,0:T(8,128)(2,1)S(1)}, f32[8,768]{1,0:T(8,128)}) custom-call(f32[2,2,144,768]{3,2,1,0:T(8,128)S(1)} %bitcast.47, bf16[2,2,144,768]{3,2,1,0:T(8,128)(2,1)S(1)} %bitcast.48, f32[2,2,144,768]{3,2,1,0:T(8,128)S(1)} %copy-done.2, ...), custom_call_target="tpu_custom_call" | custom-call | flops 679477248 | bytes 10485760 | tf_op jit(solution)/shard_map/second_back/pallas_call | solution.py:460
  66.1 5.0 %collective-permute-done.3.got = bf16[8,384,768]{2,1,0:T(8,128)(2,1)S(1)} collective-permute-done((bf16[8,384,768]{2,1,0:T(8,128)(2,1)}, bf16[8,384,768]{2,1,0:T(8,128)(2,1)S(1)}, u32[]{:S(2)}, u32[]{:S(2)}) %collective-permute-start.3) | collective-permute-done | bytes 4718624 | tf_op jit(solution)/shard_map/ppermute | solution.py:736
  71.5 1.6 collective-permute-start.4
  74.6 12.5 %attend_back.1 = (bf16[576,1536]{1,0:T(8,128)(2,1)S(1)}, bf16[768,576]{1,0:T(8,128)(2,1)S(1)}, f32[8,128]{1,0:T(8,128)}, bf16[384,2304]{1,0:T(8,128)(2,1)}, bf16[384,2304]{1,0:T(8,128)(2,1)}) custom-call(s32[32]{0:T(128)S(1)} %get-tuple-element.104.inv, bf16[2,288,768]{2,1,0:T(8,128)(2,1)S(1)} %get-tuple-element.93.br, ...), custom_call_target="tpu_custom_call" | custom-call | flops 4756340736 | bytes 16777216 | tf_op jit(solution)/shard_map/attend_back/pallas_call | solution.py:527
  87.3 5.9 %collective-permute-done.5.q1 = bf16[2,2,1,384,256]{4,3,2,1,0:T(8,128)(2,1)S(1)} collective-permute-done((bf16[2,2,1,384,256]{4,3,2,1,0:T(8,128)(2,1)S(1)}, bf16[2,2,1,384,256]{4,3,2,1,0:T(8,128)(2,1)S(1)}, u32[]{:S(2)}, u32[]{:S(2)}) %collective-permute-start.5) | collective-permute-done | bytes 786464 | tf_op jit(solution)/shard_map/ppermute | solution.py:736
  93.3 2.5 %add_convert_fusion.2 = bf16[1,1,2,384,512]{4,3,2,1,0:T(8,128)(2,1)S(1)} fusion(bf16[2,2,2,384,768]{4,3,2,1,0:T(8,128)(2,1)} %bitcast.59, bf16[2,2,2,384,768]{4,3,2,1,0:T(8,128)(2,1)} %bitcast.51, bf16[1,2,2,384,512]{4,3,2,1,0:T(8,128)(2,1)S(1)} %collective-permute-done.4.p1), kind=kLoop, calls=%fused_computation.2 | loop fusion | flops 2359296 | bytes 3145728 | tf_op jit(solution)/shard_map/convert_element_type | solution.py:765
  95.8 1.6 collective-permute-start.6
  98.0 1.3 add_convert_fusion.6
  99.3 1.6 collective-permute-start.7
  100.9 10.5 %last_back.1 = (bf16[2,144,768]{2,1,0:T(8,128)(2,1)}, bf16[2,144,768]{2,1,0:T(8,128)(2,1)}, f32[16,768]{1,0:T(8,128)}, bf16[384,896]{1,0:T(8,128)(2,1)}, bf16[384,896]{1,0:T(8,128)(2,1)}) custom-call(s32[32]{0:T(128)S(1)} %get-tuple-element.104.inv, bf16[2,144,2304]{2,1,0:T(8,128)(2,1)S(1)} %copy-done.4, bf16[2,144,2304]{2,1,0:T(8,128)(2,1)S(1)} %copy-done.6, ...), custom_call_target="tpu_custom_call" | custom-call | flops 4076863488 | bytes 16777216 | tf_op jit(solution)/shard_map/last_back/pallas_call | solution.py:656
  112.1 1.4 add_convert_fusion.9
  113.6 1.3 add_convert_fusion.5
  114.9 1.1 add_convert_fusion.1
  116.1 1.5 collective-permute-start.14
  118.2 1.6 collective-permute-start.12
  119.8 0.9 add_convert_fusion.7
  121.5 4.5 %collective-permute-done.12.q3 = bf16[1,1,1,384,256]{4,3,2,1,0:T(8,128)(2,1)S(1)} collective-permute-done((bf16[1,1,1,384,256]{4,3,2,1,0:T(8,128)(2,1)S(1)}, bf16[1,1,1,384,256]{4,3,2,1,0:T(8,128)(2,1)S(1)}, u32[]{:S(2)}, u32[]{:S(2)}) %collective-permute-start.12) | collective-permute-done | bytes 196640 | tf_op jit(solution)/shard_map/ppermute | solution.py:736
  127.4 3.0 %part_pairs.1 = (f32[192,768]{1,0:T(8,128)}, bf16[192,768]{1,0:T(8,128)(2,1)}) custom-call(bf16[8,384,768]{2,1,0:T(8,128)(2,1)} %get-tuple-element.86.keep, bf16[8,384,768]{2,1,0:T(8,128)(2,1)} %copy-done.18, bf16[1,2,2,384,512]{4,3,2,1,0:T(8,128)(2,1)} %copy-done.19, bf16[1,1,2,384,512]{4,3,2,1,0:T(8,128)(2,1)} %copy-done.22, ...), custom_call_target="tpu_custom_call" | custom-call | bytes 4194304 | tf_op jit(solution)/shard_map/part_pairs/pallas_call | solution.py:800
  130.4 1.0 collective-permute-done.14
  132.4 1.5 collective-permute-start.15
  134.0 2.7 %collective-permute-start.22 = (bf16[192,768]{1,0:T(8,128)(2,1)S(1)}, bf16[192,768]{1,0:T(8,128)(2,1)}, u32[]{:S(2)}, u32[]{:S(2)}) collective-permute-start(bf16[192,768]{1,0:T(8,128)(2,1)S(1)} %copy-done.54), channel_id=1, source_target_pairs={{0,16},{1,17},{2,18},{3,19},{4,20},{5,21},{6,22},{7,23},{8,24},{9,... | collective-permute-start | bytes 884744 | tf_op jit(solution)/shard_map/ppermute | solution.py:736
  137.2 1.0 add_convert_fusion.10
  138.2 1.6 collective-permute-start.18
  139.8 6.1 %collective-permute-done.15 = bf16[1,1,2,2,24,2304]{5,4,3,2,1,0:T(8,128)(2,1)S(1)} collective-permute-done((bf16[1,1,2,2,24,2304]{5,4,3,2,1,0:T(8,128)(2,1)S(1)}, bf16[1,1,2,2,24,2304]{5,4,3,2,1,0:T(8,128)(2,1)S(1)}, u32[]{:S(2)}, u32[]{:S(2)}) %collective-permute-start.15) | collective-permute-done | bytes 442400 | tf_op jit(solution)/shard_map/ppermute | solution.py:736
  145.8 1.2 add_convert_fusion.8
  147.1 1.5 collective-permute-start.17
  148.5 0.9 add_convert_fusion.12
  149.4 1.3 collective-permute-start.19
  150.8 2.3 %collective-permute-done.17 = bf16[1,1,1,2,24,2304]{5,4,3,2,1,0:T(8,128)(2,1)S(1)} collective-permute-done((bf16[1,1,1,2,24,2304]{5,4,3,2,1,0:T(8,128)(2,1)S(1)}, bf16[1,1,1,2,24,2304]{5,4,3,2,1,0:T(8,128)(2,1)S(1)}, u32[]{:S(2)}, u32[]{:S(2)}) %collective-permute-start.17) | collective-permute-done | bytes 221216 | tf_op jit(solution)/shard_map/ppermute | solution.py:736
  153.1 1.7 fusion
  154.9 1.5 fusion.1
  156.4 1.2 collective-permute-start.20
  157.6 1.3 copy.58
  158.9 1.8 %collective-permute-start.21 = (bf16[24,2304]{1,0:T(8,128)(2,1)}, bf16[24,2304]{1,0:T(8,128)(2,1)S(1)}, u32[]{:S(2)}, u32[]{:S(2)}) collective-permute-start(bf16[24,2304]{1,0:T(8,128)(2,1)} %fusion), channel_id=1, source_target_pairs={{0,16},{1,17},{2,18},{3,19},{4,20},{5,21},{6,22},{7,23},{8,24},{9,... | collective-permute-start | bytes 331784 | tf_op jit(solution)/shard_map/ppermute | solution.py:736
  160.7 1.3 copy.59
  162.0 2.0 %finish_pair.1 = (f32[96,768]{1,0:T(8,128)}, f32[24,3072]{1,0:T(8,128)}) custom-call(f32[192,768]{1,0:T(8,128)} %get-tuple-element.132.mine, bf16[192,768]{1,0:T(8,128)(2,1)} %collective-permute-done.22.got), custom_call_target="tpu_custom_call" | custom-call | bytes 2097152 | tf_op jit(solution)/shard_map/finish_pair/pallas_call | solution.py:826
  166.4 1.0 bitcast_add_fusion
  (185 shorter events, 13.3 us)
Async XLA Ops:
  0.6 5.7 %copy-start.20 = (bf16[4,140,768]{2,0,1:T(4,128)(2,1)S(1)}, bf16[4,140,768]{2,0,1:T(4,128)(2,1)}, u32[]{:S(2)}) copy-start(bf16[4,140,768]{2,0,1:T(4,128)(2,1)} %param.20) | copy-start | bytes 2580484
  0.7 5.6 %copy-start.39 = (f32[1536]{0:T(1024)S(1)}, f32[1536]{0:T(1024)}, u32[]{:S(2)}) copy-start(f32[1536]{0:T(1024)} %param.26) | copy-start | bytes 18436
  3.1 13.2 %collective-permute-start = (bf16[2,140,768]{2,1,0:T(8,128)(2,1)S(1)}, bf16[2,140,768]{2,1,0:T(8,128)(2,1)S(1)}, u32[]{:S(2)}, u32[]{:S(2)}) collective-permute-start(bf16[2,140,768]{2,1,0:T(8,128)(2,1)S(1)} %copy_select_fusion), channel_id=1, source_target_pairs={{0,1},{1,0},{2,3},{3,2},{4,5},{5,4},{6,7},{7,6},{8,9},{9,8},{10,11... | collective-permute-start | bytes 1290248 | tf_op jit(solution)/shard_map/ppermute | solution.py:846
  6.2 12.0 %collective-permute-start.1 = (bf16[2,140]{1,0:T(2,128)(2,1)S(1)}, bf16[2,140]{1,0:T(2,128)(2,1)S(1)}, u32[]{:S(2)}, u32[]{:S(2)}) collective-permute-start(bf16[2,140]{1,0:T(2,128)(2,1)S(1)} %get-tuple-element.81), channel_id=1, source_target_pairs={{0,1},{1,0},{2,3},{3,2},{4,5},{5,4},{6,7},{7,6},{8,9},{9,8},{10,11... | collective-permute-start | bytes 1688 | tf_op jit(solution)/shard_map/ppermute | solution.py:846
  11.7 6.4 %copy-start.42 = (f32[768]{0:T(1024)S(1)}, f32[768]{0:T(1024)}, u32[]{:S(2)}) copy-start(f32[768]{0:T(1024)} %param.29) | copy-start | bytes 9220
  11.7 6.4 %copy-start.43 = (f32[768]{0:T(1024)S(1)}, f32[768]{0:T(1024)}, u32[]{:S(2)}) copy-start(f32[768]{0:T(1024)} %param.28) | copy-start | bytes 9220
  11.7 6.5 %copy-start.44 = (f32[768]{0:T(1024)S(1)}, f32[768]{0:T(1024)}, u32[]{:S(2)}) copy-start(f32[768]{0:T(1024)} %param.30) | copy-start | bytes 9220
  11.7 6.5 %copy-start.45 = (f32[768]{0:T(1024)S(1)}, f32[768]{0:T(1024)}, u32[]{:S(2)}) copy-start(f32[768]{0:T(1024)} %param.34) | copy-start | bytes 9220
  11.7 23.5 %copy-start.12 = (bf16[3072,768]{1,0:T(8,128)(2,1)S(1)}, bf16[3072,768]{1,0:T(8,128)(2,1)}, u32[]{:S(2)}) copy-start(bf16[3072,768]{1,0:T(8,128)(2,1)} %down.1) | copy-start | bytes 14155780
  16.3 19.0 %collective-permute-start.2 = (bf16[2,140,768]{2,1,0:T(8,128)(2,1)S(1)}, bf16[2,140,768]{2,1,0:T(8,128)(2,1)S(1)}, u32[]{:S(2)}, u32[]{:S(2)}) collective-permute-start(bf16[2,140,768]{2,1,0:T(8,128)(2,1)S(1)} %get-tuple-element.84), channel_id=1, source_target_pairs={{0,1},{1,0},{2,3},{3,2},{4,5},{5,4},{6,7},{7,6},{8,9},{9,8},{10,11... | collective-permute-start | bytes 1290248 | tf_op jit(solution)/shard_map/ppermute | solution.py:846
  22.9 12.4 %copy-start.11 = (bf16[768,3072]{1,0:T(8,128)(2,1)S(1)}, bf16[768,3072]{1,0:T(8,128)(2,1)}, u32[]{:S(2)}) copy-start(bf16[768,3072]{1,0:T(8,128)(2,1)} %up.1) | copy-start | bytes 14155780
  22.9 12.4 %copy-start.15 = (f32[3072]{0:T(1024)S(1)}, f32[3072]{0:T(1024)}, u32[]{:S(2)}) copy-start(f32[3072]{0:T(1024)} %param.32) | copy-start | bytes 36868
  35.2 38.8 %slice-start = ((s8[5308416]{0:T(1024)(128)(4,1)}), s8[4194304]{0:T(1024)(128)(4,1)S(1)}, s32[]{:S(2)}) async-start(s8[5308416]{0:T(1024)(128)(4,1)} %bitcast.44), calls=%async_computation | async-start | bytes 8388608
  36.9 37.1 %slice-start.1 = ((s8[5308416]{0:T(1024)(128)(4,1)}), s8[1114112]{0:T(1024)(128)(4,1)S(1)}, s32[]{:S(2)}) async-start(s8[5308416]{0:T(1024)(128)(4,1)} %bitcast.44), calls=%async_computation.1 | async-start | bytes 2228224
  62.9 8.2 %collective-permute-start.3 = (bf16[8,384,768]{2,1,0:T(8,128)(2,1)}, bf16[8,384,768]{2,1,0:T(8,128)(2,1)S(1)}, u32[]{:S(2)}, u32[]{:S(2)}) collective-permute-start(bf16[8,384,768]{2,1,0:T(8,128)(2,1)} %get-tuple-element.87), channel_id=1, source_target_pairs={{0,2},{1,3},{2,0},{3,1},{4,6},{5,7},{6,4},{7,5},{8,10},{9,11},{10,... | collective-permute-start | bytes 14155784 | tf_op jit(solution)/shard_map/ppermute | solution.py:736
  62.9 8.1 %copy-start.17 = (bf16[8,384,768]{2,1,0:T(8,128)(2,1)S(1)}, bf16[8,384,768]{2,1,0:T(8,128)(2,1)}, u32[]{:S(2)}) copy-start(bf16[8,384,768]{2,1,0:T(8,128)(2,1)} %get-tuple-element.86.keep) | copy-start | bytes 14155780
  71.5 21.8 %collective-permute-start.4 = (bf16[1,2,2,384,512]{4,3,2,1,0:T(8,128)(2,1)S(1)}, bf16[1,2,2,384,512]{4,3,2,1,0:T(8,128)(2,1)S(1)}, u32[]{:S(2)}, u32[]{:S(2)}) collective-permute-start(bf16[1,2,2,384,512]{4,3,2,1,0:T(8,128)(2,1)S(1)} %add_convert_fusion), channel_id=1, source_target_pairs={{0,4},{1,5},{2,10},{3,11},{4,0},{5,1},{6,14},{7,15},{8,12},{9,13},... | collective-permute-start | bytes 4718600 | tf_op jit(solution)/shard_map/ppermute | solution.py:736
  73.6 19.6 %collective-permute-start.5 = (bf16[2,2,1,384,256]{4,3,2,1,0:T(8,128)(2,1)S(1)}, bf16[2,2,1,384,256]{4,3,2,1,0:T(8,128)(2,1)S(1)}, u32[]{:S(2)}, u32[]{:S(2)}) collective-permute-start(bf16[2,2,1,384,256]{4,3,2,1,0:T(8,128)(2,1)S(1)} %add_convert_fusion.3), channel_id=1, source_target_pairs={{0,1},{1,0},{2,3},{3,2},{4,5},{5,4},{6,7},{7,6},{8,9},{9,8},{10,11... | collective-permute-start | bytes 2359304 | tf_op jit(solution)/shard_map/ppermute | solution.py:736
  87.1 10.4 %copy-start.53 = (bf16[2,144,768]{2,1,0:T(8,128)(2,1)S(1)}, bf16[2,144,768]{2,1,0:T(8,128)(2,1)}, u32[]{:S(2)}) copy-start(bf16[2,144,768]{2,1,0:T(8,128)(2,1)} %get-tuple-element.102) | copy-start | bytes 1327108
  87.1 13.8 %copy-start.1 = (f32[2,288,768]{2,1,0:T(8,128)S(1)}, f32[2,288,768]{2,1,0:T(8,128)}, u32[]{:S(2)}) copy-start(f32[2,288,768]{2,1,0:T(8,128)} %get-tuple-element.107.ga) | copy-start | bytes 5308420
  87.1 13.8 %copy-start.4 = (bf16[2,144,2304]{2,1,0:T(8,128)(2,1)S(1)}, bf16[2,144,2304]{2,1,0:T(8,128)(2,1)}, u32[]{:S(2)}) copy-start(bf16[2,144,2304]{2,1,0:T(8,128)(2,1)} %get-tuple-element.76.qo) | copy-start | bytes 3981316
  87.1 13.8 %copy-start.8 = (f32[8,768]{1,0:T(8,128)S(1)}, f32[8,768]{1,0:T(8,128)}, u32[]{:S(2)}) copy-start(f32[8,768]{1,0:T(8,128)} %get-tuple-element.90.v2) | copy-start | bytes 73732
  87.1 13.8 %copy-start.9 = (f32[1,3072]{1,0:T(1,128)S(1)}, f32[1,3072]{1,0:T(1,128)}, u32[]{:S(2)}) copy-start(f32[1,3072]{1,0:T(1,128)} %get-tuple-element.108.upbg) | copy-start | bytes 36868
  87.1 13.8 %copy-start.10 = (f32[1,768]{1,0:T(1,128)S(1)}, f32[1,768]{1,0:T(1,128)}, u32[]{:S(2)}) copy-start(f32[1,768]{1,0:T(1,128)} %get-tuple-element.109.dbg) | copy-start | bytes 9220
  87.1 24.4 %collective-permute-start.9 = (bf16[384,2304]{1,0:T(8,128)(2,1)}, bf16[384,2304]{1,0:T(8,128)(2,1)S(1)}, u32[]{:S(2)}, u32[]{:S(2)}) collective-permute-start(bf16[384,2304]{1,0:T(8,128)(2,1)} %get-tuple-element.103), channel_id=1, source_target_pairs={{0,2},{1,3},{2,0},{3,1},{4,6},{5,7},{6,4},{7,5},{8,10},{9,11},{10,... | collective-permute-start | bytes 5308424 | tf_op jit(solution)/shard_map/ppermute | solution.py:736
  93.3 18.8 %copy-start.21 = (bf16[2,2,1,384,256]{4,3,2,1,0:T(8,128)(2,1)}, bf16[2,2,1,384,256]{4,3,2,1,0:T(8,128)(2,1)S(1)}, u32[]{:S(2)}) copy-start(bf16[2,2,1,384,256]{4,3,2,1,0:T(8,128)(2,1)S(1)} %collective-permute-done.5.q1) | copy-start | bytes 2359300
  93.3 20.3 %copy-start.19 = (bf16[1,2,2,384,512]{4,3,2,1,0:T(8,128)(2,1)}, bf16[1,2,2,384,512]{4,3,2,1,0:T(8,128)(2,1)S(1)}, u32[]{:S(2)}) copy-start(bf16[1,2,2,384,512]{4,3,2,1,0:T(8,128)(2,1)S(1)} %collective-permute-done.4.p1) | copy-start | bytes 4718596
  95.8 16.3 %collective-permute-start.6 = (bf16[1,1,2,384,512]{4,3,2,1,0:T(8,128)(2,1)S(1)}, bf16[1,1,2,384,512]{4,3,2,1,0:T(8,128)(2,1)S(1)}, u32[]{:S(2)}, u32[]{:S(2)}) collective-permute-start(bf16[1,1,2,384,512]{4,3,2,1,0:T(8,128)(2,1)S(1)} %add_convert_fusion.2), channel_id=1, source_target_pairs={{0,8},{1,9},{2,6},{3,7},{4,12},{5,13},{6,2},{7,3},{8,0},{9,1},{10,... | collective-permute-start | bytes 2359304 | tf_op jit(solution)/shard_map/ppermute | solution.py:736
  97.5 14.1 %collective-permute-start.8 = (bf16[2,144,768]{2,1,0:T(8,128)(2,1)S(1)}, bf16[2,144,768]{2,1,0:T(8,128)(2,1)S(1)}, u32[]{:S(2)}, u32[]{:S(2)}) collective-permute-start(bf16[2,144,768]{2,1,0:T(8,128)(2,1)S(1)} %copy-done.53), channel_id=1, source_target_pairs={{0,1},{1,0},{2,3},{3,2},{4,5},{5,4},{6,7},{7,6},{8,9},{9,8},{10,11... | collective-permute-start | bytes 1327112 | tf_op jit(solution)/shard_map/ppermute | solution.py:846
  99.3 12.3 %collective-permute-start.7 = (bf16[1,2,1,384,256]{4,3,2,1,0:T(8,128)(2,1)S(1)}, bf16[1,2,1,384,256]{4,3,2,1,0:T(8,128)(2,1)S(1)}, u32[]{:S(2)}, u32[]{:S(2)}) collective-permute-start(bf16[1,2,1,384,256]{4,3,2,1,0:T(8,128)(2,1)S(1)} %add_convert_fusion.6), channel_id=1, source_target_pairs={{0,4},{1,5},{2,10},{3,11},{4,0},{5,1},{6,14},{7,15},{8,12},{9,13},... | collective-permute-start | bytes 1179656 | tf_op jit(solution)/shard_map/ppermute | solution.py:736
  111.5 8.3 %collective-permute-start.11 = (bf16[384,896]{1,0:T(8,128)(2,1)}, bf16[384,896]{1,0:T(8,128)(2,1)S(1)}, u32[]{:S(2)}, u32[]{:S(2)}) collective-permute-start(bf16[384,896]{1,0:T(8,128)(2,1)} %get-tuple-element.115), channel_id=1, source_target_pairs={{0,2},{1,3},{2,0},{3,1},{4,6},{5,7},{6,4},{7,5},{8,10},{9,11},{10,... | collective-permute-start | bytes 2064392 | tf_op jit(solution)/shard_map/ppermute | solution.py:736
  116.1 15.4 %collective-permute-start.14 = (bf16[1,2,2,2,24,2304]{5,4,3,2,1,0:T(8,128)(2,1)}, bf16[1,2,2,2,24,2304]{5,4,3,2,1,0:T(8,128)(2,1)S(1)}, u32[]{:S(2)}, u32[]{:S(2)}) collective-permute-start(bf16[1,2,2,2,24,2304]{5,4,3,2,1,0:T(8,128)(2,1)} %bitcast.9), channel_id=1, source_target_pairs={{0,4},{1,5},{2,10},{3,11},{4,0},{5,1},{6,14},{7,15},{8,12},{9,13},... | collective-permute-start | bytes 2654216 | tf_op jit(solution)/shard_map/ppermute | solution.py:736
  117.5 9.9 %collective-permute-start.10 = (bf16[1,1,1,384,512]{4,3,2,1,0:T(8,128)(2,1)S(1)}, bf16[1,1,1,384,512]{4,3,2,1,0:T(8,128)(2,1)}, u32[]{:S(2)}, u32[]{:S(2)}) collective-permute-start(bf16[1,1,1,384,512]{4,3,2,1,0:T(8,128)(2,1)S(1)} %add_convert_fusion.5), channel_id=1, source_target_pairs={{0,1},{1,0},{2,3},{3,2},{4,5},{5,4},{6,7},{7,6},{8,9},{9,8},{10,11... | collective-permute-start | bytes 1179656 | tf_op jit(solution)/shard_map/ppermute | solution.py:736
  118.2 7.9 %collective-permute-start.12 = (bf16[1,1,1,384,256]{4,3,2,1,0:T(8,128)(2,1)S(1)}, bf16[1,1,1,384,256]{4,3,2,1,0:T(8,128)(2,1)S(1)}, u32[]{:S(2)}, u32[]{:S(2)}) collective-permute-start(bf16[1,1,1,384,256]{4,3,2,1,0:T(8,128)(2,1)S(1)} %add_convert_fusion.9), channel_id=1, source_target_pairs={{0,8},{1,9},{2,6},{3,7},{4,12},{5,13},{6,2},{7,3},{8,0},{9,1},{10,... | collective-permute-start | bytes 589832 | tf_op jit(solution)/shard_map/ppermute | solution.py:736
  120.8 16.4 %collective-permute-start.16 = (bf16[1,2,2,2,24,896]{5,4,3,2,1,0:T(8,128)(2,1)}, bf16[1,2,2,2,24,896]{5,4,3,2,1,0:T(8,128)(2,1)}, u32[]{:S(2)}, u32[]{:S(2)}) collective-permute-start(bf16[1,2,2,2,24,896]{5,4,3,2,1,0:T(8,128)(2,1)} %bitcast.10), channel_id=1, source_target_pairs={{0,4},{1,5},{2,10},{3,11},{4,0},{5,1},{6,14},{7,15},{8,12},{9,13},... | collective-permute-start | bytes 1032200 | tf_op jit(solution)/shard_map/ppermute | solution.py:736
  130.4 6.3 %copy-start.52 = (bf16[2,144,768]{2,1,0:T(8,128)(2,1)S(1)}, bf16[2,144,768]{2,1,0:T(8,128)(2,1)}, u32[]{:S(2)}) copy-start(bf16[2,144,768]{2,1,0:T(8,128)(2,1)} %get-tuple-element.124) | copy-start | bytes 1327108
  132.4 13.5 %collective-permute-start.15 = (bf16[1,1,2,2,24,2304]{5,4,3,2,1,0:T(8,128)(2,1)S(1)}, bf16[1,1,2,2,24,2304]{5,4,3,2,1,0:T(8,128)(2,1)S(1)}, u32[]{:S(2)}, u32[]{:S(2)}) collective-permute-start(bf16[1,1,2,2,24,2304]{5,4,3,2,1,0:T(8,128)(2,1)S(1)} %add_convert_fusion.4), channel_id=1, source_target_pairs={{0,8},{1,9},{2,6},{3,7},{4,12},{5,13},{6,2},{7,3},{8,0},{9,1},{10,... | collective-permute-start | bytes 1327112 | tf_op jit(solution)/shard_map/ppermute | solution.py:736
  133.9 20.8 %copy-start.31 = (bf16[2,144,768]{2,1,0:T(8,128)(2,1)S(1)}, bf16[2,144,768]{2,1,0:T(8,128)(2,1)}, u32[]{:S(2)}) copy-start(bf16[2,144,768]{2,1,0:T(8,128)(2,1)} %get-tuple-element.110) | copy-start | bytes 1327108
  134.0 28.0 %collective-permute-start.22 = (bf16[192,768]{1,0:T(8,128)(2,1)S(1)}, bf16[192,768]{1,0:T(8,128)(2,1)}, u32[]{:S(2)}, u32[]{:S(2)}) collective-permute-start(bf16[192,768]{1,0:T(8,128)(2,1)S(1)} %copy-done.54), channel_id=1, source_target_pairs={{0,16},{1,17},{2,18},{3,19},{4,20},{5,21},{6,22},{7,23},{8,24},{9,... | collective-permute-start | bytes 884744 | tf_op jit(solution)/shard_map/ppermute | solution.py:736
  136.7 18.1 %collective-permute-start.13 = (bf16[2,144,768]{2,1,0:T(8,128)(2,1)S(1)}, bf16[2,144,768]{2,1,0:T(8,128)(2,1)S(1)}, u32[]{:S(2)}, u32[]{:S(2)}) collective-permute-start(bf16[2,144,768]{2,1,0:T(8,128)(2,1)S(1)} %copy-done.52), channel_id=1, source_target_pairs={{0,1},{1,0},{2,3},{3,2},{4,5},{5,4},{6,7},{7,6},{8,9},{9,8},{10,11... | collective-permute-start | bytes 1327112 | tf_op jit(solution)/shard_map/ppermute | solution.py:846
  138.2 10.3 %collective-permute-start.18 = (bf16[1,1,2,2,24,896]{5,4,3,2,1,0:T(8,128)(2,1)S(1)}, bf16[1,1,2,2,24,896]{5,4,3,2,1,0:T(8,128)(2,1)S(1)}, u32[]{:S(2)}, u32[]{:S(2)}) collective-permute-start(bf16[1,1,2,2,24,896]{5,4,3,2,1,0:T(8,128)(2,1)S(1)} %add_convert_fusion.10), channel_id=1, source_target_pairs={{0,8},{1,9},{2,6},{3,7},{4,12},{5,13},{6,2},{7,3},{8,0},{9,1},{10,... | collective-permute-start | bytes 516104 | tf_op jit(solution)/shard_map/ppermute | solution.py:736
  145.8 8.9 %copy-start.33 = (bf16[1,1,2,2,24,2304]{5,4,3,2,1,0:T(8,128)(2,1)}, bf16[1,1,2,2,24,2304]{5,4,3,2,1,0:T(8,128)(2,1)S(1)}, u32[]{:S(2)}) copy-start(bf16[1,1,2,2,24,2304]{5,4,3,2,1,0:T(8,128)(2,1)S(1)} %collective-permute-done.15) | copy-start | bytes 1327108
  147.1 6.0 %collective-permute-start.17 = (bf16[1,1,1,2,24,2304]{5,4,3,2,1,0:T(8,128)(2,1)S(1)}, bf16[1,1,1,2,24,2304]{5,4,3,2,1,0:T(8,128)(2,1)S(1)}, u32[]{:S(2)}, u32[]{:S(2)}) collective-permute-start(bf16[1,1,1,2,24,2304]{5,4,3,2,1,0:T(8,128)(2,1)S(1)} %add_convert_fusion.8), channel_id=1, source_target_pairs={{0,1},{1,0},{2,3},{3,2},{4,5},{5,4},{6,7},{7,6},{8,9},{9,8},{10,11... | collective-permute-start | bytes 663560 | tf_op jit(solution)/shard_map/ppermute | solution.py:736
  149.4 5.5 %collective-permute-start.19 = (bf16[1,1,1,2,24,896]{5,4,3,2,1,0:T(8,128)(2,1)S(1)}, bf16[1,1,1,2,24,896]{5,4,3,2,1,0:T(8,128)(2,1)S(1)}, u32[]{:S(2)}, u32[]{:S(2)}) collective-permute-start(bf16[1,1,1,2,24,896]{5,4,3,2,1,0:T(8,128)(2,1)S(1)} %add_convert_fusion.12), channel_id=1, source_target_pairs={{0,1},{1,0},{2,3},{3,2},{4,5},{5,4},{6,7},{7,6},{8,9},{9,8},{10,11... | collective-permute-start | bytes 258056 | tf_op jit(solution)/shard_map/ppermute | solution.py:736
  154.9 7.1 %copy-start.37 = (bf16[1,1,1,2,24,896]{5,4,3,2,1,0:T(8,128)(2,1)}, bf16[1,1,1,2,24,896]{5,4,3,2,1,0:T(8,128)(2,1)S(1)}, u32[]{:S(2)}) copy-start(bf16[1,1,1,2,24,896]{5,4,3,2,1,0:T(8,128)(2,1)S(1)} %collective-permute-done.19) | copy-start | bytes 258052
  156.4 7.6 %collective-permute-start.20 = (bf16[24,896]{1,0:T(8,128)(2,1)}, bf16[24,896]{1,0:T(8,128)(2,1)}, u32[]{:S(2)}, u32[]{:S(2)}) collective-permute-start(bf16[24,896]{1,0:T(8,128)(2,1)} %fusion.1), channel_id=1, source_target_pairs={{0,16},{1,17},{2,18},{3,19},{4,20},{5,21},{6,22},{7,23},{8,24},{9,... | collective-permute-start | bytes 129032 | tf_op jit(solution)/shard_map/ppermute | solution.py:736
  158.9 7.5 %copy-start.35 = (bf16[1,1,1,2,24,2304]{5,4,3,2,1,0:T(8,128)(2,1)S(1)}, bf16[1,1,1,2,24,2304]{5,4,3,2,1,0:T(8,128)(2,1)}, u32[]{:S(2)}) copy-start(bf16[1,1,1,2,24,2304]{5,4,3,2,1,0:T(8,128)(2,1)} %copy-done.34) | copy-start | bytes 663556
  158.9 7.5 %collective-permute-start.21 = (bf16[24,2304]{1,0:T(8,128)(2,1)}, bf16[24,2304]{1,0:T(8,128)(2,1)S(1)}, u32[]{:S(2)}, u32[]{:S(2)}) collective-permute-start(bf16[24,2304]{1,0:T(8,128)(2,1)} %fusion), channel_id=1, source_target_pairs={{0,16},{1,17},{2,18},{3,19},{4,20},{5,21},{6,22},{7,23},{8,24},{9,... | collective-permute-start | bytes 331784 | tf_op jit(solution)/shard_map/ppermute | solution.py:736
  (32 other events, 90.3 us)

commit v4 on v3

--- a/solution.py
+++ b/solution.py
@@ -126,7 +126,7 @@
     qkv_ref[...] = out.astype(BF16).reshape(qkv_ref.shape)
 
 
-def norm_qkv(x, gain, shift, weight, qv_bias):
+def norm_qkv(x, gain, shift, weight, qv_bias, place=kept):
     pairs, half, width = x.shape
     return pl.pallas_call(
         norm_qkv_kernel,
@@ -139,7 +139,7 @@
             pl.BlockSpec((1, 1, width), lambda j: (j // 2, 0, 0)),
         ],
         out_specs=[spec_of(x), pl.BlockSpec((pairs, half, width), lambda j: (0, 0, j))],
-        out_shape=[kept((pairs, half, width), BF16), kept((pairs, half, 3 * width), BF16)],
+        out_shape=[kept((pairs, half, width), BF16), place((pairs, half, 3 * width), BF16)],
         compiler_params=params_of(24),
         cost_estimate=pl.CostEstimate(
             flops=6 * pairs * half * width * width,
@@ -184,7 +184,7 @@
         mix_s[:, lane_block(hp)] = dot_tn(prob, stacked(both(2 * tiles + hp))).astype(BF16)
         return carry
 
-    lax.fori_loop(0, tiles, two_heads, 0)
+    lax.fori_loop(0, tiles, two_heads, 0, unroll=2)
     mixed = mix_s[...]
     mixed_ref[...] = mixed.reshape(mixed_ref.shape)
     x = jnp.concatenate([xo[0], xr[0]], axis=0).astype(F32)
@@ -347,7 +347,7 @@
             grid=(ff // tile,),
             in_specs=[
                 spec_of(sn),
-                pl.BlockSpec(memory_space=pl.ANY),
+                pl.BlockSpec(memory_space=pltpu.HBM),
                 spec_of(cot_own),
                 spec_of(cot_far),
                 resident(),
@@ -421,7 +421,7 @@
             dqkv[pl.ds(base, rows), lane_block(part * count + i)] = d.astype(BF16)
         return carry
 
-    lax.fori_loop(0, count, two_heads, 0)
+    lax.fori_loop(0, count, two_heads, 0, unroll=2)
 
 
 def wire_out(left_t, right, keep, send, at):
@@ -888,7 +888,7 @@
     x_raw, cot_sent, _ = tie(x_raw, cot_sent, fn_own)
     x_far = padded(x_raw)
     cot_far = padded(swap_sides(cot_sent))
-    fn_far, qkv_far = norm_qkv(x_far, g1, b1, qkv_weight, qvb)
+    fn_far, qkv_far = norm_qkv(x_far, g1, b1, qkv_weight, qvb, struct)
     mixed, att, sn, probs = attend(
         qkv_own, qkv_far, x_own, x_far, ok_row, out_weight, row(out_bias), g2, b2
     )

time: 170 us -> 167 us (0.982)
  Pallas kernels: 75.7 us -> 73.5 us
    unnamed x121 -> x123, local copies, waits for them, and re-layouts: 10.6 us -> 9.27 us
where the time goes in v4:
time: 167 us; the launch traced here: 166 us
  Pallas kernels  73.5 us (44%)
  waiting for transfers between devices  30.9 us (19%)
  starting transfers between devices  27.4 us (16%)
  other arithmetic  18.5 us (11%)
  local copies, waits for them, and re-layouts  14.2 us (9%)
    ppermute x18, waiting for transfers between devices, exchange(): lax.ppermute(block, AXES, [(i, i ^ bit) for i, bit in enumerate(bits)])  26.4 us
    pallas_call x1, Pallas kernels, mlp(): pl.pallas_call(partial(mlp_kernel, shards=shards), grid_spec=pltpu.Prefet...  26 us
    ppermute x18, starting transfers between devices, exchange(): lax.ppermute(block, AXES, [(i, i ^ bit) for i, bit in enumerate(bits)])  21.5 us
    convert_element_type x14, other arithmetic, parts(): return add_up([p[1] for p in pieces]).astype(BF16)  15.6 us
    pallas_call x1, Pallas kernels, attend_back(): pl.pallas_call(partial(attend_back_kernel, shard=width // shards if packe...  11.9 us
    pallas_call x1, Pallas kernels, attend(): pl.pallas_call(attend_kernel, grid=(pairs,), in_specs=[pl.BlockSpec((1, h...  11.3 us
    pallas_call x1, Pallas kernels, last_back(): pl.pallas_call(partial(last_back_kernel, shard=width // shards if packed...  10.4 us
    unnamed x123, local copies, waits for them, and re-layouts  9.27 us
  transfers between devices with their start and end apart: 23, of which 9 were waited for; matrix products, arithmetic and copies ran while one was open for 13% of the time, Pallas kernels for 29%

profile of v4, /device:TPU:0, one launch (start us, length us, event | category | flops | bytes accessed | tf_op | source)
XLA Modules:
  0.0 165.9 jit_solution(18211860118696558484)
XLA Ops:
  0.7 2.2 %fusion.3 = (bf16[2,140,768]{2,0,1:T(2,128)(2,1)S(1)}, bf16[2,140,768]{2,0,1:T(2,128)(2,1)S(1)}) fusion(bf16[4,140,768]{2,0,1:T(4,128)(2,1)} %param.20), kind=kLoop, calls=%fused_computation.52 | loop fusion | bytes 1720320 | tf_op jit(solution)/shard_map/slice | solution.py:862
  3.1 3.0 %collective-permute-start = (bf16[2,140,768]{2,1,0:T(8,128)(2,1)S(1)}, bf16[2,140,768]{2,1,0:T(8,128)(2,1)S(1)}, u32[]{:S(2)}, u32[]{:S(2)}) collective-permute-start(bf16[2,140,768]{2,1,0:T(8,128)(2,1)S(1)} %copy_select_fusion), channel_id=1, source_target_pairs={{0,1},{1,0},{2,3},{3,2},{4,5},{5,4},{6,7},{7,6},{8,9},{9,8},{10,11... | collective-permute-start | bytes 1290248 | tf_op jit(solution)/shard_map/ppermute | solution.py:846
  7.3 1.2 copy-done
  8.5 3.2 %norm_qkv.2 = (bf16[2,144,768]{2,1,0:T(8,128)(2,1)}, bf16[2,144,2304]{2,1,0:T(8,128)(2,1)}) custom-call(bf16[2,144,768]{2,1,0:T(8,128)(2,1)S(1)} %pad.13.x_ref.xo, f32[1,768]{1,0:T(1,128)S(1)} %reshape.202.g_ref.g1, f32[1,768]{1,0:T(1,128)S(1)} %reshape.203.b_ref, bf16[768,2304]{1,0:T(8,128)(2,1)S(1)} %copy-done, f32[2,1,768]{2,1,0:T(1,128)S(1)} %reshape.204.qvb_ref), custom_call_target="tpu_custom_call" | custom-call | flops 1019215872 | bytes 5750784 | tf_op jit(solution)/shard_map/norm_qkv/pallas_call | solution.py:131
  11.8 4.4 %collective-permute-done = bf16[2,140,768]{2,1,0:T(8,128)(2,1)S(1)} collective-permute-done((bf16[2,140,768]{2,1,0:T(8,128)(2,1)S(1)}, bf16[2,140,768]{2,1,0:T(8,128)(2,1)S(1)}, u32[]{:S(2)}, u32[]{:S(2)}) %collective-permute-start) | collective-permute-done | bytes 430112 | tf_op jit(solution)/shard_map/ppermute | solution.py:846
  16.3 1.7 %collective-permute-start.2 = (bf16[2,140,768]{2,1,0:T(8,128)(2,1)S(1)}, bf16[2,140,768]{2,1,0:T(8,128)(2,1)S(1)}, u32[]{:S(2)}, u32[]{:S(2)}) collective-permute-start(bf16[2,140,768]{2,1,0:T(8,128)(2,1)S(1)} %get-tuple-element.84), channel_id=1, source_target_pairs={{0,1},{1,0},{2,3},{3,2},{4,5},{5,4},{6,7},{7,6},{8,9},{9,8},{10,11... | collective-permute-start | bytes 1290248 | tf_op jit(solution)/shard_map/ppermute | solution.py:846
  18.4 2.8 %norm_qkv.3 = (bf16[2,144,768]{2,1,0:T(8,128)(2,1)}, bf16[2,144,2304]{2,1,0:T(8,128)(2,1)S(1)}) custom-call(bf16[2,144,768]{2,1,0:T(8,128)(2,1)S(1)} %pad.14.x_ref.xr, f32[1,768]{1,0:T(1,128)S(1)} %reshape.202.g_ref.g1, f32[1,768]{1,0:T(1,128)S(1)} %reshape.203.b_ref, bf16[768,2304]{1,0:T(8,128)(2,1)S(1)} %copy-done, f32[2,1,768]{2,1,0:T(1,128)S(1)} %reshape.204.qvb_ref), custom_call_target="tpu_custom_call" | custom-call | flops 1019215872 | bytes 5750784 | tf_op jit(solution)/shard_map/norm_qkv/pallas_call | solution.py:131
  21.2 11.3 %attend.1 = (bf16[2,2,144,768]{3,2,1,0:T(8,128)(2,1)}, f32[2,2,144,768]{3,2,1,0:T(8,128)}, bf16[2,2,144,768]{3,2,1,0:T(8,128)(2,1)S(1)}, bf16[2,6,576,288]{3,2,1,0:T(8,128)(2,1)}) custom-call(bf16[2,144,2304]{2,1,0:T(8,128)(2,1)S(1)} %copy-done.3, bf16[2,144,2304]{2,1,0:T(8,128)(2,1)S(1)} %get-tuple-element.80.qr, bf16[2,144,768]{2,1,0:T(8,128)(2,1)S(1)} %pad.13.x_ref.xo, ...), custom_call_target="tpu_custom_call" | custom-call | flops 2038431744 | bytes 11059200 | tf_op jit(solution)/shard_map/attend/pallas_call | solution.py:203
  32.5 1.6 copy-done.2
  34.2 26.0 %mlp.1 = (bf16[2,144,768]{2,1,0:T(8,128)(2,1)}, bf16[2,144,768]{2,1,0:T(8,128)(2,1)}, bf16[576,768]{1,0:T(8,128)(2,1)S(1)}, f32[1,768]{1,0:T(1,128)}, f32[576,76...) custom-call(s32[3]{0:T(128)S(1)} %pad_add_fusion.info, ...), custom_call_target="tpu_custom_call" | custom-call | flops 16307453952 | bytes 25165824 | tf_op jit(solution)/shard_map/mlp/pallas_call | solution.py:343
  60.2 3.1 %second_back.1 = (f32[2,288,768]{2,1,0:T(8,128)}, bf16[2,288,768]{2,1,0:T(8,128)(2,1)S(1)}, bf16[2,288,768]{2,1,0:T(8,128)(2,1)S(1)}, f32[8,768]{1,0:T(8,128)}) custom-call(f32[2,2,144,768]{3,2,1,0:T(8,128)S(1)} %bitcast.47, bf16[2,2,144,768]{3,2,1,0:T(8,128)(2,1)S(1)} %bitcast.48, f32[2,2,144,768]{3,2,1,0:T(8,128)S(1)} %copy-done.2, ...), custom_call_target="tpu_custom_call" | custom-call | flops 679477248 | bytes 10485760 | tf_op jit(solution)/shard_map/second_back/pallas_call | solution.py:460
  63.4 5.0 %collective-permute-done.3.got = bf16[8,384,768]{2,1,0:T(8,128)(2,1)S(1)} collective-permute-done((bf16[8,384,768]{2,1,0:T(8,128)(2,1)}, bf16[8,384,768]{2,1,0:T(8,128)(2,1)S(1)}, u32[]{:S(2)}, u32[]{:S(2)}) %collective-permute-start.3) | collective-permute-done | bytes 4718624 | tf_op jit(solution)/shard_map/ppermute | solution.py:736
  68.7 1.6 collective-permute-start.4
  71.8 11.9 %attend_back.1 = (bf16[576,1536]{1,0:T(8,128)(2,1)S(1)}, bf16[768,576]{1,0:T(8,128)(2,1)S(1)}, f32[8,128]{1,0:T(8,128)}, bf16[384,2304]{1,0:T(8,128)(2,1)}, bf16[384,2304]{1,0:T(8,128)(2,1)}) custom-call(s32[32]{0:T(128)S(1)} %get-tuple-element.104.inv, bf16[2,288,768]{2,1,0:T(8,128)(2,1)S(1)} %get-tuple-element.93.br, ...), custom_call_target="tpu_custom_call" | custom-call | flops 4756340736 | bytes 16777216 | tf_op jit(solution)/shard_map/attend_back/pallas_call | solution.py:527
  84.0 6.6 %collective-permute-done.5.q1 = bf16[2,2,1,384,256]{4,3,2,1,0:T(8,128)(2,1)S(1)} collective-permute-done((bf16[2,2,1,384,256]{4,3,2,1,0:T(8,128)(2,1)S(1)}, bf16[2,2,1,384,256]{4,3,2,1,0:T(8,128)(2,1)S(1)}, u32[]{:S(2)}, u32[]{:S(2)}) %collective-permute-start.5) | collective-permute-done | bytes 786464 | tf_op jit(solution)/shard_map/ppermute | solution.py:736
  90.6 2.5 %add_convert_fusion.2 = bf16[1,1,2,384,512]{4,3,2,1,0:T(8,128)(2,1)S(1)} fusion(bf16[2,2,2,384,768]{4,3,2,1,0:T(8,128)(2,1)} %bitcast.61, bf16[2,2,2,384,768]{4,3,2,1,0:T(8,128)(2,1)} %bitcast.53, bf16[1,2,2,384,512]{4,3,2,1,0:T(8,128)(2,1)S(1)} %collective-permute-done.4.p1), kind=kLoop, calls=%fused_computation.2 | loop fusion | flops 2359296 | bytes 3145728 | tf_op jit(solution)/shard_map/convert_element_type | solution.py:765
  93.1 1.6 collective-permute-start.6
  95.3 1.3 add_convert_fusion.6
  96.6 1.6 collective-permute-start.7
  98.2 10.4 %last_back.1 = (bf16[2,144,768]{2,1,0:T(8,128)(2,1)}, bf16[2,144,768]{2,1,0:T(8,128)(2,1)}, f32[16,768]{1,0:T(8,128)}, bf16[384,896]{1,0:T(8,128)(2,1)}, bf16[384,896]{1,0:T(8,128)(2,1)}) custom-call(s32[32]{0:T(128)S(1)} %get-tuple-element.104.inv, bf16[2,144,2304]{2,1,0:T(8,128)(2,1)S(1)} %copy-done.4, bf16[2,144,2304]{2,1,0:T(8,128)(2,1)S(1)} %copy-done.6, ...), custom_call_target="tpu_custom_call" | custom-call | flops 4076863488 | bytes 16777216 | tf_op jit(solution)/shard_map/last_back/pallas_call | solution.py:656
  109.4 1.4 add_convert_fusion.9
  110.8 1.3 add_convert_fusion.5
  112.2 1.1 add_convert_fusion.1
  113.3 1.5 collective-permute-start.14
  115.4 1.6 collective-permute-start.12
  117.1 0.9 add_convert_fusion.7
  118.8 4.6 %collective-permute-done.12.q3 = bf16[1,1,1,384,256]{4,3,2,1,0:T(8,128)(2,1)S(1)} collective-permute-done((bf16[1,1,1,384,256]{4,3,2,1,0:T(8,128)(2,1)S(1)}, bf16[1,1,1,384,256]{4,3,2,1,0:T(8,128)(2,1)S(1)}, u32[]{:S(2)}, u32[]{:S(2)}) %collective-permute-start.12) | collective-permute-done | bytes 196640 | tf_op jit(solution)/shard_map/ppermute | solution.py:736
  124.5 3.0 %part_pairs.1 = (f32[192,768]{1,0:T(8,128)}, bf16[192,768]{1,0:T(8,128)(2,1)}) custom-call(bf16[8,384,768]{2,1,0:T(8,128)(2,1)} %get-tuple-element.86.keep, bf16[8,384,768]{2,1,0:T(8,128)(2,1)} %copy-done.17, bf16[1,2,2,384,512]{4,3,2,1,0:T(8,128)(2,1)} %copy-done.18, bf16[1,1,2,384,512]{4,3,2,1,0:T(8,128)(2,1)} %copy-done.21, ...), custom_call_target="tpu_custom_call" | custom-call | bytes 4194304 | tf_op jit(solution)/shard_map/part_pairs/pallas_call | solution.py:800
  127.5 1.2 collective-permute-done.14
  129.6 1.6 collective-permute-start.15
  131.3 2.6 %collective-permute-start.22 = (bf16[192,768]{1,0:T(8,128)(2,1)S(1)}, bf16[192,768]{1,0:T(8,128)(2,1)}, u32[]{:S(2)}, u32[]{:S(2)}) collective-permute-start(bf16[192,768]{1,0:T(8,128)(2,1)S(1)} %copy-done.53), channel_id=1, source_target_pairs={{0,16},{1,17},{2,18},{3,19},{4,20},{5,21},{6,22},{7,23},{8,24},{9,... | collective-permute-start | bytes 884744 | tf_op jit(solution)/shard_map/ppermute | solution.py:736
  134.4 1.0 add_convert_fusion.10
  135.4 1.8 %collective-permute-start.18 = (bf16[1,1,2,2,24,896]{5,4,3,2,1,0:T(8,128)(2,1)S(1)}, bf16[1,1,2,2,24,896]{5,4,3,2,1,0:T(8,128)(2,1)S(1)}, u32[]{:S(2)}, u32[]{:S(2)}) collective-permute-start(bf16[1,1,2,2,24,896]{5,4,3,2,1,0:T(8,128)(2,1)S(1)} %add_convert_fusion.10), channel_id=1, source_target_pairs={{0,8},{1,9},{2,6},{3,7},{4,12},{5,13},{6,2},{7,3},{8,0},{9,1},{10,... | collective-permute-start | bytes 516104 | tf_op jit(solution)/shard_map/ppermute | solution.py:736
  137.2 5.7 %collective-permute-done.15 = bf16[1,1,2,2,24,2304]{5,4,3,2,1,0:T(8,128)(2,1)S(1)} collective-permute-done((bf16[1,1,2,2,24,2304]{5,4,3,2,1,0:T(8,128)(2,1)S(1)}, bf16[1,1,2,2,24,2304]{5,4,3,2,1,0:T(8,128)(2,1)S(1)}, u32[]{:S(2)}, u32[]{:S(2)}) %collective-permute-start.15) | collective-permute-done | bytes 442400 | tf_op jit(solution)/shard_map/ppermute | solution.py:736
  142.9 1.2 add_convert_fusion.8
  144.1 1.5 collective-permute-start.17
  145.6 0.9 add_convert_fusion.12
  146.5 1.3 collective-permute-start.19
  147.8 2.3 %collective-permute-done.17 = bf16[1,1,1,2,24,2304]{5,4,3,2,1,0:T(8,128)(2,1)S(1)} collective-permute-done((bf16[1,1,1,2,24,2304]{5,4,3,2,1,0:T(8,128)(2,1)S(1)}, bf16[1,1,1,2,24,2304]{5,4,3,2,1,0:T(8,128)(2,1)S(1)}, u32[]{:S(2)}, u32[]{:S(2)}) %collective-permute-start.17) | collective-permute-done | bytes 221216 | tf_op jit(solution)/shard_map/ppermute | solution.py:736
  150.1 1.7 %fusion = bf16[24,2304]{1,0:T(8,128)(2,1)} fusion(bf16[1,2,2,2,24,2304]{5,4,3,2,1,0:T(8,128)(2,1)S(1)} %bitcast.71, bf16[1,2,2,2,24,2304]{5,4,3,2,1,0:T(8,128)(2,1)S(1)} %bitcast.67, bf16[1,1,1,2,24,2304]{5,4,3,2,1,0:T(8,128)(2,1)S(1)} %collective-permute-done.17, bf16[1,1,2,2,24,2304]{5,4,3,2,1,0:T(8,128)(2,1)S(1)} %collective-permute-done.15, ...), kind=kLoop, calls=%fused_computation.20 | loop fusion | flops 552960 | bytes 663552 | tf_op jit(solution)/shard_map/convert_element_type | solution.py:765
  152.0 1.5 fusion.1
  153.5 1.3 collective-permute-start.20
  154.8 1.3 copy.58
  156.1 1.6 collective-permute-start.21
  157.7 1.3 copy.59
  159.1 2.0 %finish_pair.1 = (f32[96,768]{1,0:T(8,128)}, f32[24,3072]{1,0:T(8,128)}) custom-call(f32[192,768]{1,0:T(8,128)} %get-tuple-element.132.mine, bf16[192,768]{1,0:T(8,128)(2,1)} %collective-permute-done.22.got), custom_call_target="tpu_custom_call" | custom-call | bytes 2097152 | tf_op jit(solution)/shard_map/finish_pair/pallas_call | solution.py:826
  161.1 0.9 bitcast_add_fusion.1
  163.5 1.0 bitcast_add_fusion
  (188 shorter events, 12.4 us)
Async XLA Ops:
  3.1 13.2 %collective-permute-start = (bf16[2,140,768]{2,1,0:T(8,128)(2,1)S(1)}, bf16[2,140,768]{2,1,0:T(8,128)(2,1)S(1)}, u32[]{:S(2)}, u32[]{:S(2)}) collective-permute-start(bf16[2,140,768]{2,1,0:T(8,128)(2,1)S(1)} %copy_select_fusion), channel_id=1, source_target_pairs={{0,1},{1,0},{2,3},{3,2},{4,5},{5,4},{6,7},{7,6},{8,9},{9,8},{10,11... | collective-permute-start | bytes 1290248 | tf_op jit(solution)/shard_map/ppermute | solution.py:846
  6.2 12.0 %collective-permute-start.1 = (bf16[2,140]{1,0:T(2,128)(2,1)S(1)}, bf16[2,140]{1,0:T(2,128)(2,1)S(1)}, u32[]{:S(2)}, u32[]{:S(2)}) collective-permute-start(bf16[2,140]{1,0:T(2,128)(2,1)S(1)} %get-tuple-element.81), channel_id=1, source_target_pairs={{0,1},{1,0},{2,3},{3,2},{4,5},{5,4},{6,7},{7,6},{8,9},{9,8},{10,11... | collective-permute-start | bytes 1688 | tf_op jit(solution)/shard_map/ppermute | solution.py:846
  8.5 24.0 %slice-start.2 = ((s8[4718592]{0:T(1024)(128)(4,1)}), s8[4194304]{0:T(1024)(128)(4,1)S(1)}, s32[]{:S(2)}) async-start(s8[4718592]{0:T(1024)(128)(4,1)} %bitcast.49), calls=%async_computation.2 | async-start | bytes 8388608
  11.7 6.4 %copy-start.41 = (f32[768]{0:T(1024)S(1)}, f32[768]{0:T(1024)}, u32[]{:S(2)}) copy-start(f32[768]{0:T(1024)} %param.29) | copy-start | bytes 9220
  11.7 6.4 %copy-start.42 = (f32[768]{0:T(1024)S(1)}, f32[768]{0:T(1024)}, u32[]{:S(2)}) copy-start(f32[768]{0:T(1024)} %param.28) | copy-start | bytes 9220
  11.7 6.4 %copy-start.43 = (f32[768]{0:T(1024)S(1)}, f32[768]{0:T(1024)}, u32[]{:S(2)}) copy-start(f32[768]{0:T(1024)} %param.30) | copy-start | bytes 9220
  11.7 6.4 %copy-start.44 = (f32[768]{0:T(1024)S(1)}, f32[768]{0:T(1024)}, u32[]{:S(2)}) copy-start(f32[768]{0:T(1024)} %param.34) | copy-start | bytes 9220
  16.3 16.2 %collective-permute-start.2 = (bf16[2,140,768]{2,1,0:T(8,128)(2,1)S(1)}, bf16[2,140,768]{2,1,0:T(8,128)(2,1)S(1)}, u32[]{:S(2)}, u32[]{:S(2)}) collective-permute-start(bf16[2,140,768]{2,1,0:T(8,128)(2,1)S(1)} %get-tuple-element.84), channel_id=1, source_target_pairs={{0,1},{1,0},{2,3},{3,2},{4,5},{5,4},{6,7},{7,6},{8,9},{9,8},{10,11... | collective-permute-start | bytes 1290248 | tf_op jit(solution)/shard_map/ppermute | solution.py:846
  18.4 14.1 %slice-start.3 = ((s8[4718592]{0:T(1024)(128)(4,1)}), s8[524288]{0:T(1024)(128)(4,1)S(1)}, s32[]{:S(2)}) async-start(s8[4718592]{0:T(1024)(128)(4,1)} %bitcast.49), calls=%async_computation.3 | async-start | bytes 1048576
  21.1 11.3 %copy-start.5 = (bf16[2,144,2304]{2,1,0:T(8,128)(2,1)}, bf16[2,144,2304]{2,1,0:T(8,128)(2,1)S(1)}, u32[]{:S(2)}) copy-start(bf16[2,144,2304]{2,1,0:T(8,128)(2,1)S(1)} %get-tuple-element.80.qr) | copy-start | bytes 3981316
  21.2 11.4 %copy-start.11 = (bf16[3072,768]{1,0:T(8,128)(2,1)S(1)}, bf16[3072,768]{1,0:T(8,128)(2,1)}, u32[]{:S(2)}) copy-start(bf16[3072,768]{1,0:T(8,128)(2,1)} %down.1) | copy-start | bytes 14155780
  21.2 11.4 %copy-start.14 = (f32[3072]{0:T(1024)S(1)}, f32[3072]{0:T(1024)}, u32[]{:S(2)}) copy-start(f32[3072]{0:T(1024)} %param.32) | copy-start | bytes 36868
  32.5 38.8 %slice-start = ((s8[5308416]{0:T(1024)(128)(4,1)}), s8[4194304]{0:T(1024)(128)(4,1)S(1)}, s32[]{:S(2)}) async-start(s8[5308416]{0:T(1024)(128)(4,1)} %bitcast.44), calls=%async_computation | async-start | bytes 8388608
  34.2 37.1 %slice-start.1 = ((s8[5308416]{0:T(1024)(128)(4,1)}), s8[1114112]{0:T(1024)(128)(4,1)S(1)}, s32[]{:S(2)}) async-start(s8[5308416]{0:T(1024)(128)(4,1)} %bitcast.44), calls=%async_computation.1 | async-start | bytes 2228224
  60.1 8.2 %collective-permute-start.3 = (bf16[8,384,768]{2,1,0:T(8,128)(2,1)}, bf16[8,384,768]{2,1,0:T(8,128)(2,1)S(1)}, u32[]{:S(2)}, u32[]{:S(2)}) collective-permute-start(bf16[8,384,768]{2,1,0:T(8,128)(2,1)} %get-tuple-element.87), channel_id=1, source_target_pairs={{0,2},{1,3},{2,0},{3,1},{4,6},{5,7},{6,4},{7,5},{8,10},{9,11},{10,... | collective-permute-start | bytes 14155784 | tf_op jit(solution)/shard_map/ppermute | solution.py:736
  60.2 8.1 %copy-start.16 = (bf16[8,384,768]{2,1,0:T(8,128)(2,1)S(1)}, bf16[8,384,768]{2,1,0:T(8,128)(2,1)}, u32[]{:S(2)}) copy-start(bf16[8,384,768]{2,1,0:T(8,128)(2,1)} %get-tuple-element.86.keep) | copy-start | bytes 14155780
  68.7 21.8 %collective-permute-start.4 = (bf16[1,2,2,384,512]{4,3,2,1,0:T(8,128)(2,1)S(1)}, bf16[1,2,2,384,512]{4,3,2,1,0:T(8,128)(2,1)S(1)}, u32[]{:S(2)}, u32[]{:S(2)}) collective-permute-start(bf16[1,2,2,384,512]{4,3,2,1,0:T(8,128)(2,1)S(1)} %add_convert_fusion), channel_id=1, source_target_pairs={{0,4},{1,5},{2,10},{3,11},{4,0},{5,1},{6,14},{7,15},{8,12},{9,13},... | collective-permute-start | bytes 4718600 | tf_op jit(solution)/shard_map/ppermute | solution.py:736
  70.9 19.6 %collective-permute-start.5 = (bf16[2,2,1,384,256]{4,3,2,1,0:T(8,128)(2,1)S(1)}, bf16[2,2,1,384,256]{4,3,2,1,0:T(8,128)(2,1)S(1)}, u32[]{:S(2)}, u32[]{:S(2)}) collective-permute-start(bf16[2,2,1,384,256]{4,3,2,1,0:T(8,128)(2,1)S(1)} %add_convert_fusion.3), channel_id=1, source_target_pairs={{0,1},{1,0},{2,3},{3,2},{4,5},{5,4},{6,7},{7,6},{8,9},{9,8},{10,11... | collective-permute-start | bytes 2359304 | tf_op jit(solution)/shard_map/ppermute | solution.py:736
  83.8 11.0 %copy-start.52 = (bf16[2,144,768]{2,1,0:T(8,128)(2,1)S(1)}, bf16[2,144,768]{2,1,0:T(8,128)(2,1)}, u32[]{:S(2)}) copy-start(bf16[2,144,768]{2,1,0:T(8,128)(2,1)} %get-tuple-element.102) | copy-start | bytes 1327108
  83.8 14.4 %copy-start.1 = (f32[2,288,768]{2,1,0:T(8,128)S(1)}, f32[2,288,768]{2,1,0:T(8,128)}, u32[]{:S(2)}) copy-start(f32[2,288,768]{2,1,0:T(8,128)} %get-tuple-element.107.ga) | copy-start | bytes 5308420
  83.8 14.4 %copy-start.4 = (bf16[2,144,2304]{2,1,0:T(8,128)(2,1)S(1)}, bf16[2,144,2304]{2,1,0:T(8,128)(2,1)}, u32[]{:S(2)}) copy-start(bf16[2,144,2304]{2,1,0:T(8,128)(2,1)} %get-tuple-element.76.qo) | copy-start | bytes 3981316
  83.8 14.4 %copy-start.8 = (f32[8,768]{1,0:T(8,128)S(1)}, f32[8,768]{1,0:T(8,128)}, u32[]{:S(2)}) copy-start(f32[8,768]{1,0:T(8,128)} %get-tuple-element.90.v2) | copy-start | bytes 73732
  83.8 14.4 %copy-start.9 = (f32[1,3072]{1,0:T(1,128)S(1)}, f32[1,3072]{1,0:T(1,128)}, u32[]{:S(2)}) copy-start(f32[1,3072]{1,0:T(1,128)} %get-tuple-element.108.upbg) | copy-start | bytes 36868
  83.8 14.4 %copy-start.10 = (f32[1,768]{1,0:T(1,128)S(1)}, f32[1,768]{1,0:T(1,128)}, u32[]{:S(2)}) copy-start(f32[1,768]{1,0:T(1,128)} %get-tuple-element.109.dbg) | copy-start | bytes 9220
  83.8 24.9 %collective-permute-start.9 = (bf16[384,2304]{1,0:T(8,128)(2,1)}, bf16[384,2304]{1,0:T(8,128)(2,1)S(1)}, u32[]{:S(2)}, u32[]{:S(2)}) collective-permute-start(bf16[384,2304]{1,0:T(8,128)(2,1)} %get-tuple-element.103), channel_id=1, source_target_pairs={{0,2},{1,3},{2,0},{3,1},{4,6},{5,7},{6,4},{7,5},{8,10},{9,11},{10,... | collective-permute-start | bytes 5308424 | tf_op jit(solution)/shard_map/ppermute | solution.py:736
  90.6 18.8 %copy-start.20 = (bf16[2,2,1,384,256]{4,3,2,1,0:T(8,128)(2,1)}, bf16[2,2,1,384,256]{4,3,2,1,0:T(8,128)(2,1)S(1)}, u32[]{:S(2)}) copy-start(bf16[2,2,1,384,256]{4,3,2,1,0:T(8,128)(2,1)S(1)} %collective-permute-done.5.q1) | copy-start | bytes 2359300
  90.6 20.2 %copy-start.18 = (bf16[1,2,2,384,512]{4,3,2,1,0:T(8,128)(2,1)}, bf16[1,2,2,384,512]{4,3,2,1,0:T(8,128)(2,1)S(1)}, u32[]{:S(2)}) copy-start(bf16[1,2,2,384,512]{4,3,2,1,0:T(8,128)(2,1)S(1)} %collective-permute-done.4.p1) | copy-start | bytes 4718596
  93.1 16.3 %collective-permute-start.6 = (bf16[1,1,2,384,512]{4,3,2,1,0:T(8,128)(2,1)S(1)}, bf16[1,1,2,384,512]{4,3,2,1,0:T(8,128)(2,1)S(1)}, u32[]{:S(2)}, u32[]{:S(2)}) collective-permute-start(bf16[1,1,2,384,512]{4,3,2,1,0:T(8,128)(2,1)S(1)} %add_convert_fusion.2), channel_id=1, source_target_pairs={{0,8},{1,9},{2,6},{3,7},{4,12},{5,13},{6,2},{7,3},{8,0},{9,1},{10,... | collective-permute-start | bytes 2359304 | tf_op jit(solution)/shard_map/ppermute | solution.py:736
  94.8 13.9 %collective-permute-start.8 = (bf16[2,144,768]{2,1,0:T(8,128)(2,1)S(1)}, bf16[2,144,768]{2,1,0:T(8,128)(2,1)S(1)}, u32[]{:S(2)}, u32[]{:S(2)}) collective-permute-start(bf16[2,144,768]{2,1,0:T(8,128)(2,1)S(1)} %copy-done.52), channel_id=1, source_target_pairs={{0,1},{1,0},{2,3},{3,2},{4,5},{5,4},{6,7},{7,6},{8,9},{9,8},{10,11... | collective-permute-start | bytes 1327112 | tf_op jit(solution)/shard_map/ppermute | solution.py:846
  96.6 12.1 %collective-permute-start.7 = (bf16[1,2,1,384,256]{4,3,2,1,0:T(8,128)(2,1)S(1)}, bf16[1,2,1,384,256]{4,3,2,1,0:T(8,128)(2,1)S(1)}, u32[]{:S(2)}, u32[]{:S(2)}) collective-permute-start(bf16[1,2,1,384,256]{4,3,2,1,0:T(8,128)(2,1)S(1)} %add_convert_fusion.6), channel_id=1, source_target_pairs={{0,4},{1,5},{2,10},{3,11},{4,0},{5,1},{6,14},{7,15},{8,12},{9,13},... | collective-permute-start | bytes 1179656 | tf_op jit(solution)/shard_map/ppermute | solution.py:736
  108.6 8.5 %collective-permute-start.11 = (bf16[384,896]{1,0:T(8,128)(2,1)}, bf16[384,896]{1,0:T(8,128)(2,1)S(1)}, u32[]{:S(2)}, u32[]{:S(2)}) collective-permute-start(bf16[384,896]{1,0:T(8,128)(2,1)} %get-tuple-element.115), channel_id=1, source_target_pairs={{0,2},{1,3},{2,0},{3,1},{4,6},{5,7},{6,4},{7,5},{8,10},{9,11},{10,... | collective-permute-start | bytes 2064392 | tf_op jit(solution)/shard_map/ppermute | solution.py:736
  113.3 15.4 %collective-permute-start.14 = (bf16[1,2,2,2,24,2304]{5,4,3,2,1,0:T(8,128)(2,1)}, bf16[1,2,2,2,24,2304]{5,4,3,2,1,0:T(8,128)(2,1)S(1)}, u32[]{:S(2)}, u32[]{:S(2)}) collective-permute-start(bf16[1,2,2,2,24,2304]{5,4,3,2,1,0:T(8,128)(2,1)} %bitcast.9), channel_id=1, source_target_pairs={{0,4},{1,5},{2,10},{3,11},{4,0},{5,1},{6,14},{7,15},{8,12},{9,13},... | collective-permute-start | bytes 2654216 | tf_op jit(solution)/shard_map/ppermute | solution.py:736
  114.8 9.7 %collective-permute-start.10 = (bf16[1,1,1,384,512]{4,3,2,1,0:T(8,128)(2,1)S(1)}, bf16[1,1,1,384,512]{4,3,2,1,0:T(8,128)(2,1)}, u32[]{:S(2)}, u32[]{:S(2)}) collective-permute-start(bf16[1,1,1,384,512]{4,3,2,1,0:T(8,128)(2,1)S(1)} %add_convert_fusion.5), channel_id=1, source_target_pairs={{0,1},{1,0},{2,3},{3,2},{4,5},{5,4},{6,7},{7,6},{8,9},{9,8},{10,11... | collective-permute-start | bytes 1179656 | tf_op jit(solution)/shard_map/ppermute | solution.py:736
  115.4 7.9 %collective-permute-start.12 = (bf16[1,1,1,384,256]{4,3,2,1,0:T(8,128)(2,1)S(1)}, bf16[1,1,1,384,256]{4,3,2,1,0:T(8,128)(2,1)S(1)}, u32[]{:S(2)}, u32[]{:S(2)}) collective-permute-start(bf16[1,1,1,384,256]{4,3,2,1,0:T(8,128)(2,1)S(1)} %add_convert_fusion.9), channel_id=1, source_target_pairs={{0,8},{1,9},{2,6},{3,7},{4,12},{5,13},{6,2},{7,3},{8,0},{9,1},{10,... | collective-permute-start | bytes 589832 | tf_op jit(solution)/shard_map/ppermute | solution.py:736
  118.0 16.4 %collective-permute-start.16 = (bf16[1,2,2,2,24,896]{5,4,3,2,1,0:T(8,128)(2,1)}, bf16[1,2,2,2,24,896]{5,4,3,2,1,0:T(8,128)(2,1)}, u32[]{:S(2)}, u32[]{:S(2)}) collective-permute-start(bf16[1,2,2,2,24,896]{5,4,3,2,1,0:T(8,128)(2,1)} %bitcast.10), channel_id=1, source_target_pairs={{0,4},{1,5},{2,10},{3,11},{4,0},{5,1},{6,14},{7,15},{8,12},{9,13},... | collective-permute-start | bytes 1032200 | tf_op jit(solution)/shard_map/ppermute | solution.py:736
  127.5 6.4 %copy-start.51 = (bf16[2,144,768]{2,1,0:T(8,128)(2,1)S(1)}, bf16[2,144,768]{2,1,0:T(8,128)(2,1)}, u32[]{:S(2)}) copy-start(bf16[2,144,768]{2,1,0:T(8,128)(2,1)} %get-tuple-element.124) | copy-start | bytes 1327108
  129.6 13.3 %collective-permute-start.15 = (bf16[1,1,2,2,24,2304]{5,4,3,2,1,0:T(8,128)(2,1)S(1)}, bf16[1,1,2,2,24,2304]{5,4,3,2,1,0:T(8,128)(2,1)S(1)}, u32[]{:S(2)}, u32[]{:S(2)}) collective-permute-start(bf16[1,1,2,2,24,2304]{5,4,3,2,1,0:T(8,128)(2,1)S(1)} %add_convert_fusion.4), channel_id=1, source_target_pairs={{0,8},{1,9},{2,6},{3,7},{4,12},{5,13},{6,2},{7,3},{8,0},{9,1},{10,... | collective-permute-start | bytes 1327112 | tf_op jit(solution)/shard_map/ppermute | solution.py:736
  131.2 20.6 %copy-start.30 = (bf16[2,144,768]{2,1,0:T(8,128)(2,1)S(1)}, bf16[2,144,768]{2,1,0:T(8,128)(2,1)}, u32[]{:S(2)}) copy-start(bf16[2,144,768]{2,1,0:T(8,128)(2,1)} %get-tuple-element.110) | copy-start | bytes 1327108
  131.3 27.8 %collective-permute-start.22 = (bf16[192,768]{1,0:T(8,128)(2,1)S(1)}, bf16[192,768]{1,0:T(8,128)(2,1)}, u32[]{:S(2)}, u32[]{:S(2)}) collective-permute-start(bf16[192,768]{1,0:T(8,128)(2,1)S(1)} %copy-done.53), channel_id=1, source_target_pairs={{0,16},{1,17},{2,18},{3,19},{4,20},{5,21},{6,22},{7,23},{8,24},{9,... | collective-permute-start | bytes 884744 | tf_op jit(solution)/shard_map/ppermute | solution.py:736
  133.9 17.9 %collective-permute-start.13 = (bf16[2,144,768]{2,1,0:T(8,128)(2,1)S(1)}, bf16[2,144,768]{2,1,0:T(8,128)(2,1)S(1)}, u32[]{:S(2)}, u32[]{:S(2)}) collective-permute-start(bf16[2,144,768]{2,1,0:T(8,128)(2,1)S(1)} %copy-done.51), channel_id=1, source_target_pairs={{0,1},{1,0},{2,3},{3,2},{4,5},{5,4},{6,7},{7,6},{8,9},{9,8},{10,11... | collective-permute-start | bytes 1327112 | tf_op jit(solution)/shard_map/ppermute | solution.py:846
  135.4 10.1 %collective-permute-start.18 = (bf16[1,1,2,2,24,896]{5,4,3,2,1,0:T(8,128)(2,1)S(1)}, bf16[1,1,2,2,24,896]{5,4,3,2,1,0:T(8,128)(2,1)S(1)}, u32[]{:S(2)}, u32[]{:S(2)}) collective-permute-start(bf16[1,1,2,2,24,896]{5,4,3,2,1,0:T(8,128)(2,1)S(1)} %add_convert_fusion.10), channel_id=1, source_target_pairs={{0,8},{1,9},{2,6},{3,7},{4,12},{5,13},{6,2},{7,3},{8,0},{9,1},{10,... | collective-permute-start | bytes 516104 | tf_op jit(solution)/shard_map/ppermute | solution.py:736
  142.9 8.9 %copy-start.32 = (bf16[1,1,2,2,24,2304]{5,4,3,2,1,0:T(8,128)(2,1)}, bf16[1,1,2,2,24,2304]{5,4,3,2,1,0:T(8,128)(2,1)S(1)}, u32[]{:S(2)}) copy-start(bf16[1,1,2,2,24,2304]{5,4,3,2,1,0:T(8,128)(2,1)S(1)} %collective-permute-done.15) | copy-start | bytes 1327108
  144.1 6.0 %collective-permute-start.17 = (bf16[1,1,1,2,24,2304]{5,4,3,2,1,0:T(8,128)(2,1)S(1)}, bf16[1,1,1,2,24,2304]{5,4,3,2,1,0:T(8,128)(2,1)S(1)}, u32[]{:S(2)}, u32[]{:S(2)}) collective-permute-start(bf16[1,1,1,2,24,2304]{5,4,3,2,1,0:T(8,128)(2,1)S(1)} %add_convert_fusion.8), channel_id=1, source_target_pairs={{0,1},{1,0},{2,3},{3,2},{4,5},{5,4},{6,7},{7,6},{8,9},{9,8},{10,11... | collective-permute-start | bytes 663560 | tf_op jit(solution)/shard_map/ppermute | solution.py:736
  146.5 5.5 %collective-permute-start.19 = (bf16[1,1,1,2,24,896]{5,4,3,2,1,0:T(8,128)(2,1)S(1)}, bf16[1,1,1,2,24,896]{5,4,3,2,1,0:T(8,128)(2,1)S(1)}, u32[]{:S(2)}, u32[]{:S(2)}) collective-permute-start(bf16[1,1,1,2,24,896]{5,4,3,2,1,0:T(8,128)(2,1)S(1)} %add_convert_fusion.12), channel_id=1, source_target_pairs={{0,1},{1,0},{2,3},{3,2},{4,5},{5,4},{6,7},{7,6},{8,9},{9,8},{10,11... | collective-permute-start | bytes 258056 | tf_op jit(solution)/shard_map/ppermute | solution.py:736
  152.0 7.1 %copy-start.36 = (bf16[1,1,1,2,24,896]{5,4,3,2,1,0:T(8,128)(2,1)}, bf16[1,1,1,2,24,896]{5,4,3,2,1,0:T(8,128)(2,1)S(1)}, u32[]{:S(2)}) copy-start(bf16[1,1,1,2,24,896]{5,4,3,2,1,0:T(8,128)(2,1)S(1)} %collective-permute-done.19) | copy-start | bytes 258052
  153.5 7.6 %collective-permute-start.20 = (bf16[24,896]{1,0:T(8,128)(2,1)}, bf16[24,896]{1,0:T(8,128)(2,1)}, u32[]{:S(2)}, u32[]{:S(2)}) collective-permute-start(bf16[24,896]{1,0:T(8,128)(2,1)} %fusion.1), channel_id=1, source_target_pairs={{0,16},{1,17},{2,18},{3,19},{4,20},{5,21},{6,22},{7,23},{8,24},{9,... | collective-permute-start | bytes 129032 | tf_op jit(solution)/shard_map/ppermute | solution.py:736
  156.1 7.4 %copy-start.34 = (bf16[1,1,1,2,24,2304]{5,4,3,2,1,0:T(8,128)(2,1)S(1)}, bf16[1,1,1,2,24,2304]{5,4,3,2,1,0:T(8,128)(2,1)}, u32[]{:S(2)}) copy-start(bf16[1,1,1,2,24,2304]{5,4,3,2,1,0:T(8,128)(2,1)} %copy-done.33) | copy-start | bytes 663556
  156.1 7.4 %collective-permute-start.21 = (bf16[24,2304]{1,0:T(8,128)(2,1)}, bf16[24,2304]{1,0:T(8,128)(2,1)S(1)}, u32[]{:S(2)}, u32[]{:S(2)}) collective-permute-start(bf16[24,2304]{1,0:T(8,128)(2,1)} %fusion), channel_id=1, source_target_pairs={{0,16},{1,17},{2,18},{3,19},{4,20},{5,21},{6,22},{7,23},{8,24},{9,... | collective-permute-start | bytes 331784 | tf_op jit(solution)/shard_map/ppermute | solution.py:736
  (33 other events, 100.2 us)

commit v5 on v4

--- a/solution.py
+++ b/solution.py
@@ -224,7 +224,7 @@
             kept((pairs, tiles, 2 * rows, rows), BF16),
         ],
         scratch_shapes=[pltpu.VMEM((rows, width), BF16)],
-        compiler_params=params_of(32),
+        compiler_params=params_of(20),
         cost_estimate=pl.CostEstimate(
             flops=pairs * 16 * tiles * rows * rows * LANES,
             bytes_accessed=2 * pairs * rows * width * 8 + 4 * pairs * tiles * rows * rows,
@@ -390,7 +390,10 @@
             flops=12 * rows * width * ff, bytes_accessed=24 * MIB, transcendentals=2 * rows * ff
         ),
         name="mlp",
-    )(info, inv, place, sn, att, cot_own, cot_far, up, up_bias, down, down_bias)
+    )(
+        info, inv, place, sn, pltpu.with_memory_space_constraint(att, pltpu.HBM), cot_own, cot_far, up,
+        up_bias, down, down_bias,
+    )
 
 
 def heads_back(qo, qr, gm_ref, p_ref, dqkv, base, rows, hp0, count):
@@ -468,7 +471,7 @@
             struct((pairs, rows, width), BF16),
             vec,
         ],
-        compiler_params=params_of(24),
+        compiler_params=params_of(16),
         cost_estimate=pl.CostEstimate(
             flops=2 * pairs * rows * width * width, bytes_accessed=10 * MIB, transcendentals=0
         ),
@@ -548,7 +551,7 @@
             ],
         ),
         out_shape=outs,
-        compiler_params=params_of(40 if packed else 50),
+        compiler_params=params_of(28 if packed else 50),
         cost_estimate=pl.CostEstimate(
             flops=pairs * 32 * EARLY * rows * rows * LANES + 6 * pairs * rows * width * width,
             bytes_accessed=16 * MIB,
@@ -679,7 +682,7 @@
             scratch_shapes=[pltpu.VMEM((pairs * rows, cols), BF16)],
         ),
         out_shape=[kept((pairs, half, width), BF16)] * 2 + [vec] + wire,
-        compiler_params=params_of(36),
+        compiler_params=params_of(22),
         cost_estimate=pl.CostEstimate(
             flops=pairs * 32 * late * rows * rows * LANES + 8 * pairs * rows * width * width,
             bytes_accessed=16 * MIB,
@@ -806,6 +809,48 @@
         cost_estimate=pl.CostEstimate(flops=0, bytes_accessed=4 * MIB, transcendentals=0),
         name="part_pairs",
     )(*args)
+
+
+def finish_rest_kernel(*refs, count, early):
+    mids, lasts, outs = refs[:count], refs[count : 2 * count], refs[2 * count :]
+    flat = lambda ref: ref[...].reshape(ref.shape[-2:]).astype(F32)
+
+    def total(part):
+        value = flat(part[0])
+        for ref in part[1:]:
+            value = value + flat(ref)
+        return value
+
+    mid, last = total(mids), total(lasts)
+    qkv_ref, out_ref, *vecs = outs
+    width = out_ref.shape[1]
+    out_ref[...] = mid[:, early:]
+    ca = early // 3
+    cb = width - ca
+    for i in range(3):
+        qkv_ref[:, i * width : i * width + ca] = mid[:, i * ca : (i + 1) * ca]
+        qkv_ref[:, i * width + ca : (i + 1) * width] = last[:, i * cb : (i + 1) * cb]
+    for i, ref in enumerate(vecs):
+        ref[...] = last[i, 3 * cb : 3 * cb + ref.shape[0]]
+
+
+def finish_rest(mid, last, early):
+    rows = mid[0].shape[-2]
+    width = mid[0].shape[-1] - early
+    outs = [struct((rows, 3 * width), F32), struct((rows, width), F32)]
+    outs += [struct((n * rows,), F32) for n in (1, 1, 1, 1, 1, 1, 2, 4)]
+    first = lambda a: pl.BlockSpec(
+        (1,) * (len(a.shape) - 2) + a.shape[-2:], lambda i: (0,) * len(a.shape)
+    )
+    return pl.pallas_call(
+        partial(finish_rest_kernel, count=len(mid), early=early),
+        grid=(1,),
+        in_specs=[first(a) for a in mid + last],
+        out_specs=[spec_of(o) for o in outs],
+        out_shape=outs,
+        cost_estimate=pl.CostEstimate(flops=0, bytes_accessed=2 * MIB, transcendentals=0),
+        name="finish_rest",
+    )(*mid, *last)
 
 
 def finish_pair_kernel(mine, got, down_ref, up_ref):
@@ -960,11 +1005,14 @@
         r4.hold(sent, input_grad)
         got1 = after(got1, r4.step())
         down_g, up_g = finish_pair(mine1, got1, tall, rows)
-        mid, last = r3.result(), r4.result()
-        vecs = last[:8, -LANES:]
-        last = last[:, :-LANES]
-        ln1g, ln1b, outb, ln2g, ln2b, downb = (vecs[i, :rows] for i in range(6))
-        qvg, upg = vecs[6, : 2 * rows], vecs[7, : 4 * rows]
+        r3.fold()
+        r4.fold()
+        qkv_g, out_g, *vecs = finish_rest(
+            [by_bits(keep3, shards), by_bits(got3, shards)] + r3.came,
+            [by_bits(keep4, shards), by_bits(got4, shards)] + r4.came,
+            early,
+        )
+        ln1g, ln1b, outb, ln2g, ln2b, downb, qvg, upg = vecs
     else:
         layer_out = settle(lo_own, lo_back)
         input_grad = settle(ig_own, ig_back)
@@ -972,12 +1020,12 @@
         down_g, up_g, mid, last = total(keep1), total(send1), total(keep3), total(keep4)
         ln1g, ln1b, outb, ln2g, ln2b, downb = (total(vec[i]) for i in (0, 1, 4, 5, 6, 7))
         qvg, upg = total(vec[2:4].reshape(-1)), total(vec[8:12].reshape(-1))
-    out_g = mid[:, early:]
-    ca, cb = early // 3, last.shape[1] // 3
-    parts = []
-    for i in range(3):
-        parts += [mid[:, i * ca : (i + 1) * ca], last[:, i * cb : (i + 1) * cb]]
-    qkv_g = jnp.concatenate(parts, axis=1)
+        out_g = mid[:, early:]
+        ca, cb = early // 3, last.shape[1] // 3
+        parts = []
+        for i in range(3):
+            parts += [mid[:, i * ca : (i + 1) * ca], last[:, i * cb : (i + 1) * cb]]
+        qkv_g = jnp.concatenate(parts, axis=1)
     return (
         layer_out, input_grad, ln1g, ln1b, qkv_g, qvg, out_g, outb, ln2g, ln2b, up_g, upg,
         down_g, downb,

time: 167 us -> 157 us (0.940)
  other arithmetic: 18.5 us -> 10.8 us
  local copies, waits for them, and re-layouts: 14.2 us -> 11.5 us
  starting transfers between devices: 27.4 us -> 24.8 us
  waiting for transfers between devices: 30.9 us -> 32.7 us
    convert_element_type x14, other arithmetic: 15.6 us -> 9.76 us  [parts(): return add_up([p[1] for p in pieces]).astype(BF16)]
    ppermute x18, starting transfers between devices: 21.5 us -> 18.4 us  [exchange(): lax.ppermute(block, AXES, [(i, i ^ bit) for i, bit in enumerate(bits)])]
    unnamed x123 -> x120, local copies, waits for them, and re-layouts: 9.27 us -> 6.81 us
    pallas_call x0 -> x1, Pallas kernels: none -> 2.04 us  [finish_rest(): pl.pallas_call(partial(finish_rest_kernel, count=len(mid), early=early),...]
    add x2 -> x0, other arithmetic: 1.9 us -> none  [add_up(): total = total + t.astype(F32)]
    slice x4, local copies, waits for them, and re-layouts: 0.17 us -> 2.07 us  [halves(): lax.slice_in_dim(block, i, i + 1, axis=axis)]
    ppermute x18, waiting for transfers between devices: 26.4 us -> 28.2 us  [exchange(): lax.ppermute(block, AXES, [(i, i ^ bit) for i, bit in enumerate(bits)])]
  transfers between devices with their start and end apart: 23 -> 23, of which waited for: 9 -> 10; matrix products, arithmetic and copies ran while one was open for 13% -> 10% of each run, Pallas kernels for 29% -> 30%
where the time goes in v5:
time: 157 us; the launch traced here: 156 us
  Pallas kernels  74.8 us (48%)
  waiting for transfers between devices  32.7 us (21%)
  starting transfers between devices  24.8 us (16%)
  local copies, waits for them, and re-layouts  11.5 us (7%)
  other arithmetic  10.8 us (7%)
  between operations  1.57 us (1%)
    ppermute x18, waiting for transfers between devices, exchange(): lax.ppermute(block, AXES, [(i, i ^ bit) for i, bit in enumerate(bits)])  28.2 us
    pallas_call x1, Pallas kernels, mlp(): pl.pallas_call(partial(mlp_kernel, shards=shards), grid_spec=pltpu.Prefet...  25.2 us
    ppermute x18, starting transfers between devices, exchange(): lax.ppermute(block, AXES, [(i, i ^ bit) for i, bit in enumerate(bits)])  18.4 us
    pallas_call x1, Pallas kernels, attend_back(): pl.pallas_call(partial(attend_back_kernel, shard=width // shards if packe...  11.9 us
    pallas_call x1, Pallas kernels, attend(): pl.pallas_call(attend_kernel, grid=(pairs,), in_specs=[pl.BlockSpec((1, h...  11.3 us
    pallas_call x1, Pallas kernels, last_back(): pl.pallas_call(partial(last_back_kernel, shard=width // shards if packed...  10.3 us
    convert_element_type x14, other arithmetic, parts(): return add_up([p[1] for p in pieces]).astype(BF16)  9.76 us
    unnamed x120, local copies, waits for them, and re-layouts  6.81 us
  transfers between devices with their start and end apart: 23, of which 10 were waited for; matrix products, arithmetic and copies ran while one was open for 10% of the time, Pallas kernels for 30%

profile of v5, /device:TPU:0, one launch (start us, length us, event | category | flops | bytes accessed | tf_op | source)
XLA Modules:
  0.0 156.1 jit_solution(11864998163059532169)
XLA Ops:
  0.7 2.2 %fusion.3 = (bf16[2,140,768]{2,0,1:T(2,128)(2,1)S(1)}, bf16[2,140,768]{2,0,1:T(2,128)(2,1)S(1)}) fusion(bf16[4,140,768]{2,0,1:T(4,128)(2,1)} %param.20), kind=kLoop, calls=%fused_computation.36 | loop fusion | bytes 1720320 | tf_op jit(solution)/shard_map/slice | solution.py:907
  3.1 3.0 %collective-permute-start = (bf16[2,140,768]{2,1,0:T(8,128)(2,1)S(1)}, bf16[2,140,768]{2,1,0:T(8,128)(2,1)S(1)}, u32[]{:S(2)}, u32[]{:S(2)}) collective-permute-start(bf16[2,140,768]{2,1,0:T(8,128)(2,1)S(1)} %copy_select_fusion), channel_id=1, source_target_pairs={{0,1},{1,0},{2,3},{3,2},{4,5},{5,4},{6,7},{7,6},{8,9},{9,8},{10,11... | collective-permute-start | bytes 1290248 | tf_op jit(solution)/shard_map/ppermute | solution.py:891
  7.3 1.2 copy-done
  8.5 3.1 %norm_qkv.2 = (bf16[2,144,768]{2,1,0:T(8,128)(2,1)}, bf16[2,144,2304]{2,1,0:T(8,128)(2,1)}) custom-call(bf16[2,144,768]{2,1,0:T(8,128)(2,1)S(1)} %pad.13.x_ref.xo, f32[1,768]{1,0:T(1,128)S(1)} %reshape.196.g_ref.g1, f32[1,768]{1,0:T(1,128)S(1)} %reshape.197.b_ref, bf16[768,2304]{1,0:T(8,128)(2,1)S(1)} %copy-done, f32[2,1,768]{2,1,0:T(1,128)S(1)} %reshape.198.qvb_ref), custom_call_target="tpu_custom_call" | custom-call | flops 1019215872 | bytes 5750784 | tf_op jit(solution)/shard_map/norm_qkv/pallas_call | solution.py:131
  11.8 4.5 %collective-permute-done = bf16[2,140,768]{2,1,0:T(8,128)(2,1)S(1)} collective-permute-done((bf16[2,140,768]{2,1,0:T(8,128)(2,1)S(1)}, bf16[2,140,768]{2,1,0:T(8,128)(2,1)S(1)}, u32[]{:S(2)}, u32[]{:S(2)}) %collective-permute-start) | collective-permute-done | bytes 430112 | tf_op jit(solution)/shard_map/ppermute | solution.py:891
  16.3 1.7 %collective-permute-start.2 = (bf16[2,140,768]{2,1,0:T(8,128)(2,1)S(1)}, bf16[2,140,768]{2,1,0:T(8,128)(2,1)S(1)}, u32[]{:S(2)}, u32[]{:S(2)}) collective-permute-start(bf16[2,140,768]{2,1,0:T(8,128)(2,1)S(1)} %get-tuple-element.94), channel_id=1, source_target_pairs={{0,1},{1,0},{2,3},{3,2},{4,5},{5,4},{6,7},{7,6},{8,9},{9,8},{10,11... | collective-permute-start | bytes 1290248 | tf_op jit(solution)/shard_map/ppermute | solution.py:891
  18.4 2.8 %norm_qkv.3 = (bf16[2,144,768]{2,1,0:T(8,128)(2,1)}, bf16[2,144,2304]{2,1,0:T(8,128)(2,1)S(1)}) custom-call(bf16[2,144,768]{2,1,0:T(8,128)(2,1)S(1)} %pad.14.x_ref.xr, f32[1,768]{1,0:T(1,128)S(1)} %reshape.196.g_ref.g1, f32[1,768]{1,0:T(1,128)S(1)} %reshape.197.b_ref, bf16[768,2304]{1,0:T(8,128)(2,1)S(1)} %copy-done, f32[2,1,768]{2,1,0:T(1,128)S(1)} %reshape.198.qvb_ref), custom_call_target="tpu_custom_call" | custom-call | flops 1019215872 | bytes 5750784 | tf_op jit(solution)/shard_map/norm_qkv/pallas_call | solution.py:131
  21.2 11.3 %attend.1 = (bf16[2,2,144,768]{3,2,1,0:T(8,128)(2,1)}, f32[2,2,144,768]{3,2,1,0:T(8,128)}, bf16[2,2,144,768]{3,2,1,0:T(8,128)(2,1)S(1)}, bf16[2,6,576,288]{3,2,1,0:T(8,128)(2,1)}) custom-call(bf16[2,144,2304]{2,1,0:T(8,128)(2,1)S(1)} %copy-done.3, bf16[2,144,2304]{2,1,0:T(8,128)(2,1)S(1)} %get-tuple-element.90.qr, bf16[2,144,768]{2,1,0:T(8,128)(2,1)S(1)} %pad.13.x_ref.xo, ...), custom_call_target="tpu_custom_call" | custom-call | flops 2038431744 | bytes 11059200 | tf_op jit(solution)/shard_map/attend/pallas_call | solution.py:203
  32.5 25.2 %mlp.1 = (bf16[2,144,768]{2,1,0:T(8,128)(2,1)}, bf16[2,144,768]{2,1,0:T(8,128)(2,1)}, bf16[576,768]{1,0:T(8,128)(2,1)S(1)}, f32[1,768]{1,0:T(1,128)}, f32[576,76...) custom-call(s32[3]{0:T(128)S(1)} %pad_add_fusion.info, ...), custom_call_target="tpu_custom_call" | custom-call | flops 16307453952 | bytes 25165824 | tf_op jit(solution)/shard_map/mlp/pallas_call | solution.py:343
  57.9 3.2 %second_back.1 = (f32[2,288,768]{2,1,0:T(8,128)}, bf16[2,288,768]{2,1,0:T(8,128)(2,1)S(1)}, bf16[2,288,768]{2,1,0:T(8,128)(2,1)S(1)}, f32[8,768]{1,0:T(8,128)}) custom-call(f32[2,2,144,768]{3,2,1,0:T(8,128)S(1)} %bitcast.31, bf16[2,2,144,768]{3,2,1,0:T(8,128)(2,1)S(1)} %bitcast.32, f32[2,2,144,768]{3,2,1,0:T(8,128)S(1)} %copy-done.2, ...), custom_call_target="tpu_custom_call" | custom-call | flops 679477248 | bytes 10485760 | tf_op jit(solution)/shard_map/second_back/pallas_call | solution.py:463
  61.1 4.9 %collective-permute-done.3.got = bf16[8,384,768]{2,1,0:T(8,128)(2,1)S(1)} collective-permute-done((bf16[8,384,768]{2,1,0:T(8,128)(2,1)}, bf16[8,384,768]{2,1,0:T(8,128)(2,1)S(1)}, u32[]{:S(2)}, u32[]{:S(2)}) %collective-permute-start.3) | collective-permute-done | bytes 4718624 | tf_op jit(solution)/shard_map/ppermute | solution.py:739
  66.4 1.6 %collective-permute-start.4 = (bf16[1,2,2,384,512]{4,3,2,1,0:T(8,128)(2,1)S(1)}, bf16[1,2,2,384,512]{4,3,2,1,0:T(8,128)(2,1)S(1)}, u32[]{:S(2)}, u32[]{:S(2)}) collective-permute-start(bf16[1,2,2,384,512]{4,3,2,1,0:T(8,128)(2,1)S(1)} %add_convert_fusion), channel_id=1, source_target_pairs={{0,4},{1,5},{2,10},{3,11},{4,0},{5,1},{6,14},{7,15},{8,12},{9,13},... | collective-permute-start | bytes 4718600 | tf_op jit(solution)/shard_map/ppermute | solution.py:739
  69.1 11.9 %attend_back.1 = (bf16[576,1536]{1,0:T(8,128)(2,1)S(1)}, bf16[768,576]{1,0:T(8,128)(2,1)S(1)}, f32[8,128]{1,0:T(8,128)}, bf16[384,2304]{1,0:T(8,128)(2,1)}, bf16[384,2304]{1,0:T(8,128)(2,1)}) custom-call(s32[32]{0:T(128)S(1)} %get-tuple-element.114.inv, bf16[2,288,768]{2,1,0:T(8,128)(2,1)S(1)} %get-tuple-element.103.br, ...), custom_call_target="tpu_custom_call" | custom-call | flops 4756340736 | bytes 16777216 | tf_op jit(solution)/shard_map/attend_back/pallas_call | solution.py:530
  81.2 6.4 %collective-permute-done.5.q1 = bf16[2,2,1,384,256]{4,3,2,1,0:T(8,128)(2,1)S(1)} collective-permute-done((bf16[2,2,1,384,256]{4,3,2,1,0:T(8,128)(2,1)S(1)}, bf16[2,2,1,384,256]{4,3,2,1,0:T(8,128)(2,1)S(1)}, u32[]{:S(2)}, u32[]{:S(2)}) %collective-permute-start.5) | collective-permute-done | bytes 786464 | tf_op jit(solution)/shard_map/ppermute | solution.py:739
  88.0 0.9 collective-permute-start.6
  89.6 1.6 %collective-permute-start.7 = (bf16[1,2,1,384,256]{4,3,2,1,0:T(8,128)(2,1)S(1)}, bf16[1,2,1,384,256]{4,3,2,1,0:T(8,128)(2,1)S(1)}, u32[]{:S(2)}, u32[]{:S(2)}) collective-permute-start(bf16[1,2,1,384,256]{4,3,2,1,0:T(8,128)(2,1)S(1)} %add_convert_fusion.6), channel_id=1, source_target_pairs={{0,4},{1,5},{2,10},{3,11},{4,0},{5,1},{6,14},{7,15},{8,12},{9,13},... | collective-permute-start | bytes 1179656 | tf_op jit(solution)/shard_map/ppermute | solution.py:739
  91.2 10.3 %last_back.1 = (bf16[2,144,768]{2,1,0:T(8,128)(2,1)}, bf16[2,144,768]{2,1,0:T(8,128)(2,1)}, f32[16,768]{1,0:T(8,128)}, bf16[384,896]{1,0:T(8,128)(2,1)}, bf16[384,896]{1,0:T(8,128)(2,1)}) custom-call(s32[32]{0:T(128)S(1)} %get-tuple-element.114.inv, bf16[2,144,2304]{2,1,0:T(8,128)(2,1)S(1)} %copy-done.3, bf16[2,144,2304]{2,1,0:T(8,128)(2,1)S(1)} %get-tuple-element.90.qr, ...), custom_call_target="tpu_custom_call" | custom-call | flops 4076863488 | bytes 16777216 | tf_op jit(solution)/shard_map/last_back/pallas_call | solution.py:659
  101.7 2.6 %collective-permute-done.6.p2 = bf16[1,1,2,384,512]{4,3,2,1,0:T(8,128)(2,1)S(1)} collective-permute-done((bf16[1,1,2,384,512]{4,3,2,1,0:T(8,128)(2,1)S(1)}, bf16[1,1,2,384,512]{4,3,2,1,0:T(8,128)(2,1)S(1)}, u32[]{:S(2)}, u32[]{:S(2)}) %collective-permute-start.6) | collective-permute-done | bytes 786464 | tf_op jit(solution)/shard_map/ppermute | solution.py:739
  104.6 1.1 add_convert_fusion.1
  105.7 1.0 collective-permute-start.14
  107.4 1.0 slice.317
  108.4 1.3 collective-permute-start.12
  109.7 0.9 add_convert_fusion.7
  110.6 1.0 slice.320
  111.6 1.0 collective-permute-start.16
  112.7 3.5 %collective-permute-done.12.q3 = bf16[1,1,1,384,256]{4,3,2,1,0:T(8,128)(2,1)S(1)} collective-permute-done((bf16[1,1,1,384,256]{4,3,2,1,0:T(8,128)(2,1)S(1)}, bf16[1,1,1,384,256]{4,3,2,1,0:T(8,128)(2,1)S(1)}, u32[]{:S(2)}, u32[]{:S(2)}) %collective-permute-start.12) | collective-permute-done | bytes 196640 | tf_op jit(solution)/shard_map/ppermute | solution.py:739
  116.9 3.0 %part_pairs.1 = (f32[192,768]{1,0:T(8,128)}, bf16[192,768]{1,0:T(8,128)(2,1)}) custom-call(bf16[8,384,768]{2,1,0:T(8,128)(2,1)} %get-tuple-element.96.keep, bf16[8,384,768]{2,1,0:T(8,128)(2,1)} %copy-done.14, bf16[1,2,2,384,512]{4,3,2,1,0:T(8,128)(2,1)} %copy-done.17, bf16[1,1,2,384,512]{4,3,2,1,0:T(8,128)(2,1)} %copy-done.26, ...), custom_call_target="tpu_custom_call" | custom-call | bytes 4194304 | tf_op jit(solution)/shard_map/part_pairs/pallas_call | solution.py:803
  119.9 1.1 collective-permute-done.14.refs_2_
  121.1 1.2 add_convert_fusion.4
  122.2 0.9 collective-permute-start.15
  123.2 2.8 %collective-permute-start.22 = (bf16[192,768]{1,0:T(8,128)(2,1)S(1)}, bf16[192,768]{1,0:T(8,128)(2,1)S(1)}, u32[]{:S(2)}, u32[]{:S(2)}) collective-permute-start(bf16[192,768]{1,0:T(8,128)(2,1)S(1)} %copy-done.54), channel_id=1, source_target_pairs={{0,16},{1,17},{2,18},{3,19},{4,20},{5,21},{6,22},{7,23},{8,24},{9,... | collective-permute-start | bytes 884744 | tf_op jit(solution)/shard_map/ppermute | solution.py:739
  126.0 1.0 collective-permute-start.13
  127.0 1.0 add_convert_fusion.10
  128.0 1.1 collective-permute-start.18
  129.1 6.3 %collective-permute-done.15.refs_3_ = bf16[1,1,2,2,24,2304]{5,4,3,2,1,0:T(8,128)(2,1)S(1)} collective-permute-done((bf16[1,1,2,2,24,2304]{5,4,3,2,1,0:T(8,128)(2,1)S(1)}, bf16[1,1,2,2,24,2304]{5,4,3,2,1,0:T(8,128)(2,1)S(1)}, u32[]{:S(2)}, u32[]{:S(2)}) %collective-permute-start.15) | collective-permute-done | bytes 442400 | tf_op jit(solution)/shard_map/ppermute | solution.py:739
  135.4 1.2 add_convert_fusion.8
  136.7 0.9 collective-permute-start.17
  137.5 1.2 collective-permute-done.18.refs_9_
  138.8 1.0 add_convert_fusion.12
  139.8 0.9 collective-permute-start.20
  140.6 2.0 %collective-permute-done.17.refs_4_ = bf16[1,1,1,2,24,2304]{5,4,3,2,1,0:T(8,128)(2,1)S(1)} collective-permute-done((bf16[1,1,1,2,24,2304]{5,4,3,2,1,0:T(8,128)(2,1)S(1)}, bf16[1,1,1,2,24,2304]{5,4,3,2,1,0:T(8,128)(2,1)S(1)}, u32[]{:S(2)}, u32[]{:S(2)}) %collective-permute-start.17) | collective-permute-done | bytes 221216 | tf_op jit(solution)/shard_map/ppermute | solution.py:739
  142.7 1.1 fusion
  144.7 0.9 fusion.1
  145.5 2.3 %collective-permute-start.21 = (bf16[24,896]{1,0:T(8,128)(2,1)S(1)}, bf16[24,896]{1,0:T(8,128)(2,1)S(1)}, u32[]{:S(2)}, u32[]{:S(2)}) collective-permute-start(bf16[24,896]{1,0:T(8,128)(2,1)S(1)} %fusion.1), channel_id=1, source_target_pairs={{0,16},{1,17},{2,18},{3,19},{4,20},{5,21},{6,22},{7,23},{8,24},{9,... | collective-permute-start | bytes 129032 | tf_op jit(solution)/shard_map/ppermute | solution.py:739
  147.8 1.3 copy.58
  149.2 1.3 copy.59
  151.2 2.0 %finish_pair.1 = (f32[96,768]{1,0:T(8,128)}, f32[24,3072]{1,0:T(8,128)}) custom-call(f32[192,768]{1,0:T(8,128)} %get-tuple-element.150.mine, bf16[192,768]{1,0:T(8,128)(2,1)} %copy-done.34), custom_call_target="tpu_custom_call" | custom-call | bytes 2097152 | tf_op jit(solution)/shard_map/finish_pair/pallas_call | solution.py:871
  153.9 2.0 %finish_rest.1 = (f32[24,2304]{1,0:T(8,128)}, f32[24,768]{1,0:T(8,128)}, f32[24]{0:T(128)}, f32[24]{0:T(128)}, f32[24]{0:T(128)}, /*index=5*/f32[24]{0:T(128)}, ...) custom-call(bf16[2,2,2,2,24,2304]{5,4,3,2,1,0:T(8,128)(2,1)} %bitcast.49, bf16[2,2,2,2,24,2304]{5,4,3,2,1,0:T(8,128)(2,1)} %bitcast.50, ...), custom_call_target="tpu_custom_call" | custom-call | bytes 2097152 | tf_op jit(solution)/shard_map/finish_rest/pallas_call | solution.py:845
  (179 shorter events, 8.9 us)
Async XLA Ops:
  3.1 13.2 %collective-permute-start = (bf16[2,140,768]{2,1,0:T(8,128)(2,1)S(1)}, bf16[2,140,768]{2,1,0:T(8,128)(2,1)S(1)}, u32[]{:S(2)}, u32[]{:S(2)}) collective-permute-start(bf16[2,140,768]{2,1,0:T(8,128)(2,1)S(1)} %copy_select_fusion), channel_id=1, source_target_pairs={{0,1},{1,0},{2,3},{3,2},{4,5},{5,4},{6,7},{7,6},{8,9},{9,8},{10,11... | collective-permute-start | bytes 1290248 | tf_op jit(solution)/shard_map/ppermute | solution.py:891
  6.2 12.0 %collective-permute-start.1 = (bf16[2,140]{1,0:T(2,128)(2,1)S(1)}, bf16[2,140]{1,0:T(2,128)(2,1)S(1)}, u32[]{:S(2)}, u32[]{:S(2)}) collective-permute-start(bf16[2,140]{1,0:T(2,128)(2,1)S(1)} %get-tuple-element.91), channel_id=1, source_target_pairs={{0,1},{1,0},{2,3},{3,2},{4,5},{5,4},{6,7},{7,6},{8,9},{9,8},{10,11... | collective-permute-start | bytes 1688 | tf_op jit(solution)/shard_map/ppermute | solution.py:891
  11.7 6.5 %copy-start.44 = (f32[768]{0:T(1024)S(1)}, f32[768]{0:T(1024)}, u32[]{:S(2)}) copy-start(f32[768]{0:T(1024)} %param.30) | copy-start | bytes 9220
  11.7 6.5 %copy-start.45 = (f32[768]{0:T(1024)S(1)}, f32[768]{0:T(1024)}, u32[]{:S(2)}) copy-start(f32[768]{0:T(1024)} %param.34) | copy-start | bytes 9220
  16.3 16.2 %collective-permute-start.2 = (bf16[2,140,768]{2,1,0:T(8,128)(2,1)S(1)}, bf16[2,140,768]{2,1,0:T(8,128)(2,1)S(1)}, u32[]{:S(2)}, u32[]{:S(2)}) collective-permute-start(bf16[2,140,768]{2,1,0:T(8,128)(2,1)S(1)} %get-tuple-element.94), channel_id=1, source_target_pairs={{0,1},{1,0},{2,3},{3,2},{4,5},{5,4},{6,7},{7,6},{8,9},{9,8},{10,11... | collective-permute-start | bytes 1290248 | tf_op jit(solution)/shard_map/ppermute | solution.py:891
  18.4 14.1 %slice-start.2 = ((s8[4718592]{0:T(1024)(128)(4,1)}), s8[4194304]{0:T(1024)(128)(4,1)S(1)}, s32[]{:S(2)}) async-start(s8[4718592]{0:T(1024)(128)(4,1)} %bitcast.33), calls=%async_computation.2 | async-start | bytes 8388608
  21.2 11.3 %slice-start.3 = ((s8[4718592]{0:T(1024)(128)(4,1)}), s8[524288]{0:T(1024)(128)(4,1)S(1)}, s32[]{:S(2)}) async-start(s8[4718592]{0:T(1024)(128)(4,1)} %bitcast.33), calls=%async_computation.3 | async-start | bytes 1048576
  21.2 11.3 %copy-start.8 = (bf16[3072,768]{1,0:T(8,128)(2,1)S(1)}, bf16[3072,768]{1,0:T(8,128)(2,1)}, u32[]{:S(2)}) copy-start(bf16[3072,768]{1,0:T(8,128)(2,1)} %down.1) | copy-start | bytes 14155780
  21.2 11.3 %copy-start.11 = (f32[3072]{0:T(1024)S(1)}, f32[3072]{0:T(1024)}, u32[]{:S(2)}) copy-start(f32[3072]{0:T(1024)} %param.32) | copy-start | bytes 36868
  32.4 36.4 %slice-start = ((s8[5308416]{0:T(1024)(128)(4,1)}), s8[4194304]{0:T(1024)(128)(4,1)S(1)}, s32[]{:S(2)}) async-start(s8[5308416]{0:T(1024)(128)(4,1)} %bitcast.28), calls=%async_computation | async-start | bytes 8388608
  32.5 25.3 %copy-start.2 = (f32[2,2,144,768]{3,2,1,0:T(8,128)S(1)}, f32[2,2,144,768]{3,2,1,0:T(8,128)}, u32[]{:S(2)}) copy-start(f32[2,2,144,768]{3,2,1,0:T(8,128)} %get-tuple-element.93.att) | copy-start | bytes 5308420
  32.5 36.3 %slice-start.1 = ((s8[5308416]{0:T(1024)(128)(4,1)}), s8[1114112]{0:T(1024)(128)(4,1)S(1)}, s32[]{:S(2)}) async-start(s8[5308416]{0:T(1024)(128)(4,1)} %bitcast.28), calls=%async_computation.1 | async-start | bytes 2228224
  57.8 8.2 %collective-permute-start.3 = (bf16[8,384,768]{2,1,0:T(8,128)(2,1)}, bf16[8,384,768]{2,1,0:T(8,128)(2,1)S(1)}, u32[]{:S(2)}, u32[]{:S(2)}) collective-permute-start(bf16[8,384,768]{2,1,0:T(8,128)(2,1)} %get-tuple-element.97), channel_id=1, source_target_pairs={{0,2},{1,3},{2,0},{3,1},{4,6},{5,7},{6,4},{7,5},{8,10},{9,11},{10,... | collective-permute-start | bytes 14155784 | tf_op jit(solution)/shard_map/ppermute | solution.py:739
  57.9 8.1 %copy-start.13 = (bf16[8,384,768]{2,1,0:T(8,128)(2,1)S(1)}, bf16[8,384,768]{2,1,0:T(8,128)(2,1)}, u32[]{:S(2)}) copy-start(bf16[8,384,768]{2,1,0:T(8,128)(2,1)} %get-tuple-element.96.keep) | copy-start | bytes 14155780
  66.0 38.4 %copy-start.14 = (bf16[8,384,768]{2,1,0:T(8,128)(2,1)}, bf16[8,384,768]{2,1,0:T(8,128)(2,1)S(1)}, u32[]{:S(2)}) copy-start(bf16[8,384,768]{2,1,0:T(8,128)(2,1)S(1)} %collective-permute-done.3.got) | copy-start | bytes 14155780
  66.4 21.2 %collective-permute-start.4 = (bf16[1,2,2,384,512]{4,3,2,1,0:T(8,128)(2,1)S(1)}, bf16[1,2,2,384,512]{4,3,2,1,0:T(8,128)(2,1)S(1)}, u32[]{:S(2)}, u32[]{:S(2)}) collective-permute-start(bf16[1,2,2,384,512]{4,3,2,1,0:T(8,128)(2,1)S(1)} %add_convert_fusion), channel_id=1, source_target_pairs={{0,4},{1,5},{2,10},{3,11},{4,0},{5,1},{6,14},{7,15},{8,12},{9,13},... | collective-permute-start | bytes 4718600 | tf_op jit(solution)/shard_map/ppermute | solution.py:739
  68.2 19.4 %collective-permute-start.5 = (bf16[2,2,1,384,256]{4,3,2,1,0:T(8,128)(2,1)S(1)}, bf16[2,2,1,384,256]{4,3,2,1,0:T(8,128)(2,1)S(1)}, u32[]{:S(2)}, u32[]{:S(2)}) collective-permute-start(bf16[2,2,1,384,256]{4,3,2,1,0:T(8,128)(2,1)S(1)} %add_convert_fusion.3), channel_id=1, source_target_pairs={{0,1},{1,0},{2,3},{3,2},{4,5},{5,4},{6,7},{7,6},{8,9},{9,8},{10,11... | collective-permute-start | bytes 2359304 | tf_op jit(solution)/shard_map/ppermute | solution.py:739
  81.0 7.9 %copy-start.53 = (bf16[2,144,768]{2,1,0:T(8,128)(2,1)S(1)}, bf16[2,144,768]{2,1,0:T(8,128)(2,1)}, u32[]{:S(2)}) copy-start(bf16[2,144,768]{2,1,0:T(8,128)(2,1)} %get-tuple-element.112) | copy-start | bytes 1327108
  81.0 10.1 %copy-start.1 = (f32[2,288,768]{2,1,0:T(8,128)S(1)}, f32[2,288,768]{2,1,0:T(8,128)}, u32[]{:S(2)}) copy-start(f32[2,288,768]{2,1,0:T(8,128)} %get-tuple-element.117.ga) | copy-start | bytes 5308420
  81.0 10.1 %copy-start.5 = (f32[8,768]{1,0:T(8,128)S(1)}, f32[8,768]{1,0:T(8,128)}, u32[]{:S(2)}) copy-start(f32[8,768]{1,0:T(8,128)} %get-tuple-element.100.v2) | copy-start | bytes 73732
  81.0 10.1 %copy-start.6 = (f32[1,3072]{1,0:T(1,128)S(1)}, f32[1,3072]{1,0:T(1,128)}, u32[]{:S(2)}) copy-start(f32[1,3072]{1,0:T(1,128)} %get-tuple-element.118.upbg) | copy-start | bytes 36868
  81.0 10.1 %copy-start.7 = (f32[1,768]{1,0:T(1,128)S(1)}, f32[1,768]{1,0:T(1,128)}, u32[]{:S(2)}) copy-start(f32[1,768]{1,0:T(1,128)} %get-tuple-element.119.dbg) | copy-start | bytes 9220
  81.0 20.5 %collective-permute-start.9 = (bf16[384,2304]{1,0:T(8,128)(2,1)}, bf16[384,2304]{1,0:T(8,128)(2,1)S(1)}, u32[]{:S(2)}, u32[]{:S(2)}) collective-permute-start(bf16[384,2304]{1,0:T(8,128)(2,1)} %get-tuple-element.113), channel_id=1, source_target_pairs={{0,2},{1,3},{2,0},{3,1},{4,6},{5,7},{6,4},{7,5},{8,10},{9,11},{10,... | collective-permute-start | bytes 5308424 | tf_op jit(solution)/shard_map/ppermute | solution.py:739
  87.7 16.6 %copy-start.25 = (bf16[2,2,1,384,256]{4,3,2,1,0:T(8,128)(2,1)}, bf16[2,2,1,384,256]{4,3,2,1,0:T(8,128)(2,1)S(1)}, u32[]{:S(2)}) copy-start(bf16[2,2,1,384,256]{4,3,2,1,0:T(8,128)(2,1)S(1)} %collective-permute-done.5.q1) | copy-start | bytes 2359300
  87.7 16.7 %copy-start.17 = (bf16[1,2,2,384,512]{4,3,2,1,0:T(8,128)(2,1)}, bf16[1,2,2,384,512]{4,3,2,1,0:T(8,128)(2,1)S(1)}, u32[]{:S(2)}) copy-start(bf16[1,2,2,384,512]{4,3,2,1,0:T(8,128)(2,1)S(1)} %collective-permute-done.4.p1) | copy-start | bytes 4718596
  88.0 16.3 %collective-permute-start.6 = (bf16[1,1,2,384,512]{4,3,2,1,0:T(8,128)(2,1)S(1)}, bf16[1,1,2,384,512]{4,3,2,1,0:T(8,128)(2,1)S(1)}, u32[]{:S(2)}, u32[]{:S(2)}) collective-permute-start(bf16[1,1,2,384,512]{4,3,2,1,0:T(8,128)(2,1)S(1)} %add_convert_fusion.2), channel_id=1, source_target_pairs={{0,8},{1,9},{2,6},{3,7},{4,12},{5,13},{6,2},{7,3},{8,0},{9,1},{10,... | collective-permute-start | bytes 2359304 | tf_op jit(solution)/shard_map/ppermute | solution.py:739
  88.9 12.7 %collective-permute-start.8 = (bf16[2,144,768]{2,1,0:T(8,128)(2,1)S(1)}, bf16[2,144,768]{2,1,0:T(8,128)(2,1)S(1)}, u32[]{:S(2)}, u32[]{:S(2)}) collective-permute-start(bf16[2,144,768]{2,1,0:T(8,128)(2,1)S(1)} %copy-done.53), channel_id=1, source_target_pairs={{0,1},{1,0},{2,3},{3,2},{4,5},{5,4},{6,7},{7,6},{8,9},{9,8},{10,11... | collective-permute-start | bytes 1327112 | tf_op jit(solution)/shard_map/ppermute | solution.py:891
  89.6 12.1 %collective-permute-start.7 = (bf16[1,2,1,384,256]{4,3,2,1,0:T(8,128)(2,1)S(1)}, bf16[1,2,1,384,256]{4,3,2,1,0:T(8,128)(2,1)S(1)}, u32[]{:S(2)}, u32[]{:S(2)}) collective-permute-start(bf16[1,2,1,384,256]{4,3,2,1,0:T(8,128)(2,1)S(1)} %add_convert_fusion.6), channel_id=1, source_target_pairs={{0,4},{1,5},{2,10},{3,11},{4,0},{5,1},{6,14},{7,15},{8,12},{9,13},... | collective-permute-start | bytes 1179656 | tf_op jit(solution)/shard_map/ppermute | solution.py:739
  101.5 8.2 %collective-permute-start.11 = (bf16[384,896]{1,0:T(8,128)(2,1)}, bf16[384,896]{1,0:T(8,128)(2,1)S(1)}, u32[]{:S(2)}, u32[]{:S(2)}) collective-permute-start(bf16[384,896]{1,0:T(8,128)(2,1)} %get-tuple-element.125), channel_id=1, source_target_pairs={{0,2},{1,3},{2,0},{3,1},{4,6},{5,7},{6,4},{7,5},{8,10},{9,11},{10,... | collective-permute-start | bytes 2064392 | tf_op jit(solution)/shard_map/ppermute | solution.py:739
  101.6 9.0 %copy-start.16 = (bf16[384,2304]{1,0:T(8,128)(2,1)}, bf16[384,2304]{1,0:T(8,128)(2,1)S(1)}, u32[]{:S(2)}) copy-start(bf16[384,2304]{1,0:T(8,128)(2,1)S(1)} %collective-permute-done.9) | copy-start | bytes 5308420
  105.7 15.3 %collective-permute-start.14 = (bf16[1,2,2,2,24,2304]{5,4,3,2,1,0:T(8,128)(2,1)}, bf16[1,2,2,2,24,2304]{5,4,3,2,1,0:T(8,128)(2,1)}, u32[]{:S(2)}, u32[]{:S(2)}) collective-permute-start(bf16[1,2,2,2,24,2304]{5,4,3,2,1,0:T(8,128)(2,1)} %bitcast.9), channel_id=1, source_target_pairs={{0,4},{1,5},{2,10},{3,11},{4,0},{5,1},{6,14},{7,15},{8,12},{9,13},... | collective-permute-start | bytes 2654216 | tf_op jit(solution)/shard_map/ppermute | solution.py:739
  106.7 10.2 %collective-permute-start.10 = (bf16[1,1,1,384,512]{4,3,2,1,0:T(8,128)(2,1)S(1)}, bf16[1,1,1,384,512]{4,3,2,1,0:T(8,128)(2,1)}, u32[]{:S(2)}, u32[]{:S(2)}) collective-permute-start(bf16[1,1,1,384,512]{4,3,2,1,0:T(8,128)(2,1)S(1)} %add_convert_fusion.5), channel_id=1, source_target_pairs={{0,1},{1,0},{2,3},{3,2},{4,5},{5,4},{6,7},{7,6},{8,9},{9,8},{10,11... | collective-permute-start | bytes 1179656 | tf_op jit(solution)/shard_map/ppermute | solution.py:739
  108.4 7.8 %collective-permute-start.12 = (bf16[1,1,1,384,256]{4,3,2,1,0:T(8,128)(2,1)S(1)}, bf16[1,1,1,384,256]{4,3,2,1,0:T(8,128)(2,1)S(1)}, u32[]{:S(2)}, u32[]{:S(2)}) collective-permute-start(bf16[1,1,1,384,256]{4,3,2,1,0:T(8,128)(2,1)S(1)} %add_convert_fusion.9), channel_id=1, source_target_pairs={{0,8},{1,9},{2,6},{3,7},{4,12},{5,13},{6,2},{7,3},{8,0},{9,1},{10,... | collective-permute-start | bytes 589832 | tf_op jit(solution)/shard_map/ppermute | solution.py:739
  111.6 15.5 %collective-permute-start.16 = (bf16[1,2,2,2,24,896]{5,4,3,2,1,0:T(8,128)(2,1)}, bf16[1,2,2,2,24,896]{5,4,3,2,1,0:T(8,128)(2,1)}, u32[]{:S(2)}, u32[]{:S(2)}) collective-permute-start(bf16[1,2,2,2,24,896]{5,4,3,2,1,0:T(8,128)(2,1)} %bitcast.10), channel_id=1, source_target_pairs={{0,4},{1,5},{2,10},{3,11},{4,0},{5,1},{6,14},{7,15},{8,12},{9,13},... | collective-permute-start | bytes 1032200 | tf_op jit(solution)/shard_map/ppermute | solution.py:739
  112.7 8.3 %copy-start.19 = (bf16[192,2304]{1,0:T(8,128)(2,1)S(1)}, bf16[192,2304]{1,0:T(8,128)(2,1)}, u32[]{:S(2)}) copy-start(bf16[192,2304]{1,0:T(8,128)(2,1)} %slice.317) | copy-start | bytes 2654212
  112.7 8.3 %copy-start.20 = (bf16[192,2304]{1,0:T(8,128)(2,1)S(1)}, bf16[192,2304]{1,0:T(8,128)(2,1)}, u32[]{:S(2)}) copy-start(bf16[192,2304]{1,0:T(8,128)(2,1)} %slice.320) | copy-start | bytes 2654212
  122.2 13.2 %collective-permute-start.15 = (bf16[1,1,2,2,24,2304]{5,4,3,2,1,0:T(8,128)(2,1)S(1)}, bf16[1,1,2,2,24,2304]{5,4,3,2,1,0:T(8,128)(2,1)S(1)}, u32[]{:S(2)}, u32[]{:S(2)}) collective-permute-start(bf16[1,1,2,2,24,2304]{5,4,3,2,1,0:T(8,128)(2,1)S(1)} %add_convert_fusion.4), channel_id=1, source_target_pairs={{0,8},{1,9},{2,6},{3,7},{4,12},{5,13},{6,2},{7,3},{8,0},{9,1},{10,... | collective-permute-start | bytes 1327112 | tf_op jit(solution)/shard_map/ppermute | solution.py:739
  123.2 21.3 %copy-start.32 = (bf16[2,144,768]{2,1,0:T(8,128)(2,1)S(1)}, bf16[2,144,768]{2,1,0:T(8,128)(2,1)}, u32[]{:S(2)}) copy-start(bf16[2,144,768]{2,1,0:T(8,128)(2,1)} %get-tuple-element.120) | copy-start | bytes 1327108
  123.2 27.3 %collective-permute-start.22 = (bf16[192,768]{1,0:T(8,128)(2,1)S(1)}, bf16[192,768]{1,0:T(8,128)(2,1)S(1)}, u32[]{:S(2)}, u32[]{:S(2)}) collective-permute-start(bf16[192,768]{1,0:T(8,128)(2,1)S(1)} %copy-done.54), channel_id=1, source_target_pairs={{0,16},{1,17},{2,18},{3,19},{4,20},{5,21},{6,22},{7,23},{8,24},{9,... | collective-permute-start | bytes 884744 | tf_op jit(solution)/shard_map/ppermute | solution.py:739
  126.0 18.5 %collective-permute-start.13 = (bf16[2,144,768]{2,1,0:T(8,128)(2,1)S(1)}, bf16[2,144,768]{2,1,0:T(8,128)(2,1)S(1)}, u32[]{:S(2)}, u32[]{:S(2)}) collective-permute-start(bf16[2,144,768]{2,1,0:T(8,128)(2,1)S(1)} %copy-done.52), channel_id=1, source_target_pairs={{0,1},{1,0},{2,3},{3,2},{4,5},{5,4},{6,7},{7,6},{8,9},{9,8},{10,11... | collective-permute-start | bytes 1327112 | tf_op jit(solution)/shard_map/ppermute | solution.py:891
  128.0 10.7 %collective-permute-start.18 = (bf16[1,1,2,2,24,896]{5,4,3,2,1,0:T(8,128)(2,1)S(1)}, bf16[1,1,2,2,24,896]{5,4,3,2,1,0:T(8,128)(2,1)S(1)}, u32[]{:S(2)}, u32[]{:S(2)}) collective-permute-start(bf16[1,1,2,2,24,896]{5,4,3,2,1,0:T(8,128)(2,1)S(1)} %add_convert_fusion.10), channel_id=1, source_target_pairs={{0,8},{1,9},{2,6},{3,7},{4,12},{5,13},{6,2},{7,3},{8,0},{9,1},{10,... | collective-permute-start | bytes 516104 | tf_op jit(solution)/shard_map/ppermute | solution.py:739
  135.4 9.1 %copy-start.27 = (bf16[1,1,2,2,24,2304]{5,4,3,2,1,0:T(8,128)(2,1)}, bf16[1,1,2,2,24,2304]{5,4,3,2,1,0:T(8,128)(2,1)S(1)}, u32[]{:S(2)}) copy-start(bf16[1,1,2,2,24,2304]{5,4,3,2,1,0:T(8,128)(2,1)S(1)} %collective-permute-done.15.refs_3_) | copy-start | bytes 1327108
  136.7 6.0 %collective-permute-start.17 = (bf16[1,1,1,2,24,2304]{5,4,3,2,1,0:T(8,128)(2,1)S(1)}, bf16[1,1,1,2,24,2304]{5,4,3,2,1,0:T(8,128)(2,1)S(1)}, u32[]{:S(2)}, u32[]{:S(2)}) collective-permute-start(bf16[1,1,1,2,24,2304]{5,4,3,2,1,0:T(8,128)(2,1)S(1)} %add_convert_fusion.8), channel_id=1, source_target_pairs={{0,1},{1,0},{2,3},{3,2},{4,5},{5,4},{6,7},{7,6},{8,9},{9,8},{10,11... | collective-permute-start | bytes 663560 | tf_op jit(solution)/shard_map/ppermute | solution.py:739
  138.8 10.4 %copy-start.30 = (bf16[1,1,2,2,24,896]{5,4,3,2,1,0:T(8,128)(2,1)}, bf16[1,1,2,2,24,896]{5,4,3,2,1,0:T(8,128)(2,1)S(1)}, u32[]{:S(2)}) copy-start(bf16[1,1,2,2,24,896]{5,4,3,2,1,0:T(8,128)(2,1)S(1)} %collective-permute-done.18.refs_9_) | copy-start | bytes 516100
  139.8 4.9 %collective-permute-start.20 = (bf16[1,1,1,2,24,896]{5,4,3,2,1,0:T(8,128)(2,1)S(1)}, bf16[1,1,1,2,24,896]{5,4,3,2,1,0:T(8,128)(2,1)S(1)}, u32[]{:S(2)}, u32[]{:S(2)}) collective-permute-start(bf16[1,1,1,2,24,896]{5,4,3,2,1,0:T(8,128)(2,1)S(1)} %add_convert_fusion.12), channel_id=1, source_target_pairs={{0,1},{1,0},{2,3},{3,2},{4,5},{5,4},{6,7},{7,6},{8,9},{9,8},{10,11... | collective-permute-start | bytes 258056 | tf_op jit(solution)/shard_map/ppermute | solution.py:739
  142.7 6.5 %copy-start.31 = (bf16[1,1,1,2,24,2304]{5,4,3,2,1,0:T(8,128)(2,1)}, bf16[1,1,1,2,24,2304]{5,4,3,2,1,0:T(8,128)(2,1)S(1)}, u32[]{:S(2)}) copy-start(bf16[1,1,1,2,24,2304]{5,4,3,2,1,0:T(8,128)(2,1)S(1)} %collective-permute-done.17.refs_4_) | copy-start | bytes 663556
  143.7 9.5 %collective-permute-start.19 = (bf16[24,2304]{1,0:T(8,128)(2,1)S(1)}, bf16[24,2304]{1,0:T(8,128)(2,1)S(1)}, u32[]{:S(2)}, u32[]{:S(2)}) collective-permute-start(bf16[24,2304]{1,0:T(8,128)(2,1)S(1)} %fusion), channel_id=1, source_target_pairs={{0,16},{1,17},{2,18},{3,19},{4,20},{5,21},{6,22},{7,23},{8,24},{9,... | collective-permute-start | bytes 331784 | tf_op jit(solution)/shard_map/ppermute | solution.py:739
  145.5 7.7 %collective-permute-start.21 = (bf16[24,896]{1,0:T(8,128)(2,1)S(1)}, bf16[24,896]{1,0:T(8,128)(2,1)S(1)}, u32[]{:S(2)}, u32[]{:S(2)}) collective-permute-start(bf16[24,896]{1,0:T(8,128)(2,1)S(1)} %fusion.1), channel_id=1, source_target_pairs={{0,16},{1,17},{2,18},{3,19},{4,20},{5,21},{6,22},{7,23},{8,24},{9,... | collective-permute-start | bytes 129032 | tf_op jit(solution)/shard_map/ppermute | solution.py:739
  (34 other events, 113.1 us)

commit v6 on v5

--- a/solution.py
+++ b/solution.py
@@ -997,7 +997,7 @@
         r2.fold()
         mine1, sent = part_pairs(keep1, whole1, r1.came, r2.came, tall, rows)
         got1 = exchange(sent, 3, shards)
-        ig_back = swap_sides(after(ig_far, sent))
+        ig_back = swap_sides(after(ig_far, r1.came[-1]))
         for r in (r3, r4, r3, r4, r3):
             r.hold(sent)
             sent = r.step()

time: 157 us -> 157 us (level)
  no operation moved by 1% of the time
where the time goes in v6:
time: 157 us; the launch traced here: 156 us
  Pallas kernels  74.8 us (48%)
  waiting for transfers between devices  32.7 us (21%)
  starting transfers between devices  24.8 us (16%)
  local copies, waits for them, and re-layouts  11.5 us (7%)
  other arithmetic  10.8 us (7%)
  between operations  1.57 us (1%)
    ppermute x18, waiting for transfers between devices, exchange(): lax.ppermute(block, AXES, [(i, i ^ bit) for i, bit in enumerate(bits)])  28.2 us
    pallas_call x1, Pallas kernels, mlp(): pl.pallas_call(partial(mlp_kernel, shards=shards), grid_spec=pltpu.Prefet...  25.2 us
    ppermute x18, starting transfers between devices, exchange(): lax.ppermute(block, AXES, [(i, i ^ bit) for i, bit in enumerate(bits)])  18.4 us
    pallas_call x1, Pallas kernels, attend_back(): pl.pallas_call(partial(attend_back_kernel, shard=width // shards if packe...  11.9 us
    pallas_call x1, Pallas kernels, attend(): pl.pallas_call(attend_kernel, grid=(pairs,), in_specs=[pl.BlockSpec((1, h...  11.3 us
    pallas_call x1, Pallas kernels, last_back(): pl.pallas_call(partial(last_back_kernel, shard=width // shards if packed...  10.3 us
    convert_element_type x14, other arithmetic, parts(): return add_up([p[1] for p in pieces]).astype(BF16)  9.76 us
    unnamed x120, local copies, waits for them, and re-layouts  6.81 us
  transfers between devices with their start and end apart: 23, of which 10 were waited for; matrix products, arithmetic and copies ran while one was open for 10% of the time, Pallas kernels for 30%

profile of v6, /device:TPU:0, one launch (start us, length us, event | category | flops | bytes accessed | tf_op | source)
XLA Modules:
  0.0 156.1 jit_solution(11864998163059532169)
XLA Ops:
  0.7 2.2 %fusion.3 = (bf16[2,140,768]{2,0,1:T(2,128)(2,1)S(1)}, bf16[2,140,768]{2,0,1:T(2,128)(2,1)S(1)}) fusion(bf16[4,140,768]{2,0,1:T(4,128)(2,1)} %param.20), kind=kLoop, calls=%fused_computation.36 | loop fusion | bytes 1720320 | tf_op jit(solution)/shard_map/slice | solution.py:907
  3.1 3.0 %collective-permute-start = (bf16[2,140,768]{2,1,0:T(8,128)(2,1)S(1)}, bf16[2,140,768]{2,1,0:T(8,128)(2,1)S(1)}, u32[]{:S(2)}, u32[]{:S(2)}) collective-permute-start(bf16[2,140,768]{2,1,0:T(8,128)(2,1)S(1)} %copy_select_fusion), channel_id=1, source_target_pairs={{0,1},{1,0},{2,3},{3,2},{4,5},{5,4},{6,7},{7,6},{8,9},{9,8},{10,11... | collective-permute-start | bytes 1290248 | tf_op jit(solution)/shard_map/ppermute | solution.py:891
  7.3 1.2 copy-done
  8.5 3.1 %norm_qkv.2 = (bf16[2,144,768]{2,1,0:T(8,128)(2,1)}, bf16[2,144,2304]{2,1,0:T(8,128)(2,1)}) custom-call(bf16[2,144,768]{2,1,0:T(8,128)(2,1)S(1)} %pad.13.x_ref.xo, f32[1,768]{1,0:T(1,128)S(1)} %reshape.196.g_ref.g1, f32[1,768]{1,0:T(1,128)S(1)} %reshape.197.b_ref, bf16[768,2304]{1,0:T(8,128)(2,1)S(1)} %copy-done, f32[2,1,768]{2,1,0:T(1,128)S(1)} %reshape.198.qvb_ref), custom_call_target="tpu_custom_call" | custom-call | flops 1019215872 | bytes 5750784 | tf_op jit(solution)/shard_map/norm_qkv/pallas_call | solution.py:131
  11.8 4.5 %collective-permute-done = bf16[2,140,768]{2,1,0:T(8,128)(2,1)S(1)} collective-permute-done((bf16[2,140,768]{2,1,0:T(8,128)(2,1)S(1)}, bf16[2,140,768]{2,1,0:T(8,128)(2,1)S(1)}, u32[]{:S(2)}, u32[]{:S(2)}) %collective-permute-start) | collective-permute-done | bytes 430112 | tf_op jit(solution)/shard_map/ppermute | solution.py:891
  16.3 1.7 %collective-permute-start.2 = (bf16[2,140,768]{2,1,0:T(8,128)(2,1)S(1)}, bf16[2,140,768]{2,1,0:T(8,128)(2,1)S(1)}, u32[]{:S(2)}, u32[]{:S(2)}) collective-permute-start(bf16[2,140,768]{2,1,0:T(8,128)(2,1)S(1)} %get-tuple-element.94), channel_id=1, source_target_pairs={{0,1},{1,0},{2,3},{3,2},{4,5},{5,4},{6,7},{7,6},{8,9},{9,8},{10,11... | collective-permute-start | bytes 1290248 | tf_op jit(solution)/shard_map/ppermute | solution.py:891
  18.4 2.8 %norm_qkv.3 = (bf16[2,144,768]{2,1,0:T(8,128)(2,1)}, bf16[2,144,2304]{2,1,0:T(8,128)(2,1)S(1)}) custom-call(bf16[2,144,768]{2,1,0:T(8,128)(2,1)S(1)} %pad.14.x_ref.xr, f32[1,768]{1,0:T(1,128)S(1)} %reshape.196.g_ref.g1, f32[1,768]{1,0:T(1,128)S(1)} %reshape.197.b_ref, bf16[768,2304]{1,0:T(8,128)(2,1)S(1)} %copy-done, f32[2,1,768]{2,1,0:T(1,128)S(1)} %reshape.198.qvb_ref), custom_call_target="tpu_custom_call" | custom-call | flops 1019215872 | bytes 5750784 | tf_op jit(solution)/shard_map/norm_qkv/pallas_call | solution.py:131
  21.2 11.3 %attend.1 = (bf16[2,2,144,768]{3,2,1,0:T(8,128)(2,1)}, f32[2,2,144,768]{3,2,1,0:T(8,128)}, bf16[2,2,144,768]{3,2,1,0:T(8,128)(2,1)S(1)}, bf16[2,6,576,288]{3,2,1,0:T(8,128)(2,1)}) custom-call(bf16[2,144,2304]{2,1,0:T(8,128)(2,1)S(1)} %copy-done.3, bf16[2,144,2304]{2,1,0:T(8,128)(2,1)S(1)} %get-tuple-element.90.qr, bf16[2,144,768]{2,1,0:T(8,128)(2,1)S(1)} %pad.13.x_ref.xo, ...), custom_call_target="tpu_custom_call" | custom-call | flops 2038431744 | bytes 11059200 | tf_op jit(solution)/shard_map/attend/pallas_call | solution.py:203
  32.5 25.2 %mlp.1 = (bf16[2,144,768]{2,1,0:T(8,128)(2,1)}, bf16[2,144,768]{2,1,0:T(8,128)(2,1)}, bf16[576,768]{1,0:T(8,128)(2,1)S(1)}, f32[1,768]{1,0:T(1,128)}, f32[576,76...) custom-call(s32[3]{0:T(128)S(1)} %pad_add_fusion.info, ...), custom_call_target="tpu_custom_call" | custom-call | flops 16307453952 | bytes 25165824 | tf_op jit(solution)/shard_map/mlp/pallas_call | solution.py:343
  57.9 3.2 %second_back.1 = (f32[2,288,768]{2,1,0:T(8,128)}, bf16[2,288,768]{2,1,0:T(8,128)(2,1)S(1)}, bf16[2,288,768]{2,1,0:T(8,128)(2,1)S(1)}, f32[8,768]{1,0:T(8,128)}) custom-call(f32[2,2,144,768]{3,2,1,0:T(8,128)S(1)} %bitcast.31, bf16[2,2,144,768]{3,2,1,0:T(8,128)(2,1)S(1)} %bitcast.32, f32[2,2,144,768]{3,2,1,0:T(8,128)S(1)} %copy-done.2, ...), custom_call_target="tpu_custom_call" | custom-call | flops 679477248 | bytes 10485760 | tf_op jit(solution)/shard_map/second_back/pallas_call | solution.py:463
  61.1 4.9 %collective-permute-done.3.got = bf16[8,384,768]{2,1,0:T(8,128)(2,1)S(1)} collective-permute-done((bf16[8,384,768]{2,1,0:T(8,128)(2,1)}, bf16[8,384,768]{2,1,0:T(8,128)(2,1)S(1)}, u32[]{:S(2)}, u32[]{:S(2)}) %collective-permute-start.3) | collective-permute-done | bytes 4718624 | tf_op jit(solution)/shard_map/ppermute | solution.py:739
  66.4 1.6 %collective-permute-start.4 = (bf16[1,2,2,384,512]{4,3,2,1,0:T(8,128)(2,1)S(1)}, bf16[1,2,2,384,512]{4,3,2,1,0:T(8,128)(2,1)S(1)}, u32[]{:S(2)}, u32[]{:S(2)}) collective-permute-start(bf16[1,2,2,384,512]{4,3,2,1,0:T(8,128)(2,1)S(1)} %add_convert_fusion), channel_id=1, source_target_pairs={{0,4},{1,5},{2,10},{3,11},{4,0},{5,1},{6,14},{7,15},{8,12},{9,13},... | collective-permute-start | bytes 4718600 | tf_op jit(solution)/shard_map/ppermute | solution.py:739
  69.1 11.9 %attend_back.1 = (bf16[576,1536]{1,0:T(8,128)(2,1)S(1)}, bf16[768,576]{1,0:T(8,128)(2,1)S(1)}, f32[8,128]{1,0:T(8,128)}, bf16[384,2304]{1,0:T(8,128)(2,1)}, bf16[384,2304]{1,0:T(8,128)(2,1)}) custom-call(s32[32]{0:T(128)S(1)} %get-tuple-element.114.inv, bf16[2,288,768]{2,1,0:T(8,128)(2,1)S(1)} %get-tuple-element.103.br, ...), custom_call_target="tpu_custom_call" | custom-call | flops 4756340736 | bytes 16777216 | tf_op jit(solution)/shard_map/attend_back/pallas_call | solution.py:530
  81.2 6.4 %collective-permute-done.5.q1 = bf16[2,2,1,384,256]{4,3,2,1,0:T(8,128)(2,1)S(1)} collective-permute-done((bf16[2,2,1,384,256]{4,3,2,1,0:T(8,128)(2,1)S(1)}, bf16[2,2,1,384,256]{4,3,2,1,0:T(8,128)(2,1)S(1)}, u32[]{:S(2)}, u32[]{:S(2)}) %collective-permute-start.5) | collective-permute-done | bytes 786464 | tf_op jit(solution)/shard_map/ppermute | solution.py:739
  88.0 0.9 collective-permute-start.6
  89.6 1.6 %collective-permute-start.7 = (bf16[1,2,1,384,256]{4,3,2,1,0:T(8,128)(2,1)S(1)}, bf16[1,2,1,384,256]{4,3,2,1,0:T(8,128)(2,1)S(1)}, u32[]{:S(2)}, u32[]{:S(2)}) collective-permute-start(bf16[1,2,1,384,256]{4,3,2,1,0:T(8,128)(2,1)S(1)} %add_convert_fusion.6), channel_id=1, source_target_pairs={{0,4},{1,5},{2,10},{3,11},{4,0},{5,1},{6,14},{7,15},{8,12},{9,13},... | collective-permute-start | bytes 1179656 | tf_op jit(solution)/shard_map/ppermute | solution.py:739
  91.2 10.3 %last_back.1 = (bf16[2,144,768]{2,1,0:T(8,128)(2,1)}, bf16[2,144,768]{2,1,0:T(8,128)(2,1)}, f32[16,768]{1,0:T(8,128)}, bf16[384,896]{1,0:T(8,128)(2,1)}, bf16[384,896]{1,0:T(8,128)(2,1)}) custom-call(s32[32]{0:T(128)S(1)} %get-tuple-element.114.inv, bf16[2,144,2304]{2,1,0:T(8,128)(2,1)S(1)} %copy-done.3, bf16[2,144,2304]{2,1,0:T(8,128)(2,1)S(1)} %get-tuple-element.90.qr, ...), custom_call_target="tpu_custom_call" | custom-call | flops 4076863488 | bytes 16777216 | tf_op jit(solution)/shard_map/last_back/pallas_call | solution.py:659
  101.7 2.6 %collective-permute-done.6.p2 = bf16[1,1,2,384,512]{4,3,2,1,0:T(8,128)(2,1)S(1)} collective-permute-done((bf16[1,1,2,384,512]{4,3,2,1,0:T(8,128)(2,1)S(1)}, bf16[1,1,2,384,512]{4,3,2,1,0:T(8,128)(2,1)S(1)}, u32[]{:S(2)}, u32[]{:S(2)}) %collective-permute-start.6) | collective-permute-done | bytes 786464 | tf_op jit(solution)/shard_map/ppermute | solution.py:739
  104.6 1.1 add_convert_fusion.1
  105.7 1.0 collective-permute-start.13
  107.4 1.0 slice.317
  108.4 1.3 collective-permute-start.14
  109.7 0.9 add_convert_fusion.7
  110.6 1.0 slice.320
  111.6 1.0 collective-permute-start.16
  112.7 3.5 %collective-permute-done.14.q3 = bf16[1,1,1,384,256]{4,3,2,1,0:T(8,128)(2,1)S(1)} collective-permute-done((bf16[1,1,1,384,256]{4,3,2,1,0:T(8,128)(2,1)S(1)}, bf16[1,1,1,384,256]{4,3,2,1,0:T(8,128)(2,1)S(1)}, u32[]{:S(2)}, u32[]{:S(2)}) %collective-permute-start.14) | collective-permute-done | bytes 196640 | tf_op jit(solution)/shard_map/ppermute | solution.py:739
  116.9 3.0 %part_pairs.1 = (f32[192,768]{1,0:T(8,128)}, bf16[192,768]{1,0:T(8,128)(2,1)}) custom-call(bf16[8,384,768]{2,1,0:T(8,128)(2,1)} %get-tuple-element.96.keep, bf16[8,384,768]{2,1,0:T(8,128)(2,1)} %copy-done.14, bf16[1,2,2,384,512]{4,3,2,1,0:T(8,128)(2,1)} %copy-done.17, bf16[1,1,2,384,512]{4,3,2,1,0:T(8,128)(2,1)} %copy-done.26, ...), custom_call_target="tpu_custom_call" | custom-call | bytes 4194304 | tf_op jit(solution)/shard_map/part_pairs/pallas_call | solution.py:803
  119.9 1.1 collective-permute-done.13.refs_2_
  121.1 1.2 add_convert_fusion.4
  122.2 0.9 collective-permute-start.15
  123.2 2.8 %collective-permute-start.22 = (bf16[192,768]{1,0:T(8,128)(2,1)S(1)}, bf16[192,768]{1,0:T(8,128)(2,1)S(1)}, u32[]{:S(2)}, u32[]{:S(2)}) collective-permute-start(bf16[192,768]{1,0:T(8,128)(2,1)S(1)} %copy-done.54), channel_id=1, source_target_pairs={{0,16},{1,17},{2,18},{3,19},{4,20},{5,21},{6,22},{7,23},{8,24},{9,... | collective-permute-start | bytes 884744 | tf_op jit(solution)/shard_map/ppermute | solution.py:739
  126.0 1.0 collective-permute-start.12
  127.0 1.0 add_convert_fusion.10
  128.0 1.1 collective-permute-start.18
  129.1 6.3 %collective-permute-done.15.refs_3_ = bf16[1,1,2,2,24,2304]{5,4,3,2,1,0:T(8,128)(2,1)S(1)} collective-permute-done((bf16[1,1,2,2,24,2304]{5,4,3,2,1,0:T(8,128)(2,1)S(1)}, bf16[1,1,2,2,24,2304]{5,4,3,2,1,0:T(8,128)(2,1)S(1)}, u32[]{:S(2)}, u32[]{:S(2)}) %collective-permute-start.15) | collective-permute-done | bytes 442400 | tf_op jit(solution)/shard_map/ppermute | solution.py:739
  135.4 1.2 add_convert_fusion.8
  136.7 0.9 collective-permute-start.17
  137.5 1.2 collective-permute-done.18.refs_9_
  138.8 1.0 add_convert_fusion.12
  139.8 0.9 collective-permute-start.20
  140.6 2.0 %collective-permute-done.17.refs_4_ = bf16[1,1,1,2,24,2304]{5,4,3,2,1,0:T(8,128)(2,1)S(1)} collective-permute-done((bf16[1,1,1,2,24,2304]{5,4,3,2,1,0:T(8,128)(2,1)S(1)}, bf16[1,1,1,2,24,2304]{5,4,3,2,1,0:T(8,128)(2,1)S(1)}, u32[]{:S(2)}, u32[]{:S(2)}) %collective-permute-start.17) | collective-permute-done | bytes 221216 | tf_op jit(solution)/shard_map/ppermute | solution.py:739
  142.7 1.1 fusion
  144.7 0.9 fusion.1
  145.5 2.3 %collective-permute-start.21 = (bf16[24,896]{1,0:T(8,128)(2,1)S(1)}, bf16[24,896]{1,0:T(8,128)(2,1)S(1)}, u32[]{:S(2)}, u32[]{:S(2)}) collective-permute-start(bf16[24,896]{1,0:T(8,128)(2,1)S(1)} %fusion.1), channel_id=1, source_target_pairs={{0,16},{1,17},{2,18},{3,19},{4,20},{5,21},{6,22},{7,23},{8,24},{9,... | collective-permute-start | bytes 129032 | tf_op jit(solution)/shard_map/ppermute | solution.py:739
  147.8 1.3 copy.58
  149.2 1.3 copy.59
  151.2 2.0 %finish_pair.1 = (f32[96,768]{1,0:T(8,128)}, f32[24,3072]{1,0:T(8,128)}) custom-call(f32[192,768]{1,0:T(8,128)} %get-tuple-element.150.mine, bf16[192,768]{1,0:T(8,128)(2,1)} %copy-done.34), custom_call_target="tpu_custom_call" | custom-call | bytes 2097152 | tf_op jit(solution)/shard_map/finish_pair/pallas_call | solution.py:871
  153.9 2.0 %finish_rest.1 = (f32[24,2304]{1,0:T(8,128)}, f32[24,768]{1,0:T(8,128)}, f32[24]{0:T(128)}, f32[24]{0:T(128)}, f32[24]{0:T(128)}, /*index=5*/f32[24]{0:T(128)}, ...) custom-call(bf16[2,2,2,2,24,2304]{5,4,3,2,1,0:T(8,128)(2,1)} %bitcast.49, bf16[2,2,2,2,24,2304]{5,4,3,2,1,0:T(8,128)(2,1)} %bitcast.50, ...), custom_call_target="tpu_custom_call" | custom-call | bytes 2097152 | tf_op jit(solution)/shard_map/finish_rest/pallas_call | solution.py:845
  (179 shorter events, 8.9 us)
Async XLA Ops:
  3.1 13.2 %collective-permute-start = (bf16[2,140,768]{2,1,0:T(8,128)(2,1)S(1)}, bf16[2,140,768]{2,1,0:T(8,128)(2,1)S(1)}, u32[]{:S(2)}, u32[]{:S(2)}) collective-permute-start(bf16[2,140,768]{2,1,0:T(8,128)(2,1)S(1)} %copy_select_fusion), channel_id=1, source_target_pairs={{0,1},{1,0},{2,3},{3,2},{4,5},{5,4},{6,7},{7,6},{8,9},{9,8},{10,11... | collective-permute-start | bytes 1290248 | tf_op jit(solution)/shard_map/ppermute | solution.py:891
  6.2 12.0 %collective-permute-start.1 = (bf16[2,140]{1,0:T(2,128)(2,1)S(1)}, bf16[2,140]{1,0:T(2,128)(2,1)S(1)}, u32[]{:S(2)}, u32[]{:S(2)}) collective-permute-start(bf16[2,140]{1,0:T(2,128)(2,1)S(1)} %get-tuple-element.91), channel_id=1, source_target_pairs={{0,1},{1,0},{2,3},{3,2},{4,5},{5,4},{6,7},{7,6},{8,9},{9,8},{10,11... | collective-permute-start | bytes 1688 | tf_op jit(solution)/shard_map/ppermute | solution.py:891
  11.7 6.5 %copy-start.44 = (f32[768]{0:T(1024)S(1)}, f32[768]{0:T(1024)}, u32[]{:S(2)}) copy-start(f32[768]{0:T(1024)} %param.30) | copy-start | bytes 9220
  11.7 6.5 %copy-start.45 = (f32[768]{0:T(1024)S(1)}, f32[768]{0:T(1024)}, u32[]{:S(2)}) copy-start(f32[768]{0:T(1024)} %param.34) | copy-start | bytes 9220
  16.3 16.2 %collective-permute-start.2 = (bf16[2,140,768]{2,1,0:T(8,128)(2,1)S(1)}, bf16[2,140,768]{2,1,0:T(8,128)(2,1)S(1)}, u32[]{:S(2)}, u32[]{:S(2)}) collective-permute-start(bf16[2,140,768]{2,1,0:T(8,128)(2,1)S(1)} %get-tuple-element.94), channel_id=1, source_target_pairs={{0,1},{1,0},{2,3},{3,2},{4,5},{5,4},{6,7},{7,6},{8,9},{9,8},{10,11... | collective-permute-start | bytes 1290248 | tf_op jit(solution)/shard_map/ppermute | solution.py:891
  18.4 14.1 %slice-start.2 = ((s8[4718592]{0:T(1024)(128)(4,1)}), s8[4194304]{0:T(1024)(128)(4,1)S(1)}, s32[]{:S(2)}) async-start(s8[4718592]{0:T(1024)(128)(4,1)} %bitcast.33), calls=%async_computation.2 | async-start | bytes 8388608
  21.2 11.3 %slice-start.3 = ((s8[4718592]{0:T(1024)(128)(4,1)}), s8[524288]{0:T(1024)(128)(4,1)S(1)}, s32[]{:S(2)}) async-start(s8[4718592]{0:T(1024)(128)(4,1)} %bitcast.33), calls=%async_computation.3 | async-start | bytes 1048576
  21.2 11.3 %copy-start.8 = (bf16[3072,768]{1,0:T(8,128)(2,1)S(1)}, bf16[3072,768]{1,0:T(8,128)(2,1)}, u32[]{:S(2)}) copy-start(bf16[3072,768]{1,0:T(8,128)(2,1)} %down.1) | copy-start | bytes 14155780
  21.2 11.3 %copy-start.11 = (f32[3072]{0:T(1024)S(1)}, f32[3072]{0:T(1024)}, u32[]{:S(2)}) copy-start(f32[3072]{0:T(1024)} %param.32) | copy-start | bytes 36868
  32.4 36.4 %slice-start = ((s8[5308416]{0:T(1024)(128)(4,1)}), s8[4194304]{0:T(1024)(128)(4,1)S(1)}, s32[]{:S(2)}) async-start(s8[5308416]{0:T(1024)(128)(4,1)} %bitcast.28), calls=%async_computation | async-start | bytes 8388608
  32.5 25.3 %copy-start.2 = (f32[2,2,144,768]{3,2,1,0:T(8,128)S(1)}, f32[2,2,144,768]{3,2,1,0:T(8,128)}, u32[]{:S(2)}) copy-start(f32[2,2,144,768]{3,2,1,0:T(8,128)} %get-tuple-element.93.att) | copy-start | bytes 5308420
  32.5 36.3 %slice-start.1 = ((s8[5308416]{0:T(1024)(128)(4,1)}), s8[1114112]{0:T(1024)(128)(4,1)S(1)}, s32[]{:S(2)}) async-start(s8[5308416]{0:T(1024)(128)(4,1)} %bitcast.28), calls=%async_computation.1 | async-start | bytes 2228224
  57.8 8.2 %collective-permute-start.3 = (bf16[8,384,768]{2,1,0:T(8,128)(2,1)}, bf16[8,384,768]{2,1,0:T(8,128)(2,1)S(1)}, u32[]{:S(2)}, u32[]{:S(2)}) collective-permute-start(bf16[8,384,768]{2,1,0:T(8,128)(2,1)} %get-tuple-element.97), channel_id=1, source_target_pairs={{0,2},{1,3},{2,0},{3,1},{4,6},{5,7},{6,4},{7,5},{8,10},{9,11},{10,... | collective-permute-start | bytes 14155784 | tf_op jit(solution)/shard_map/ppermute | solution.py:739
  57.9 8.1 %copy-start.13 = (bf16[8,384,768]{2,1,0:T(8,128)(2,1)S(1)}, bf16[8,384,768]{2,1,0:T(8,128)(2,1)}, u32[]{:S(2)}) copy-start(bf16[8,384,768]{2,1,0:T(8,128)(2,1)} %get-tuple-element.96.keep) | copy-start | bytes 14155780
  66.0 38.4 %copy-start.14 = (bf16[8,384,768]{2,1,0:T(8,128)(2,1)}, bf16[8,384,768]{2,1,0:T(8,128)(2,1)S(1)}, u32[]{:S(2)}) copy-start(bf16[8,384,768]{2,1,0:T(8,128)(2,1)S(1)} %collective-permute-done.3.got) | copy-start | bytes 14155780
  66.4 21.2 %collective-permute-start.4 = (bf16[1,2,2,384,512]{4,3,2,1,0:T(8,128)(2,1)S(1)}, bf16[1,2,2,384,512]{4,3,2,1,0:T(8,128)(2,1)S(1)}, u32[]{:S(2)}, u32[]{:S(2)}) collective-permute-start(bf16[1,2,2,384,512]{4,3,2,1,0:T(8,128)(2,1)S(1)} %add_convert_fusion), channel_id=1, source_target_pairs={{0,4},{1,5},{2,10},{3,11},{4,0},{5,1},{6,14},{7,15},{8,12},{9,13},... | collective-permute-start | bytes 4718600 | tf_op jit(solution)/shard_map/ppermute | solution.py:739
  68.2 19.4 %collective-permute-start.5 = (bf16[2,2,1,384,256]{4,3,2,1,0:T(8,128)(2,1)S(1)}, bf16[2,2,1,384,256]{4,3,2,1,0:T(8,128)(2,1)S(1)}, u32[]{:S(2)}, u32[]{:S(2)}) collective-permute-start(bf16[2,2,1,384,256]{4,3,2,1,0:T(8,128)(2,1)S(1)} %add_convert_fusion.3), channel_id=1, source_target_pairs={{0,1},{1,0},{2,3},{3,2},{4,5},{5,4},{6,7},{7,6},{8,9},{9,8},{10,11... | collective-permute-start | bytes 2359304 | tf_op jit(solution)/shard_map/ppermute | solution.py:739
  81.0 7.9 %copy-start.53 = (bf16[2,144,768]{2,1,0:T(8,128)(2,1)S(1)}, bf16[2,144,768]{2,1,0:T(8,128)(2,1)}, u32[]{:S(2)}) copy-start(bf16[2,144,768]{2,1,0:T(8,128)(2,1)} %get-tuple-element.112) | copy-start | bytes 1327108
  81.0 10.1 %copy-start.1 = (f32[2,288,768]{2,1,0:T(8,128)S(1)}, f32[2,288,768]{2,1,0:T(8,128)}, u32[]{:S(2)}) copy-start(f32[2,288,768]{2,1,0:T(8,128)} %get-tuple-element.117.ga) | copy-start | bytes 5308420
  81.0 10.1 %copy-start.5 = (f32[8,768]{1,0:T(8,128)S(1)}, f32[8,768]{1,0:T(8,128)}, u32[]{:S(2)}) copy-start(f32[8,768]{1,0:T(8,128)} %get-tuple-element.100.v2) | copy-start | bytes 73732
  81.0 10.1 %copy-start.6 = (f32[1,3072]{1,0:T(1,128)S(1)}, f32[1,3072]{1,0:T(1,128)}, u32[]{:S(2)}) copy-start(f32[1,3072]{1,0:T(1,128)} %get-tuple-element.118.upbg) | copy-start | bytes 36868
  81.0 10.1 %copy-start.7 = (f32[1,768]{1,0:T(1,128)S(1)}, f32[1,768]{1,0:T(1,128)}, u32[]{:S(2)}) copy-start(f32[1,768]{1,0:T(1,128)} %get-tuple-element.119.dbg) | copy-start | bytes 9220
  81.0 20.5 %collective-permute-start.9 = (bf16[384,2304]{1,0:T(8,128)(2,1)}, bf16[384,2304]{1,0:T(8,128)(2,1)S(1)}, u32[]{:S(2)}, u32[]{:S(2)}) collective-permute-start(bf16[384,2304]{1,0:T(8,128)(2,1)} %get-tuple-element.113), channel_id=1, source_target_pairs={{0,2},{1,3},{2,0},{3,1},{4,6},{5,7},{6,4},{7,5},{8,10},{9,11},{10,... | collective-permute-start | bytes 5308424 | tf_op jit(solution)/shard_map/ppermute | solution.py:739
  87.7 16.6 %copy-start.25 = (bf16[2,2,1,384,256]{4,3,2,1,0:T(8,128)(2,1)}, bf16[2,2,1,384,256]{4,3,2,1,0:T(8,128)(2,1)S(1)}, u32[]{:S(2)}) copy-start(bf16[2,2,1,384,256]{4,3,2,1,0:T(8,128)(2,1)S(1)} %collective-permute-done.5.q1) | copy-start | bytes 2359300
  87.7 16.7 %copy-start.17 = (bf16[1,2,2,384,512]{4,3,2,1,0:T(8,128)(2,1)}, bf16[1,2,2,384,512]{4,3,2,1,0:T(8,128)(2,1)S(1)}, u32[]{:S(2)}) copy-start(bf16[1,2,2,384,512]{4,3,2,1,0:T(8,128)(2,1)S(1)} %collective-permute-done.4.p1) | copy-start | bytes 4718596
  88.0 16.3 %collective-permute-start.6 = (bf16[1,1,2,384,512]{4,3,2,1,0:T(8,128)(2,1)S(1)}, bf16[1,1,2,384,512]{4,3,2,1,0:T(8,128)(2,1)S(1)}, u32[]{:S(2)}, u32[]{:S(2)}) collective-permute-start(bf16[1,1,2,384,512]{4,3,2,1,0:T(8,128)(2,1)S(1)} %add_convert_fusion.2), channel_id=1, source_target_pairs={{0,8},{1,9},{2,6},{3,7},{4,12},{5,13},{6,2},{7,3},{8,0},{9,1},{10,... | collective-permute-start | bytes 2359304 | tf_op jit(solution)/shard_map/ppermute | solution.py:739
  88.9 12.7 %collective-permute-start.8 = (bf16[2,144,768]{2,1,0:T(8,128)(2,1)S(1)}, bf16[2,144,768]{2,1,0:T(8,128)(2,1)S(1)}, u32[]{:S(2)}, u32[]{:S(2)}) collective-permute-start(bf16[2,144,768]{2,1,0:T(8,128)(2,1)S(1)} %copy-done.53), channel_id=1, source_target_pairs={{0,1},{1,0},{2,3},{3,2},{4,5},{5,4},{6,7},{7,6},{8,9},{9,8},{10,11... | collective-permute-start | bytes 1327112 | tf_op jit(solution)/shard_map/ppermute | solution.py:891
  89.6 12.1 %collective-permute-start.7 = (bf16[1,2,1,384,256]{4,3,2,1,0:T(8,128)(2,1)S(1)}, bf16[1,2,1,384,256]{4,3,2,1,0:T(8,128)(2,1)S(1)}, u32[]{:S(2)}, u32[]{:S(2)}) collective-permute-start(bf16[1,2,1,384,256]{4,3,2,1,0:T(8,128)(2,1)S(1)} %add_convert_fusion.6), channel_id=1, source_target_pairs={{0,4},{1,5},{2,10},{3,11},{4,0},{5,1},{6,14},{7,15},{8,12},{9,13},... | collective-permute-start | bytes 1179656 | tf_op jit(solution)/shard_map/ppermute | solution.py:739
  101.5 8.2 %collective-permute-start.11 = (bf16[384,896]{1,0:T(8,128)(2,1)}, bf16[384,896]{1,0:T(8,128)(2,1)S(1)}, u32[]{:S(2)}, u32[]{:S(2)}) collective-permute-start(bf16[384,896]{1,0:T(8,128)(2,1)} %get-tuple-element.125), channel_id=1, source_target_pairs={{0,2},{1,3},{2,0},{3,1},{4,6},{5,7},{6,4},{7,5},{8,10},{9,11},{10,... | collective-permute-start | bytes 2064392 | tf_op jit(solution)/shard_map/ppermute | solution.py:739
  101.6 9.0 %copy-start.16 = (bf16[384,2304]{1,0:T(8,128)(2,1)}, bf16[384,2304]{1,0:T(8,128)(2,1)S(1)}, u32[]{:S(2)}) copy-start(bf16[384,2304]{1,0:T(8,128)(2,1)S(1)} %collective-permute-done.9) | copy-start | bytes 5308420
  105.7 15.3 %collective-permute-start.13 = (bf16[1,2,2,2,24,2304]{5,4,3,2,1,0:T(8,128)(2,1)}, bf16[1,2,2,2,24,2304]{5,4,3,2,1,0:T(8,128)(2,1)}, u32[]{:S(2)}, u32[]{:S(2)}) collective-permute-start(bf16[1,2,2,2,24,2304]{5,4,3,2,1,0:T(8,128)(2,1)} %bitcast.9), channel_id=1, source_target_pairs={{0,4},{1,5},{2,10},{3,11},{4,0},{5,1},{6,14},{7,15},{8,12},{9,13},... | collective-permute-start | bytes 2654216 | tf_op jit(solution)/shard_map/ppermute | solution.py:739
  106.7 10.2 %collective-permute-start.10 = (bf16[1,1,1,384,512]{4,3,2,1,0:T(8,128)(2,1)S(1)}, bf16[1,1,1,384,512]{4,3,2,1,0:T(8,128)(2,1)}, u32[]{:S(2)}, u32[]{:S(2)}) collective-permute-start(bf16[1,1,1,384,512]{4,3,2,1,0:T(8,128)(2,1)S(1)} %add_convert_fusion.5), channel_id=1, source_target_pairs={{0,1},{1,0},{2,3},{3,2},{4,5},{5,4},{6,7},{7,6},{8,9},{9,8},{10,11... | collective-permute-start | bytes 1179656 | tf_op jit(solution)/shard_map/ppermute | solution.py:739
  108.4 7.8 %collective-permute-start.14 = (bf16[1,1,1,384,256]{4,3,2,1,0:T(8,128)(2,1)S(1)}, bf16[1,1,1,384,256]{4,3,2,1,0:T(8,128)(2,1)S(1)}, u32[]{:S(2)}, u32[]{:S(2)}) collective-permute-start(bf16[1,1,1,384,256]{4,3,2,1,0:T(8,128)(2,1)S(1)} %add_convert_fusion.9), channel_id=1, source_target_pairs={{0,8},{1,9},{2,6},{3,7},{4,12},{5,13},{6,2},{7,3},{8,0},{9,1},{10,... | collective-permute-start | bytes 589832 | tf_op jit(solution)/shard_map/ppermute | solution.py:739
  111.6 15.5 %collective-permute-start.16 = (bf16[1,2,2,2,24,896]{5,4,3,2,1,0:T(8,128)(2,1)}, bf16[1,2,2,2,24,896]{5,4,3,2,1,0:T(8,128)(2,1)}, u32[]{:S(2)}, u32[]{:S(2)}) collective-permute-start(bf16[1,2,2,2,24,896]{5,4,3,2,1,0:T(8,128)(2,1)} %bitcast.10), channel_id=1, source_target_pairs={{0,4},{1,5},{2,10},{3,11},{4,0},{5,1},{6,14},{7,15},{8,12},{9,13},... | collective-permute-start | bytes 1032200 | tf_op jit(solution)/shard_map/ppermute | solution.py:739
  112.7 8.3 %copy-start.19 = (bf16[192,2304]{1,0:T(8,128)(2,1)S(1)}, bf16[192,2304]{1,0:T(8,128)(2,1)}, u32[]{:S(2)}) copy-start(bf16[192,2304]{1,0:T(8,128)(2,1)} %slice.317) | copy-start | bytes 2654212
  112.7 8.3 %copy-start.20 = (bf16[192,2304]{1,0:T(8,128)(2,1)S(1)}, bf16[192,2304]{1,0:T(8,128)(2,1)}, u32[]{:S(2)}) copy-start(bf16[192,2304]{1,0:T(8,128)(2,1)} %slice.320) | copy-start | bytes 2654212
  122.2 13.2 %collective-permute-start.15 = (bf16[1,1,2,2,24,2304]{5,4,3,2,1,0:T(8,128)(2,1)S(1)}, bf16[1,1,2,2,24,2304]{5,4,3,2,1,0:T(8,128)(2,1)S(1)}, u32[]{:S(2)}, u32[]{:S(2)}) collective-permute-start(bf16[1,1,2,2,24,2304]{5,4,3,2,1,0:T(8,128)(2,1)S(1)} %add_convert_fusion.4), channel_id=1, source_target_pairs={{0,8},{1,9},{2,6},{3,7},{4,12},{5,13},{6,2},{7,3},{8,0},{9,1},{10,... | collective-permute-start | bytes 1327112 | tf_op jit(solution)/shard_map/ppermute | solution.py:739
  123.2 21.3 %copy-start.32 = (bf16[2,144,768]{2,1,0:T(8,128)(2,1)S(1)}, bf16[2,144,768]{2,1,0:T(8,128)(2,1)}, u32[]{:S(2)}) copy-start(bf16[2,144,768]{2,1,0:T(8,128)(2,1)} %get-tuple-element.120) | copy-start | bytes 1327108
  123.2 27.3 %collective-permute-start.22 = (bf16[192,768]{1,0:T(8,128)(2,1)S(1)}, bf16[192,768]{1,0:T(8,128)(2,1)S(1)}, u32[]{:S(2)}, u32[]{:S(2)}) collective-permute-start(bf16[192,768]{1,0:T(8,128)(2,1)S(1)} %copy-done.54), channel_id=1, source_target_pairs={{0,16},{1,17},{2,18},{3,19},{4,20},{5,21},{6,22},{7,23},{8,24},{9,... | collective-permute-start | bytes 884744 | tf_op jit(solution)/shard_map/ppermute | solution.py:739
  126.0 18.5 %collective-permute-start.12 = (bf16[2,144,768]{2,1,0:T(8,128)(2,1)S(1)}, bf16[2,144,768]{2,1,0:T(8,128)(2,1)S(1)}, u32[]{:S(2)}, u32[]{:S(2)}) collective-permute-start(bf16[2,144,768]{2,1,0:T(8,128)(2,1)S(1)} %copy-done.52), channel_id=1, source_target_pairs={{0,1},{1,0},{2,3},{3,2},{4,5},{5,4},{6,7},{7,6},{8,9},{9,8},{10,11... | collective-permute-start | bytes 1327112 | tf_op jit(solution)/shard_map/ppermute | solution.py:891
  128.0 10.7 %collective-permute-start.18 = (bf16[1,1,2,2,24,896]{5,4,3,2,1,0:T(8,128)(2,1)S(1)}, bf16[1,1,2,2,24,896]{5,4,3,2,1,0:T(8,128)(2,1)S(1)}, u32[]{:S(2)}, u32[]{:S(2)}) collective-permute-start(bf16[1,1,2,2,24,896]{5,4,3,2,1,0:T(8,128)(2,1)S(1)} %add_convert_fusion.10), channel_id=1, source_target_pairs={{0,8},{1,9},{2,6},{3,7},{4,12},{5,13},{6,2},{7,3},{8,0},{9,1},{10,... | collective-permute-start | bytes 516104 | tf_op jit(solution)/shard_map/ppermute | solution.py:739
  135.4 9.1 %copy-start.27 = (bf16[1,1,2,2,24,2304]{5,4,3,2,1,0:T(8,128)(2,1)}, bf16[1,1,2,2,24,2304]{5,4,3,2,1,0:T(8,128)(2,1)S(1)}, u32[]{:S(2)}) copy-start(bf16[1,1,2,2,24,2304]{5,4,3,2,1,0:T(8,128)(2,1)S(1)} %collective-permute-done.15.refs_3_) | copy-start | bytes 1327108
  136.7 6.0 %collective-permute-start.17 = (bf16[1,1,1,2,24,2304]{5,4,3,2,1,0:T(8,128)(2,1)S(1)}, bf16[1,1,1,2,24,2304]{5,4,3,2,1,0:T(8,128)(2,1)S(1)}, u32[]{:S(2)}, u32[]{:S(2)}) collective-permute-start(bf16[1,1,1,2,24,2304]{5,4,3,2,1,0:T(8,128)(2,1)S(1)} %add_convert_fusion.8), channel_id=1, source_target_pairs={{0,1},{1,0},{2,3},{3,2},{4,5},{5,4},{6,7},{7,6},{8,9},{9,8},{10,11... | collective-permute-start | bytes 663560 | tf_op jit(solution)/shard_map/ppermute | solution.py:739
  138.8 10.4 %copy-start.30 = (bf16[1,1,2,2,24,896]{5,4,3,2,1,0:T(8,128)(2,1)}, bf16[1,1,2,2,24,896]{5,4,3,2,1,0:T(8,128)(2,1)S(1)}, u32[]{:S(2)}) copy-start(bf16[1,1,2,2,24,896]{5,4,3,2,1,0:T(8,128)(2,1)S(1)} %collective-permute-done.18.refs_9_) | copy-start | bytes 516100
  139.8 4.9 %collective-permute-start.20 = (bf16[1,1,1,2,24,896]{5,4,3,2,1,0:T(8,128)(2,1)S(1)}, bf16[1,1,1,2,24,896]{5,4,3,2,1,0:T(8,128)(2,1)S(1)}, u32[]{:S(2)}, u32[]{:S(2)}) collective-permute-start(bf16[1,1,1,2,24,896]{5,4,3,2,1,0:T(8,128)(2,1)S(1)} %add_convert_fusion.12), channel_id=1, source_target_pairs={{0,1},{1,0},{2,3},{3,2},{4,5},{5,4},{6,7},{7,6},{8,9},{9,8},{10,11... | collective-permute-start | bytes 258056 | tf_op jit(solution)/shard_map/ppermute | solution.py:739
  142.7 6.5 %copy-start.31 = (bf16[1,1,1,2,24,2304]{5,4,3,2,1,0:T(8,128)(2,1)}, bf16[1,1,1,2,24,2304]{5,4,3,2,1,0:T(8,128)(2,1)S(1)}, u32[]{:S(2)}) copy-start(bf16[1,1,1,2,24,2304]{5,4,3,2,1,0:T(8,128)(2,1)S(1)} %collective-permute-done.17.refs_4_) | copy-start | bytes 663556
  143.7 9.5 %collective-permute-start.19 = (bf16[24,2304]{1,0:T(8,128)(2,1)S(1)}, bf16[24,2304]{1,0:T(8,128)(2,1)S(1)}, u32[]{:S(2)}, u32[]{:S(2)}) collective-permute-start(bf16[24,2304]{1,0:T(8,128)(2,1)S(1)} %fusion), channel_id=1, source_target_pairs={{0,16},{1,17},{2,18},{3,19},{4,20},{5,21},{6,22},{7,23},{8,24},{9,... | collective-permute-start | bytes 331784 | tf_op jit(solution)/shard_map/ppermute | solution.py:739
  145.5 7.7 %collective-permute-start.21 = (bf16[24,896]{1,0:T(8,128)(2,1)S(1)}, bf16[24,896]{1,0:T(8,128)(2,1)S(1)}, u32[]{:S(2)}, u32[]{:S(2)}) collective-permute-start(bf16[24,896]{1,0:T(8,128)(2,1)S(1)} %fusion.1), channel_id=1, source_target_pairs={{0,16},{1,17},{2,18},{3,19},{4,20},{5,21},{6,22},{7,23},{8,24},{9,... | collective-permute-start | bytes 129032 | tf_op jit(solution)/shard_map/ppermute | solution.py:739
  (34 other events, 113.1 us)
